TPU v7x, 32 devices: a whole 2x2x4 slice. The times are simulated.
32 devices in a mesh: period: 8 (over z, y), refinery: 4 (over x, core).
Axes of the slice: x: 2, y: 2, z: 4, core: 2. Of those that a mesh axis runs over, the one named last changes fastest.
Arguments:
- local_blocks: bfloat16 [3072, 128, 128], P(('period', 'refinery')), may hold values from -0.15625 to 0.15625
- local_rows: int32 [3072], P(('period', 'refinery')), may hold values from 0 to 7
- local_cols: int32 [3072], P(('period', 'refinery')), may hold values from 0 to 7
- band_count: int32 [32], P(('period', 'refinery')), may hold values from 12 to 96, as said below
- swing_blocks: bfloat16 [256, 128, 128], P(('period', 'refinery')), may hold values from -0.5 to 0.5
- swing_rows: int32 [256], P(('period', 'refinery')), may hold values from 0 to 7
- swing_src: int32 [256], P(('period', 'refinery')), may hold values from 0 to 7
- carry_blocks: bfloat16 [32, 128, 128], P(('period', 'refinery')), may hold values from -0.5 to 0.5
- annual_blocks: bfloat16 [256, 128, 128], P(('period', 'refinery')), may hold values from -0.1875 to 0.1875
- annual_ids: int32 [256], P(('period', 'refinery')), may hold values from 0 to 7
- annual_cols: int32 [256], P(('period', 'refinery')), may hold values from 0 to 7
- cost: float32 [32768, 128], P(('period', 'refinery')), may hold values from -6 to 6
- upper: float32 [32768], P(('period', 'refinery')), may hold values from 0.25 to 1.5
- demand: float32 [32768], P(('period', 'refinery')), may hold values from -6 to 6
- annual_bound: float32 [4096], P(('period', 'refinery')), may hold values from -6 to 6
- x_start: float32 [32768, 128], P(('period', 'refinery')), may hold values from 0 to 1
- y_start: float32 [32768, 128], P(('period', 'refinery')), may hold values from 0 to 1
- annual_start: float32 [4096, 128], P(('period', 'refinery')), may hold values from 0 to 1
Outputs:
- primal: float32 [32768, 128], P(('period', 'refinery'))
- dual_rows: float32 [32768, 128], P(('period', 'refinery'))
- annual_dual: float32 [4096, 128], P(('period', 'refinery'))
Inputs may be any that keep to these rules, and one draw needn't show every extreme that they name: `band_count`: live block slots of a group; exactly 96 on one or more groups in every draw.
All inputs are finite; a program needn't handle non-finite values.
Results may differ from a plain program's by a relative error of at most 0.0027.
Values may be sent and summed in bfloat16 or wider, within the bound.
No kernel may reach another device: no remote copies, remote signals or barrier semaphores. Data moves between devices by JAX's collectives and lax.ppermute only.
A program may use at most 128 MiB of HBM per device.

v0:
```python
import jax
import jax.numpy as jnp
from jax import lax
from jax.sharding import PartitionSpec as P

SC = 2
ITERS = 2


PRIMAL_STEP = 0.5
DUAL_STEP = 0.5
PRECISE = lax.Precision.HIGHEST


def shifted(block, axis, distance):
    devices = range(lax.axis_size(axis))
    route = [((i - distance) % len(devices), i) for i in devices]
    return lax.ppermute(block, axis, route)


def selector(index, number):
    return (index[None, :] == jnp.arange(number, dtype=jnp.int32)[:, None]).astype(jnp.float32)


def collect(select, products):
    return jnp.einsum("rn,nas->ras", select, products, precision=PRECISE)


def body(
    local_blocks,
    local_rows,
    local_cols,
    band_count,
    swing_blocks,
    swing_rows,
    swing_src,
    carry_blocks,
    annual_blocks,
    annual_ids,
    annual_cols,
    cost,
    upper,
    demand,
    annual_bound,
    x_start,
    y_start,
    annual_start,
):
    scenarios = cost.shape[1]
    block_size = local_blocks.shape[1]
    columns_count = cost.shape[0] // block_size
    rows_count = y_start.shape[0] // block_size
    slots = local_blocks.shape[0]
    week_count = lax.axis_size("period")
    streams_total = lax.axis_size("refinery") * SC
    live_mask = (jnp.arange(slots, dtype=jnp.int32) < band_count[0]).astype(jnp.float32)
    row_select = selector(local_rows, rows_count) * live_mask[None, :]
    col_select = selector(local_cols, columns_count) * live_mask[None, :]
    swing_select = selector(swing_rows, rows_count)
    annual_select = selector(annual_ids, week_count)
    annual_col_select = selector(annual_cols, columns_count)
    carry = carry_blocks[0]
    stream_select = selector(swing_src, streams_total)
    primal = x_start.reshape(columns_count, block_size, scenarios)
    dual_state = y_start.reshape(rows_count, block_size, scenarios)
    bound_up = upper.reshape(columns_count, block_size, 1)
    prices = cost.reshape(columns_count, block_size, scenarios)
    demand_col = demand.reshape(rows_count, block_size, 1)
    annual = annual_start
    annual_need = annual_bound.reshape(block_size, 1)
    for iteration in range(ITERS):
        dual_q = dual_state.astype(jnp.bfloat16)
        annual_whole = lax.all_gather(
            annual.astype(jnp.bfloat16)[None], "period", axis=0, tiled=True
        )
        swing_products = jnp.einsum(
            "nab,nas->nbs", swing_blocks, dual_q[swing_rows], preferred_element_type=jnp.float32
        )
        returned = lax.psum_scatter(
            collect(stream_select, swing_products), "refinery", scatter_dimension=0, tiled=True
        )
        carried = jnp.dot(carry.T, dual_q[0], preferred_element_type=jnp.float32)
        carried_back = shifted(carried, "period", -1)
        products = jnp.einsum(
            "nab,nas->nbs", local_blocks, dual_q[local_rows], preferred_element_type=jnp.float32
        )
        mapped = collect(col_select, products)
        annual_products = jnp.einsum(
            "nab,nas->nbs",
            annual_blocks,
            annual_whole[annual_ids],
            preferred_element_type=jnp.float32,
        )
        mapped = mapped + collect(annual_col_select, annual_products)
        mapped = mapped.at[:SC].add(returned)
        adjoint = mapped.at[columns_count - 1].add(carried_back)
        updated = jnp.clip(primal - PRIMAL_STEP * (prices - adjoint), 0.0, bound_up)
        extrap = (2.0 * updated - primal).astype(jnp.bfloat16)
        apply_products = jnp.einsum(
            "nab,nbs->nas", local_blocks, extrap[local_cols], preferred_element_type=jnp.float32
        )
        apply_annual_products = jnp.einsum(
            "nab,nbs->nas", annual_blocks, extrap[annual_cols], preferred_element_type=jnp.float32
        )
        annual_terms = collect(annual_select, apply_annual_products)
        annual_image = lax.psum_scatter(annual_terms, "period", scatter_dimension=0, tiled=True)[0]
        streams = lax.all_gather(extrap[:SC], "refinery", axis=0, tiled=True)
        previous = shifted(extrap[columns_count - 1], "period", 1)
        apply_mapped = collect(row_select, apply_products)
        apply_swing_products = jnp.einsum(
            "nab,nbs->nas", swing_blocks, streams[swing_src], preferred_element_type=jnp.float32
        )
        apply_mapped = apply_mapped + collect(swing_select, apply_swing_products)
        apply_mapped = apply_mapped.at[0].add(
            jnp.dot(carry, previous, preferred_element_type=jnp.float32)
        )
        mapped, annual_image = (apply_mapped, annual_image)
        dual_state = jnp.maximum(dual_state + DUAL_STEP * (demand_col - mapped), 0.0)
        annual = jnp.maximum(annual + DUAL_STEP * (annual_need - annual_image), 0.0)
        primal = updated
    return (primal.reshape(-1, scenarios), dual_state.reshape(-1, scenarios), annual)


def solution(mesh):
    return jax.shard_map(
        body,
        mesh=mesh,
        in_specs=(
            P(("period", "refinery"), None, None),
            P(("period", "refinery")),
            P(("period", "refinery")),
            P(("period", "refinery")),
            P(("period", "refinery"), None, None),
            P(("period", "refinery")),
            P(("period", "refinery")),
            P(("period", "refinery"), None, None),
            P(("period", "refinery"), None, None),
            P(("period", "refinery")),
            P(("period", "refinery")),
            P(("period", "refinery"), None),
            P(("period", "refinery")),
            P(("period", "refinery")),
            P(("period", "refinery")),
            P(("period", "refinery"), None),
            P(("period", "refinery"), None),
            P(("period", "refinery"), None),
        ),
        out_specs=(
            P(("period", "refinery"), None),
            P(("period", "refinery"), None),
            P(("period", "refinery"), None),
        ),
        check_vma=False,
    )
```

profile of v0, /device:TPU:0, one launch (start us, length us, event | category | flops | bytes accessed | tf_op | source)
XLA Modules:
  0.0 323.1 jit_solution(1699879179162030868)
XLA Ops:
  10.1 6.0 %collective-permute-start = (f32[128,128]{1,0:T(8,128)}, f32[128,128]{1,0:T(8,128)}, u32[]{:S(2)}, u32[]{:S(2)}) collective-permute-start(f32[128,128]{1,0:T(8,128)} %fusion.10), channel_id=1, source_target_pairs={{4,0},{8,4},{12,8},{16,12},{20,16},{24,20},{28,24},{0,28},{5,1},{9... | collective-permute-start | bytes 196616 | tf_op jit(solution)/shard_map/ppermute | solution.py:18
  25.4 32.8 %all-gather = bf16[1024,128]{1,0:T(8,128)(2,1)} all-gather(bf16[128,128]{1,0:T(8,128)(2,1)S(1)} %convert_element_type.33), channel_id=2, replica_groups=mesh['period'=8,'refinery'=4] {'period'}, dimensions={0}, use_global_device_ids=true | all-gather | bytes 294912 | tf_op jit(solution)/shard_map/all_gather | solution.py:73
  58.2 2.8 gather_fusion
  64.6 5.8 %convolution_bitcast_fusion.3 = f32[96,128,128]{1,2,0:T(8,128)} fusion(bf16[96,128,128]{2,1,0:T(8,128)(2,1)} %gather_fusion, bf16[96,128,128]{2,1,0:T(8,128)(2,1)S(1)} %copy-done), kind=kOutput, calls=%fused_computation.15 | convolution fusion | flops 402653184 | bytes 12582912 | tf_op jit(solution)/shard_map/nab,nas->nbs/dot_general | solution.py:84
  73.2 6.6 %copy.136 = f32[96,128,128]{2,0,1:T(8,128)} copy(f32[96,128,128]{1,2,0:T(8,128)} %convolution_bitcast_fusion.3) | data formatting | bytes 12582912 | tf_op jit(solution)/shard_map/nab,nas->nbs/dot_general | solution.py:84
  79.9 5.1 %fusion.27 = f32[8,128,128]{2,0,1:T(8,128)S(1)} fusion(f32[96,128,128]{2,0,1:T(8,128)} %copy.136, f32[96]{0:T(128)S(1)} %compare_convert_fusion, s32[96]{0:T(128)S(1)} %copy-done.18), kind=kOutput, calls=%fused_computation.79 | convolution fusion | flops 150996480 | bytes 6816512 | tf_op jit(solution)/shard_map/rn,nas->ras/dot_general | solution.py:26
  89.2 2.9 scatter-add.21
  92.1 2.8 subtract_convert_fusion.1
  95.8 6.2 %all_gather.13 = bf16[8,128,128]{2,1,0:T(8,128)(2,1)} all-gather(bf16[2,128,128]{2,1,0:T(8,128)(2,1)S(1)} %copy.150), channel_id=1, replica_groups=mesh['period'=8,'refinery'=4] {'refinery'}, dimensions={0}, use_global_device_ids=true | all-gather | bytes 327680 | tf_op jit(solution)/shard_map/all_gather | solution.py:107
  102.0 2.2 gather_fusion.4
  116.4 2.8 gather_fusion.3
  119.2 6.9 %convolution_bitcast_fusion.2 = f32[96,128,128]{1,2,0:T(8,128)} fusion(bf16[96,128,128]{2,1,0:T(8,128)(2,1)} %gather_fusion.3, bf16[96,128,128]{2,1,0:T(8,128)(2,1)S(1)} %copy-done), kind=kOutput, calls=%fused_computation.14 | convolution fusion | flops 402653184 | bytes 12582912 | tf_op jit(solution)/shard_map/nab,nbs->nas/dot_general | solution.py:99
  126.1 6.6 %copy.149 = f32[96,128,128]{2,0,1:T(8,128)} copy(f32[96,128,128]{1,2,0:T(8,128)} %convolution_bitcast_fusion.2) | data formatting | bytes 12582912 | tf_op jit(solution)/shard_map/nab,nbs->nas/dot_general | solution.py:99
  132.7 5.1 %fusion.21 = f32[8,128,128]{2,0,1:T(8,128)S(1)} fusion(f32[96,128,128]{2,0,1:T(8,128)} %copy.149, s32[96]{0:T(128)S(1)} %copy-done.21, f32[96]{0:T(128)S(1)} %compare_convert_fusion), kind=kOutput, calls=%fused_computation.73 | convolution fusion | flops 150996480 | bytes 6816512 | tf_op jit(solution)/shard_map/rn,nas->ras/dot_general | solution.py:26
  139.3 2.9 scatter-add.24
  146.1 2.9 gather_fusion.5
  149.0 4.7 %collective-permute-start.2 = (f32[128,128]{1,0:T(8,128)}, f32[128,128]{1,0:T(8,128)}, u32[]{:S(2)}, u32[]{:S(2)}) collective-permute-start(f32[128,128]{1,0:T(8,128)} %convolution_bitcast_fusion.12), channel_id=1, source_target_pairs={{4,0},{8,4},{12,8},{16,12},{20,16},{24,20},{28,24},{0,28},{5,1},{9... | collective-permute-start | bytes 196616 | tf_op jit(solution)/shard_map/ppermute | solution.py:18
  160.2 5.7 %convolution_bitcast_fusion.1 = f32[96,128,128]{1,2,0:T(8,128)} fusion(bf16[96,128,128]{2,1,0:T(8,128)(2,1)} %gather_fusion.5, bf16[96,128,128]{2,1,0:T(8,128)(2,1)S(1)} %copy-done), kind=kOutput, calls=%fused_computation.13 | convolution fusion | flops 402653184 | bytes 12582912 | tf_op jit(solution)/shard_map/nab,nas->nbs/dot_general | solution.py:84
  165.9 6.6 %copy.156 = f32[96,128,128]{2,0,1:T(8,128)} copy(f32[96,128,128]{1,2,0:T(8,128)} %convolution_bitcast_fusion.1) | data formatting | bytes 12582912 | tf_op jit(solution)/shard_map/nab,nas->nbs/dot_general | solution.py:84
  172.6 5.8 %fusion.25 = f32[8,128,128]{2,0,1:T(8,128)} fusion(f32[96,128,128]{2,0,1:T(8,128)} %copy.156, f32[96]{0:T(128)S(1)} %compare_convert_fusion, s32[96]{0:T(128)} %param.32), kind=kOutput, calls=%fused_computation.77 | convolution fusion | flops 150996480 | bytes 6816512 | tf_op jit(solution)/shard_map/rn,nas->ras/dot_general | solution.py:26
  181.4 33.0 %all-gather.1 = bf16[1024,128]{1,0:T(8,128)(2,1)} all-gather(bf16[128,128]{1,0:T(8,128)(2,1)S(1)} %fusion.67), channel_id=3, replica_groups=mesh['period'=8,'refinery'=4] {'period'}, dimensions={0}, use_global_device_ids=true | all-gather | bytes 294912 | tf_op jit(solution)/shard_map/all_gather | solution.py:73
  214.3 2.4 gather_fusion.7
  220.8 2.4 convolution_add_fusion.1
  226.1 2.9 scatter-add.26
  229.0 2.6 subtract_convert_fusion
  233.7 2.8 gather_fusion.9
  237.9 5.8 %all_gather.15 = bf16[8,128,128]{2,1,0:T(8,128)(2,1)S(1)} all-gather(bf16[2,128,128]{2,1,0:T(8,128)(2,1)S(1)} %copy.174), channel_id=1, replica_groups=mesh['period'=8,'refinery'=4] {'refinery'}, dimensions={0}, use_global_device_ids=true | all-gather | bytes 327680 | tf_op jit(solution)/shard_map/all_gather | solution.py:107
  251.5 6.9 %convolution_bitcast_fusion = f32[96,128,128]{1,2,0:T(8,128)} fusion(bf16[96,128,128]{2,1,0:T(8,128)(2,1)} %gather_fusion.9, bf16[96,128,128]{2,1,0:T(8,128)(2,1)S(1)} %copy-done), kind=kOutput, calls=%fused_computation.12 | convolution fusion | flops 402653184 | bytes 12582912 | tf_op jit(solution)/shard_map/nab,nbs->nas/dot_general | solution.py:99
  258.4 6.6 %copy.173 = f32[96,128,128]{2,0,1:T(8,128)} copy(f32[96,128,128]{1,2,0:T(8,128)} %convolution_bitcast_fusion) | data formatting | bytes 12582912 | tf_op jit(solution)/shard_map/nab,nbs->nas/dot_general | solution.py:99
  265.0 5.8 %fusion.19 = f32[8,128,128]{2,0,1:T(8,128)} fusion(f32[96,128,128]{2,0,1:T(8,128)} %copy.173, s32[96]{0:T(128)S(1)} %copy-done.22, f32[96]{0:T(128)S(1)} %compare_convert_fusion), kind=kOutput, calls=%fused_computation.71 | convolution fusion | flops 150996480 | bytes 6816512 | tf_op jit(solution)/shard_map/rn,nas->ras/dot_general | solution.py:26
  278.8 2.9 scatter-add.29
  284.4 30.6 %reduce-scatter.11.cloned.1.call-done = f32[1,128,128]{2,1,0:T(8,128)} async-done(((f32[8,128,128]{2,1,0:T(8,128)}), f32[1,128,128]{2,1,0:T(8,128)}) %reduce-scatter.11.cloned.1.call-update) | async-done | bytes 65552 | tf_op jit(solution)/shard_map/reduce_scatter | solution.py:106
  (155 shorter events, 80.2 us)
Async XLA Ops:
  7.2 57.4 %copy-start = (bf16[96,128,128]{2,1,0:T(8,128)(2,1)S(1)}, bf16[96,128,128]{2,1,0:T(8,128)(2,1)}, u32[]{:S(2)}) copy-start(bf16[96,128,128]{2,1,0:T(8,128)(2,1)} %param.30) | copy-start | bytes 9437188
  7.2 15.0 %copy-start.27 = (s32[8]{0:T(128)S(1)}, s32[8]{0:T(128)}, u32[]{:S(2)}) copy-start(s32[8]{0:T(128)} %param.36) | copy-start | bytes 100
  7.2 18.1 %copy-start.28 = (s32[8]{0:T(128)S(1)}, s32[8]{0:T(128)}, u32[]{:S(2)}) copy-start(s32[8]{0:T(128)} %param.39) | copy-start | bytes 100
  7.2 18.1 %copy-start.17 = (s32[96]{0:T(128)S(1)}, s32[96]{0:T(128)}, u32[]{:S(2)}) copy-start(s32[96]{0:T(128)} %param.32) | copy-start | bytes 1156
  7.2 18.1 %copy-start.20 = (s32[96]{0:T(128)S(1)}, s32[96]{0:T(128)}, u32[]{:S(2)}) copy-start(s32[96]{0:T(128)} %param.31) | copy-start | bytes 1156
  7.2 18.2 %copy-start.8 = (f32[128,128]{1,0:T(8,128)S(1)}, f32[128,128]{1,0:T(8,128)}, u32[]{:S(2)}) copy-start(f32[128,128]{1,0:T(8,128)} %param.47) | copy-start | bytes 196612
  7.2 78.9 %reduce-scatter.5.cloned.1.call-start = ((), (), s32[]{:S(2)}) async-start(), calls=%async_computation.4 | async-start | bytes 655360 | tf_op jit(solution)/shard_map/reduce_scatter | solution.py:79
  10.1 77.9 %collective-permute-start = (f32[128,128]{1,0:T(8,128)}, f32[128,128]{1,0:T(8,128)}, u32[]{:S(2)}, u32[]{:S(2)}) collective-permute-start(f32[128,128]{1,0:T(8,128)} %fusion.10), channel_id=1, source_target_pairs={{4,0},{8,4},{12,8},{16,12},{20,16},{24,20},{28,24},{0,28},{5,1},{9... | collective-permute-start | bytes 196616 | tf_op jit(solution)/shard_map/ppermute | solution.py:18
  16.8 8.6 %copy-start.15 = (s32[1024]{0:T(1024)}, s32[1024]{0:T(1024)S(1)}, u32[]{:S(2)}) copy-start(s32[1024]{0:T(1024)S(1)} %pad_clamp_fusion.3) | copy-start | bytes 12292
  24.6 155.9 %reduce-scatter.7.cloned.1.call-start = ((), (), s32[]{:S(2)}) async-start(), calls=%async_computation.5 | async-start | bytes 589824 | tf_op jit(solution)/shard_map/reduce_scatter | solution.py:106
  25.3 35.6 %copy-start.14 = (s32[1024]{0:T(1024)}, s32[1024]{0:T(1024)S(1)}, u32[]{:S(2)}) copy-start(s32[1024]{0:T(1024)S(1)} %pad_clamp_fusion.4) | copy-start | bytes 12292
  25.4 35.6 %copy-start.16 = (s32[1024]{0:T(1024)}, s32[1024]{0:T(1024)S(1)}, u32[]{:S(2)}) copy-start(s32[1024]{0:T(1024)S(1)} %pad_clamp_fusion.5) | copy-start | bytes 12292
  64.6 5.8 %copy-start.25 = (f32[1024]{0:T(1024)S(1)}, f32[1024]{0:T(1024)}, u32[]{:S(2)}) copy-start(f32[1024]{0:T(1024)} %param.42) | copy-start | bytes 12292
  64.6 5.9 %copy-start.26 = (f32[1024]{0:T(1024)S(1)}, f32[1024]{0:T(1024)}, u32[]{:S(2)}) copy-start(f32[1024]{0:T(1024)} %param.43) | copy-start | bytes 12292
  73.2 6.6 %copy-start.18 = (s32[96]{0:T(128)S(1)}, s32[96]{0:T(128)}, u32[]{:S(2)}) copy-start(s32[96]{0:T(128)} %param.32) | copy-start | bytes 1156
  95.7 42.6 %collective-permute-start.1 = (bf16[128,128]{1,0:T(8,128)(2,1)}, bf16[128,128]{1,0:T(8,128)(2,1)}, u32[]{:S(2)}, u32[]{:S(2)}) collective-permute-start(bf16[128,128]{1,0:T(8,128)(2,1)} %bitcast.148), channel_id=1, source_target_pairs={{28,0},{0,4},{4,8},{8,12},{12,16},{16,20},{20,24},{24,28},{29,1},{... | collective-permute-start | bytes 98312 | tf_op jit(solution)/shard_map/ppermute | solution.py:18
  116.2 106.9 %reduce-scatter.9.cloned.1.call-start = ((), (), s32[]{:S(2)}) async-start(), calls=%async_computation.6 | async-start | bytes 655360 | tf_op jit(solution)/shard_map/reduce_scatter | solution.py:79
  126.1 6.6 %copy-start.21 = (s32[96]{0:T(128)S(1)}, s32[96]{0:T(128)}, u32[]{:S(2)}) copy-start(s32[96]{0:T(128)} %param.31) | copy-start | bytes 1156
  132.7 9.5 %copy-start.9 = (f32[8,128]{0,1:T(8,128)S(1)}, f32[8,128]{0,1:T(8,128)}, u32[]{:S(2)}) copy-start(f32[8,128]{0,1:T(8,128)} %copy.145) | copy-start | bytes 12292
  149.0 75.9 %collective-permute-start.2 = (f32[128,128]{1,0:T(8,128)}, f32[128,128]{1,0:T(8,128)}, u32[]{:S(2)}, u32[]{:S(2)}) collective-permute-start(f32[128,128]{1,0:T(8,128)} %convolution_bitcast_fusion.12), channel_id=1, source_target_pairs={{4,0},{8,4},{12,8},{16,12},{20,16},{24,20},{28,24},{0,28},{5,1},{9... | collective-permute-start | bytes 196616 | tf_op jit(solution)/shard_map/ppermute | solution.py:18
  172.6 44.1 %copy-start.2 = (bf16[8,128,128]{2,1,0:T(8,128)(2,1)S(1)}, bf16[8,128,128]{2,1,0:T(8,128)(2,1)}, u32[]{:S(2)}) copy-start(bf16[8,128,128]{2,1,0:T(8,128)(2,1)} %param.38) | copy-start | bytes 786436
  172.6 142.4 %reduce-scatter.11.cloned.1.call-start = ((), (), s32[]{:S(2)}) async-start(), calls=%async_computation.7 | async-start | bytes 589824 | tf_op jit(solution)/shard_map/reduce_scatter | solution.py:106
  236.4 12.7 %copy-start.29 = (s32[8]{0:T(128)S(1)}, s32[8]{0:T(128)}, u32[]{:S(2)}) copy-start(s32[8]{0:T(128)} %param.39) | copy-start | bytes 100
  237.1 40.8 %collective-permute-start.3 = (bf16[128,128]{1,0:T(8,128)(2,1)}, bf16[128,128]{1,0:T(8,128)(2,1)}, u32[]{:S(2)}, u32[]{:S(2)}) collective-permute-start(bf16[128,128]{1,0:T(8,128)(2,1)} %bitcast.147), channel_id=1, source_target_pairs={{28,0},{0,4},{4,8},{8,12},{12,16},{16,20},{20,24},{24,28},{29,1},{... | collective-permute-start | bytes 98312 | tf_op jit(solution)/shard_map/ppermute | solution.py:18
  258.4 6.6 %copy-start.22 = (s32[96]{0:T(128)S(1)}, s32[96]{0:T(128)}, u32[]{:S(2)}) copy-start(s32[96]{0:T(128)} %param.31) | copy-start | bytes 1156
  265.0 5.9 %copy-start.3 = (bf16[8,128,128]{2,1,0:T(8,128)(2,1)S(1)}, bf16[8,128,128]{2,1,0:T(8,128)(2,1)}, u32[]{:S(2)}) copy-start(bf16[8,128,128]{2,1,0:T(8,128)(2,1)} %param.34) | copy-start | bytes 786436
  265.0 5.9 %copy-start.7 = (bf16[8,128,128]{2,1,0:T(8,128)(2,1)S(1)}, bf16[8,128,128]{2,1,0:T(8,128)(2,1)}, u32[]{:S(2)}) copy-start(bf16[8,128,128]{2,1,0:T(8,128)(2,1)} %gather_fusion.10) | copy-start | bytes 786436
  265.0 9.0 %copy-start.24 = (s32[8]{0:T(128)S(1)}, s32[8]{0:T(128)}, u32[]{:S(2)}) copy-start(s32[8]{0:T(128)} %param.35) | copy-start | bytes 100
  270.9 6.9 %copy-start.12 = (bf16[1,128,128]{2,1,0:T(8,128)(2,1)S(1)}, bf16[1,128,128]{2,1,0:T(8,128)(2,1)}, u32[]{:S(2)}) copy-start(bf16[1,128,128]{2,1,0:T(8,128)(2,1)} %param.37) | copy-start | bytes 98308
  270.9 10.8 %copy-start.10 = (f32[8,128]{0,1:T(8,128)S(1)}, f32[8,128]{0,1:T(8,128)}, u32[]{:S(2)}) copy-start(f32[8,128]{0,1:T(8,128)} %copy.145) | copy-start | bytes 12292
  274.0 40.9 %copy-start.13 = (f32[1,128,128]{2,1,0:T(8,128)S(1)}, f32[1,128,128]{2,1,0:T(8,128)}, u32[]{:S(2)}) copy-start(f32[1,128,128]{2,1,0:T(8,128)} %reduce-scatter.7.cloned.1.call-done) | copy-start | bytes 196612
  274.0 40.9 %copy-start.30 = (f32[128]{0:T(128)S(1)}, f32[128]{0:T(128)}, u32[]{:S(2)}) copy-start(f32[128]{0:T(128)} %param.44) | copy-start | bytes 1540
  (7 other events, 30.2 us)
Sparse Core Ops, SparseCore 0:
  24.7 18.8 reduce-scatter.4
  116.3 64.0 reduce-scatter.6
  182.9 20.6 reduce-scatter.8
  251.6 63.2 reduce-scatter.10
where the time goes:
time: 325 us; the launch traced here: 323 us
  local copies, waits for them, and re-layouts  88.9 us (27%)
  matrix products  78.4 us (24%)
  blocking collectives  77.8 us (24%)
  waiting for transfers between devices  32.6 us (10%)
  other arithmetic  19.4 us (6%)
  between operations  14.9 us (5%)
  starting transfers between devices  11.1 us (3%)
    all_gather x2, blocking collectives, body(): lax.all_gather(annual.astype(jnp.bfloat16)[None], 'period', axis=0, tiled...  65.8 us
    dot_general x12, matrix products, collect(): return jnp.einsum('rn,nas->ras', select, products, precision=PRECISE)  33.1 us
    reduce_scatter x2, waiting for transfers between devices, body(): lax.psum_scatter(annual_terms, 'period', scatter_dimension=0, tiled=True)[0]  32.5 us
    dot_general x2, matrix products, body(): jnp.einsum('nab,nbs->nas', local_blocks, extrap[local_cols], preferred_el...  13.7 us
    dot_general x2, local copies, waits for them, and re-layouts, body(): jnp.einsum('nab,nbs->nas', local_blocks, extrap[local_cols], preferred_el...  13.2 us
    dot_general x2, local copies, waits for them, and re-layouts, body(): jnp.einsum('nab,nas->nbs', local_blocks, dual_q[local_rows], preferred_el...  13.2 us
    all_gather x2, blocking collectives, body(): streams = lax.all_gather(extrap[:SC], 'refinery', axis=0, tiled=True)  12 us
    dot_general x2, matrix products, body(): jnp.einsum('nab,nas->nbs', local_blocks, dual_q[local_rows], preferred_el...  11.5 us
  transfers between devices with their start and end apart: 8, of which 2 were waited for; matrix products, arithmetic and copies ran while one was open for 50% of the time, Pallas kernels for 0%

commit v1 on v0

v1 whole, which is shorter than its diff:
```python
import functools

import jax
import jax.numpy as jnp
from jax import lax
from jax.experimental import pallas as pl
from jax.experimental.pallas import tpu as pltpu
from jax.sharding import PartitionSpec as P

SC = 2
ITERS = 2

PRIMAL_STEP = 0.5
DUAL_STEP = 0.5
F32 = jnp.float32
BF16 = jnp.bfloat16
VMEM = pl.BlockSpec(memory_space=pltpu.VMEM)
SMEM = pl.BlockSpec(memory_space=pltpu.SMEM)


def shape(dims, dtype):
    return jax.ShapeDtypeStruct(dims, dtype)


def call(kernel, name, specs, outs, scratch, flops, moved, mib=24):
    return pl.pallas_call(
        kernel,
        name=name,
        in_specs=specs,
        out_specs=tuple(VMEM for _ in outs),
        out_shape=tuple(outs),
        scratch_shapes=scratch,
        compiler_params=pltpu.CompilerParams(vmem_limit_bytes=mib << 20),
        cost_estimate=pl.CostEstimate(flops=flops, bytes_accessed=moved, transcendentals=0),
    )


def dot(a, b):
    return jnp.dot(a, b, preferred_element_type=F32)


def dot_transposed(a, b):
    return dot(a.T, b)


def column_of(row_vector, width):
    return jnp.broadcast_to(row_vector, (width, row_vector.shape[1])).T


def wrap(value, number):
    return jnp.where(value >= number, value - number, value)


def send_duals(refineries, dual_q, me, rows, src, swing, carry, own, sends, carried, acc):
    acc[...] = jnp.zeros_like(acc)
    for m in range(swing.shape[0]):
        acc[src[m]] += dot_transposed(swing[m], dual_q[rows[m]])
    own[...] = acc[pl.ds(me * SC, SC)]
    for d, send in enumerate(sends, 1):
        send[...] = acc[pl.ds(wrap(me + d, refineries) * SC, SC)].astype(BF16)
    carried[...] = dot_transposed(carry[0], dual_q[0]).astype(BF16)


def first_duals_kernel(refineries, me, rows, src, swing, carry, dual, *refs):
    sends = refs[1:refineries]
    own, carried, dual_q, acc = refs[0], *refs[refineries:]
    size = swing.shape[1]
    for i in range(dual_q.shape[0]):
        dual_q[i] = dual[i * size : (i + 1) * size].astype(BF16)
    send_duals(refineries, dual_q, me[0], rows, src, swing, carry, own, sends, carried, acc)


def dense_kernel(count, rows, cols, blocks, upper, high, low, upper_full, acc):
    size = blocks.shape[1]
    width = upper_full.shape[1]
    tiles = high.shape[1] // size
    acc[...] = jnp.zeros_like(acc)

    def step(n, _):
        acc[rows[n] * tiles + cols[n]] += blocks[n].astype(F32)
        return 0

    lax.fori_loop(0, count[0], step, 0)
    for i in range(high.shape[0] // size):
        for j in range(tiles):
            whole = acc[i * tiles + j]
            top = whole.astype(BF16)
            high[i * size : (i + 1) * size, j * size : (j + 1) * size] = top
            low[i * size : (i + 1) * size, j * size : (j + 1) * size] = (
                whole - top.astype(F32)
            ).astype(BF16)
    for j in range(tiles):
        upper_full[j * size : (j + 1) * size] = column_of(upper[j : j + 1], width)


def adjoint_kernel(high, low, dual_q, primal, prices, out):
    blocks, size, _ = dual_q.shape
    turned = jnp.concatenate([dual_q[i].T for i in range(blocks)], axis=1)
    step = 2 * size
    for j in range(high.shape[1] // step):
        part = dot(turned, high[:, j * step : (j + 1) * step]) + dot(
            turned, low[:, j * step : (j + 1) * step]
        )
        for h in range(2):
            at = slice(j * step + h * size, j * step + (h + 1) * size)
            out[at] = primal[at] - PRIMAL_STEP * (
                prices[at] - part[:, h * size : (h + 1) * size].T
            )


def primal_kernel(
    refineries, ids, cols, annual, annual_q, own, carried, partial, primal, upper_full, *refs
):
    arrived = refs[: refineries - 1]
    updated, extrap, streams, last, image, acc, image_acc = refs[refineries - 1 :]
    blocks, size, _ = extrap.shape
    acc[...] = jnp.zeros_like(acc)
    image_acc[...] = jnp.zeros_like(image_acc)
    slots = annual.shape[0]
    for k in range(slots):
        acc[cols[k]] += dot_transposed(annual[k], annual_q[ids[k]])
    total = own[...]
    for piece in arrived:
        total = total + piece[...].astype(F32)
    acc[:SC] += total
    acc[blocks - 1] += carried[...].astype(F32)
    for j in range(blocks):
        at = slice(j * size, (j + 1) * size)
        new = jnp.clip(partial[at] + PRIMAL_STEP * acc[j], 0.0, upper_full[at])
        updated[at] = new
        ahead = (2.0 * new - primal[at]).astype(BF16)
        extrap[j] = ahead
        if j < SC:
            streams[j] = ahead
        if j == blocks - 1:
            last[...] = ahead
    for k in range(slots):
        image_acc[ids[k]] += dot(annual[k], extrap[cols[k]])
    image[...] = image_acc[...].astype(BF16)


def forward_kernel(high, low, extrap, dual, demand, out):
    blocks, size, width = extrap.shape
    right = jnp.concatenate([extrap[j] for j in range(blocks)], axis=0)
    step = 2 * size
    for i in range(high.shape[0] // step):
        part = dot(high[i * step : (i + 1) * step], right) + dot(
            low[i * step : (i + 1) * step], right
        )
        for h in range(2):
            at = slice(i * step + h * size, i * step + (h + 1) * size)
            row = 2 * i + h
            out[at] = dual[at] + DUAL_STEP * (
                column_of(demand[row : row + 1], width) - part[h * size : (h + 1) * size]
            )


def dual_kernel(
    refineries, more, me, rows, src, swing, carry, partial, previous, streams, *refs
):
    arrived = refs[: refineries - 1]
    refs = refs[refineries - 1 :]
    dual = refs[0]
    gathered, acc = refs[-2:]
    size = swing.shape[1]
    blocks = dual.shape[0] // size
    mine = me[0]
    gathered[pl.ds(mine * SC, SC)] = streams[...]
    for d, piece in enumerate(arrived, 1):
        gathered[pl.ds(wrap(mine + refineries - d, refineries) * SC, SC)] = piece[...]
    acc[...] = jnp.zeros_like(acc)
    for m in range(swing.shape[0]):
        acc[rows[m]] += dot(swing[m], gathered[src[m]])
    acc[0] += dot(carry[0], previous[...])
    for i in range(blocks):
        at = slice(i * size, (i + 1) * size)
        dual[at] = jnp.maximum(partial[at] - DUAL_STEP * acc[i], 0.0)
    if more:
        own = refs[1]
        sends = refs[2 : refineries + 1]
        carried, dual_q, stream_acc = refs[refineries + 1 : refineries + 4]
        for i in range(blocks):
            dual_q[i] = dual[i * size : (i + 1) * size].astype(BF16)
        send_duals(refineries, dual_q, mine, rows, src, swing, carry, own, sends, carried, stream_acc)


def annual_kernel(more, annual, need, parts, *outs):
    total = parts[0].astype(F32)
    for w in range(1, parts.shape[0]):
        total = total + parts[w].astype(F32)
    new = jnp.maximum(
        annual[...] + DUAL_STEP * (column_of(need[...], annual.shape[1]) - total), 0.0
    )
    outs[0][...] = new
    if more:
        rounded = new.astype(BF16)
        for w in range(outs[1].shape[0]):
            outs[1][w] = rounded


def shifted(block, axis, distance):
    number = lax.axis_size(axis)
    route = [((i - distance) % number, i) for i in range(number)]
    return lax.ppermute(block, axis, route)


def body(
    local_blocks,
    local_rows,
    local_cols,
    band_count,
    swing_blocks,
    swing_rows,
    swing_src,
    carry_blocks,
    annual_blocks,
    annual_ids,
    annual_cols,
    cost,
    upper,
    demand,
    annual_bound,
    x_start,
    y_start,
    annual_start,
):
    scenarios = cost.shape[1]
    size = local_blocks.shape[1]
    columns = cost.shape[0] // size
    rows = y_start.shape[0] // size
    weeks = lax.axis_size("period")
    refineries = lax.axis_size("refinery")
    others = refineries - 1
    streams_total = refineries * SC
    me = lax.axis_index("refinery").astype(jnp.int32).reshape(1)
    block = size * scenarios
    tile = shape((size, scenarios), BF16)
    pair_q = shape((SC, size, scenarios), BF16)
    pair = shape((SC, size, scenarios), F32)
    state_x = shape((columns * size, scenarios), F32)
    state_y = shape((rows * size, scenarios), F32)
    blocks_x = shape((columns, size, scenarios), BF16)
    blocks_y = shape((rows, size, scenarios), BF16)
    weekly = shape((weeks, size, scenarios), BF16)
    swings = swing_blocks.shape[0]
    annuals = annual_blocks.shape[0]
    unit = 2 * size * size * scenarios
    duals_scratch = pltpu.VMEM((streams_total, size, scenarios), F32)

    first_duals = call(
        functools.partial(first_duals_kernel, refineries),
        "first_duals",
        [SMEM] * 3 + [VMEM] * 3,
        [pair] + [pair_q] * others + [tile, blocks_y],
        [duals_scratch],
        (swings + 1) * unit,
        2_000_000,
    )
    dense = call(
        dense_kernel,
        "dense",
        [SMEM] * 3 + [VMEM] * 2,
        [shape((rows * size, columns * size), BF16)] * 2 + [state_x],
        [pltpu.VMEM((rows * columns, size, size), F32)],
        unit,
        8_000_000,
    )
    adjoint = call(
        adjoint_kernel,
        "adjoint",
        [VMEM] * 5,
        [state_x],
        [],
        2 * rows * columns * unit,
        5_000_000,
    )
    primal_step = call(
        functools.partial(primal_kernel, refineries),
        "primal_step",
        [SMEM] * 2 + [VMEM] * (7 + others),
        [state_x, blocks_x, pair_q, tile, weekly],
        [pltpu.VMEM((columns, size, scenarios), F32), pltpu.VMEM((weeks, size, scenarios), F32)],
        2 * annuals * unit,
        3_000_000,
    )
    forward = call(
        forward_kernel,
        "forward",
        [VMEM] * 5,
        [state_y],
        [],
        2 * rows * columns * unit,
        5_000_000,
    )

    def dual_step(more):
        sends = [pair] + [pair_q] * others + [tile, blocks_y] if more else []
        scratch = [pltpu.VMEM((streams_total, size, scenarios), BF16), pltpu.VMEM((rows, size, scenarios), F32)]
        return call(
            functools.partial(dual_kernel, refineries, more),
            "dual_step",
            [SMEM] * 3 + [VMEM] * (5 + others),
            [state_y] + sends,
            ([duals_scratch] if more else []) + scratch,
            2 * swings * unit,
            2_000_000,
        )

    def annual_step(more):
        return call(
            functools.partial(annual_kernel, more),
            "annual_step",
            [VMEM] * 3,
            [shape((size, scenarios), F32)] + ([weekly] if more else []),
            [],
            block,
            1_000_000,
        )

    upper_rows = upper.reshape(columns, size)
    demand_rows = demand.reshape(rows, size)
    need = annual_bound.reshape(1, size)
    primal, dual, annual = x_start, y_start, annual_start
    annual_send = jnp.broadcast_to(annual.astype(BF16)[None], (weeks, size, scenarios))
    own, *rest = first_duals(me, swing_rows, swing_src, swing_blocks, carry_blocks, dual)
    sends, carried, dual_q = rest[:others], rest[others], rest[others + 1]
    high, low, upper_full = dense(band_count, local_rows, local_cols, local_blocks, upper_rows)
    for iteration in range(ITERS):
        more = iteration + 1 < ITERS
        annual_q = lax.all_to_all(annual_send, "period", 0, 0, tiled=True)
        arrived = [shifted(send, "refinery", d) for d, send in enumerate(sends, 1)]
        carried_back = shifted(carried, "period", -1)
        (partial_x,) = adjoint(high, low, dual_q, primal, cost)
        updated, extrap, streams, last, image = primal_step(
            annual_ids, annual_cols, annual_blocks, annual_q, own, carried_back,
            partial_x, primal, upper_full, *arrived,
        )
        parts = lax.all_to_all(image, "period", 0, 0, tiled=True)
        others_streams = [shifted(streams, "refinery", d) for d in range(1, refineries)]
        previous = shifted(last, "period", 1)
        (partial_y,) = forward(high, low, extrap, dual, demand_rows)
        dual, *rest = dual_step(more)(
            me, swing_rows, swing_src, swing_blocks, carry_blocks,
            partial_y, previous, streams, *others_streams,
        )
        if more:
            own, sends, carried, dual_q = rest[0], rest[1:refineries], rest[refineries], rest[refineries + 1]
            annual, annual_send = annual_step(more)(annual, need, parts)
        else:
            (annual,) = annual_step(more)(annual, need, parts)
        primal = updated
    return primal, dual, annual


def solution(mesh):
    both = P(("period", "refinery"))
    wide = P(("period", "refinery"), None)
    cube = P(("period", "refinery"), None, None)
    return jax.shard_map(
        body,
        mesh=mesh,
        in_specs=(
            cube, both, both, both, cube, both, both, cube, cube, both, both,
            wide, both, both, both, wide, wide, wide,
        ),
        out_specs=(wide, wide, wide),
        check_vma=False,
    )
```

time: 325 us -> 109 us (0.34)
  matrix products: 78.4 us -> 0 us
  blocking collectives: 77.8 us -> 10.7 us
  local copies, waits for them, and re-layouts: 88.9 us -> 38.7 us
  waiting for transfers between devices: 32.6 us -> 5.73 us
  starting transfers between devices: 11.1 us -> 33.8 us
  other arithmetic: 19.4 us -> 0.85 us
  Pallas kernels: 0 us -> 15.5 us
  between operations: 14.9 us -> 1.63 us
    dot_general x28 -> x0, matrix products: 78.4 us -> none  [the longest x12 33.1 us: collect(): return jnp.einsum('rn,nas->ras', select, products, precision=PRECISE)]
    all_gather x4 -> x0, blocking collectives: 77.8 us -> none  [the longest x2 65.8 us: body(): lax.all_gather(annual.astype(jnp.bfloat16)[None], 'period', axis=0, tiled...]
    dot_general x16 -> x0, local copies, waits for them, and re-layouts: 46.4 us -> none  [the longest x2 13.2 us: body(): jnp.einsum('nab,nbs->nas', local_blocks, extrap[local_cols], preferred_el...]
    unnamed x64 -> x134, local copies, waits for them, and re-layouts: 1.38 us -> 37.9 us
    reduce_scatter x4 -> x0, waiting for transfers between devices: 32.5 us -> none  [the longest x2 32.5 us: body(): lax.psum_scatter(annual_terms, 'period', scatter_dimension=0, tiled=True)[0]]
    gather x12 -> x0, local copies, waits for them, and re-layouts: 23.8 us -> none  [the longest x2 5.63 us: body(): dual_q[local_rows]]
    all_to_all x0 -> x3, starting transfers between devices: none -> 15.8 us  [the longest x2 11.5 us: body(): annual_q = lax.all_to_all(annual_send, 'period', 0, 0, tiled=True)]
    pallas_call x0 -> x12, Pallas kernels: none -> 15.5 us  [the longest x2 3.8 us: body(): primal_step(annual_ids, annual_cols, annual_blocks, annual_q, own, carrie...]
  transfers between devices with their start and end apart: 8 -> 19, of which waited for: 2 -> 3; matrix products, arithmetic and copies ran while one was open for 50% -> 0% of each run, Pallas kernels for 0% -> 10%
where the time goes in v1:
time: 109 us; the launch traced here: 107 us
  local copies, waits for them, and re-layouts  38.7 us (36%)
  starting transfers between devices  33.8 us (31%)
  Pallas kernels  15.5 us (14%)
  blocking collectives  10.7 us (10%)
  waiting for transfers between devices  5.73 us (5%)
  between operations  1.63 us (1%)
    unnamed x134, local copies, waits for them, and re-layouts  37.9 us
    ppermute x16, starting transfers between devices, shifted(): return lax.ppermute(block, axis, route)  18 us
    all_to_all x2, starting transfers between devices, body(): annual_q = lax.all_to_all(annual_send, 'period', 0, 0, tiled=True)  11.5 us
    all_to_all x1, blocking collectives, body(): parts = lax.all_to_all(image, 'period', 0, 0, tiled=True)  10.7 us
    ppermute x16, waiting for transfers between devices, shifted(): return lax.ppermute(block, axis, route)  5.72 us
    all_to_all x1, starting transfers between devices, body(): parts = lax.all_to_all(image, 'period', 0, 0, tiled=True)  4.31 us
    pallas_call x2, Pallas kernels, body(): primal_step(annual_ids, annual_cols, annual_blocks, annual_q, own, carrie...  3.8 us
    pallas_call x2, Pallas kernels, body(): dual_step(more)  2.84 us
  transfers between devices with their start and end apart: 19, of which 3 were waited for; matrix products, arithmetic and copies ran while one was open for 0% of the time, Pallas kernels for 10%

profile of v1, /device:TPU:0, one launch (start us, length us, event | category | flops | bytes accessed | tf_op | source)
XLA Modules:
  0.0 106.9 jit_solution(5014448047181987946)
XLA Ops:
  2.2 7.4 %all-to-all-start = ((bf16[8,128,128]{2,1,0:T(8,128)(2,1)}), bf16[8,128,128]{2,1,0:T(8,128)(2,1)}, u32[]{:S(2)}, u32[]{:S(2)}) async-start(bf16[8,128,128]{2,1,0:T(8,128)(2,1)} %broadcast_in_dim.2), calls=%async_computation | async-start | bytes 524288 | tf_op jit(solution)/shard_map/all_to_all | solution.py:330
  10.6 1.0 copy-done.8
  15.2 1.5 %collective-permute-start.2 = (bf16[2,128,128]{2,1,0:T(8,128)(2,1)S(1)}, bf16[2,128,128]{2,1,0:T(8,128)(2,1)S(1)}, u32[]{:S(2)}, u32[]{:S(2)}) collective-permute-start(bf16[2,128,128]{2,1,0:T(8,128)(2,1)S(1)} %get-tuple-element.38), channel_id=1, source_target_pairs={{2,0},{3,1},{0,2},{1,3},{6,4},{7,5},{4,6},{5,7},{10,8},{11,9},{8,1... | collective-permute-start | bytes 196616 | tf_op jit(solution)/shard_map/ppermute | solution.py:204
  16.8 1.4 %collective-permute-start.3 = (bf16[2,128,128]{2,1,0:T(8,128)(2,1)S(1)}, bf16[2,128,128]{2,1,0:T(8,128)(2,1)S(1)}, u32[]{:S(2)}, u32[]{:S(2)}) collective-permute-start(bf16[2,128,128]{2,1,0:T(8,128)(2,1)S(1)} %get-tuple-element.39), channel_id=1, source_target_pairs={{1,0},{2,1},{3,2},{0,3},{5,4},{6,5},{7,6},{4,7},{9,8},{10,9},{11,1... | collective-permute-start | bytes 196616 | tf_op jit(solution)/shard_map/ppermute | solution.py:204
  18.2 4.7 %collective-permute-start = (bf16[128,128]{1,0:T(8,128)(2,1)S(1)}, bf16[128,128]{1,0:T(8,128)(2,1)S(1)}, u32[]{:S(2)}, u32[]{:S(2)}) collective-permute-start(bf16[128,128]{1,0:T(8,128)(2,1)S(1)} %get-tuple-element.32), channel_id=1, source_target_pairs={{4,0},{8,4},{12,8},{16,12},{20,16},{24,20},{28,24},{0,28},{5,1},{9... | collective-permute-start | bytes 98312 | tf_op jit(solution)/shard_map/ppermute | solution.py:204
  23.6 1.9 %copy-done.4 = bf16[96,128,128]{2,1,0:T(8,128)(2,1)S(1)} copy-done((bf16[96,128,128]{2,1,0:T(8,128)(2,1)S(1)}, bf16[96,128,128]{2,1,0:T(8,128)(2,1)}, u32[]{:S(2)}) %copy-start.4) | copy-done | bytes 3145752
  27.5 2.2 %dense.1 = (bf16[1024,1024]{1,0:T(8,128)(2,1)S(1)}, bf16[1024,1024]{1,0:T(8,128)(2,1)S(1)}, f32[1024,128]{1,0:T(8,128)S(1)}) custom-call(s32[1]{0:T(128)S(6)} %copy.21.count, s32[96]{0:T(128)S(1)} %copy-done.63, s32[96]{0:T(128)S(1)} %copy-done.64, bf16[96,128,128]{2,1,0:T(8,128)(2,1)S(1)} %copy-done.4, f32[8,128]{1,0:T(8,128)S(1)} %bitcast.6), custom_call_target="tpu_custom_call" | custom-call | flops 4194304 | bytes 8000000 | tf_op jit(solution)/shard_map/dense/pallas_call | solution.py:327
  36.2 1.0 copy-done.16
  37.2 1.0 copy-done.20
  42.4 1.6 %primal_step.2 = (f32[1024,128]{1,0:T(8,128)S(1)}, bf16[8,128,128]{2,1,0:T(8,128)(2,1)S(1)}, bf16[2,128,128]{2,1,0:T(8,128)(2,1)S(1)}, bf16[128,128]{1,0:T(8,128)(2,1)S(1)}, bf16[8,128,128]{2,1,0:T(8,128)(2,1)S(1)}) custom-call(s32[8]{0:T(128)S(1)} %copy-done.58, s32[8]{0:T(128)S(1)} %copy-done.59, bf16[8,128,128]{2,1,0:T(8,128)(2,1)S(1)} %copy-done.22, ...), custom_call_target="tpu_custom_call" | custom-call | flops 67108864 | bytes 3000000 | tf_op jit(solution)/shard_map/primal_step/pallas_call | solution.py:334
  44.9 10.7 %all_to_all.20.parts = bf16[8,128,128]{2,1,0:T(8,128)(2,1)S(1)} all-to-all(bf16[8,128,128]{2,1,0:T(8,128)(2,1)S(1)} %get-tuple-element.40), channel_id=1, replica_groups=mesh['period'=8,'refinery'=4] {'period'}, dimensions={0} | all-to-all | bytes 524288 | tf_op jit(solution)/shard_map/all_to_all | solution.py:338
  57.0 4.0 %all-to-all-start.2 = ((bf16[8,128,128]{2,1,0:T(8,128)(2,1)}), bf16[8,128,128]{2,1,0:T(8,128)(2,1)}, u32[]{:S(2)}, u32[]{:S(2)}) async-start(bf16[8,128,128]{2,1,0:T(8,128)(2,1)} %get-tuple-element.41), calls=%async_computation.2 | async-start | bytes 524288 | tf_op jit(solution)/shard_map/all_to_all | solution.py:330
  61.2 1.4 %collective-permute-start.6 = (bf16[2,128,128]{2,1,0:T(8,128)(2,1)S(1)}, bf16[2,128,128]{2,1,0:T(8,128)(2,1)S(1)}, u32[]{:S(2)}, u32[]{:S(2)}) collective-permute-start(bf16[2,128,128]{2,1,0:T(8,128)(2,1)S(1)} %get-tuple-element.44.streams), channel_id=1, source_target_pairs={{2,0},{3,1},{0,2},{1,3},{6,4},{7,5},{4,6},{5,7},{10,8},{11,9},{8,1... | collective-permute-start | bytes 196616 | tf_op jit(solution)/shard_map/ppermute | solution.py:204
  62.7 1.8 %collective-permute-start.4 = (bf16[128,128]{1,0:T(8,128)(2,1)}, bf16[128,128]{1,0:T(8,128)(2,1)S(1)}, u32[]{:S(2)}, u32[]{:S(2)}) collective-permute-start(bf16[128,128]{1,0:T(8,128)(2,1)} %copy-done.66), channel_id=1, source_target_pairs={{28,0},{0,4},{4,8},{8,12},{12,16},{16,20},{20,24},{24,28},{29,1},{... | collective-permute-start | bytes 98312 | tf_op jit(solution)/shard_map/ppermute | solution.py:204
  64.6 1.6 %copy-done.1 = bf16[1024,1024]{1,0:T(8,128)(2,1)S(1)} copy-done((bf16[1024,1024]{1,0:T(8,128)(2,1)S(1)}, bf16[1024,1024]{1,0:T(8,128)(2,1)}, u32[]{:S(2)}) %copy-start.1) | copy-done | bytes 2097176
  67.2 1.3 %forward.2.partial = f32[1024,128]{1,0:T(8,128)S(1)} custom-call(bf16[1024,1024]{1,0:T(8,128)(2,1)S(1)} %get-tuple-element.33.high, bf16[1024,1024]{1,0:T(8,128)(2,1)S(1)} %copy-done.1, bf16[8,128,128]{2,1,0:T(8,128)(2,1)S(1)} %copy-done.29, f32[1024,128]{1,0:T(8,128)S(1)} %copy-done.9, f32[8,128]{1,0:T(8,128)S(1)} %bitcast.4), custom_call_target="tpu_custom_call" | custom-call | flops 536870912 | bytes 5000000 | tf_op jit(solution)/shard_map/forward/pallas_call | solution.py:341
  68.4 1.9 %collective-permute-done.4.previous = bf16[128,128]{1,0:T(8,128)(2,1)S(1)} collective-permute-done((bf16[128,128]{1,0:T(8,128)(2,1)}, bf16[128,128]{1,0:T(8,128)(2,1)S(1)}, u32[]{:S(2)}, u32[]{:S(2)}) %collective-permute-start.4) | collective-permute-done | bytes 32800 | tf_op jit(solution)/shard_map/ppermute | solution.py:204
  70.3 1.2 %dual_step.2 = (f32[1024,128]{1,0:T(8,128)S(1)}, f32[2,128,128]{2,1,0:T(8,128)S(1)}, bf16[2,128,128]{2,1,0:T(8,128)(2,1)S(1)}, bf16[2,128,128]{2,1,0:T(8,128)(2,...) custom-call(s32[1]{0:T(128)} %bitcast.1.me, ...), custom_call_target="tpu_custom_call" | custom-call | flops 67108864 | bytes 2000000 | tf_op jit(solution)/shard_map/dual_step/pallas_call | solution.py:342
  72.2 1.7 %collective-permute-start.10 = (bf16[2,128,128]{2,1,0:T(8,128)(2,1)S(1)}, bf16[2,128,128]{2,1,0:T(8,128)(2,1)S(1)}, u32[]{:S(2)}, u32[]{:S(2)}) collective-permute-start(bf16[2,128,128]{2,1,0:T(8,128)(2,1)S(1)} %get-tuple-element.50), channel_id=1, source_target_pairs={{2,0},{3,1},{0,2},{1,3},{6,4},{7,5},{4,6},{5,7},{10,8},{11,9},{8,1... | collective-permute-start | bytes 196616 | tf_op jit(solution)/shard_map/ppermute | solution.py:204
  73.9 1.4 %collective-permute-start.11 = (bf16[2,128,128]{2,1,0:T(8,128)(2,1)S(1)}, bf16[2,128,128]{2,1,0:T(8,128)(2,1)S(1)}, u32[]{:S(2)}, u32[]{:S(2)}) collective-permute-start(bf16[2,128,128]{2,1,0:T(8,128)(2,1)S(1)} %get-tuple-element.51), channel_id=1, source_target_pairs={{1,0},{2,1},{3,2},{0,3},{5,4},{6,5},{7,6},{4,7},{9,8},{10,9},{11,1... | collective-permute-start | bytes 196616 | tf_op jit(solution)/shard_map/ppermute | solution.py:204
  77.3 1.9 %collective-permute-done.8.carried = bf16[128,128]{1,0:T(8,128)(2,1)S(1)} collective-permute-done((bf16[128,128]{1,0:T(8,128)(2,1)S(1)}, bf16[128,128]{1,0:T(8,128)(2,1)S(1)}, u32[]{:S(2)}, u32[]{:S(2)}) %collective-permute-start.8) | collective-permute-done | bytes 32800 | tf_op jit(solution)/shard_map/ppermute | solution.py:204
  80.5 1.0 copy-done.18
  81.5 1.0 copy-done.21
  86.8 2.2 %primal_step.3 = (f32[1024,128]{1,0:T(8,128)}, bf16[8,128,128]{2,1,0:T(8,128)(2,1)S(1)}, bf16[2,128,128]{2,1,0:T(8,128)(2,1)S(1)}, bf16[128,128]{1,0:T(8,128)(2,1)S(1)}, bf16[8,128,128]{2,1,0:T(8,128)(2,1)S(1)}) custom-call(s32[8]{0:T(128)S(1)} %copy-done.58, s32[8]{0:T(128)S(1)} %copy-done.60, bf16[8,128,128]{2,1,0:T(8,128)(2,1)S(1)} %copy-done.23, ...), custom_call_target="tpu_custom_call" | custom-call | flops 67108864 | bytes 3000000 | tf_op jit(solution)/shard_map/primal_step/pallas_call | solution.py:334
  90.9 4.3 %all-to-all-start.3 = ((bf16[8,128,128]{2,1,0:T(8,128)(2,1)}), bf16[8,128,128]{2,1,0:T(8,128)(2,1)S(1)}, u32[]{:S(2)}, u32[]{:S(2)}) async-start(bf16[8,128,128]{2,1,0:T(8,128)(2,1)} %copy-done.31), calls=%async_computation.3 | async-start | bytes 524288 | tf_op jit(solution)/shard_map/all_to_all | solution.py:338
  95.2 1.3 %collective-permute-start.14 = (bf16[2,128,128]{2,1,0:T(8,128)(2,1)}, bf16[2,128,128]{2,1,0:T(8,128)(2,1)S(1)}, u32[]{:S(2)}, u32[]{:S(2)}) collective-permute-start(bf16[2,128,128]{2,1,0:T(8,128)(2,1)} %copy-done.48), channel_id=1, source_target_pairs={{2,0},{3,1},{0,2},{1,3},{6,4},{7,5},{4,6},{5,7},{10,8},{11,9},{8,1... | collective-permute-start | bytes 196616 | tf_op jit(solution)/shard_map/ppermute | solution.py:204
  96.6 2.0 %collective-permute-start.12 = (bf16[128,128]{1,0:T(8,128)(2,1)}, bf16[128,128]{1,0:T(8,128)(2,1)S(1)}, u32[]{:S(2)}, u32[]{:S(2)}) collective-permute-start(bf16[128,128]{1,0:T(8,128)(2,1)} %copy-done.65), channel_id=1, source_target_pairs={{28,0},{0,4},{4,8},{8,12},{12,16},{16,20},{20,24},{24,28},{29,1},{... | collective-permute-start | bytes 98312 | tf_op jit(solution)/shard_map/ppermute | solution.py:204
  98.7 1.6 %copy-done.3 = bf16[1024,1024]{1,0:T(8,128)(2,1)S(1)} copy-done((bf16[1024,1024]{1,0:T(8,128)(2,1)S(1)}, bf16[1024,1024]{1,0:T(8,128)(2,1)}, u32[]{:S(2)}) %copy-start.3) | copy-done | bytes 2097176
  100.2 1.0 copy-done.25
  101.3 1.2 %forward.3.partial = f32[1024,128]{1,0:T(8,128)S(1)} custom-call(bf16[1024,1024]{1,0:T(8,128)(2,1)S(1)} %get-tuple-element.33.high, bf16[1024,1024]{1,0:T(8,128)(2,1)S(1)} %copy-done.3, bf16[8,128,128]{2,1,0:T(8,128)(2,1)S(1)} %get-tuple-element.53.extrap, f32[1024,128]{1,0:T(8,128)S(1)} %copy-done.25, f32[8,128]{1,0:T(8,128)S(1)} %bitcast.5), custom_call_target="tpu_custom_call" | custom-call | flops 536870912 | bytes 5000000 | tf_op jit(solution)/shard_map/forward/pallas_call | solution.py:341
  102.5 1.9 %collective-permute-done.12.previous = bf16[128,128]{1,0:T(8,128)(2,1)S(1)} collective-permute-done((bf16[128,128]{1,0:T(8,128)(2,1)}, bf16[128,128]{1,0:T(8,128)(2,1)S(1)}, u32[]{:S(2)}, u32[]{:S(2)}) %collective-permute-start.12) | collective-permute-done | bytes 32800 | tf_op jit(solution)/shard_map/ppermute | solution.py:204
  104.5 1.7 %dual_step.3 = f32[1024,128]{1,0:T(8,128)} custom-call(s32[1]{0:T(128)} %bitcast.1.me, s32[8]{0:T(128)S(1)} %copy-done.54, s32[8]{0:T(128)S(1)} %copy-done.56, bf16[8,128,128]{2,1,0:T(8,128)(2,1)S(1)} %copy-done.6, bf16[1,128,128]{2,1,0:T(8,128)(2,1)S(1)} %copy-done.27, f32[1024,128]{1,0:T(8,128)S(1)} %forward.3.partial, ...), custom_call_target="tpu_custom_call" | custom-call | flops 67108864 | bytes 2000000 | tf_op jit(solution)/shard_map/dual_step/pallas_call | solution.py:342
  (155 shorter events, 33.1 us)
Async XLA Ops:
  2.2 28.3 %copy-start.7 = (f32[1024,128]{1,0:T(8,128)S(1)}, f32[1024,128]{1,0:T(8,128)}, u32[]{:S(2)}) copy-start(f32[1024,128]{1,0:T(8,128)} %prices.3) | copy-start | bytes 1572868
  2.2 32.9 %all-to-all-start = ((bf16[8,128,128]{2,1,0:T(8,128)(2,1)}), bf16[8,128,128]{2,1,0:T(8,128)(2,1)}, u32[]{:S(2)}, u32[]{:S(2)}) async-start(bf16[8,128,128]{2,1,0:T(8,128)(2,1)} %broadcast_in_dim.2), calls=%async_computation | async-start | bytes 524288 | tf_op jit(solution)/shard_map/all_to_all | solution.py:330
  13.7 16.8 %copy-start.10 = (f32[1024,128]{1,0:T(8,128)S(1)}, f32[1024,128]{1,0:T(8,128)}, u32[]{:S(2)}) copy-start(f32[1024,128]{1,0:T(8,128)} %primal.3) | copy-start | bytes 1572868
  15.2 18.0 %collective-permute-start.1 = (bf16[2,128,128]{2,1,0:T(8,128)(2,1)S(1)}, bf16[2,128,128]{2,1,0:T(8,128)(2,1)S(1)}, u32[]{:S(2)}, u32[]{:S(2)}) collective-permute-start(bf16[2,128,128]{2,1,0:T(8,128)(2,1)S(1)} %get-tuple-element.37), channel_id=1, source_target_pairs={{3,0},{0,1},{1,2},{2,3},{7,4},{4,5},{5,6},{6,7},{11,8},{8,9},{9,10... | collective-permute-start | bytes 196616 | tf_op jit(solution)/shard_map/ppermute | solution.py:204
  15.2 18.6 %collective-permute-start.2 = (bf16[2,128,128]{2,1,0:T(8,128)(2,1)S(1)}, bf16[2,128,128]{2,1,0:T(8,128)(2,1)S(1)}, u32[]{:S(2)}, u32[]{:S(2)}) collective-permute-start(bf16[2,128,128]{2,1,0:T(8,128)(2,1)S(1)} %get-tuple-element.38), channel_id=1, source_target_pairs={{2,0},{3,1},{0,2},{1,3},{6,4},{7,5},{4,6},{5,7},{10,8},{11,9},{8,1... | collective-permute-start | bytes 196616 | tf_op jit(solution)/shard_map/ppermute | solution.py:204
  16.8 17.7 %collective-permute-start.3 = (bf16[2,128,128]{2,1,0:T(8,128)(2,1)S(1)}, bf16[2,128,128]{2,1,0:T(8,128)(2,1)S(1)}, u32[]{:S(2)}, u32[]{:S(2)}) collective-permute-start(bf16[2,128,128]{2,1,0:T(8,128)(2,1)S(1)} %get-tuple-element.39), channel_id=1, source_target_pairs={{1,0},{2,1},{3,2},{0,3},{5,4},{6,5},{7,6},{4,7},{9,8},{10,9},{11,1... | collective-permute-start | bytes 196616 | tf_op jit(solution)/shard_map/ppermute | solution.py:204
  18.2 14.4 %collective-permute-start = (bf16[128,128]{1,0:T(8,128)(2,1)S(1)}, bf16[128,128]{1,0:T(8,128)(2,1)S(1)}, u32[]{:S(2)}, u32[]{:S(2)}) collective-permute-start(bf16[128,128]{1,0:T(8,128)(2,1)S(1)} %get-tuple-element.32), channel_id=1, source_target_pairs={{4,0},{8,4},{12,8},{16,12},{20,16},{24,20},{28,24},{0,28},{5,1},{9... | collective-permute-start | bytes 98312 | tf_op jit(solution)/shard_map/ppermute | solution.py:204
  30.5 25.0 %copy-start.30 = (f32[128,128]{1,0:T(8,128)S(1)}, f32[128,128]{1,0:T(8,128)}, u32[]{:S(2)}) copy-start(f32[128,128]{1,0:T(8,128)} %annual.4) | copy-start | bytes 196612
  30.6 25.0 %copy-start.61 = (f32[128]{0:T(128)S(1)}, f32[128]{0:T(128)}, u32[]{:S(2)}) copy-start(f32[128]{0:T(128)} %param.32) | copy-start | bytes 1540
  30.6 34.0 %copy-start.52 = (f32[1024]{0:T(1024)S(1)}, f32[1024]{0:T(1024)}, u32[]{:S(2)}) copy-start(f32[1024]{0:T(1024)} %param.31) | copy-start | bytes 12292
  32.6 32.0 %copy-start.9 = (f32[1024,128]{1,0:T(8,128)S(1)}, f32[1024,128]{1,0:T(8,128)}, u32[]{:S(2)}) copy-start(f32[1024,128]{1,0:T(8,128)} %dual.3) | copy-start | bytes 1572868
  44.9 11.6 %copy-start.28 = (bf16[8,128,128]{2,1,0:T(8,128)(2,1)}, bf16[8,128,128]{2,1,0:T(8,128)(2,1)S(1)}, u32[]{:S(2)}) copy-start(bf16[8,128,128]{2,1,0:T(8,128)(2,1)S(1)} %get-tuple-element.42.extrap) | copy-start | bytes 786436
  44.9 11.6 %copy-start.66 = (bf16[128,128]{1,0:T(8,128)(2,1)}, bf16[128,128]{1,0:T(8,128)(2,1)S(1)}, u32[]{:S(2)}) copy-start(bf16[128,128]{1,0:T(8,128)(2,1)S(1)} %get-tuple-element.43) | copy-start | bytes 98308
  57.0 23.5 %all-to-all-start.2 = ((bf16[8,128,128]{2,1,0:T(8,128)(2,1)}), bf16[8,128,128]{2,1,0:T(8,128)(2,1)}, u32[]{:S(2)}, u32[]{:S(2)}) async-start(bf16[8,128,128]{2,1,0:T(8,128)(2,1)} %get-tuple-element.41), calls=%async_computation.2 | async-start | bytes 524288 | tf_op jit(solution)/shard_map/all_to_all | solution.py:330
  61.1 9.2 %collective-permute-start.7 = (bf16[2,128,128]{2,1,0:T(8,128)(2,1)S(1)}, bf16[2,128,128]{2,1,0:T(8,128)(2,1)S(1)}, u32[]{:S(2)}, u32[]{:S(2)}) collective-permute-start(bf16[2,128,128]{2,1,0:T(8,128)(2,1)S(1)} %get-tuple-element.44.streams), channel_id=1, source_target_pairs={{1,0},{2,1},{3,2},{0,3},{5,4},{6,5},{7,6},{4,7},{9,8},{10,9},{11,1... | collective-permute-start | bytes 196616 | tf_op jit(solution)/shard_map/ppermute | solution.py:204
  61.2 9.1 %collective-permute-start.6 = (bf16[2,128,128]{2,1,0:T(8,128)(2,1)S(1)}, bf16[2,128,128]{2,1,0:T(8,128)(2,1)S(1)}, u32[]{:S(2)}, u32[]{:S(2)}) collective-permute-start(bf16[2,128,128]{2,1,0:T(8,128)(2,1)S(1)} %get-tuple-element.44.streams), channel_id=1, source_target_pairs={{2,0},{3,1},{0,2},{1,3},{6,4},{7,5},{4,6},{5,7},{10,8},{11,9},{8,1... | collective-permute-start | bytes 196616 | tf_op jit(solution)/shard_map/ppermute | solution.py:204
  62.6 7.7 %collective-permute-start.5 = (bf16[2,128,128]{2,1,0:T(8,128)(2,1)S(1)}, bf16[2,128,128]{2,1,0:T(8,128)(2,1)S(1)}, u32[]{:S(2)}, u32[]{:S(2)}) collective-permute-start(bf16[2,128,128]{2,1,0:T(8,128)(2,1)S(1)} %get-tuple-element.44.streams), channel_id=1, source_target_pairs={{3,0},{0,1},{1,2},{2,3},{7,4},{4,5},{5,6},{6,7},{11,8},{8,9},{9,10... | collective-permute-start | bytes 196616 | tf_op jit(solution)/shard_map/ppermute | solution.py:204
  62.7 7.5 %collective-permute-start.4 = (bf16[128,128]{1,0:T(8,128)(2,1)}, bf16[128,128]{1,0:T(8,128)(2,1)S(1)}, u32[]{:S(2)}, u32[]{:S(2)}) collective-permute-start(bf16[128,128]{1,0:T(8,128)(2,1)} %copy-done.66), channel_id=1, source_target_pairs={{28,0},{0,4},{4,8},{8,12},{12,16},{16,20},{20,24},{24,28},{29,1},{... | collective-permute-start | bytes 98312 | tf_op jit(solution)/shard_map/ppermute | solution.py:204
  67.1 8.5 %copy-start.2 = (bf16[1024,1024]{1,0:T(8,128)(2,1)S(1)}, bf16[1024,1024]{1,0:T(8,128)(2,1)}, u32[]{:S(2)}) copy-start(bf16[1024,1024]{1,0:T(8,128)(2,1)} %copy-done) | copy-start | bytes 6291460
  67.1 8.5 %copy-start.13 = (f32[1024,128]{1,0:T(8,128)S(1)}, f32[1024,128]{1,0:T(8,128)}, u32[]{:S(2)}) copy-start(f32[1024,128]{1,0:T(8,128)} %copy-done.12) | copy-start | bytes 1572868
  72.2 7.0 %collective-permute-start.9 = (bf16[2,128,128]{2,1,0:T(8,128)(2,1)S(1)}, bf16[2,128,128]{2,1,0:T(8,128)(2,1)S(1)}, u32[]{:S(2)}, u32[]{:S(2)}) collective-permute-start(bf16[2,128,128]{2,1,0:T(8,128)(2,1)S(1)} %get-tuple-element.49), channel_id=1, source_target_pairs={{3,0},{0,1},{1,2},{2,3},{7,4},{4,5},{5,6},{6,7},{11,8},{8,9},{9,10... | collective-permute-start | bytes 196616 | tf_op jit(solution)/shard_map/ppermute | solution.py:204
  72.2 7.0 %collective-permute-start.10 = (bf16[2,128,128]{2,1,0:T(8,128)(2,1)S(1)}, bf16[2,128,128]{2,1,0:T(8,128)(2,1)S(1)}, u32[]{:S(2)}, u32[]{:S(2)}) collective-permute-start(bf16[2,128,128]{2,1,0:T(8,128)(2,1)S(1)} %get-tuple-element.50), channel_id=1, source_target_pairs={{2,0},{3,1},{0,2},{1,3},{6,4},{7,5},{4,6},{5,7},{10,8},{11,9},{8,1... | collective-permute-start | bytes 196616 | tf_op jit(solution)/shard_map/ppermute | solution.py:204
  73.9 6.0 %collective-permute-start.11 = (bf16[2,128,128]{2,1,0:T(8,128)(2,1)S(1)}, bf16[2,128,128]{2,1,0:T(8,128)(2,1)S(1)}, u32[]{:S(2)}, u32[]{:S(2)}) collective-permute-start(bf16[2,128,128]{2,1,0:T(8,128)(2,1)S(1)} %get-tuple-element.51), channel_id=1, source_target_pairs={{1,0},{2,1},{3,2},{0,3},{5,4},{6,5},{7,6},{4,7},{9,8},{10,9},{11,1... | collective-permute-start | bytes 196616 | tf_op jit(solution)/shard_map/ppermute | solution.py:204
  75.3 3.9 %collective-permute-start.8 = (bf16[128,128]{1,0:T(8,128)(2,1)S(1)}, bf16[128,128]{1,0:T(8,128)(2,1)S(1)}, u32[]{:S(2)}, u32[]{:S(2)}) collective-permute-start(bf16[128,128]{1,0:T(8,128)(2,1)S(1)} %get-tuple-element.46), channel_id=1, source_target_pairs={{4,0},{8,4},{12,8},{16,12},{20,16},{24,20},{28,24},{0,28},{5,1},{9... | collective-permute-start | bytes 98312 | tf_op jit(solution)/shard_map/ppermute | solution.py:204
  75.6 4.9 %copy-start.14 = (f32[1024,128]{1,0:T(8,128)S(1)}, f32[1024,128]{1,0:T(8,128)}, u32[]{:S(2)}) copy-start(f32[1024,128]{1,0:T(8,128)} %copy-done.12) | copy-start | bytes 1572868
  90.9 15.3 %all-to-all-start.3 = ((bf16[8,128,128]{2,1,0:T(8,128)(2,1)}), bf16[8,128,128]{2,1,0:T(8,128)(2,1)S(1)}, u32[]{:S(2)}, u32[]{:S(2)}) async-start(bf16[8,128,128]{2,1,0:T(8,128)(2,1)} %copy-done.31), calls=%async_computation.3 | async-start | bytes 524288 | tf_op jit(solution)/shard_map/all_to_all | solution.py:338
  95.2 9.3 %collective-permute-start.15 = (bf16[2,128,128]{2,1,0:T(8,128)(2,1)}, bf16[2,128,128]{2,1,0:T(8,128)(2,1)S(1)}, u32[]{:S(2)}, u32[]{:S(2)}) collective-permute-start(bf16[2,128,128]{2,1,0:T(8,128)(2,1)} %copy-done.48), channel_id=1, source_target_pairs={{1,0},{2,1},{3,2},{0,3},{5,4},{6,5},{7,6},{4,7},{9,8},{10,9},{11,1... | collective-permute-start | bytes 196616 | tf_op jit(solution)/shard_map/ppermute | solution.py:204
  95.2 9.3 %collective-permute-start.14 = (bf16[2,128,128]{2,1,0:T(8,128)(2,1)}, bf16[2,128,128]{2,1,0:T(8,128)(2,1)S(1)}, u32[]{:S(2)}, u32[]{:S(2)}) collective-permute-start(bf16[2,128,128]{2,1,0:T(8,128)(2,1)} %copy-done.48), channel_id=1, source_target_pairs={{2,0},{3,1},{0,2},{1,3},{6,4},{7,5},{4,6},{5,7},{10,8},{11,9},{8,1... | collective-permute-start | bytes 196616 | tf_op jit(solution)/shard_map/ppermute | solution.py:204
  96.5 8.0 %collective-permute-start.13 = (bf16[2,128,128]{2,1,0:T(8,128)(2,1)}, bf16[2,128,128]{2,1,0:T(8,128)(2,1)S(1)}, u32[]{:S(2)}, u32[]{:S(2)}) collective-permute-start(bf16[2,128,128]{2,1,0:T(8,128)(2,1)} %copy-done.48), channel_id=1, source_target_pairs={{3,0},{0,1},{1,2},{2,3},{7,4},{4,5},{5,6},{6,7},{11,8},{8,9},{9,10... | collective-permute-start | bytes 196616 | tf_op jit(solution)/shard_map/ppermute | solution.py:204
  96.6 7.8 %collective-permute-start.12 = (bf16[128,128]{1,0:T(8,128)(2,1)}, bf16[128,128]{1,0:T(8,128)(2,1)S(1)}, u32[]{:S(2)}, u32[]{:S(2)}) collective-permute-start(bf16[128,128]{1,0:T(8,128)(2,1)} %copy-done.65), channel_id=1, source_target_pairs={{28,0},{0,4},{4,8},{8,12},{12,16},{16,20},{20,24},{24,28},{29,1},{... | collective-permute-start | bytes 98312 | tf_op jit(solution)/shard_map/ppermute | solution.py:204
  101.3 4.9 %copy-start.47 = (f32[128,128]{1,0:T(8,128)S(1)}, f32[128,128]{1,0:T(8,128)}, u32[]{:S(2)}) copy-start(f32[128,128]{1,0:T(8,128)} %copy-done.46) | copy-start | bytes 196612
  101.3 4.9 %copy-start.62 = (f32[128]{0:T(128)S(1)}, f32[128]{0:T(128)}, u32[]{:S(2)}) copy-start(f32[128]{0:T(128)} %param.32) | copy-start | bytes 1540
  (54 other events, 72.8 us)

commit v2 on v1

v2 whole, which is shorter than its diff:
```python
import functools

import jax
import jax.numpy as jnp
from jax import lax
from jax.experimental import pallas as pl
from jax.experimental.pallas import tpu as pltpu
from jax.sharding import PartitionSpec as P

SC = 2
ITERS = 2

PRIMAL_STEP = 0.5
DUAL_STEP = 0.5
F32 = jnp.float32
BF16 = jnp.bfloat16
HBM = pl.BlockSpec(memory_space=pltpu.HBM)
SMEM = pl.BlockSpec(memory_space=pltpu.SMEM)


def shape(dims, dtype):
    return jax.ShapeDtypeStruct(dims, dtype)


class Arriving:
    def __init__(self, source, target, sems, at, pieces):
        length = source.shape[0] // pieces
        self.target = target
        self.copies = []
        for p in range(pieces):
            rows = pl.ds(p * length, length)
            self.copies.append(
                pltpu.make_async_copy(source.at[rows], target.at[rows], sems.at[at + p])
            )
        for copy in self.copies:
            copy.start()

    def piece(self):
        self.copies.pop(0).wait()
        return self.target

    def __call__(self):
        while self.copies:
            self.piece()
        return self.target


class Leaving:
    def __init__(self, source, target, sem):
        self.ref = source
        self.copy = pltpu.make_async_copy(source, target, sem)
        self.sent = False

    def send(self):
        self.copy.start()
        self.sent = True


def run(body, name, scalars, arrays, outs, scratch, flops, pieces={}):
    counts = [pieces.get(i, 1) for i in range(len(arrays))]
    ns, na, no = len(scalars), len(arrays), len(outs)

    def kernel(*refs):
        scalar_refs, refs = refs[:ns], refs[ns:]
        sources, refs = refs[:na], refs[na:]
        targets, refs = refs[:no], refs[no:]
        landing, refs = refs[:na], refs[na:]
        staging, refs = refs[:no], refs[no:]
        (in_sems, out_sems), extra = refs[:2], refs[2:]
        at = 0
        arriving = []
        for source, target, count in zip(sources, landing, counts):
            arriving.append(Arriving(source, target, in_sems, at, count))
            at += count
        leaving = [
            Leaving(source, target, out_sems.at[i])
            for i, (source, target) in enumerate(zip(staging, targets))
        ]
        body(scalar_refs, arriving, leaving, *extra)
        for item in arriving:
            item()
        for item in leaving:
            if not item.sent:
                item.send()
        for item in leaving:
            item.copy.wait()

    moved = sum(a.size * a.dtype.itemsize for a in (*arrays, *outs))
    return pl.pallas_call(
        kernel,
        name=name,
        in_specs=[SMEM] * ns + [HBM] * na,
        out_specs=(HBM,) * no,
        out_shape=tuple(outs),
        scratch_shapes=[pltpu.VMEM(a.shape, a.dtype) for a in (*arrays, *outs)]
        + [pltpu.SemaphoreType.DMA((sum(counts),)), pltpu.SemaphoreType.DMA((no,))]
        + scratch,
        compiler_params=pltpu.CompilerParams(vmem_limit_bytes=64 << 20),
        cost_estimate=pl.CostEstimate(flops=flops, bytes_accessed=moved, transcendentals=0),
    )(*scalars, *arrays)


def dot(a, b):
    return jnp.dot(a, b, preferred_element_type=F32)


def dot_transposed(a, b):
    return dot(a.T, b)


def column_of(row_vector, width):
    return jnp.broadcast_to(row_vector, (width, row_vector.shape[1])).T


def wrap(value, number):
    return jnp.where(value >= number, value - number, value)


def send_duals(refineries, dual_q, me, rows, src, swing, carry, outs, acc):
    own, *sends, carried = outs
    acc[...] = jnp.zeros_like(acc)
    carried.ref[...] = dot_transposed(carry[0], dual_q[0]).astype(BF16)
    carried.send()
    for m in range(swing.shape[0]):
        acc[src[m]] += dot_transposed(swing[m], dual_q[rows[m]])
    for d, send in enumerate(sends, 1):
        send.ref[...] = acc[pl.ds(wrap(me + d, refineries) * SC, SC)].astype(BF16)
        send.send()
    own.ref[...] = acc[pl.ds(me * SC, SC)]
    own.send()


def first_duals_body(refineries, scalars, ins, outs, acc):
    me, rows, src = scalars
    annual, dual, carry, swing = ins
    weekly, dual_q = outs[0], outs[1]
    rounded = annual()[...].astype(BF16)
    for w in range(weekly.ref.shape[0]):
        weekly.ref[w] = rounded
    weekly.send()
    size = rounded.shape[0]
    dual = dual()
    for i in range(dual_q.ref.shape[0]):
        dual_q.ref[i] = dual[i * size : (i + 1) * size].astype(BF16)
    dual_q.send()
    send_duals(refineries, dual_q.ref, me[0], rows, src, swing(), carry(), outs[2:], acc)


def adjoint(high, low, dual_q, primal, prices, out):
    blocks, size, _ = dual_q.shape
    turned = jnp.concatenate([dual_q[i].T for i in range(blocks)], axis=1)
    step = 2 * size
    for j in range(high.shape[1] // step):
        part = dot(turned, high[:, j * step : (j + 1) * step]) + dot(
            turned, low[:, j * step : (j + 1) * step]
        )
        for h in range(2):
            at = slice(j * step + h * size, j * step + (h + 1) * size)
            out[at] = primal[at] - PRIMAL_STEP * (
                prices[at] - part[:, h * size : (h + 1) * size].T
            )


def dense_body(chunks, scalars, ins, outs, acc):
    count, rows, cols = scalars
    blocks, upper, dual_q, primal, prices = ins
    high, low, upper_full, out = outs
    size = upper.target.shape[1]
    width = upper_full.ref.shape[1]
    tiles = high.ref.shape[1] // size
    acc[...] = jnp.zeros_like(acc)
    slots = blocks.target.shape[0] // chunks
    for c in range(chunks):
        here = blocks.piece()

        def step(n, _):
            acc[rows[n] * tiles + cols[n]] += here[n].astype(F32)
            return 0

        lax.fori_loop(c * slots, jnp.minimum(count[0], (c + 1) * slots), step, 0)
    for i in range(high.ref.shape[0] // size):
        for j in range(tiles):
            whole = acc[i * tiles + j]
            top = whole.astype(BF16)
            at = (slice(i * size, (i + 1) * size), slice(j * size, (j + 1) * size))
            high.ref[at] = top
            low.ref[at] = (whole - top.astype(F32)).astype(BF16)
    high.send()
    low.send()
    upper = upper()
    for j in range(tiles):
        upper_full.ref[j * size : (j + 1) * size] = column_of(upper[j : j + 1], width)
    upper_full.send()
    adjoint(high.ref, low.ref, dual_q(), primal(), prices(), out.ref)


def adjoint_body(scalars, ins, outs):
    dual_q, primal, prices, high, low = ins
    adjoint(high(), low(), dual_q(), primal(), prices(), outs[0].ref)


def primal_body(scalars, ins, outs, acc, image_acc):
    ids, cols = scalars
    annual_q, annual, own, carried, primal, upper_full, partial, *arrived = ins
    image, streams, last, extrap, updated = outs
    blocks, size, _ = extrap.ref.shape
    acc[...] = jnp.zeros_like(acc)
    image_acc[...] = jnp.zeros_like(image_acc)
    annual, annual_q = annual(), annual_q()
    slots = annual.shape[0]
    for k in range(slots):
        acc[cols[k]] += dot_transposed(annual[k], annual_q[ids[k]])
    total = own()[...]
    for piece in arrived:
        total = total + piece()[...].astype(F32)
    acc[:SC] += total
    acc[blocks - 1] += carried()[...].astype(F32)
    partial, primal, upper_full = partial(), primal(), upper_full()
    for j in range(blocks):
        at = slice(j * size, (j + 1) * size)
        new = jnp.clip(partial[at] + PRIMAL_STEP * acc[j], 0.0, upper_full[at])
        updated.ref[at] = new
        ahead = (2.0 * new - primal[at]).astype(BF16)
        extrap.ref[j] = ahead
        if j < SC:
            streams.ref[j] = ahead
        if j == SC - 1:
            streams.send()
        if j == blocks - 1:
            last.ref[...] = ahead
            last.send()
    extrap.send()
    updated.send()
    for k in range(slots):
        image_acc[ids[k]] += dot(annual[k], extrap.ref[cols[k]])
    image.ref[...] = image_acc[...].astype(BF16)


def forward_body(scalars, ins, outs):
    extrap, dual, demand, high, low = ins
    out = outs[0].ref
    extrap, dual, demand = extrap(), dual(), demand()
    blocks, size, width = extrap.shape
    right = jnp.concatenate([extrap[j] for j in range(blocks)], axis=0)
    high, low = high(), low()
    step = 2 * size
    for i in range(high.shape[0] // step):
        part = dot(high[i * step : (i + 1) * step], right) + dot(
            low[i * step : (i + 1) * step], right
        )
        for h in range(2):
            at = slice(i * step + h * size, i * step + (h + 1) * size)
            row = 2 * i + h
            out[at] = dual[at] + DUAL_STEP * (
                column_of(demand[row : row + 1], width) - part[h * size : (h + 1) * size]
            )


def dual_body(refineries, more, scalars, ins, outs, gathered, acc, *stream_acc):
    me, rows, src = scalars
    swing, carry, streams, partial, previous, *arrived = ins
    dual = outs[0]
    swing, carry = swing(), carry()
    size = swing.shape[1]
    mine = me[0]
    gathered[pl.ds(mine * SC, SC)] = streams()[...]
    for d, piece in enumerate(arrived, 1):
        gathered[pl.ds(wrap(mine + refineries - d, refineries) * SC, SC)] = piece()[...]
    acc[...] = jnp.zeros_like(acc)
    for m in range(swing.shape[0]):
        acc[rows[m]] += dot(swing[m], gathered[src[m]])
    acc[0] += dot(carry[0], previous()[...])
    partial = partial()
    for i in range(acc.shape[0]):
        at = slice(i * size, (i + 1) * size)
        new = jnp.maximum(partial[at] - DUAL_STEP * acc[i], 0.0)
        dual.ref[at] = new
        if more:
            outs[1].ref[i] = new.astype(BF16)
    dual.send()
    if more:
        outs[1].send()
        send_duals(
            refineries, outs[1].ref, mine, rows, src, swing, carry, outs[2:], *stream_acc
        )


def annual_body(more, scalars, ins, outs):
    annual, need, parts, *_ = ins
    parts = parts()
    total = parts[0].astype(F32)
    for w in range(1, parts.shape[0]):
        total = total + parts[w].astype(F32)
    annual = annual()
    new = jnp.maximum(
        annual[...] + DUAL_STEP * (column_of(need()[...], annual.shape[1]) - total), 0.0
    )
    outs[-1].ref[...] = new
    if more:
        rounded = new.astype(BF16)
        for w in range(parts.shape[0]):
            outs[0].ref[w] = rounded


def shifted(block, axis, distance):
    number = lax.axis_size(axis)
    route = [((i - distance) % number, i) for i in range(number)]
    return lax.ppermute(block, axis, route)


def body(
    local_blocks,
    local_rows,
    local_cols,
    band_count,
    swing_blocks,
    swing_rows,
    swing_src,
    carry_blocks,
    annual_blocks,
    annual_ids,
    annual_cols,
    cost,
    upper,
    demand,
    annual_bound,
    x_start,
    y_start,
    annual_start,
):
    scenarios = cost.shape[1]
    size = local_blocks.shape[1]
    columns = cost.shape[0] // size
    rows = y_start.shape[0] // size
    slots = local_blocks.shape[0]
    weeks = lax.axis_size("period")
    refineries = lax.axis_size("refinery")
    others = refineries - 1
    me = lax.axis_index("refinery").astype(jnp.int32).reshape(1)
    tile = shape((size, scenarios), BF16)
    pair_q = shape((SC, size, scenarios), BF16)
    pair = shape((SC, size, scenarios), F32)
    state_x = shape((columns * size, scenarios), F32)
    state_y = shape((rows * size, scenarios), F32)
    blocks_x = shape((columns, size, scenarios), BF16)
    blocks_y = shape((rows, size, scenarios), BF16)
    weekly = shape((weeks, size, scenarios), BF16)
    matrix = shape((rows * size, columns * size), BF16)
    swings = swing_blocks.shape[0]
    annuals = annual_blocks.shape[0]
    unit = 2 * size * size * scenarios
    stream_scratch = pltpu.VMEM((refineries * SC, size, scenarios), F32)
    sends_shape = [pair] + [pair_q] * others + [tile]
    chunks = 4 if slots % 4 == 0 else 1

    upper_rows = upper.reshape(columns, size)
    demand_rows = demand.reshape(rows, size)
    need = annual_bound.reshape(1, size)
    primal, dual, annual = x_start, y_start, annual_start
    annual_send, dual_q, own, *rest = run(
        functools.partial(first_duals_body, refineries),
        "first_duals",
        [me, swing_rows, swing_src],
        [annual, dual, carry_blocks, swing_blocks],
        [weekly, blocks_y] + sends_shape,
        [stream_scratch],
        (swings + 1) * unit,
    )
    for iteration in range(ITERS):
        more = iteration + 1 < ITERS
        sends, carried = rest[:others], rest[others]
        annual_q = lax.all_to_all(annual_send, "period", 0, 0, tiled=True)
        arrived = [shifted(send, "refinery", d) for d, send in enumerate(sends, 1)]
        carried_back = shifted(carried, "period", -1)
        if iteration == 0:
            high, low, upper_full, partial_x = run(
                functools.partial(dense_body, chunks),
                "dense",
                [band_count, local_rows, local_cols],
                [local_blocks, upper_rows, dual_q, primal, cost],
                [matrix, matrix, state_x, state_x],
                [pltpu.VMEM((rows * columns, size, size), F32)],
                3 * rows * columns * unit,
                {0: chunks},
            )
        else:
            (partial_x,) = run(
                adjoint_body,
                "adjoint",
                [],
                [dual_q, primal, cost, high, low],
                [state_x],
                [],
                2 * rows * columns * unit,
            )
        image, streams, last, extrap, updated = run(
            primal_body,
            "primal_step",
            [annual_ids, annual_cols],
            [annual_q, annual_blocks, own, carried_back, primal, upper_full, partial_x, *arrived],
            [weekly, pair_q, tile, blocks_x, state_x],
            [
                pltpu.VMEM((columns, size, scenarios), F32),
                pltpu.VMEM((weeks, size, scenarios), F32),
            ],
            2 * annuals * unit,
        )
        parts = lax.all_to_all(image, "period", 0, 0, tiled=True)
        others_streams = [shifted(streams, "refinery", d) for d in range(1, refineries)]
        previous = shifted(last, "period", 1)
        (partial_y,) = run(
            forward_body,
            "forward",
            [],
            [extrap, dual, demand_rows, high, low],
            [state_y],
            [],
            2 * rows * columns * unit,
        )
        dual, *rest = run(
            functools.partial(dual_body, refineries, more),
            "dual_step",
            [me, swing_rows, swing_src],
            [swing_blocks, carry_blocks, streams, partial_y, previous, *others_streams],
            [state_y] + ([blocks_y] + sends_shape if more else []),
            [
                pltpu.VMEM((refineries * SC, size, scenarios), BF16),
                pltpu.VMEM((rows, size, scenarios), F32),
            ]
            + ([stream_scratch] if more else []),
            2 * swings * unit,
        )
        if more:
            dual_q, own, *rest = rest
        *next_send, annual = run(
            functools.partial(annual_body, more),
            "annual_step",
            [],
            [annual, need, parts] + ([own] if more else []),
            ([weekly] if more else []) + [shape((size, scenarios), F32)],
            [],
            size * scenarios * weeks,
        )
        if more:
            (annual_send,) = next_send
        primal = updated
    return primal, dual, annual


def solution(mesh):
    both = P(("period", "refinery"))
    wide = P(("period", "refinery"), None)
    cube = P(("period", "refinery"), None, None)
    return jax.shard_map(
        body,
        mesh=mesh,
        in_specs=(
            cube, both, both, both, cube, both, both, cube, cube, both, both,
            wide, both, both, both, wide, wide, wide,
        ),
        out_specs=(wide, wide, wide),
        check_vma=False,
    )
```

time: 109 us -> 85.9 us (0.79); the launches traced: 107 us -> 85.2 us
  local copies, waits for them, and re-layouts: 38.7 us -> 0 us
  Pallas kernels: 15.5 us -> 39.4 us
  blocking collectives: 10.7 us -> 0 us
  starting transfers between devices: 33.8 us -> 40 us
  waiting for transfers between devices: 5.73 us -> 4.18 us
    unnamed x134 -> x0, local copies, waits for them, and re-layouts: 37.9 us -> none
    pallas_call x12 -> x11, Pallas kernels: 15.5 us -> 39.4 us  [run(): pl.pallas_call(kernel, name=name, in_specs=[SMEM] * ns + [HBM] * na, out_...]
    all_to_all x1 -> x0, blocking collectives: 10.7 us -> none  [body(): parts = lax.all_to_all(image, 'period', 0, 0, tiled=True)]
    all_to_all x1 -> x2, starting transfers between devices: 4.31 us -> 8.11 us  [body(): parts = lax.all_to_all(image, 'period', 0, 0, tiled=True)]
    ppermute x16, starting transfers between devices: 18 us -> 20.6 us  [shifted(): return lax.ppermute(block, axis, route)]
    ppermute x16, waiting for transfers between devices: 5.72 us -> 4.16 us  [shifted(): return lax.ppermute(block, axis, route)]
  transfers between devices with their start and end apart: 19 -> 20, of which waited for: 3 -> 2; matrix products, arithmetic and copies ran while one was open for 0% -> 0% of each run, Pallas kernels for 10% -> 30%
where the time goes in v2:
time: 85.9 us; the launch traced here: 85.2 us
  starting transfers between devices  40 us (47%)
  Pallas kernels  39.4 us (46%)
  waiting for transfers between devices  4.18 us (5%)
  between operations  1.52 us (2%)
    pallas_call x11, Pallas kernels, run(): pl.pallas_call(kernel, name=name, in_specs=[SMEM] * ns + [HBM] * na, out_...  39.4 us
    ppermute x16, starting transfers between devices, shifted(): return lax.ppermute(block, axis, route)  20.6 us
    all_to_all x2, starting transfers between devices, body(): annual_q = lax.all_to_all(annual_send, 'period', 0, 0, tiled=True)  11.3 us
    all_to_all x2, starting transfers between devices, body(): parts = lax.all_to_all(image, 'period', 0, 0, tiled=True)  8.11 us
    ppermute x16, waiting for transfers between devices, shifted(): return lax.ppermute(block, axis, route)  4.16 us
  transfers between devices with their start and end apart: 20, of which 2 were waited for; matrix products, arithmetic and copies ran while one was open for 0% of the time, Pallas kernels for 30%

profile of v2, /device:TPU:0, one launch (start us, length us, event | category | flops | bytes accessed | tf_op | source)
XLA Modules:
  0.0 85.2 jit_solution(1893835833776995251)
XLA Ops:
  0.6 2.9 %first_duals.1 = (bf16[8,128,128]{2,1,0:T(8,128)(2,1)}, bf16[8,128,128]{2,1,0:T(8,128)(2,1)}, f32[2,128,128]{2,1,0:T(8,128)}, bf16[2,128,128]{2,1,0:T(8,128)(2,1...) custom-call(s32[1]{0:T(128)} %bitcast.1.refs_0_, s32[8]{0:T(128)} %refs_1_.13, ...), custom_call_target="tpu_custom_call" | custom-call | flops 37748736 | bytes 1769472 | tf_op jit(solution)/shard_map/first_duals/pallas_call | solution.py:89
  3.6 7.3 %all-to-all-start = ((bf16[8,128,128]{2,1,0:T(8,128)(2,1)}), bf16[8,128,128]{2,1,0:T(8,128)(2,1)}, u32[]{:S(2)}, u32[]{:S(2)}) async-start(bf16[8,128,128]{2,1,0:T(8,128)(2,1)} %get-tuple-element.33), calls=%async_computation | async-start | bytes 524288 | tf_op jit(solution)/shard_map/all_to_all | solution.py:372
  10.9 4.7 %collective-permute-start = (bf16[128,128]{1,0:T(8,128)(2,1)}, bf16[128,128]{1,0:T(8,128)(2,1)}, u32[]{:S(2)}, u32[]{:S(2)}) collective-permute-start(bf16[128,128]{1,0:T(8,128)(2,1)} %get-tuple-element.35), channel_id=1, source_target_pairs={{4,0},{8,4},{12,8},{16,12},{20,16},{24,20},{28,24},{0,28},{5,1},{9... | collective-permute-start | bytes 98312 | tf_op jit(solution)/shard_map/ppermute | solution.py:308
  15.6 1.5 %collective-permute-start.2 = (bf16[2,128,128]{2,1,0:T(8,128)(2,1)}, bf16[2,128,128]{2,1,0:T(8,128)(2,1)}, u32[]{:S(2)}, u32[]{:S(2)}) collective-permute-start(bf16[2,128,128]{2,1,0:T(8,128)(2,1)} %get-tuple-element.40), channel_id=1, source_target_pairs={{2,0},{3,1},{0,2},{1,3},{6,4},{7,5},{4,6},{5,7},{10,8},{11,9},{8,1... | collective-permute-start | bytes 196616 | tf_op jit(solution)/shard_map/ppermute | solution.py:308
  17.1 1.4 %collective-permute-start.3 = (bf16[2,128,128]{2,1,0:T(8,128)(2,1)}, bf16[2,128,128]{2,1,0:T(8,128)(2,1)}, u32[]{:S(2)}, u32[]{:S(2)}) collective-permute-start(bf16[2,128,128]{2,1,0:T(8,128)(2,1)} %get-tuple-element.41), channel_id=1, source_target_pairs={{1,0},{2,1},{3,2},{0,3},{5,4},{6,5},{7,6},{4,7},{9,8},{10,9},{11,1... | collective-permute-start | bytes 196616 | tf_op jit(solution)/shard_map/ppermute | solution.py:308
  19.2 5.5 %dense.1 = (bf16[1024,1024]{1,0:T(8,128)(2,1)}, bf16[1024,1024]{1,0:T(8,128)(2,1)}, f32[1024,128]{1,0:T(8,128)}, f32[1024,128]{1,0:T(8,128)}) custom-call(s32[1]{0:T(128)S(6)} %copy.21.refs_0_, s32[96]{0:T(128)} %refs_1_.8, s32[96]{0:T(128)} %refs_2_.6, bf16[96,128,128]{2,1,0:T(8,128)(2,1)} %refs_3_.7, f32[8,128]{1,0:T(8,128)} %bitcast.6, ...), custom_call_target="tpu_custom_call" | custom-call | flops 805306368 | bytes 9703424 | tf_op jit(solution)/shard_map/dense/pallas_call | solution.py:89
  24.8 3.5 %primal_step.2 = (bf16[8,128,128]{2,1,0:T(8,128)(2,1)}, bf16[2,128,128]{2,1,0:T(8,128)(2,1)}, bf16[128,128]{1,0:T(8,128)(2,1)}, bf16[8,128,128]{2,1,0:T(8,128)(2,1)}, f32[1024,128]{1,0:T(8,128)}) custom-call(s32[8]{0:T(128)} %refs_0_.6, s32[8]{0:T(128)} %refs_1_.12, bf16[8,128,128]{2,1,0:T(8,128)(2,1)} %all-to-all-done.refs_2_, ...), custom_call_target="tpu_custom_call" | custom-call | flops 67108864 | bytes 3604480 | tf_op jit(solution)/shard_map/primal_step/pallas_call | solution.py:89
  28.3 4.0 %all-to-all-start.1 = ((bf16[8,128,128]{2,1,0:T(8,128)(2,1)}), bf16[8,128,128]{2,1,0:T(8,128)(2,1)}, u32[]{:S(2)}, u32[]{:S(2)}) async-start(bf16[8,128,128]{2,1,0:T(8,128)(2,1)} %get-tuple-element.42), calls=%async_computation.1 | async-start | bytes 524288 | tf_op jit(solution)/shard_map/all_to_all | solution.py:408
  32.3 0.1 collective-permute-start.7
  32.4 0.7 collective-permute-start.6
  33.1 0.1 collective-permute-start.5
  33.2 1.8 %collective-permute-start.4 = (bf16[128,128]{1,0:T(8,128)(2,1)}, bf16[128,128]{1,0:T(8,128)(2,1)}, u32[]{:S(2)}, u32[]{:S(2)}) collective-permute-start(bf16[128,128]{1,0:T(8,128)(2,1)} %get-tuple-element.47), channel_id=1, source_target_pairs={{28,0},{0,4},{4,8},{8,12},{12,16},{16,20},{20,24},{24,28},{29,1},{... | collective-permute-start | bytes 98312 | tf_op jit(solution)/shard_map/ppermute | solution.py:308
  35.0 4.6 %forward.2.refs_6_ = f32[1024,128]{1,0:T(8,128)} custom-call(bf16[8,128,128]{2,1,0:T(8,128)(2,1)} %get-tuple-element.44.refs_0_, f32[1024,128]{1,0:T(8,128)} %refs_1_.10, f32[8,128]{1,0:T(8,128)} %bitcast.4, bf16[1024,1024]{1,0:T(8,128)(2,1)} %get-tuple-element.45.refs_3_, bf16[1024,1024]{1,0:T(8,128)(2,1)} %get-tuple-element.46.refs_4_), custom_call_target="tpu_custom_call" | custom-call | flops 536870912 | bytes 5509120 | tf_op jit(solution)/shard_map/forward/pallas_call | solution.py:89
  39.6 2.3 %collective-permute-done.4.refs_7_ = bf16[128,128]{1,0:T(8,128)(2,1)} collective-permute-done((bf16[128,128]{1,0:T(8,128)(2,1)}, bf16[128,128]{1,0:T(8,128)(2,1)}, u32[]{:S(2)}, u32[]{:S(2)}) %collective-permute-start.4) | collective-permute-done | bytes 32800 | tf_op jit(solution)/shard_map/ppermute | solution.py:308
  41.9 3.5 %dual_step.2 = (f32[1024,128]{1,0:T(8,128)}, bf16[8,128,128]{2,1,0:T(8,128)(2,1)}, f32[2,128,128]{2,1,0:T(8,128)}, bf16[2,128,128]{2,1,0:T(8,128)(2,1)}, bf16[2,...) custom-call(s32[1]{0:T(128)} %bitcast.1.refs_0_, s32[8]{0:T(128)} %refs_1_.13, ...), custom_call_target="tpu_custom_call" | custom-call | flops 67108864 | bytes 2260992 | tf_op jit(solution)/shard_map/dual_step/pallas_call | solution.py:89
  45.4 1.9 %annual_step.2 = (bf16[8,128,128]{2,1,0:T(8,128)(2,1)}, f32[128,128]{1,0:T(8,128)}) custom-call(f32[128,128]{1,0:T(8,128)} %refs_0_.5, f32[1,128]{1,0:T(1,128)} %bitcast.7, bf16[8,128,128]{2,1,0:T(8,128)(2,1)} %all-to-all-done.1.refs_2_, f32[2,128,128]{2,1,0:T(8,128)} %get-tuple-element.48.refs_3_.refs_4_), custom_call_target="tpu_custom_call" | custom-call | flops 131072 | bytes 786944 | tf_op jit(solution)/shard_map/annual_step/pallas_call | solution.py:89
  47.3 4.1 %all-to-all-start.2 = ((bf16[8,128,128]{2,1,0:T(8,128)(2,1)}), bf16[8,128,128]{2,1,0:T(8,128)(2,1)}, u32[]{:S(2)}, u32[]{:S(2)}) async-start(bf16[8,128,128]{2,1,0:T(8,128)(2,1)} %get-tuple-element.49), calls=%async_computation.2 | async-start | bytes 524288 | tf_op jit(solution)/shard_map/all_to_all | solution.py:372
  51.4 0.1 collective-permute-start.9
  51.5 1.4 %collective-permute-start.10 = (bf16[2,128,128]{2,1,0:T(8,128)(2,1)}, bf16[2,128,128]{2,1,0:T(8,128)(2,1)}, u32[]{:S(2)}, u32[]{:S(2)}) collective-permute-start(bf16[2,128,128]{2,1,0:T(8,128)(2,1)} %get-tuple-element.54), channel_id=1, source_target_pairs={{2,0},{3,1},{0,2},{1,3},{6,4},{7,5},{4,6},{5,7},{10,8},{11,9},{8,1... | collective-permute-start | bytes 196616 | tf_op jit(solution)/shard_map/ppermute | solution.py:308
  52.9 1.4 %collective-permute-start.11 = (bf16[2,128,128]{2,1,0:T(8,128)(2,1)}, bf16[2,128,128]{2,1,0:T(8,128)(2,1)}, u32[]{:S(2)}, u32[]{:S(2)}) collective-permute-start(bf16[2,128,128]{2,1,0:T(8,128)(2,1)} %get-tuple-element.55), channel_id=1, source_target_pairs={{1,0},{2,1},{3,2},{0,3},{5,4},{6,5},{7,6},{4,7},{9,8},{10,9},{11,1... | collective-permute-start | bytes 196616 | tf_op jit(solution)/shard_map/ppermute | solution.py:308
  54.3 4.6 %collective-permute-start.8 = (bf16[128,128]{1,0:T(8,128)(2,1)}, bf16[128,128]{1,0:T(8,128)(2,1)}, u32[]{:S(2)}, u32[]{:S(2)}) collective-permute-start(bf16[128,128]{1,0:T(8,128)(2,1)} %get-tuple-element.50), channel_id=1, source_target_pairs={{4,0},{8,4},{12,8},{16,12},{20,16},{24,20},{28,24},{0,28},{5,1},{9... | collective-permute-start | bytes 98312 | tf_op jit(solution)/shard_map/ppermute | solution.py:308
  58.8 4.3 %adjoint.1.refs_8_ = f32[1024,128]{1,0:T(8,128)} custom-call(bf16[8,128,128]{2,1,0:T(8,128)(2,1)} %get-tuple-element.52.refs_0_, f32[1024,128]{1,0:T(8,128)} %get-tuple-element.51.refs_1_.refs_6_, f32[1024,128]{1,0:T(8,128)} %refs_2_.8, bf16[1024,1024]{1,0:T(8,128)(2,1)} %get-tuple-element.45.refs_3_, bf16[1024,1024]{1,0:T(8,128)(2,1)} %get-tuple-element.46.refs_4_), custom_call_target="tpu_custom_call" | custom-call | flops 536870912 | bytes 6029312 | tf_op jit(solution)/shard_map/adjoint/pallas_call | solution.py:89
  63.2 3.5 %primal_step.3 = (bf16[8,128,128]{2,1,0:T(8,128)(2,1)}, bf16[2,128,128]{2,1,0:T(8,128)(2,1)}, bf16[128,128]{1,0:T(8,128)(2,1)}, bf16[8,128,128]{2,1,0:T(8,128)(2,1)}, f32[1024,128]{1,0:T(8,128)}) custom-call(s32[8]{0:T(128)} %refs_0_.6, s32[8]{0:T(128)} %refs_1_.12, bf16[8,128,128]{2,1,0:T(8,128)(2,1)} %all-to-all-done.2.refs_2_, ...), custom_call_target="tpu_custom_call" | custom-call | flops 67108864 | bytes 3604480 | tf_op jit(solution)/shard_map/primal_step/pallas_call | solution.py:89
  66.7 4.1 %all-to-all-start.3 = ((bf16[8,128,128]{2,1,0:T(8,128)(2,1)}), bf16[8,128,128]{2,1,0:T(8,128)(2,1)}, u32[]{:S(2)}, u32[]{:S(2)}) async-start(bf16[8,128,128]{2,1,0:T(8,128)(2,1)} %get-tuple-element.62), calls=%async_computation.3 | async-start | bytes 524288 | tf_op jit(solution)/shard_map/all_to_all | solution.py:408
  70.8 0.1 collective-permute-start.15
  70.9 0.8 collective-permute-start.14
  71.6 0.2 collective-permute-start.13
  71.8 1.8 %collective-permute-start.12 = (bf16[128,128]{1,0:T(8,128)(2,1)}, bf16[128,128]{1,0:T(8,128)(2,1)}, u32[]{:S(2)}, u32[]{:S(2)}) collective-permute-start(bf16[128,128]{1,0:T(8,128)(2,1)} %get-tuple-element.60), channel_id=1, source_target_pairs={{28,0},{0,4},{4,8},{8,12},{12,16},{16,20},{20,24},{24,28},{29,1},{... | collective-permute-start | bytes 98312 | tf_op jit(solution)/shard_map/ppermute | solution.py:308
  73.6 4.6 %forward.3.refs_6_ = f32[1024,128]{1,0:T(8,128)} custom-call(bf16[8,128,128]{2,1,0:T(8,128)(2,1)} %get-tuple-element.58.refs_0_, f32[1024,128]{1,0:T(8,128)} %get-tuple-element.59.refs_1_, f32[8,128]{1,0:T(8,128)} %bitcast.5, bf16[1024,1024]{1,0:T(8,128)(2,1)} %get-tuple-element.45.refs_3_, bf16[1024,1024]{1,0:T(8,128)(2,1)} %get-tuple-element.46.refs_4_), custom_call_target="tpu_custom_call" | custom-call | flops 536870912 | bytes 5509120 | tf_op jit(solution)/shard_map/forward/pallas_call | solution.py:89
  78.2 1.9 %collective-permute-done.12.refs_7_ = bf16[128,128]{1,0:T(8,128)(2,1)} collective-permute-done((bf16[128,128]{1,0:T(8,128)(2,1)}, bf16[128,128]{1,0:T(8,128)(2,1)}, u32[]{:S(2)}, u32[]{:S(2)}) %collective-permute-start.12) | collective-permute-done | bytes 32800 | tf_op jit(solution)/shard_map/ppermute | solution.py:308
  80.1 3.2 %dual_step.3 = f32[1024,128]{1,0:T(8,128)} custom-call(s32[1]{0:T(128)} %bitcast.1.refs_0_, s32[8]{0:T(128)} %refs_1_.13, s32[8]{0:T(128)} %refs_2_.9, bf16[8,128,128]{2,1,0:T(8,128)(2,1)} %refs_3_.11, bf16[1,128,128]{2,1,0:T(8,128)(2,1)} %refs_4_.5, bf16[2,128,128]{2,1,0:T(8,128)(2,1)} %get-tuple-element.57.refs_5_, f32[1024,128]{1,0:T(8,128)} %forward.3.refs_6_, ...), custom_call_target="tpu_custom_call" | custom-call | flops 67108864 | bytes 1638400 | tf_op jit(solution)/shard_map/dual_step/pallas_call | solution.py:89
  83.3 1.8 %annual_step.3 = f32[128,128]{1,0:T(8,128)} custom-call(f32[128,128]{1,0:T(8,128)} %get-tuple-element.61.refs_0_, f32[1,128]{1,0:T(1,128)} %bitcast.8, bf16[8,128,128]{2,1,0:T(8,128)(2,1)} %all-to-all-done.3.refs_2_), custom_call_target="tpu_custom_call" | custom-call | flops 131072 | bytes 393728 | tf_op jit(solution)/shard_map/annual_step/pallas_call | solution.py:89
  (19 shorter events, 0.0 us)
Async XLA Ops:
  3.6 21.2 %all-to-all-start = ((bf16[8,128,128]{2,1,0:T(8,128)(2,1)}), bf16[8,128,128]{2,1,0:T(8,128)(2,1)}, u32[]{:S(2)}, u32[]{:S(2)}) async-start(bf16[8,128,128]{2,1,0:T(8,128)(2,1)} %get-tuple-element.33), calls=%async_computation | async-start | bytes 524288 | tf_op jit(solution)/shard_map/all_to_all | solution.py:372
  10.9 13.8 %collective-permute-start = (bf16[128,128]{1,0:T(8,128)(2,1)}, bf16[128,128]{1,0:T(8,128)(2,1)}, u32[]{:S(2)}, u32[]{:S(2)}) collective-permute-start(bf16[128,128]{1,0:T(8,128)(2,1)} %get-tuple-element.35), channel_id=1, source_target_pairs={{4,0},{8,4},{12,8},{16,12},{20,16},{24,20},{28,24},{0,28},{5,1},{9... | collective-permute-start | bytes 98312 | tf_op jit(solution)/shard_map/ppermute | solution.py:308
  15.6 9.1 %collective-permute-start.1 = (bf16[2,128,128]{2,1,0:T(8,128)(2,1)}, bf16[2,128,128]{2,1,0:T(8,128)(2,1)}, u32[]{:S(2)}, u32[]{:S(2)}) collective-permute-start(bf16[2,128,128]{2,1,0:T(8,128)(2,1)} %get-tuple-element.39), channel_id=1, source_target_pairs={{3,0},{0,1},{1,2},{2,3},{7,4},{4,5},{5,6},{6,7},{11,8},{8,9},{9,10... | collective-permute-start | bytes 196616 | tf_op jit(solution)/shard_map/ppermute | solution.py:308
  15.6 9.1 %collective-permute-start.2 = (bf16[2,128,128]{2,1,0:T(8,128)(2,1)}, bf16[2,128,128]{2,1,0:T(8,128)(2,1)}, u32[]{:S(2)}, u32[]{:S(2)}) collective-permute-start(bf16[2,128,128]{2,1,0:T(8,128)(2,1)} %get-tuple-element.40), channel_id=1, source_target_pairs={{2,0},{3,1},{0,2},{1,3},{6,4},{7,5},{4,6},{5,7},{10,8},{11,9},{8,1... | collective-permute-start | bytes 196616 | tf_op jit(solution)/shard_map/ppermute | solution.py:308
  17.1 7.6 %collective-permute-start.3 = (bf16[2,128,128]{2,1,0:T(8,128)(2,1)}, bf16[2,128,128]{2,1,0:T(8,128)(2,1)}, u32[]{:S(2)}, u32[]{:S(2)}) collective-permute-start(bf16[2,128,128]{2,1,0:T(8,128)(2,1)} %get-tuple-element.41), channel_id=1, source_target_pairs={{1,0},{2,1},{3,2},{0,3},{5,4},{6,5},{7,6},{4,7},{9,8},{10,9},{11,1... | collective-permute-start | bytes 196616 | tf_op jit(solution)/shard_map/ppermute | solution.py:308
  28.3 17.1 %all-to-all-start.1 = ((bf16[8,128,128]{2,1,0:T(8,128)(2,1)}), bf16[8,128,128]{2,1,0:T(8,128)(2,1)}, u32[]{:S(2)}, u32[]{:S(2)}) async-start(bf16[8,128,128]{2,1,0:T(8,128)(2,1)} %get-tuple-element.42), calls=%async_computation.1 | async-start | bytes 524288 | tf_op jit(solution)/shard_map/all_to_all | solution.py:408
  32.3 9.5 %collective-permute-start.7 = (bf16[2,128,128]{2,1,0:T(8,128)(2,1)}, bf16[2,128,128]{2,1,0:T(8,128)(2,1)}, u32[]{:S(2)}, u32[]{:S(2)}) collective-permute-start(bf16[2,128,128]{2,1,0:T(8,128)(2,1)} %get-tuple-element.43.refs_5_), channel_id=1, source_target_pairs={{1,0},{2,1},{3,2},{0,3},{5,4},{6,5},{7,6},{4,7},{9,8},{10,9},{11,1... | collective-permute-start | bytes 196616 | tf_op jit(solution)/shard_map/ppermute | solution.py:308
  32.4 9.4 %collective-permute-start.6 = (bf16[2,128,128]{2,1,0:T(8,128)(2,1)}, bf16[2,128,128]{2,1,0:T(8,128)(2,1)}, u32[]{:S(2)}, u32[]{:S(2)}) collective-permute-start(bf16[2,128,128]{2,1,0:T(8,128)(2,1)} %get-tuple-element.43.refs_5_), channel_id=1, source_target_pairs={{2,0},{3,1},{0,2},{1,3},{6,4},{7,5},{4,6},{5,7},{10,8},{11,9},{8,1... | collective-permute-start | bytes 196616 | tf_op jit(solution)/shard_map/ppermute | solution.py:308
  33.1 8.8 %collective-permute-start.5 = (bf16[2,128,128]{2,1,0:T(8,128)(2,1)}, bf16[2,128,128]{2,1,0:T(8,128)(2,1)}, u32[]{:S(2)}, u32[]{:S(2)}) collective-permute-start(bf16[2,128,128]{2,1,0:T(8,128)(2,1)} %get-tuple-element.43.refs_5_), channel_id=1, source_target_pairs={{3,0},{0,1},{1,2},{2,3},{7,4},{4,5},{5,6},{6,7},{11,8},{8,9},{9,10... | collective-permute-start | bytes 196616 | tf_op jit(solution)/shard_map/ppermute | solution.py:308
  33.2 8.7 %collective-permute-start.4 = (bf16[128,128]{1,0:T(8,128)(2,1)}, bf16[128,128]{1,0:T(8,128)(2,1)}, u32[]{:S(2)}, u32[]{:S(2)}) collective-permute-start(bf16[128,128]{1,0:T(8,128)(2,1)} %get-tuple-element.47), channel_id=1, source_target_pairs={{28,0},{0,4},{4,8},{8,12},{12,16},{16,20},{20,24},{24,28},{29,1},{... | collective-permute-start | bytes 98312 | tf_op jit(solution)/shard_map/ppermute | solution.py:308
  47.3 15.9 %all-to-all-start.2 = ((bf16[8,128,128]{2,1,0:T(8,128)(2,1)}), bf16[8,128,128]{2,1,0:T(8,128)(2,1)}, u32[]{:S(2)}, u32[]{:S(2)}) async-start(bf16[8,128,128]{2,1,0:T(8,128)(2,1)} %get-tuple-element.49), calls=%async_computation.2 | async-start | bytes 524288 | tf_op jit(solution)/shard_map/all_to_all | solution.py:372
  51.4 11.8 %collective-permute-start.9 = (bf16[2,128,128]{2,1,0:T(8,128)(2,1)}, bf16[2,128,128]{2,1,0:T(8,128)(2,1)}, u32[]{:S(2)}, u32[]{:S(2)}) collective-permute-start(bf16[2,128,128]{2,1,0:T(8,128)(2,1)} %get-tuple-element.53), channel_id=1, source_target_pairs={{3,0},{0,1},{1,2},{2,3},{7,4},{4,5},{5,6},{6,7},{11,8},{8,9},{9,10... | collective-permute-start | bytes 196616 | tf_op jit(solution)/shard_map/ppermute | solution.py:308
  51.5 11.7 %collective-permute-start.10 = (bf16[2,128,128]{2,1,0:T(8,128)(2,1)}, bf16[2,128,128]{2,1,0:T(8,128)(2,1)}, u32[]{:S(2)}, u32[]{:S(2)}) collective-permute-start(bf16[2,128,128]{2,1,0:T(8,128)(2,1)} %get-tuple-element.54), channel_id=1, source_target_pairs={{2,0},{3,1},{0,2},{1,3},{6,4},{7,5},{4,6},{5,7},{10,8},{11,9},{8,1... | collective-permute-start | bytes 196616 | tf_op jit(solution)/shard_map/ppermute | solution.py:308
  52.9 10.4 %collective-permute-start.11 = (bf16[2,128,128]{2,1,0:T(8,128)(2,1)}, bf16[2,128,128]{2,1,0:T(8,128)(2,1)}, u32[]{:S(2)}, u32[]{:S(2)}) collective-permute-start(bf16[2,128,128]{2,1,0:T(8,128)(2,1)} %get-tuple-element.55), channel_id=1, source_target_pairs={{1,0},{2,1},{3,2},{0,3},{5,4},{6,5},{7,6},{4,7},{9,8},{10,9},{11,1... | collective-permute-start | bytes 196616 | tf_op jit(solution)/shard_map/ppermute | solution.py:308
  54.3 8.9 %collective-permute-start.8 = (bf16[128,128]{1,0:T(8,128)(2,1)}, bf16[128,128]{1,0:T(8,128)(2,1)}, u32[]{:S(2)}, u32[]{:S(2)}) collective-permute-start(bf16[128,128]{1,0:T(8,128)(2,1)} %get-tuple-element.50), channel_id=1, source_target_pairs={{4,0},{8,4},{12,8},{16,12},{20,16},{24,20},{28,24},{0,28},{5,1},{9... | collective-permute-start | bytes 98312 | tf_op jit(solution)/shard_map/ppermute | solution.py:308
  66.7 16.6 %all-to-all-start.3 = ((bf16[8,128,128]{2,1,0:T(8,128)(2,1)}), bf16[8,128,128]{2,1,0:T(8,128)(2,1)}, u32[]{:S(2)}, u32[]{:S(2)}) async-start(bf16[8,128,128]{2,1,0:T(8,128)(2,1)} %get-tuple-element.62), calls=%async_computation.3 | async-start | bytes 524288 | tf_op jit(solution)/shard_map/all_to_all | solution.py:408
  70.8 9.3 %collective-permute-start.15 = (bf16[2,128,128]{2,1,0:T(8,128)(2,1)}, bf16[2,128,128]{2,1,0:T(8,128)(2,1)}, u32[]{:S(2)}, u32[]{:S(2)}) collective-permute-start(bf16[2,128,128]{2,1,0:T(8,128)(2,1)} %get-tuple-element.57.refs_5_), channel_id=1, source_target_pairs={{1,0},{2,1},{3,2},{0,3},{5,4},{6,5},{7,6},{4,7},{9,8},{10,9},{11,1... | collective-permute-start | bytes 196616 | tf_op jit(solution)/shard_map/ppermute | solution.py:308
  70.9 9.2 %collective-permute-start.14 = (bf16[2,128,128]{2,1,0:T(8,128)(2,1)}, bf16[2,128,128]{2,1,0:T(8,128)(2,1)}, u32[]{:S(2)}, u32[]{:S(2)}) collective-permute-start(bf16[2,128,128]{2,1,0:T(8,128)(2,1)} %get-tuple-element.57.refs_5_), channel_id=1, source_target_pairs={{2,0},{3,1},{0,2},{1,3},{6,4},{7,5},{4,6},{5,7},{10,8},{11,9},{8,1... | collective-permute-start | bytes 196616 | tf_op jit(solution)/shard_map/ppermute | solution.py:308
  71.6 8.5 %collective-permute-start.13 = (bf16[2,128,128]{2,1,0:T(8,128)(2,1)}, bf16[2,128,128]{2,1,0:T(8,128)(2,1)}, u32[]{:S(2)}, u32[]{:S(2)}) collective-permute-start(bf16[2,128,128]{2,1,0:T(8,128)(2,1)} %get-tuple-element.57.refs_5_), channel_id=1, source_target_pairs={{3,0},{0,1},{1,2},{2,3},{7,4},{4,5},{5,6},{6,7},{11,8},{8,9},{9,10... | collective-permute-start | bytes 196616 | tf_op jit(solution)/shard_map/ppermute | solution.py:308
  71.8 8.3 %collective-permute-start.12 = (bf16[128,128]{1,0:T(8,128)(2,1)}, bf16[128,128]{1,0:T(8,128)(2,1)}, u32[]{:S(2)}, u32[]{:S(2)}) collective-permute-start(bf16[128,128]{1,0:T(8,128)(2,1)} %get-tuple-element.60), channel_id=1, source_target_pairs={{28,0},{0,4},{4,8},{8,12},{12,16},{16,20},{20,24},{24,28},{29,1},{... | collective-permute-start | bytes 98312 | tf_op jit(solution)/shard_map/ppermute | solution.py:308

commit v3 on v2

--- a/solution.py
+++ b/solution.py
@@ -23,17 +23,19 @@
 
 
 class Arriving:
-    def __init__(self, source, target, sems, at, pieces):
-        length = source.shape[0] // pieces
+    def __init__(self, source, target, sems, at, pieces, axis):
+        length = source.shape[axis] // pieces
         self.target = target
         self.copies = []
         for p in range(pieces):
-            rows = pl.ds(p * length, length)
+            part = (slice(None),) * axis + (pl.ds(p * length, length),)
             self.copies.append(
-                pltpu.make_async_copy(source.at[rows], target.at[rows], sems.at[at + p])
-            )
-        for copy in self.copies:
-            copy.start()
+                pltpu.make_async_copy(source.at[part], target.at[part], sems.at[at + p])
+            )
+
+    def start(self, piece):
+        if piece < len(self.copies):
+            self.copies[piece].start()
 
     def piece(self):
         self.copies.pop(0).wait()
@@ -46,19 +48,32 @@
 
 
 class Leaving:
-    def __init__(self, source, target, sem):
+    def __init__(self, source, target, sems, at, pieces):
+        length = source.shape[0] // pieces
         self.ref = source
-        self.copy = pltpu.make_async_copy(source, target, sem)
-        self.sent = False
+        self.waiting = []
+        for p in range(pieces):
+            part = pl.ds(p * length, length)
+            self.waiting.append(
+                pltpu.make_async_copy(source.at[part], target.at[part], sems.at[at + p])
+            )
+        self.flying = []
 
     def send(self):
-        self.copy.start()
-        self.sent = True
-
-
-def run(body, name, scalars, arrays, outs, scratch, flops, pieces={}):
-    counts = [pieces.get(i, 1) for i in range(len(arrays))]
+        copy = self.waiting.pop(0)
+        copy.start()
+        self.flying.append(copy)
+
+    def finish(self):
+        for copy in self.flying:
+            copy.wait()
+
+
+def run(body, name, scalars, arrays, outs, scratch, flops, pieces={}, out_pieces={}):
+    counts = [pieces.get(i, (1, 0)) for i in range(len(arrays))]
+    out_counts = [out_pieces.get(i, 1) for i in range(len(outs))]
     ns, na, no = len(scalars), len(arrays), len(outs)
+    most = max(count for count, _ in counts)
 
     def kernel(*refs):
         scalar_refs, refs = refs[:ns], refs[ns:]
@@ -69,21 +84,25 @@
         (in_sems, out_sems), extra = refs[:2], refs[2:]
         at = 0
         arriving = []
-        for source, target, count in zip(sources, landing, counts):
-            arriving.append(Arriving(source, target, in_sems, at, count))
+        for source, target, (count, axis) in zip(sources, landing, counts):
+            arriving.append(Arriving(source, target, in_sems, at, count, axis))
             at += count
-        leaving = [
-            Leaving(source, target, out_sems.at[i])
-            for i, (source, target) in enumerate(zip(staging, targets))
-        ]
+        for p in range(most):
+            for item in arriving:
+                item.start(p)
+        at = 0
+        leaving = []
+        for source, target, count in zip(staging, targets, out_counts):
+            leaving.append(Leaving(source, target, out_sems, at, count))
+            at += count
         body(scalar_refs, arriving, leaving, *extra)
         for item in arriving:
             item()
         for item in leaving:
-            if not item.sent:
+            while item.waiting:
                 item.send()
         for item in leaving:
-            item.copy.wait()
+            item.finish()
 
     moved = sum(a.size * a.dtype.itemsize for a in (*arrays, *outs))
     return pl.pallas_call(
@@ -93,7 +112,10 @@
         out_specs=(HBM,) * no,
         out_shape=tuple(outs),
         scratch_shapes=[pltpu.VMEM(a.shape, a.dtype) for a in (*arrays, *outs)]
-        + [pltpu.SemaphoreType.DMA((sum(counts),)), pltpu.SemaphoreType.DMA((no,))]
+        + [
+            pltpu.SemaphoreType.DMA((sum(count for count, _ in counts),)),
+            pltpu.SemaphoreType.DMA((sum(out_counts),)),
+        ]
         + scratch,
         compiler_params=pltpu.CompilerParams(vmem_limit_bytes=64 << 20),
         cost_estimate=pl.CostEstimate(flops=flops, bytes_accessed=moved, transcendentals=0),
@@ -112,8 +134,11 @@
     return jnp.broadcast_to(row_vector, (width, row_vector.shape[1])).T
 
 
-def wrap(value, number):
-    return jnp.where(value >= number, value - number, value)
+def partner(me, d, number, receive):
+    if number & (number - 1) == 0:
+        return me ^ d
+    other = me + (number - d if receive else d)
+    return jnp.where(other >= number, other - number, other)
 
 
 def send_duals(refineries, dual_q, me, rows, src, swing, carry, outs, acc):
@@ -124,7 +149,7 @@
     for m in range(swing.shape[0]):
         acc[src[m]] += dot_transposed(swing[m], dual_q[rows[m]])
     for d, send in enumerate(sends, 1):
-        send.ref[...] = acc[pl.ds(wrap(me + d, refineries) * SC, SC)].astype(BF16)
+        send.ref[...] = acc[pl.ds(partner(me, d, refineries, False) * SC, SC)].astype(BF16)
         send.send()
     own.ref[...] = acc[pl.ds(me * SC, SC)]
     own.send()
@@ -146,19 +171,21 @@
     send_duals(refineries, dual_q.ref, me[0], rows, src, swing(), carry(), outs[2:], acc)
 
 
-def adjoint(high, low, dual_q, primal, prices, out):
+def adjoint(high, low, dual_q, primal, prices, out, chunks):
     blocks, size, _ = dual_q.shape
     turned = jnp.concatenate([dual_q[i].T for i in range(blocks)], axis=1)
-    step = 2 * size
-    for j in range(high.shape[1] // step):
-        part = dot(turned, high[:, j * step : (j + 1) * step]) + dot(
-            turned, low[:, j * step : (j + 1) * step]
-        )
-        for h in range(2):
+    step = out.ref.shape[0] // chunks
+    for j in range(chunks):
+        columns = slice(j * step, (j + 1) * step)
+        part = dot(turned, high()[:, columns]) + dot(turned, low()[:, columns])
+        if j == 0:
+            primal, prices = primal(), prices()
+        for h in range(step // size):
             at = slice(j * step + h * size, j * step + (h + 1) * size)
-            out[at] = primal[at] - PRIMAL_STEP * (
+            out.ref[at] = primal[at] - PRIMAL_STEP * (
                 prices[at] - part[:, h * size : (h + 1) * size].T
             )
+        out.send()
 
 
 def dense_body(chunks, scalars, ins, outs, acc):
@@ -191,12 +218,12 @@
     for j in range(tiles):
         upper_full.ref[j * size : (j + 1) * size] = column_of(upper[j : j + 1], width)
     upper_full.send()
-    adjoint(high.ref, low.ref, dual_q(), primal(), prices(), out.ref)
-
-
-def adjoint_body(scalars, ins, outs):
-    dual_q, primal, prices, high, low = ins
-    adjoint(high(), low(), dual_q(), primal(), prices(), outs[0].ref)
+    adjoint(lambda: high.ref, lambda: low.ref, dual_q(), primal, prices, out, chunks)
+
+
+def adjoint_body(chunks, scalars, ins, outs):
+    dual_q, high, low, primal, prices = ins
+    adjoint(high.piece, low.piece, dual_q(), primal, prices, outs[0], chunks)
 
 
 def primal_body(scalars, ins, outs, acc, image_acc):
@@ -236,76 +263,81 @@
     image.ref[...] = image_acc[...].astype(BF16)
 
 
-def forward_body(scalars, ins, outs):
-    extrap, dual, demand, high, low = ins
-    out = outs[0].ref
-    extrap, dual, demand = extrap(), dual(), demand()
+def forward_body(chunks, scalars, ins, outs):
+    extrap, high, low, dual, demand = ins
+    out = outs[0]
+    extrap = extrap()
     blocks, size, width = extrap.shape
     right = jnp.concatenate([extrap[j] for j in range(blocks)], axis=0)
-    high, low = high(), low()
-    step = 2 * size
-    for i in range(high.shape[0] // step):
-        part = dot(high[i * step : (i + 1) * step], right) + dot(
-            low[i * step : (i + 1) * step], right
-        )
-        for h in range(2):
+    step = out.ref.shape[0] // chunks
+    for i in range(chunks):
+        lines = slice(i * step, (i + 1) * step)
+        part = dot(high.piece()[lines], right) + dot(low.piece()[lines], right)
+        if i == 0:
+            dual, demand = dual(), demand()
+        for h in range(step // size):
             at = slice(i * step + h * size, i * step + (h + 1) * size)
-            row = 2 * i + h
-            out[at] = dual[at] + DUAL_STEP * (
+            row = i * (step // size) + h
+            out.ref[at] = dual[at] + DUAL_STEP * (
                 column_of(demand[row : row + 1], width) - part[h * size : (h + 1) * size]
             )
+        out.send()
 
 
 def dual_body(refineries, more, scalars, ins, outs, gathered, acc, *stream_acc):
     me, rows, src = scalars
-    swing, carry, streams, partial, previous, *arrived = ins
-    dual = outs[0]
+    swing, carry, streams, partial, previous, parts, annual, need, *arrived = ins
+    dual, annual_out = outs[0], outs[1]
     swing, carry = swing(), carry()
     size = swing.shape[1]
     mine = me[0]
     gathered[pl.ds(mine * SC, SC)] = streams()[...]
     for d, piece in enumerate(arrived, 1):
-        gathered[pl.ds(wrap(mine + refineries - d, refineries) * SC, SC)] = piece()[...]
+        gathered[pl.ds(partner(mine, d, refineries, True) * SC, SC)] = piece()[...]
     acc[...] = jnp.zeros_like(acc)
     for m in range(swing.shape[0]):
         acc[rows[m]] += dot(swing[m], gathered[src[m]])
     acc[0] += dot(carry[0], previous()[...])
+    parts, annual = parts(), annual()
+    total = parts[0].astype(F32)
+    for w in range(1, parts.shape[0]):
+        total = total + parts[w].astype(F32)
+    new_annual = jnp.maximum(
+        annual[...] + DUAL_STEP * (column_of(need()[...], annual.shape[1]) - total), 0.0
+    )
+    annual_out.ref[...] = new_annual
+    annual_out.send()
+    if more:
+        rounded = new_annual.astype(BF16)
+        for w in range(parts.shape[0]):
+            outs[2].ref[w] = rounded
+        outs[2].send()
     partial = partial()
     for i in range(acc.shape[0]):
         at = slice(i * size, (i + 1) * size)
         new = jnp.maximum(partial[at] - DUAL_STEP * acc[i], 0.0)
         dual.ref[at] = new
         if more:
-            outs[1].ref[i] = new.astype(BF16)
+            outs[3].ref[i] = new.astype(BF16)
     dual.send()
     if more:
-        outs[1].send()
+        outs[3].send()
         send_duals(
-            refineries, outs[1].ref, mine, rows, src, swing, carry, outs[2:], *stream_acc
+            refineries, outs[3].ref, mine, rows, src, swing, carry, outs[4:], *stream_acc
         )
-
-
-def annual_body(more, scalars, ins, outs):
-    annual, need, parts, *_ = ins
-    parts = parts()
-    total = parts[0].astype(F32)
-    for w in range(1, parts.shape[0]):
-        total = total + parts[w].astype(F32)
-    annual = annual()
-    new = jnp.maximum(
-        annual[...] + DUAL_STEP * (column_of(need()[...], annual.shape[1]) - total), 0.0
-    )
-    outs[-1].ref[...] = new
-    if more:
-        rounded = new.astype(BF16)
-        for w in range(parts.shape[0]):
-            outs[0].ref[w] = rounded
 
 
 def shifted(block, axis, distance):
     number = lax.axis_size(axis)
     route = [((i - distance) % number, i) for i in range(number)]
     return lax.ppermute(block, axis, route)
+
+
+def exchanged(block, axis, d):
+    number = lax.axis_size(axis)
+    if number & (number - 1) == 0:
+        return lax.ppermute(block, axis, [(i, i ^ d) for i in range(number)])
+    return shifted(block, axis, d)
 
 
 def body(
@@ -351,7 +383,9 @@
     unit = 2 * size * size * scenarios
     stream_scratch = pltpu.VMEM((refineries * SC, size, scenarios), F32)
     sends_shape = [pair] + [pair_q] * others + [tile]
-    chunks = 4 if slots % 4 == 0 else 1
+    chunks = 4 if slots % 4 == 0 and columns % 4 == 0 else 1
+    parts_x = 4 if columns % 4 == 0 else 1
+    parts_y = 4 if rows % 4 == 0 else 1
 
     upper_rows = upper.reshape(columns, size)
     demand_rows = demand.reshape(rows, size)
@@ -370,7 +404,7 @@
         more = iteration + 1 < ITERS
         sends, carried = rest[:others], rest[others]
         annual_q = lax.all_to_all(annual_send, "period", 0, 0, tiled=True)
-        arrived = [shifted(send, "refinery", d) for d, send in enumerate(sends, 1)]
+        arrived = [exchanged(send, "refinery", d) for d, send in enumerate(sends, 1)]
         carried_back = shifted(carried, "period", -1)
         if iteration == 0:
             high, low, upper_full, partial_x = run(
@@ -381,17 +415,20 @@
                 [matrix, matrix, state_x, state_x],
                 [pltpu.VMEM((rows * columns, size, size), F32)],
                 3 * rows * columns * unit,
-                {0: chunks},
+                {0: (chunks, 0)},
+                {3: chunks},
             )
         else:
             (partial_x,) = run(
-                adjoint_body,
+                functools.partial(adjoint_body, parts_x),
                 "adjoint",
                 [],
-                [dual_q, primal, cost, high, low],
+                [dual_q, high, low, primal, cost],
                 [state_x],
                 [],
                 2 * rows * columns * unit,
+                {1: (parts_x, 1), 2: (parts_x, 1)},
+                {0: parts_x},
             )
         image, streams, last, extrap, updated = run(
             primal_body,
@@ -406,23 +443,29 @@
             2 * annuals * unit,
         )
         parts = lax.all_to_all(image, "period", 0, 0, tiled=True)
-        others_streams = [shifted(streams, "refinery", d) for d in range(1, refineries)]
+        others_streams = [exchanged(streams, "refinery", d) for d in range(1, refineries)]
         previous = shifted(last, "period", 1)
         (partial_y,) = run(
-            forward_body,
+            functools.partial(forward_body, parts_y),
             "forward",
             [],
-            [extrap, dual, demand_rows, high, low],
+            [extrap, high, low, dual, demand_rows],
             [state_y],
             [],
             2 * rows * columns * unit,
+            {1: (parts_y, 0), 2: (parts_y, 0)},
+            {0: parts_y},
         )
-        dual, *rest = run(
+        sent = [weekly, blocks_y] + sends_shape if more else []
+        dual, annual, *rest = run(
             functools.partial(dual_body, refineries, more),
             "dual_step",
             [me, swing_rows, swing_src],
-            [swing_blocks, carry_blocks, streams, partial_y, previous, *others_streams],
-            [state_y] + ([blocks_y] + sends_shape if more else []),
+            [
+                swing_blocks, carry_blocks, streams, partial_y, previous, parts, annual, need,
+                *others_streams,
+            ],
+            [state_y, shape((size, scenarios), F32)] + sent,
             [
                 pltpu.VMEM((refineries * SC, size, scenarios), BF16),
                 pltpu.VMEM((rows, size, scenarios), F32),
@@ -431,18 +474,7 @@
             2 * swings * unit,
         )
         if more:
-            dual_q, own, *rest = rest
-        *next_send, annual = run(
-            functools.partial(annual_body, more),
-            "annual_step",
-            [],
-            [annual, need, parts] + ([own] if more else []),
-            ([weekly] if more else []) + [shape((size, scenarios), F32)],
-            [],
-            size * scenarios * weeks,
-        )
-        if more:
-            (annual_send,) = next_send
+            annual_send, dual_q, own, *rest = rest
         primal = updated
     return primal, dual, annual
 

time: 85.9 us -> 83.8 us (0.976)
  Pallas kernels: 39.4 us -> 35.8 us
  waiting for transfers between devices: 4.18 us -> 5.65 us
    ppermute x0 -> x12, starting transfers between devices: none -> 7.7 us  [exchanged(): return lax.ppermute(block, axis, [(i, i ^ d) for i in range(number)])]
    ppermute x16 -> x4, starting transfers between devices: 20.6 us -> 12.9 us  [shifted(): return lax.ppermute(block, axis, route)]
    pallas_call x11 -> x9, Pallas kernels: 39.4 us -> 35.8 us  [run(): pl.pallas_call(kernel, name=name, in_specs=[SMEM] * ns + [HBM] * na, out_...]
    ppermute x16 -> x4, waiting for transfers between devices: 4.16 us -> 5.6 us  [shifted(): return lax.ppermute(block, axis, route)]
  transfers between devices with their start and end apart: 20 -> 20, of which waited for: 2 -> 2; matrix products, arithmetic and copies ran while one was open for 0% -> 0% of each run, Pallas kernels for 30% -> 22%
where the time goes in v3:
time: 83.8 us; the launch traced here: 83 us
  starting transfers between devices  40 us (48%)
  Pallas kernels  35.8 us (43%)
  waiting for transfers between devices  5.65 us (7%)
  between operations  1.49 us (2%)
    pallas_call x9, Pallas kernels, run(): pl.pallas_call(kernel, name=name, in_specs=[SMEM] * ns + [HBM] * na, out_...  35.8 us
    ppermute x4, starting transfers between devices, shifted(): return lax.ppermute(block, axis, route)  12.9 us
    all_to_all x2, starting transfers between devices, body(): annual_q = lax.all_to_all(annual_send, 'period', 0, 0, tiled=True)  11.3 us
    all_to_all x2, starting transfers between devices, body(): parts = lax.all_to_all(image, 'period', 0, 0, tiled=True)  8.12 us
    ppermute x12, starting transfers between devices, exchanged(): return lax.ppermute(block, axis, [(i, i ^ d) for i in range(number)])  7.7 us
    ppermute x4, waiting for transfers between devices, shifted(): return lax.ppermute(block, axis, route)  5.6 us
  transfers between devices with their start and end apart: 20, of which 2 were waited for; matrix products, arithmetic and copies ran while one was open for 0% of the time, Pallas kernels for 22%

profile of v3, /device:TPU:0, one launch (start us, length us, event | category | flops | bytes accessed | tf_op | source)
XLA Modules:
  0.0 83.0 jit_solution(4290432921403514052)
XLA Ops:
  0.6 3.0 %first_duals.1 = (bf16[8,128,128]{2,1,0:T(8,128)(2,1)}, bf16[8,128,128]{2,1,0:T(8,128)(2,1)}, f32[2,128,128]{2,1,0:T(8,128)}, bf16[2,128,128]{2,1,0:T(8,128)(2,1...) custom-call(s32[1]{0:T(128)} %bitcast.refs_0_, s32[8]{0:T(128)} %refs_1_.11, ...), custom_call_target="tpu_custom_call" | custom-call | flops 37748736 | bytes 1769472 | tf_op jit(solution)/shard_map/first_duals/pallas_call | solution.py:108
  3.6 7.3 %all-to-all-start = ((bf16[8,128,128]{2,1,0:T(8,128)(2,1)}), bf16[8,128,128]{2,1,0:T(8,128)(2,1)}, u32[]{:S(2)}, u32[]{:S(2)}) async-start(bf16[8,128,128]{2,1,0:T(8,128)(2,1)} %get-tuple-element.35), calls=%async_computation | async-start | bytes 524288 | tf_op jit(solution)/shard_map/all_to_all | solution.py:406
  10.9 4.7 %collective-permute-start = (bf16[128,128]{1,0:T(8,128)(2,1)}, bf16[128,128]{1,0:T(8,128)(2,1)}, u32[]{:S(2)}, u32[]{:S(2)}) collective-permute-start(bf16[128,128]{1,0:T(8,128)(2,1)} %get-tuple-element.37), channel_id=1, source_target_pairs={{4,0},{8,4},{12,8},{16,12},{20,16},{24,20},{28,24},{0,28},{5,1},{9... | collective-permute-start | bytes 98312 | tf_op jit(solution)/shard_map/ppermute | solution.py:333
  15.6 0.0 collective-permute-start.1
  15.6 1.5 %collective-permute-start.2 = (bf16[2,128,128]{2,1,0:T(8,128)(2,1)}, bf16[2,128,128]{2,1,0:T(8,128)(2,1)}, u32[]{:S(2)}, u32[]{:S(2)}) collective-permute-start(bf16[2,128,128]{2,1,0:T(8,128)(2,1)} %get-tuple-element.42), channel_id=1, source_target_pairs={{0,2},{1,3},{2,0},{3,1},{4,6},{5,7},{6,4},{7,5},{8,10},{9,11},{10,... | collective-permute-start | bytes 196616 | tf_op jit(solution)/shard_map/ppermute | solution.py:339
  17.1 0.4 collective-permute-start.3
  18.1 6.2 %dense.1 = (bf16[1024,1024]{1,0:T(8,128)(2,1)}, bf16[1024,1024]{1,0:T(8,128)(2,1)}, f32[1024,128]{1,0:T(8,128)}, f32[1024,128]{1,0:T(8,128)}) custom-call(s32[1]{0:T(128)S(6)} %copy.21.refs_0_, s32[96]{0:T(128)} %refs_1_.7, s32[96]{0:T(128)} %refs_2_.5, bf16[96,128,128]{2,1,0:T(8,128)(2,1)} %refs_3_.8, f32[8,128]{1,0:T(8,128)} %bitcast.6, ...), custom_call_target="tpu_custom_call" | custom-call | flops 805306368 | bytes 9703424 | tf_op jit(solution)/shard_map/dense/pallas_call | solution.py:108
  24.3 0.0 collective-permute-done.2.refs_10_
  24.3 3.5 %primal_step.2 = (bf16[8,128,128]{2,1,0:T(8,128)(2,1)}, bf16[2,128,128]{2,1,0:T(8,128)(2,1)}, bf16[128,128]{1,0:T(8,128)(2,1)}, bf16[8,128,128]{2,1,0:T(8,128)(2,1)}, f32[1024,128]{1,0:T(8,128)}) custom-call(s32[8]{0:T(128)} %refs_0_.4, s32[8]{0:T(128)} %refs_1_.10, bf16[8,128,128]{2,1,0:T(8,128)(2,1)} %all-to-all-done.refs_2_, ...), custom_call_target="tpu_custom_call" | custom-call | flops 67108864 | bytes 3604480 | tf_op jit(solution)/shard_map/primal_step/pallas_call | solution.py:108
  27.9 4.1 %all-to-all-start.1 = ((bf16[8,128,128]{2,1,0:T(8,128)(2,1)}), bf16[8,128,128]{2,1,0:T(8,128)(2,1)}, u32[]{:S(2)}, u32[]{:S(2)}) async-start(bf16[8,128,128]{2,1,0:T(8,128)(2,1)} %get-tuple-element.49), calls=%async_computation.1 | async-start | bytes 524288 | tf_op jit(solution)/shard_map/all_to_all | solution.py:445
  31.9 1.4 %collective-permute-start.7 = (bf16[2,128,128]{2,1,0:T(8,128)(2,1)}, bf16[2,128,128]{2,1,0:T(8,128)(2,1)}, u32[]{:S(2)}, u32[]{:S(2)}) collective-permute-start(bf16[2,128,128]{2,1,0:T(8,128)(2,1)} %get-tuple-element.44.refs_5_), channel_id=1, source_target_pairs={{0,3},{1,2},{2,1},{3,0},{4,7},{5,6},{6,5},{7,4},{8,11},{9,10},{10,... | collective-permute-start | bytes 196616 | tf_op jit(solution)/shard_map/ppermute | solution.py:339
  33.4 0.5 collective-permute-start.6
  33.9 1.8 %collective-permute-start.4 = (bf16[128,128]{1,0:T(8,128)(2,1)}, bf16[128,128]{1,0:T(8,128)(2,1)}, u32[]{:S(2)}, u32[]{:S(2)}) collective-permute-start(bf16[128,128]{1,0:T(8,128)(2,1)} %get-tuple-element.48), channel_id=1, source_target_pairs={{28,0},{0,4},{4,8},{8,12},{12,16},{16,20},{20,24},{24,28},{29,1},{... | collective-permute-start | bytes 98312 | tf_op jit(solution)/shard_map/ppermute | solution.py:333
  35.7 4.0 %forward.2.refs_6_ = f32[1024,128]{1,0:T(8,128)} custom-call(bf16[8,128,128]{2,1,0:T(8,128)(2,1)} %get-tuple-element.45.refs_0_, bf16[1024,1024]{1,0:T(8,128)(2,1)} %get-tuple-element.46.refs_1_, bf16[1024,1024]{1,0:T(8,128)(2,1)} %get-tuple-element.47.refs_2_, f32[1024,128]{1,0:T(8,128)} %refs_3_.10, f32[8,128]{1,0:T(8,128)} %bitcast.4), custom_call_target="tpu_custom_call" | custom-call | flops 536870912 | bytes 5509120 | tf_op jit(solution)/shard_map/forward/pallas_call | solution.py:108
  39.7 2.9 %collective-permute-done.4.refs_7_ = bf16[128,128]{1,0:T(8,128)(2,1)} collective-permute-done((bf16[128,128]{1,0:T(8,128)(2,1)}, bf16[128,128]{1,0:T(8,128)(2,1)}, u32[]{:S(2)}, u32[]{:S(2)}) %collective-permute-start.4) | collective-permute-done | bytes 32800 | tf_op jit(solution)/shard_map/ppermute | solution.py:333
  42.7 0.0 all-to-all-done.1.refs_8_
  42.7 3.8 %dual_step.2 = (f32[1024,128]{1,0:T(8,128)}, f32[128,128]{1,0:T(8,128)}, bf16[8,128,128]{2,1,0:T(8,128)(2,1)}, bf16[8,128,128]{2,1,0:T(8,128)(2,1)}, f32[2,128,1...) custom-call(s32[1]{0:T(128)} %bitcast.refs_0_, ...), custom_call_target="tpu_custom_call" | custom-call | flops 67108864 | bytes 2916864 | tf_op jit(solution)/shard_map/dual_step/pallas_call | solution.py:108
  46.5 4.1 %all-to-all-start.2 = ((bf16[8,128,128]{2,1,0:T(8,128)(2,1)}), bf16[8,128,128]{2,1,0:T(8,128)(2,1)}, u32[]{:S(2)}, u32[]{:S(2)}) async-start(bf16[8,128,128]{2,1,0:T(8,128)(2,1)} %get-tuple-element.50), calls=%async_computation.2 | async-start | bytes 524288 | tf_op jit(solution)/shard_map/all_to_all | solution.py:406
  50.6 0.1 collective-permute-start.9
  50.7 1.6 %collective-permute-start.10 = (bf16[2,128,128]{2,1,0:T(8,128)(2,1)}, bf16[2,128,128]{2,1,0:T(8,128)(2,1)}, u32[]{:S(2)}, u32[]{:S(2)}) collective-permute-start(bf16[2,128,128]{2,1,0:T(8,128)(2,1)} %get-tuple-element.56), channel_id=1, source_target_pairs={{0,2},{1,3},{2,0},{3,1},{4,6},{5,7},{6,4},{7,5},{8,10},{9,11},{10,... | collective-permute-start | bytes 196616 | tf_op jit(solution)/shard_map/ppermute | solution.py:339
  52.2 0.3 collective-permute-start.11
  52.5 4.6 %collective-permute-start.8 = (bf16[128,128]{1,0:T(8,128)(2,1)}, bf16[128,128]{1,0:T(8,128)(2,1)}, u32[]{:S(2)}, u32[]{:S(2)}) collective-permute-start(bf16[128,128]{1,0:T(8,128)(2,1)} %get-tuple-element.52), channel_id=1, source_target_pairs={{4,0},{8,4},{12,8},{16,12},{20,16},{24,20},{28,24},{0,28},{5,1},{9... | collective-permute-start | bytes 98312 | tf_op jit(solution)/shard_map/ppermute | solution.py:333
  57.1 4.3 %adjoint.1.refs_8_ = f32[1024,128]{1,0:T(8,128)} custom-call(bf16[8,128,128]{2,1,0:T(8,128)(2,1)} %get-tuple-element.54.refs_0_, bf16[1024,1024]{1,0:T(8,128)(2,1)} %get-tuple-element.46.refs_1_, bf16[1024,1024]{1,0:T(8,128)(2,1)} %get-tuple-element.47.refs_2_, f32[1024,128]{1,0:T(8,128)} %get-tuple-element.53.refs_3_.refs_6_, f32[1024,128]{1,0:T(8,128)} %refs_4_.6), custom_call_target="tpu_custom_call" | custom-call | flops 536870912 | bytes 6029312 | tf_op jit(solution)/shard_map/adjoint/pallas_call | solution.py:108
  61.5 3.5 %primal_step.3 = (bf16[8,128,128]{2,1,0:T(8,128)(2,1)}, bf16[2,128,128]{2,1,0:T(8,128)(2,1)}, bf16[128,128]{1,0:T(8,128)(2,1)}, bf16[8,128,128]{2,1,0:T(8,128)(2,1)}, f32[1024,128]{1,0:T(8,128)}) custom-call(s32[8]{0:T(128)} %refs_0_.4, s32[8]{0:T(128)} %refs_1_.10, bf16[8,128,128]{2,1,0:T(8,128)(2,1)} %all-to-all-done.2.refs_2_, ...), custom_call_target="tpu_custom_call" | custom-call | flops 67108864 | bytes 3604480 | tf_op jit(solution)/shard_map/primal_step/pallas_call | solution.py:108
  65.0 4.1 %all-to-all-start.3 = ((bf16[8,128,128]{2,1,0:T(8,128)(2,1)}), bf16[8,128,128]{2,1,0:T(8,128)(2,1)}, u32[]{:S(2)}, u32[]{:S(2)}) async-start(bf16[8,128,128]{2,1,0:T(8,128)(2,1)} %get-tuple-element.63), calls=%async_computation.3 | async-start | bytes 524288 | tf_op jit(solution)/shard_map/all_to_all | solution.py:445
  69.0 1.2 %collective-permute-start.15 = (bf16[2,128,128]{2,1,0:T(8,128)(2,1)}, bf16[2,128,128]{2,1,0:T(8,128)(2,1)}, u32[]{:S(2)}, u32[]{:S(2)}) collective-permute-start(bf16[2,128,128]{2,1,0:T(8,128)(2,1)} %get-tuple-element.59.refs_5_), channel_id=1, source_target_pairs={{0,3},{1,2},{2,1},{3,0},{4,7},{5,6},{6,5},{7,4},{8,11},{9,10},{10,... | collective-permute-start | bytes 196616 | tf_op jit(solution)/shard_map/ppermute | solution.py:339
  70.2 0.5 collective-permute-start.14
  70.7 0.2 collective-permute-start.13
  71.0 1.8 %collective-permute-start.12 = (bf16[128,128]{1,0:T(8,128)(2,1)}, bf16[128,128]{1,0:T(8,128)(2,1)}, u32[]{:S(2)}, u32[]{:S(2)}) collective-permute-start(bf16[128,128]{1,0:T(8,128)(2,1)} %get-tuple-element.62), channel_id=1, source_target_pairs={{28,0},{0,4},{4,8},{8,12},{12,16},{16,20},{20,24},{24,28},{29,1},{... | collective-permute-start | bytes 98312 | tf_op jit(solution)/shard_map/ppermute | solution.py:333
  72.8 4.0 %forward.3.refs_6_ = f32[1024,128]{1,0:T(8,128)} custom-call(bf16[8,128,128]{2,1,0:T(8,128)(2,1)} %get-tuple-element.60.refs_0_, bf16[1024,1024]{1,0:T(8,128)(2,1)} %get-tuple-element.46.refs_1_, bf16[1024,1024]{1,0:T(8,128)(2,1)} %get-tuple-element.47.refs_2_, f32[1024,128]{1,0:T(8,128)} %get-tuple-element.61.refs_3_, f32[8,128]{1,0:T(8,128)} %bitcast.5), custom_call_target="tpu_custom_call" | custom-call | flops 536870912 | bytes 5509120 | tf_op jit(solution)/shard_map/forward/pallas_call | solution.py:108
  76.8 2.7 %collective-permute-done.12.refs_7_ = bf16[128,128]{1,0:T(8,128)(2,1)} collective-permute-done((bf16[128,128]{1,0:T(8,128)(2,1)}, bf16[128,128]{1,0:T(8,128)(2,1)}, u32[]{:S(2)}, u32[]{:S(2)}) %collective-permute-start.12) | collective-permute-done | bytes 32800 | tf_op jit(solution)/shard_map/ppermute | solution.py:333
  79.5 3.5 %dual_step.3 = (f32[1024,128]{1,0:T(8,128)}, f32[128,128]{1,0:T(8,128)}) custom-call(s32[1]{0:T(128)} %bitcast.refs_0_, s32[8]{0:T(128)} %refs_1_.11, s32[8]{0:T(128)} %refs_2_.7, bf16[8,128,128]{2,1,0:T(8,128)(2,1)} %refs_3_.13, bf16[1,128,128]{2,1,0:T(8,128)(2,1)} %refs_4_.7, bf16[2,128,128]{2,1,0:T(8,128)(2,1)} %get-tuple-element.59.refs_5_, ...), custom_call_target="tpu_custom_call" | custom-call | flops 67108864 | bytes 2032128 | tf_op jit(solution)/shard_map/dual_step/pallas_call | solution.py:108
  (17 shorter events, 0.0 us)
Async XLA Ops:
  3.6 20.8 %all-to-all-start = ((bf16[8,128,128]{2,1,0:T(8,128)(2,1)}), bf16[8,128,128]{2,1,0:T(8,128)(2,1)}, u32[]{:S(2)}, u32[]{:S(2)}) async-start(bf16[8,128,128]{2,1,0:T(8,128)(2,1)} %get-tuple-element.35), calls=%async_computation | async-start | bytes 524288 | tf_op jit(solution)/shard_map/all_to_all | solution.py:406
  10.9 13.4 %collective-permute-start = (bf16[128,128]{1,0:T(8,128)(2,1)}, bf16[128,128]{1,0:T(8,128)(2,1)}, u32[]{:S(2)}, u32[]{:S(2)}) collective-permute-start(bf16[128,128]{1,0:T(8,128)(2,1)} %get-tuple-element.37), channel_id=1, source_target_pairs={{4,0},{8,4},{12,8},{16,12},{20,16},{24,20},{28,24},{0,28},{5,1},{9... | collective-permute-start | bytes 98312 | tf_op jit(solution)/shard_map/ppermute | solution.py:333
  15.6 8.7 %collective-permute-start.1 = (bf16[2,128,128]{2,1,0:T(8,128)(2,1)}, bf16[2,128,128]{2,1,0:T(8,128)(2,1)}, u32[]{:S(2)}, u32[]{:S(2)}) collective-permute-start(bf16[2,128,128]{2,1,0:T(8,128)(2,1)} %get-tuple-element.41), channel_id=1, source_target_pairs={{0,1},{1,0},{2,3},{3,2},{4,5},{5,4},{6,7},{7,6},{8,9},{9,8},{10,11... | collective-permute-start | bytes 196616 | tf_op jit(solution)/shard_map/ppermute | solution.py:339
  15.6 8.7 %collective-permute-start.2 = (bf16[2,128,128]{2,1,0:T(8,128)(2,1)}, bf16[2,128,128]{2,1,0:T(8,128)(2,1)}, u32[]{:S(2)}, u32[]{:S(2)}) collective-permute-start(bf16[2,128,128]{2,1,0:T(8,128)(2,1)} %get-tuple-element.42), channel_id=1, source_target_pairs={{0,2},{1,3},{2,0},{3,1},{4,6},{5,7},{6,4},{7,5},{8,10},{9,11},{10,... | collective-permute-start | bytes 196616 | tf_op jit(solution)/shard_map/ppermute | solution.py:339
  17.1 7.2 %collective-permute-start.3 = (bf16[2,128,128]{2,1,0:T(8,128)(2,1)}, bf16[2,128,128]{2,1,0:T(8,128)(2,1)}, u32[]{:S(2)}, u32[]{:S(2)}) collective-permute-start(bf16[2,128,128]{2,1,0:T(8,128)(2,1)} %get-tuple-element.43), channel_id=1, source_target_pairs={{0,3},{1,2},{2,1},{3,0},{4,7},{5,6},{6,5},{7,4},{8,11},{9,10},{10,... | collective-permute-start | bytes 196616 | tf_op jit(solution)/shard_map/ppermute | solution.py:339
  27.9 14.8 %all-to-all-start.1 = ((bf16[8,128,128]{2,1,0:T(8,128)(2,1)}), bf16[8,128,128]{2,1,0:T(8,128)(2,1)}, u32[]{:S(2)}, u32[]{:S(2)}) async-start(bf16[8,128,128]{2,1,0:T(8,128)(2,1)} %get-tuple-element.49), calls=%async_computation.1 | async-start | bytes 524288 | tf_op jit(solution)/shard_map/all_to_all | solution.py:445
  31.9 10.7 %collective-permute-start.7 = (bf16[2,128,128]{2,1,0:T(8,128)(2,1)}, bf16[2,128,128]{2,1,0:T(8,128)(2,1)}, u32[]{:S(2)}, u32[]{:S(2)}) collective-permute-start(bf16[2,128,128]{2,1,0:T(8,128)(2,1)} %get-tuple-element.44.refs_5_), channel_id=1, source_target_pairs={{0,3},{1,2},{2,1},{3,0},{4,7},{5,6},{6,5},{7,4},{8,11},{9,10},{10,... | collective-permute-start | bytes 196616 | tf_op jit(solution)/shard_map/ppermute | solution.py:339
  33.4 9.3 %collective-permute-start.6 = (bf16[2,128,128]{2,1,0:T(8,128)(2,1)}, bf16[2,128,128]{2,1,0:T(8,128)(2,1)}, u32[]{:S(2)}, u32[]{:S(2)}) collective-permute-start(bf16[2,128,128]{2,1,0:T(8,128)(2,1)} %get-tuple-element.44.refs_5_), channel_id=1, source_target_pairs={{0,2},{1,3},{2,0},{3,1},{4,6},{5,7},{6,4},{7,5},{8,10},{9,11},{10,... | collective-permute-start | bytes 196616 | tf_op jit(solution)/shard_map/ppermute | solution.py:339
  33.9 8.7 %collective-permute-start.5 = (bf16[2,128,128]{2,1,0:T(8,128)(2,1)}, bf16[2,128,128]{2,1,0:T(8,128)(2,1)}, u32[]{:S(2)}, u32[]{:S(2)}) collective-permute-start(bf16[2,128,128]{2,1,0:T(8,128)(2,1)} %get-tuple-element.44.refs_5_), channel_id=1, source_target_pairs={{0,1},{1,0},{2,3},{3,2},{4,5},{5,4},{6,7},{7,6},{8,9},{9,8},{10,11... | collective-permute-start | bytes 196616 | tf_op jit(solution)/shard_map/ppermute | solution.py:339
  33.9 8.7 %collective-permute-start.4 = (bf16[128,128]{1,0:T(8,128)(2,1)}, bf16[128,128]{1,0:T(8,128)(2,1)}, u32[]{:S(2)}, u32[]{:S(2)}) collective-permute-start(bf16[128,128]{1,0:T(8,128)(2,1)} %get-tuple-element.48), channel_id=1, source_target_pairs={{28,0},{0,4},{4,8},{8,12},{12,16},{16,20},{20,24},{24,28},{29,1},{... | collective-permute-start | bytes 98312 | tf_op jit(solution)/shard_map/ppermute | solution.py:333
  46.5 14.9 %all-to-all-start.2 = ((bf16[8,128,128]{2,1,0:T(8,128)(2,1)}), bf16[8,128,128]{2,1,0:T(8,128)(2,1)}, u32[]{:S(2)}, u32[]{:S(2)}) async-start(bf16[8,128,128]{2,1,0:T(8,128)(2,1)} %get-tuple-element.50), calls=%async_computation.2 | async-start | bytes 524288 | tf_op jit(solution)/shard_map/all_to_all | solution.py:406
  50.6 10.8 %collective-permute-start.9 = (bf16[2,128,128]{2,1,0:T(8,128)(2,1)}, bf16[2,128,128]{2,1,0:T(8,128)(2,1)}, u32[]{:S(2)}, u32[]{:S(2)}) collective-permute-start(bf16[2,128,128]{2,1,0:T(8,128)(2,1)} %get-tuple-element.55), channel_id=1, source_target_pairs={{0,1},{1,0},{2,3},{3,2},{4,5},{5,4},{6,7},{7,6},{8,9},{9,8},{10,11... | collective-permute-start | bytes 196616 | tf_op jit(solution)/shard_map/ppermute | solution.py:339
  50.7 10.8 %collective-permute-start.10 = (bf16[2,128,128]{2,1,0:T(8,128)(2,1)}, bf16[2,128,128]{2,1,0:T(8,128)(2,1)}, u32[]{:S(2)}, u32[]{:S(2)}) collective-permute-start(bf16[2,128,128]{2,1,0:T(8,128)(2,1)} %get-tuple-element.56), channel_id=1, source_target_pairs={{0,2},{1,3},{2,0},{3,1},{4,6},{5,7},{6,4},{7,5},{8,10},{9,11},{10,... | collective-permute-start | bytes 196616 | tf_op jit(solution)/shard_map/ppermute | solution.py:339
  52.2 9.2 %collective-permute-start.11 = (bf16[2,128,128]{2,1,0:T(8,128)(2,1)}, bf16[2,128,128]{2,1,0:T(8,128)(2,1)}, u32[]{:S(2)}, u32[]{:S(2)}) collective-permute-start(bf16[2,128,128]{2,1,0:T(8,128)(2,1)} %get-tuple-element.57), channel_id=1, source_target_pairs={{0,3},{1,2},{2,1},{3,0},{4,7},{5,6},{6,5},{7,4},{8,11},{9,10},{10,... | collective-permute-start | bytes 196616 | tf_op jit(solution)/shard_map/ppermute | solution.py:339
  52.5 8.9 %collective-permute-start.8 = (bf16[128,128]{1,0:T(8,128)(2,1)}, bf16[128,128]{1,0:T(8,128)(2,1)}, u32[]{:S(2)}, u32[]{:S(2)}) collective-permute-start(bf16[128,128]{1,0:T(8,128)(2,1)} %get-tuple-element.52), channel_id=1, source_target_pairs={{4,0},{8,4},{12,8},{16,12},{20,16},{24,20},{28,24},{0,28},{5,1},{9... | collective-permute-start | bytes 98312 | tf_op jit(solution)/shard_map/ppermute | solution.py:333
  65.0 14.5 %all-to-all-start.3 = ((bf16[8,128,128]{2,1,0:T(8,128)(2,1)}), bf16[8,128,128]{2,1,0:T(8,128)(2,1)}, u32[]{:S(2)}, u32[]{:S(2)}) async-start(bf16[8,128,128]{2,1,0:T(8,128)(2,1)} %get-tuple-element.63), calls=%async_computation.3 | async-start | bytes 524288 | tf_op jit(solution)/shard_map/all_to_all | solution.py:445
  69.0 10.4 %collective-permute-start.15 = (bf16[2,128,128]{2,1,0:T(8,128)(2,1)}, bf16[2,128,128]{2,1,0:T(8,128)(2,1)}, u32[]{:S(2)}, u32[]{:S(2)}) collective-permute-start(bf16[2,128,128]{2,1,0:T(8,128)(2,1)} %get-tuple-element.59.refs_5_), channel_id=1, source_target_pairs={{0,3},{1,2},{2,1},{3,0},{4,7},{5,6},{6,5},{7,4},{8,11},{9,10},{10,... | collective-permute-start | bytes 196616 | tf_op jit(solution)/shard_map/ppermute | solution.py:339
  70.2 9.3 %collective-permute-start.14 = (bf16[2,128,128]{2,1,0:T(8,128)(2,1)}, bf16[2,128,128]{2,1,0:T(8,128)(2,1)}, u32[]{:S(2)}, u32[]{:S(2)}) collective-permute-start(bf16[2,128,128]{2,1,0:T(8,128)(2,1)} %get-tuple-element.59.refs_5_), channel_id=1, source_target_pairs={{0,2},{1,3},{2,0},{3,1},{4,6},{5,7},{6,4},{7,5},{8,10},{9,11},{10,... | collective-permute-start | bytes 196616 | tf_op jit(solution)/shard_map/ppermute | solution.py:339
  70.7 8.7 %collective-permute-start.13 = (bf16[2,128,128]{2,1,0:T(8,128)(2,1)}, bf16[2,128,128]{2,1,0:T(8,128)(2,1)}, u32[]{:S(2)}, u32[]{:S(2)}) collective-permute-start(bf16[2,128,128]{2,1,0:T(8,128)(2,1)} %get-tuple-element.59.refs_5_), channel_id=1, source_target_pairs={{0,1},{1,0},{2,3},{3,2},{4,5},{5,4},{6,7},{7,6},{8,9},{9,8},{10,11... | collective-permute-start | bytes 196616 | tf_op jit(solution)/shard_map/ppermute | solution.py:339
  71.0 8.5 %collective-permute-start.12 = (bf16[128,128]{1,0:T(8,128)(2,1)}, bf16[128,128]{1,0:T(8,128)(2,1)}, u32[]{:S(2)}, u32[]{:S(2)}) collective-permute-start(bf16[128,128]{1,0:T(8,128)(2,1)} %get-tuple-element.62), channel_id=1, source_target_pairs={{28,0},{0,4},{4,8},{8,12},{12,16},{16,20},{20,24},{24,28},{29,1},{... | collective-permute-start | bytes 98312 | tf_op jit(solution)/shard_map/ppermute | solution.py:333

commit v4 on v3

--- a/solution.py
+++ b/solution.py
@@ -33,9 +33,9 @@
                 pltpu.make_async_copy(source.at[part], target.at[part], sems.at[at + p])
             )
 
-    def start(self, piece):
-        if piece < len(self.copies):
-            self.copies[piece].start()
+    def start(self):
+        for copy in self.copies:
+            copy.start()
 
     def piece(self):
         self.copies.pop(0).wait()
@@ -73,7 +73,6 @@
     counts = [pieces.get(i, (1, 0)) for i in range(len(arrays))]
     out_counts = [out_pieces.get(i, 1) for i in range(len(outs))]
     ns, na, no = len(scalars), len(arrays), len(outs)
-    most = max(count for count, _ in counts)
 
     def kernel(*refs):
         scalar_refs, refs = refs[:ns], refs[ns:]
@@ -87,9 +86,8 @@
         for source, target, (count, axis) in zip(sources, landing, counts):
             arriving.append(Arriving(source, target, in_sems, at, count, axis))
             at += count
-        for p in range(most):
-            for item in arriving:
-                item.start(p)
+        for item in arriving:
+            item.start()
         at = 0
         leaving = []
         for source, target, count in zip(staging, targets, out_counts):
@@ -141,13 +139,15 @@
     return jnp.where(other >= number, other - number, other)
 
 
-def send_duals(refineries, dual_q, me, rows, src, swing, carry, outs, acc):
+def send_duals(refineries, dual_q, me, rows, src, swing, carry, outs, acc, product):
     own, *sends, carried = outs
     acc[...] = jnp.zeros_like(acc)
     carried.ref[...] = dot_transposed(carry[0], dual_q[0]).astype(BF16)
     carried.send()
     for m in range(swing.shape[0]):
-        acc[src[m]] += dot_transposed(swing[m], dual_q[rows[m]])
+        product[m] = dot_transposed(swing[m], dual_q[rows[m]])
+    for m in range(swing.shape[0]):
+        acc[src[m]] += product[m]
     for d, send in enumerate(sends, 1):
         send.ref[...] = acc[pl.ds(partner(me, d, refineries, False) * SC, SC)].astype(BF16)
         send.send()
@@ -155,29 +155,28 @@
     own.send()
 
 
-def first_duals_body(refineries, scalars, ins, outs, acc):
+def first_duals_body(refineries, scalars, ins, outs, acc, product, dual_q):
     me, rows, src = scalars
     annual, dual, carry, swing = ins
-    weekly, dual_q = outs[0], outs[1]
+    weekly = outs[0]
     rounded = annual()[...].astype(BF16)
     for w in range(weekly.ref.shape[0]):
         weekly.ref[w] = rounded
     weekly.send()
     size = rounded.shape[0]
     dual = dual()
-    for i in range(dual_q.ref.shape[0]):
-        dual_q.ref[i] = dual[i * size : (i + 1) * size].astype(BF16)
-    dual_q.send()
-    send_duals(refineries, dual_q.ref, me[0], rows, src, swing(), carry(), outs[2:], acc)
-
-
-def adjoint(high, low, dual_q, primal, prices, out, chunks):
-    blocks, size, _ = dual_q.shape
-    turned = jnp.concatenate([dual_q[i].T for i in range(blocks)], axis=1)
+    for i in range(dual_q.shape[0]):
+        dual_q[i] = dual[i * size : (i + 1) * size].astype(BF16)
+    send_duals(
+        refineries, dual_q, me[0], rows, src, swing(), carry(), outs[1:], acc, product
+    )
+
+
+def adjoint(matrix, turned, size, primal, prices, out, chunks):
     step = out.ref.shape[0] // chunks
     for j in range(chunks):
         columns = slice(j * step, (j + 1) * step)
-        part = dot(turned, high()[:, columns]) + dot(turned, low()[:, columns])
+        part = dot(turned, matrix()[:, columns])
         if j == 0:
             primal, prices = primal(), prices()
         for h in range(step // size):
@@ -190,11 +189,11 @@
 
 def dense_body(chunks, scalars, ins, outs, acc):
     count, rows, cols = scalars
-    blocks, upper, dual_q, primal, prices = ins
-    high, low, upper_full, out = outs
+    blocks, upper, dual, primal, prices = ins
+    matrix, upper_full, out = outs
     size = upper.target.shape[1]
     width = upper_full.ref.shape[1]
-    tiles = high.ref.shape[1] // size
+    tiles = matrix.ref.shape[1] // size
     acc[...] = jnp.zeros_like(acc)
     slots = blocks.target.shape[0] // chunks
     for c in range(chunks):
@@ -205,28 +204,31 @@
             return 0
 
         lax.fori_loop(c * slots, jnp.minimum(count[0], (c + 1) * slots), step, 0)
-    for i in range(high.ref.shape[0] // size):
+    for i in range(matrix.ref.shape[0] // size):
         for j in range(tiles):
-            whole = acc[i * tiles + j]
-            top = whole.astype(BF16)
             at = (slice(i * size, (i + 1) * size), slice(j * size, (j + 1) * size))
-            high.ref[at] = top
-            low.ref[at] = (whole - top.astype(F32)).astype(BF16)
-    high.send()
-    low.send()
+            matrix.ref[at] = acc[i * tiles + j].astype(BF16)
+    matrix.send()
     upper = upper()
     for j in range(tiles):
         upper_full.ref[j * size : (j + 1) * size] = column_of(upper[j : j + 1], width)
     upper_full.send()
-    adjoint(lambda: high.ref, lambda: low.ref, dual_q(), primal, prices, out, chunks)
+    dual = dual()
+    turned = jnp.concatenate(
+        [dual[i * size : (i + 1) * size].astype(BF16).T for i in range(dual.shape[0] // size)], axis=1
+    )
+    adjoint(lambda: matrix.ref, turned, size, primal, prices, out, chunks)
 
 
 def adjoint_body(chunks, scalars, ins, outs):
-    dual_q, high, low, primal, prices = ins
-    adjoint(high.piece, low.piece, dual_q(), primal, prices, outs[0], chunks)
-
-
-def primal_body(scalars, ins, outs, acc, image_acc):
+    dual_q, matrix, primal, prices = ins
+    dual_q = dual_q()
+    blocks, size, _ = dual_q.shape
+    turned = jnp.concatenate([dual_q[i].T for i in range(blocks)], axis=1)
+    adjoint(matrix.piece, turned, size, primal, prices, outs[0], chunks)
+
+
+def primal_body(scalars, ins, outs, acc, image_acc, product):
     ids, cols = scalars
     annual_q, annual, own, carried, primal, upper_full, partial, *arrived = ins
     image, streams, last, extrap, updated = outs
@@ -236,7 +238,9 @@
     annual, annual_q = annual(), annual_q()
     slots = annual.shape[0]
     for k in range(slots):
-        acc[cols[k]] += dot_transposed(annual[k], annual_q[ids[k]])
+        product[k] = dot_transposed(annual[k], annual_q[ids[k]])
+    for k in range(slots):
+        acc[cols[k]] += product[k]
     total = own()[...]
     for piece in arrived:
         total = total + piece()[...].astype(F32)
@@ -259,12 +263,14 @@
     extrap.send()
     updated.send()
     for k in range(slots):
-        image_acc[ids[k]] += dot(annual[k], extrap.ref[cols[k]])
+        product[k] = dot(annual[k], extrap.ref[cols[k]])
+    for k in range(slots):
+        image_acc[ids[k]] += product[k]
     image.ref[...] = image_acc[...].astype(BF16)
 
 
 def forward_body(chunks, scalars, ins, outs):
-    extrap, high, low, dual, demand = ins
+    extrap, matrix, dual, demand = ins
     out = outs[0]
     extrap = extrap()
     blocks, size, width = extrap.shape
@@ -272,7 +278,7 @@
     step = out.ref.shape[0] // chunks
     for i in range(chunks):
         lines = slice(i * step, (i + 1) * step)
-        part = dot(high.piece()[lines], right) + dot(low.piece()[lines], right)
+        part = dot(matrix.piece()[lines], right)
         if i == 0:
             dual, demand = dual(), demand()
         for h in range(step // size):
@@ -284,7 +290,7 @@
         out.send()
 
 
-def dual_body(refineries, more, scalars, ins, outs, gathered, acc, *stream_acc):
+def dual_body(refineries, more, scalars, ins, outs, gathered, acc, product, *stream_acc):
     me, rows, src = scalars
     swing, carry, streams, partial, previous, parts, annual, need, *arrived = ins
     dual, annual_out = outs[0], outs[1]
@@ -296,7 +302,9 @@
         gathered[pl.ds(partner(mine, d, refineries, True) * SC, SC)] = piece()[...]
     acc[...] = jnp.zeros_like(acc)
     for m in range(swing.shape[0]):
-        acc[rows[m]] += dot(swing[m], gathered[src[m]])
+        product[m] = dot(swing[m], gathered[src[m]])
+    for m in range(swing.shape[0]):
+        acc[rows[m]] += product[m]
     acc[0] += dot(carry[0], previous()[...])
     parts, annual = parts(), annual()
     total = parts[0].astype(F32)
@@ -323,7 +331,7 @@
     if more:
         outs[3].send()
         send_duals(
-            refineries, outs[3].ref, mine, rows, src, swing, carry, outs[4:], *stream_acc
+            refineries, outs[3].ref, mine, rows, src, swing, carry, outs[4:], *stream_acc, product
         )
 
 
@@ -382,6 +390,8 @@
     annuals = annual_blocks.shape[0]
     unit = 2 * size * size * scenarios
     stream_scratch = pltpu.VMEM((refineries * SC, size, scenarios), F32)
+    swing_scratch = pltpu.VMEM((swings, size, scenarios), F32)
+    annual_scratch = pltpu.VMEM((annuals, size, scenarios), F32)
     sends_shape = [pair] + [pair_q] * others + [tile]
     chunks = 4 if slots % 4 == 0 and columns % 4 == 0 else 1
     parts_x = 4 if columns % 4 == 0 else 1
@@ -391,43 +401,43 @@
     demand_rows = demand.reshape(rows, size)
     need = annual_bound.reshape(1, size)
     primal, dual, annual = x_start, y_start, annual_start
-    annual_send, dual_q, own, *rest = run(
+    annual_send, own, *rest = run(
         functools.partial(first_duals_body, refineries),
         "first_duals",
         [me, swing_rows, swing_src],
         [annual, dual, carry_blocks, swing_blocks],
-        [weekly, blocks_y] + sends_shape,
-        [stream_scratch],
+        [weekly] + sends_shape,
+        [stream_scratch, swing_scratch, pltpu.VMEM(blocks_y.shape, BF16)],
         (swings + 1) * unit,
     )
     for iteration in range(ITERS):
         more = iteration + 1 < ITERS
         sends, carried = rest[:others], rest[others]
         annual_q = lax.all_to_all(annual_send, "period", 0, 0, tiled=True)
+        carried_back = shifted(carried, "period", -1)
         arrived = [exchanged(send, "refinery", d) for d, send in enumerate(sends, 1)]
-        carried_back = shifted(carried, "period", -1)
         if iteration == 0:
-            high, low, upper_full, partial_x = run(
+            matrix_q, upper_full, partial_x = run(
                 functools.partial(dense_body, chunks),
                 "dense",
                 [band_count, local_rows, local_cols],
-                [local_blocks, upper_rows, dual_q, primal, cost],
-                [matrix, matrix, state_x, state_x],
+                [local_blocks, upper_rows, dual, primal, cost],
+                [matrix, state_x, state_x],
                 [pltpu.VMEM((rows * columns, size, size), F32)],
                 3 * rows * columns * unit,
                 {0: (chunks, 0)},
-                {3: chunks},
+                {2: chunks},
             )
         else:
             (partial_x,) = run(
                 functools.partial(adjoint_body, parts_x),
                 "adjoint",
                 [],
-                [dual_q, high, low, primal, cost],
+                [dual_q, matrix_q, primal, cost],
                 [state_x],
                 [],
                 2 * rows * columns * unit,
-                {1: (parts_x, 1), 2: (parts_x, 1)},
+                {1: (parts_x, 1)},
                 {0: parts_x},
             )
         image, streams, last, extrap, updated = run(
@@ -439,21 +449,22 @@
             [
                 pltpu.VMEM((columns, size, scenarios), F32),
                 pltpu.VMEM((weeks, size, scenarios), F32),
+                annual_scratch,
             ],
             2 * annuals * unit,
         )
         parts = lax.all_to_all(image, "period", 0, 0, tiled=True)
+        previous = shifted(last, "period", 1)
         others_streams = [exchanged(streams, "refinery", d) for d in range(1, refineries)]
-        previous = shifted(last, "period", 1)
         (partial_y,) = run(
             functools.partial(forward_body, parts_y),
             "forward",
             [],
-            [extrap, high, low, dual, demand_rows],
+            [extrap, matrix_q, dual, demand_rows],
             [state_y],
             [],
             2 * rows * columns * unit,
-            {1: (parts_y, 0), 2: (parts_y, 0)},
+            {1: (parts_y, 0)},
             {0: parts_y},
         )
         sent = [weekly, blocks_y] + sends_shape if more else []
@@ -469,6 +480,7 @@
             [
                 pltpu.VMEM((refineries * SC, size, scenarios), BF16),
                 pltpu.VMEM((rows, size, scenarios), F32),
+                swing_scratch,
             ]
             + ([stream_scratch] if more else []),
             2 * swings * unit,

time: 83.8 us -> 82 us (0.979)
  Pallas kernels: 35.8 us -> 32.9 us
    pallas_call x9, Pallas kernels: 35.8 us -> 32.9 us  [run(): pl.pallas_call(kernel, name=name, in_specs=[SMEM] * ns + [HBM] * na, out_...]
  transfers between devices with their start and end apart: 20 -> 20, of which waited for: 2 -> 2; matrix products, arithmetic and copies ran while one was open for 0% -> 0% of each run, Pallas kernels for 22% -> 19%
where the time goes in v4:
time: 82 us; the launch traced here: 81.1 us
  starting transfers between devices  40.4 us (49%)
  Pallas kernels  32.9 us (40%)
  waiting for transfers between devices  6.33 us (8%)
  between operations  1.49 us (2%)
    pallas_call x9, Pallas kernels, run(): pl.pallas_call(kernel, name=name, in_specs=[SMEM] * ns + [HBM] * na, out_...  32.9 us
    ppermute x4, starting transfers between devices, shifted(): return lax.ppermute(block, axis, route)  13.1 us
    all_to_all x2, starting transfers between devices, body(): annual_q = lax.all_to_all(annual_send, 'period', 0, 0, tiled=True)  11.3 us
    all_to_all x2, starting transfers between devices, body(): parts = lax.all_to_all(image, 'period', 0, 0, tiled=True)  8.36 us
    ppermute x12, starting transfers between devices, exchanged(): return lax.ppermute(block, axis, [(i, i ^ d) for i in range(number)])  7.64 us
    ppermute x4, waiting for transfers between devices, shifted(): return lax.ppermute(block, axis, route)  6.29 us
  transfers between devices with their start and end apart: 20, of which 2 were waited for; matrix products, arithmetic and copies ran while one was open for 0% of the time, Pallas kernels for 19%

profile of v4, /device:TPU:0, one launch (start us, length us, event | category | flops | bytes accessed | tf_op | source)
XLA Modules:
  0.0 81.1 jit_solution(15446695301777444016)
XLA Ops:
  0.6 2.9 %first_duals.1 = (bf16[8,128,128]{2,1,0:T(8,128)(2,1)}, f32[2,128,128]{2,1,0:T(8,128)}, bf16[2,128,128]{2,1,0:T(8,128)(2,1)}, bf16[2,128,128]{2,1,0:T(8,128)(2,1...) custom-call(s32[1]{0:T(128)} %bitcast.refs_0_, s32[8]{0:T(128)} %refs_1_.11, s32[8]{0:T(128)} %refs_2_.9, ...), custom_call_target="tpu_custom_call" | custom-call | flops 37748736 | bytes 1507328 | tf_op jit(solution)/shard_map/first_duals/pallas_call | solution.py:106
  3.6 7.3 %all-to-all-start = ((bf16[8,128,128]{2,1,0:T(8,128)(2,1)}), bf16[8,128,128]{2,1,0:T(8,128)(2,1)}, u32[]{:S(2)}, u32[]{:S(2)}) async-start(bf16[8,128,128]{2,1,0:T(8,128)(2,1)} %get-tuple-element.33), calls=%async_computation | async-start | bytes 524288 | tf_op jit(solution)/shard_map/all_to_all | solution.py:416
  10.9 4.7 %collective-permute-start = (bf16[128,128]{1,0:T(8,128)(2,1)}, bf16[128,128]{1,0:T(8,128)(2,1)}, u32[]{:S(2)}, u32[]{:S(2)}) collective-permute-start(bf16[128,128]{1,0:T(8,128)(2,1)} %get-tuple-element.35), channel_id=1, source_target_pairs={{4,0},{8,4},{12,8},{16,12},{20,16},{24,20},{28,24},{0,28},{5,1},{9... | collective-permute-start | bytes 98312 | tf_op jit(solution)/shard_map/ppermute | solution.py:341
  15.6 0.0 collective-permute-start.1
  15.6 1.5 %collective-permute-start.2 = (bf16[2,128,128]{2,1,0:T(8,128)(2,1)}, bf16[2,128,128]{2,1,0:T(8,128)(2,1)}, u32[]{:S(2)}, u32[]{:S(2)}) collective-permute-start(bf16[2,128,128]{2,1,0:T(8,128)(2,1)} %get-tuple-element.39), channel_id=1, source_target_pairs={{0,2},{1,3},{2,0},{3,1},{4,6},{5,7},{6,4},{7,5},{8,10},{9,11},{10,... | collective-permute-start | bytes 196616 | tf_op jit(solution)/shard_map/ppermute | solution.py:347
  17.1 0.4 collective-permute-start.3
  18.1 4.8 %dense.1 = (bf16[1024,1024]{1,0:T(8,128)(2,1)}, f32[1024,128]{1,0:T(8,128)}, f32[1024,128]{1,0:T(8,128)}) custom-call(s32[1]{0:T(128)S(6)} %copy.21.refs_0_, s32[96]{0:T(128)} %refs_1_.7, s32[96]{0:T(128)} %refs_2_.6, bf16[96,128,128]{2,1,0:T(8,128)(2,1)} %refs_3_.8, f32[8,128]{1,0:T(8,128)} %bitcast.6, f32[1024,128]{1,0:T(8,128)} %refs_2_.7, ...), custom_call_target="tpu_custom_call" | custom-call | flops 805306368 | bytes 7868416 | tf_op jit(solution)/shard_map/dense/pallas_call | solution.py:106
  22.9 0.0 collective-permute-done.1.refs_9_
  22.9 0.0 collective-permute-done.2.refs_10_
  22.9 3.6 %primal_step.2 = (bf16[8,128,128]{2,1,0:T(8,128)(2,1)}, bf16[2,128,128]{2,1,0:T(8,128)(2,1)}, bf16[128,128]{1,0:T(8,128)(2,1)}, bf16[8,128,128]{2,1,0:T(8,128)(2,1)}, f32[1024,128]{1,0:T(8,128)}) custom-call(s32[8]{0:T(128)} %refs_0_.4, s32[8]{0:T(128)} %refs_1_.10, bf16[8,128,128]{2,1,0:T(8,128)(2,1)} %all-to-all-done.refs_2_, ...), custom_call_target="tpu_custom_call" | custom-call | flops 67108864 | bytes 3604480 | tf_op jit(solution)/shard_map/primal_step/pallas_call | solution.py:106
  26.5 4.1 %all-to-all-start.1 = ((bf16[8,128,128]{2,1,0:T(8,128)(2,1)}), bf16[8,128,128]{2,1,0:T(8,128)(2,1)}, u32[]{:S(2)}, u32[]{:S(2)}) async-start(bf16[8,128,128]{2,1,0:T(8,128)(2,1)} %get-tuple-element.45), calls=%async_computation.1 | async-start | bytes 524288 | tf_op jit(solution)/shard_map/all_to_all | solution.py:456
  30.6 1.4 %collective-permute-start.7 = (bf16[2,128,128]{2,1,0:T(8,128)(2,1)}, bf16[2,128,128]{2,1,0:T(8,128)(2,1)}, u32[]{:S(2)}, u32[]{:S(2)}) collective-permute-start(bf16[2,128,128]{2,1,0:T(8,128)(2,1)} %get-tuple-element.41.refs_5_), channel_id=1, source_target_pairs={{0,3},{1,2},{2,1},{3,0},{4,7},{5,6},{6,5},{7,4},{8,11},{9,10},{10,... | collective-permute-start | bytes 196616 | tf_op jit(solution)/shard_map/ppermute | solution.py:347
  32.0 0.5 collective-permute-start.6
  32.6 1.8 %collective-permute-start.4 = (bf16[128,128]{1,0:T(8,128)(2,1)}, bf16[128,128]{1,0:T(8,128)(2,1)}, u32[]{:S(2)}, u32[]{:S(2)}) collective-permute-start(bf16[128,128]{1,0:T(8,128)(2,1)} %get-tuple-element.44), channel_id=1, source_target_pairs={{28,0},{0,4},{4,8},{8,12},{12,16},{16,20},{20,24},{24,28},{29,1},{... | collective-permute-start | bytes 98312 | tf_op jit(solution)/shard_map/ppermute | solution.py:341
  34.3 3.5 %forward.2.refs_6_ = f32[1024,128]{1,0:T(8,128)} custom-call(bf16[8,128,128]{2,1,0:T(8,128)(2,1)} %get-tuple-element.42.refs_0_, bf16[1024,1024]{1,0:T(8,128)(2,1)} %get-tuple-element.43.refs_1_, f32[1024,128]{1,0:T(8,128)} %refs_2_.7, f32[8,128]{1,0:T(8,128)} %bitcast.4), custom_call_target="tpu_custom_call" | custom-call | flops 536870912 | bytes 3411968 | tf_op jit(solution)/shard_map/forward/pallas_call | solution.py:106
  37.8 3.5 %collective-permute-done.4.refs_7_ = bf16[128,128]{1,0:T(8,128)(2,1)} collective-permute-done((bf16[128,128]{1,0:T(8,128)(2,1)}, bf16[128,128]{1,0:T(8,128)(2,1)}, u32[]{:S(2)}, u32[]{:S(2)}) %collective-permute-start.4) | collective-permute-done | bytes 32800 | tf_op jit(solution)/shard_map/ppermute | solution.py:341
  41.3 3.8 %dual_step.2 = (f32[1024,128]{1,0:T(8,128)}, f32[128,128]{1,0:T(8,128)}, bf16[8,128,128]{2,1,0:T(8,128)(2,1)}, bf16[8,128,128]{2,1,0:T(8,128)(2,1)}, f32[2,128,1...) custom-call(s32[1]{0:T(128)} %bitcast.refs_0_, ...), custom_call_target="tpu_custom_call" | custom-call | flops 67108864 | bytes 2916864 | tf_op jit(solution)/shard_map/dual_step/pallas_call | solution.py:106
  45.1 4.1 %all-to-all-start.2 = ((bf16[8,128,128]{2,1,0:T(8,128)(2,1)}), bf16[8,128,128]{2,1,0:T(8,128)(2,1)}, u32[]{:S(2)}, u32[]{:S(2)}) async-start(bf16[8,128,128]{2,1,0:T(8,128)(2,1)} %get-tuple-element.46), calls=%async_computation.2 | async-start | bytes 524288 | tf_op jit(solution)/shard_map/all_to_all | solution.py:416
  49.2 0.1 collective-permute-start.9
  49.3 1.6 %collective-permute-start.10 = (bf16[2,128,128]{2,1,0:T(8,128)(2,1)}, bf16[2,128,128]{2,1,0:T(8,128)(2,1)}, u32[]{:S(2)}, u32[]{:S(2)}) collective-permute-start(bf16[2,128,128]{2,1,0:T(8,128)(2,1)} %get-tuple-element.52), channel_id=1, source_target_pairs={{0,2},{1,3},{2,0},{3,1},{4,6},{5,7},{6,4},{7,5},{8,10},{9,11},{10,... | collective-permute-start | bytes 196616 | tf_op jit(solution)/shard_map/ppermute | solution.py:347
  50.8 0.3 collective-permute-start.11
  51.1 4.6 %collective-permute-start.8 = (bf16[128,128]{1,0:T(8,128)(2,1)}, bf16[128,128]{1,0:T(8,128)(2,1)}, u32[]{:S(2)}, u32[]{:S(2)}) collective-permute-start(bf16[128,128]{1,0:T(8,128)(2,1)} %get-tuple-element.48), channel_id=1, source_target_pairs={{4,0},{8,4},{12,8},{16,12},{20,16},{24,20},{28,24},{0,28},{5,1},{9... | collective-permute-start | bytes 98312 | tf_op jit(solution)/shard_map/ppermute | solution.py:341
  55.7 3.9 %adjoint.1.refs_8_ = f32[1024,128]{1,0:T(8,128)} custom-call(bf16[8,128,128]{2,1,0:T(8,128)(2,1)} %get-tuple-element.50.refs_0_, bf16[1024,1024]{1,0:T(8,128)(2,1)} %get-tuple-element.43.refs_1_, f32[1024,128]{1,0:T(8,128)} %get-tuple-element.49.refs_2_.refs_6_, f32[1024,128]{1,0:T(8,128)} %refs_3_.11), custom_call_target="tpu_custom_call" | custom-call | flops 536870912 | bytes 3932160 | tf_op jit(solution)/shard_map/adjoint/pallas_call | solution.py:106
  59.6 3.5 %primal_step.3 = (bf16[8,128,128]{2,1,0:T(8,128)(2,1)}, bf16[2,128,128]{2,1,0:T(8,128)(2,1)}, bf16[128,128]{1,0:T(8,128)(2,1)}, bf16[8,128,128]{2,1,0:T(8,128)(2,1)}, f32[1024,128]{1,0:T(8,128)}) custom-call(s32[8]{0:T(128)} %refs_0_.4, s32[8]{0:T(128)} %refs_1_.10, bf16[8,128,128]{2,1,0:T(8,128)(2,1)} %all-to-all-done.2.refs_2_, ...), custom_call_target="tpu_custom_call" | custom-call | flops 67108864 | bytes 3604480 | tf_op jit(solution)/shard_map/primal_step/pallas_call | solution.py:106
  63.1 4.3 %all-to-all-start.3 = ((bf16[8,128,128]{2,1,0:T(8,128)(2,1)}), bf16[8,128,128]{2,1,0:T(8,128)(2,1)}, u32[]{:S(2)}, u32[]{:S(2)}) async-start(bf16[8,128,128]{2,1,0:T(8,128)(2,1)} %get-tuple-element.59), calls=%async_computation.3 | async-start | bytes 524288 | tf_op jit(solution)/shard_map/all_to_all | solution.py:456
  67.4 0.9 %collective-permute-start.15 = (bf16[2,128,128]{2,1,0:T(8,128)(2,1)}, bf16[2,128,128]{2,1,0:T(8,128)(2,1)}, u32[]{:S(2)}, u32[]{:S(2)}) collective-permute-start(bf16[2,128,128]{2,1,0:T(8,128)(2,1)} %get-tuple-element.55.refs_5_), channel_id=1, source_target_pairs={{0,3},{1,2},{2,1},{3,0},{4,7},{5,6},{6,5},{7,4},{8,11},{9,10},{10,... | collective-permute-start | bytes 196616 | tf_op jit(solution)/shard_map/ppermute | solution.py:347
  68.3 0.6 collective-permute-start.14
  69.0 0.3 collective-permute-start.13
  69.3 2.0 %collective-permute-start.12 = (bf16[128,128]{1,0:T(8,128)(2,1)}, bf16[128,128]{1,0:T(8,128)(2,1)}, u32[]{:S(2)}, u32[]{:S(2)}) collective-permute-start(bf16[128,128]{1,0:T(8,128)(2,1)} %get-tuple-element.58), channel_id=1, source_target_pairs={{28,0},{0,4},{4,8},{8,12},{12,16},{16,20},{20,24},{24,28},{29,1},{... | collective-permute-start | bytes 98312 | tf_op jit(solution)/shard_map/ppermute | solution.py:341
  71.3 3.5 %forward.3.refs_6_ = f32[1024,128]{1,0:T(8,128)} custom-call(bf16[8,128,128]{2,1,0:T(8,128)(2,1)} %get-tuple-element.56.refs_0_, bf16[1024,1024]{1,0:T(8,128)(2,1)} %get-tuple-element.43.refs_1_, f32[1024,128]{1,0:T(8,128)} %get-tuple-element.57.refs_2_, f32[8,128]{1,0:T(8,128)} %bitcast.5), custom_call_target="tpu_custom_call" | custom-call | flops 536870912 | bytes 3411968 | tf_op jit(solution)/shard_map/forward/pallas_call | solution.py:106
  74.8 2.8 %collective-permute-done.12.refs_7_ = bf16[128,128]{1,0:T(8,128)(2,1)} collective-permute-done((bf16[128,128]{1,0:T(8,128)(2,1)}, bf16[128,128]{1,0:T(8,128)(2,1)}, u32[]{:S(2)}, u32[]{:S(2)}) %collective-permute-start.12) | collective-permute-done | bytes 32800 | tf_op jit(solution)/shard_map/ppermute | solution.py:341
  77.6 3.5 %dual_step.3 = (f32[1024,128]{1,0:T(8,128)}, f32[128,128]{1,0:T(8,128)}) custom-call(s32[1]{0:T(128)} %bitcast.refs_0_, s32[8]{0:T(128)} %refs_1_.11, s32[8]{0:T(128)} %refs_2_.9, bf16[8,128,128]{2,1,0:T(8,128)(2,1)} %refs_3_.13, bf16[1,128,128]{2,1,0:T(8,128)(2,1)} %refs_4_.5, bf16[2,128,128]{2,1,0:T(8,128)(2,1)} %get-tuple-element.55.refs_5_, ...), custom_call_target="tpu_custom_call" | custom-call | flops 67108864 | bytes 2032128 | tf_op jit(solution)/shard_map/dual_step/pallas_call | solution.py:106
  (17 shorter events, 0.0 us)
Async XLA Ops:
  3.6 19.3 %all-to-all-start = ((bf16[8,128,128]{2,1,0:T(8,128)(2,1)}), bf16[8,128,128]{2,1,0:T(8,128)(2,1)}, u32[]{:S(2)}, u32[]{:S(2)}) async-start(bf16[8,128,128]{2,1,0:T(8,128)(2,1)} %get-tuple-element.33), calls=%async_computation | async-start | bytes 524288 | tf_op jit(solution)/shard_map/all_to_all | solution.py:416
  10.9 12.0 %collective-permute-start = (bf16[128,128]{1,0:T(8,128)(2,1)}, bf16[128,128]{1,0:T(8,128)(2,1)}, u32[]{:S(2)}, u32[]{:S(2)}) collective-permute-start(bf16[128,128]{1,0:T(8,128)(2,1)} %get-tuple-element.35), channel_id=1, source_target_pairs={{4,0},{8,4},{12,8},{16,12},{20,16},{24,20},{28,24},{0,28},{5,1},{9... | collective-permute-start | bytes 98312 | tf_op jit(solution)/shard_map/ppermute | solution.py:341
  15.6 7.3 %collective-permute-start.1 = (bf16[2,128,128]{2,1,0:T(8,128)(2,1)}, bf16[2,128,128]{2,1,0:T(8,128)(2,1)}, u32[]{:S(2)}, u32[]{:S(2)}) collective-permute-start(bf16[2,128,128]{2,1,0:T(8,128)(2,1)} %get-tuple-element.38), channel_id=1, source_target_pairs={{0,1},{1,0},{2,3},{3,2},{4,5},{5,4},{6,7},{7,6},{8,9},{9,8},{10,11... | collective-permute-start | bytes 196616 | tf_op jit(solution)/shard_map/ppermute | solution.py:347
  15.6 7.3 %collective-permute-start.2 = (bf16[2,128,128]{2,1,0:T(8,128)(2,1)}, bf16[2,128,128]{2,1,0:T(8,128)(2,1)}, u32[]{:S(2)}, u32[]{:S(2)}) collective-permute-start(bf16[2,128,128]{2,1,0:T(8,128)(2,1)} %get-tuple-element.39), channel_id=1, source_target_pairs={{0,2},{1,3},{2,0},{3,1},{4,6},{5,7},{6,4},{7,5},{8,10},{9,11},{10,... | collective-permute-start | bytes 196616 | tf_op jit(solution)/shard_map/ppermute | solution.py:347
  17.1 5.8 %collective-permute-start.3 = (bf16[2,128,128]{2,1,0:T(8,128)(2,1)}, bf16[2,128,128]{2,1,0:T(8,128)(2,1)}, u32[]{:S(2)}, u32[]{:S(2)}) collective-permute-start(bf16[2,128,128]{2,1,0:T(8,128)(2,1)} %get-tuple-element.40), channel_id=1, source_target_pairs={{0,3},{1,2},{2,1},{3,0},{4,7},{5,6},{6,5},{7,4},{8,11},{9,10},{10,... | collective-permute-start | bytes 196616 | tf_op jit(solution)/shard_map/ppermute | solution.py:347
  26.5 14.8 %all-to-all-start.1 = ((bf16[8,128,128]{2,1,0:T(8,128)(2,1)}), bf16[8,128,128]{2,1,0:T(8,128)(2,1)}, u32[]{:S(2)}, u32[]{:S(2)}) async-start(bf16[8,128,128]{2,1,0:T(8,128)(2,1)} %get-tuple-element.45), calls=%async_computation.1 | async-start | bytes 524288 | tf_op jit(solution)/shard_map/all_to_all | solution.py:456
  30.6 10.7 %collective-permute-start.7 = (bf16[2,128,128]{2,1,0:T(8,128)(2,1)}, bf16[2,128,128]{2,1,0:T(8,128)(2,1)}, u32[]{:S(2)}, u32[]{:S(2)}) collective-permute-start(bf16[2,128,128]{2,1,0:T(8,128)(2,1)} %get-tuple-element.41.refs_5_), channel_id=1, source_target_pairs={{0,3},{1,2},{2,1},{3,0},{4,7},{5,6},{6,5},{7,4},{8,11},{9,10},{10,... | collective-permute-start | bytes 196616 | tf_op jit(solution)/shard_map/ppermute | solution.py:347
  32.0 9.3 %collective-permute-start.6 = (bf16[2,128,128]{2,1,0:T(8,128)(2,1)}, bf16[2,128,128]{2,1,0:T(8,128)(2,1)}, u32[]{:S(2)}, u32[]{:S(2)}) collective-permute-start(bf16[2,128,128]{2,1,0:T(8,128)(2,1)} %get-tuple-element.41.refs_5_), channel_id=1, source_target_pairs={{0,2},{1,3},{2,0},{3,1},{4,6},{5,7},{6,4},{7,5},{8,10},{9,11},{10,... | collective-permute-start | bytes 196616 | tf_op jit(solution)/shard_map/ppermute | solution.py:347
  32.5 8.7 %collective-permute-start.5 = (bf16[2,128,128]{2,1,0:T(8,128)(2,1)}, bf16[2,128,128]{2,1,0:T(8,128)(2,1)}, u32[]{:S(2)}, u32[]{:S(2)}) collective-permute-start(bf16[2,128,128]{2,1,0:T(8,128)(2,1)} %get-tuple-element.41.refs_5_), channel_id=1, source_target_pairs={{0,1},{1,0},{2,3},{3,2},{4,5},{5,4},{6,7},{7,6},{8,9},{9,8},{10,11... | collective-permute-start | bytes 196616 | tf_op jit(solution)/shard_map/ppermute | solution.py:347
  32.6 8.7 %collective-permute-start.4 = (bf16[128,128]{1,0:T(8,128)(2,1)}, bf16[128,128]{1,0:T(8,128)(2,1)}, u32[]{:S(2)}, u32[]{:S(2)}) collective-permute-start(bf16[128,128]{1,0:T(8,128)(2,1)} %get-tuple-element.44), channel_id=1, source_target_pairs={{28,0},{0,4},{4,8},{8,12},{12,16},{16,20},{20,24},{24,28},{29,1},{... | collective-permute-start | bytes 98312 | tf_op jit(solution)/shard_map/ppermute | solution.py:341
  45.1 14.5 %all-to-all-start.2 = ((bf16[8,128,128]{2,1,0:T(8,128)(2,1)}), bf16[8,128,128]{2,1,0:T(8,128)(2,1)}, u32[]{:S(2)}, u32[]{:S(2)}) async-start(bf16[8,128,128]{2,1,0:T(8,128)(2,1)} %get-tuple-element.46), calls=%async_computation.2 | async-start | bytes 524288 | tf_op jit(solution)/shard_map/all_to_all | solution.py:416
  49.2 10.4 %collective-permute-start.9 = (bf16[2,128,128]{2,1,0:T(8,128)(2,1)}, bf16[2,128,128]{2,1,0:T(8,128)(2,1)}, u32[]{:S(2)}, u32[]{:S(2)}) collective-permute-start(bf16[2,128,128]{2,1,0:T(8,128)(2,1)} %get-tuple-element.51), channel_id=1, source_target_pairs={{0,1},{1,0},{2,3},{3,2},{4,5},{5,4},{6,7},{7,6},{8,9},{9,8},{10,11... | collective-permute-start | bytes 196616 | tf_op jit(solution)/shard_map/ppermute | solution.py:347
  49.3 10.3 %collective-permute-start.10 = (bf16[2,128,128]{2,1,0:T(8,128)(2,1)}, bf16[2,128,128]{2,1,0:T(8,128)(2,1)}, u32[]{:S(2)}, u32[]{:S(2)}) collective-permute-start(bf16[2,128,128]{2,1,0:T(8,128)(2,1)} %get-tuple-element.52), channel_id=1, source_target_pairs={{0,2},{1,3},{2,0},{3,1},{4,6},{5,7},{6,4},{7,5},{8,10},{9,11},{10,... | collective-permute-start | bytes 196616 | tf_op jit(solution)/shard_map/ppermute | solution.py:347
  50.8 8.8 %collective-permute-start.11 = (bf16[2,128,128]{2,1,0:T(8,128)(2,1)}, bf16[2,128,128]{2,1,0:T(8,128)(2,1)}, u32[]{:S(2)}, u32[]{:S(2)}) collective-permute-start(bf16[2,128,128]{2,1,0:T(8,128)(2,1)} %get-tuple-element.53), channel_id=1, source_target_pairs={{0,3},{1,2},{2,1},{3,0},{4,7},{5,6},{6,5},{7,4},{8,11},{9,10},{10,... | collective-permute-start | bytes 196616 | tf_op jit(solution)/shard_map/ppermute | solution.py:347
  51.1 8.4 %collective-permute-start.8 = (bf16[128,128]{1,0:T(8,128)(2,1)}, bf16[128,128]{1,0:T(8,128)(2,1)}, u32[]{:S(2)}, u32[]{:S(2)}) collective-permute-start(bf16[128,128]{1,0:T(8,128)(2,1)} %get-tuple-element.48), channel_id=1, source_target_pairs={{4,0},{8,4},{12,8},{16,12},{20,16},{24,20},{28,24},{0,28},{5,1},{9... | collective-permute-start | bytes 98312 | tf_op jit(solution)/shard_map/ppermute | solution.py:341
  63.1 14.5 %all-to-all-start.3 = ((bf16[8,128,128]{2,1,0:T(8,128)(2,1)}), bf16[8,128,128]{2,1,0:T(8,128)(2,1)}, u32[]{:S(2)}, u32[]{:S(2)}) async-start(bf16[8,128,128]{2,1,0:T(8,128)(2,1)} %get-tuple-element.59), calls=%async_computation.3 | async-start | bytes 524288 | tf_op jit(solution)/shard_map/all_to_all | solution.py:456
  67.4 10.2 %collective-permute-start.15 = (bf16[2,128,128]{2,1,0:T(8,128)(2,1)}, bf16[2,128,128]{2,1,0:T(8,128)(2,1)}, u32[]{:S(2)}, u32[]{:S(2)}) collective-permute-start(bf16[2,128,128]{2,1,0:T(8,128)(2,1)} %get-tuple-element.55.refs_5_), channel_id=1, source_target_pairs={{0,3},{1,2},{2,1},{3,0},{4,7},{5,6},{6,5},{7,4},{8,11},{9,10},{10,... | collective-permute-start | bytes 196616 | tf_op jit(solution)/shard_map/ppermute | solution.py:347
  68.3 9.3 %collective-permute-start.14 = (bf16[2,128,128]{2,1,0:T(8,128)(2,1)}, bf16[2,128,128]{2,1,0:T(8,128)(2,1)}, u32[]{:S(2)}, u32[]{:S(2)}) collective-permute-start(bf16[2,128,128]{2,1,0:T(8,128)(2,1)} %get-tuple-element.55.refs_5_), channel_id=1, source_target_pairs={{0,2},{1,3},{2,0},{3,1},{4,6},{5,7},{6,4},{7,5},{8,10},{9,11},{10,... | collective-permute-start | bytes 196616 | tf_op jit(solution)/shard_map/ppermute | solution.py:347
  69.0 8.6 %collective-permute-start.13 = (bf16[2,128,128]{2,1,0:T(8,128)(2,1)}, bf16[2,128,128]{2,1,0:T(8,128)(2,1)}, u32[]{:S(2)}, u32[]{:S(2)}) collective-permute-start(bf16[2,128,128]{2,1,0:T(8,128)(2,1)} %get-tuple-element.55.refs_5_), channel_id=1, source_target_pairs={{0,1},{1,0},{2,3},{3,2},{4,5},{5,4},{6,7},{7,6},{8,9},{9,8},{10,11... | collective-permute-start | bytes 196616 | tf_op jit(solution)/shard_map/ppermute | solution.py:347
  69.3 8.3 %collective-permute-start.12 = (bf16[128,128]{1,0:T(8,128)(2,1)}, bf16[128,128]{1,0:T(8,128)(2,1)}, u32[]{:S(2)}, u32[]{:S(2)}) collective-permute-start(bf16[128,128]{1,0:T(8,128)(2,1)} %get-tuple-element.58), channel_id=1, source_target_pairs={{28,0},{0,4},{4,8},{8,12},{12,16},{16,20},{20,24},{24,28},{29,1},{... | collective-permute-start | bytes 98312 | tf_op jit(solution)/shard_map/ppermute | solution.py:341

commit v5 on v4

--- a/solution.py
+++ b/solution.py
@@ -187,7 +187,7 @@
         out.send()
 
 
-def dense_body(chunks, scalars, ins, outs, acc):
+def dense_body(chunks, parts, scalars, ins, outs, acc):
     count, rows, cols = scalars
     blocks, upper, dual, primal, prices = ins
     matrix, upper_full, out = outs
@@ -217,7 +217,7 @@
     turned = jnp.concatenate(
         [dual[i * size : (i + 1) * size].astype(BF16).T for i in range(dual.shape[0] // size)], axis=1
     )
-    adjoint(lambda: matrix.ref, turned, size, primal, prices, out, chunks)
+    adjoint(lambda: matrix.ref, turned, size, primal, prices, out, parts)
 
 
 def adjoint_body(chunks, scalars, ins, outs):
@@ -231,7 +231,7 @@
 def primal_body(scalars, ins, outs, acc, image_acc, product):
     ids, cols = scalars
     annual_q, annual, own, carried, primal, upper_full, partial, *arrived = ins
-    image, streams, last, extrap, updated = outs
+    image, last, extrap, updated, *streams = outs
     blocks, size, _ = extrap.ref.shape
     acc[...] = jnp.zeros_like(acc)
     image_acc[...] = jnp.zeros_like(image_acc)
@@ -254,9 +254,11 @@
         ahead = (2.0 * new - primal[at]).astype(BF16)
         extrap.ref[j] = ahead
         if j < SC:
-            streams.ref[j] = ahead
+            for copy in streams:
+                copy.ref[j] = ahead
         if j == SC - 1:
-            streams.send()
+            for copy in streams:
+                copy.send()
         if j == blocks - 1:
             last.ref[...] = ahead
             last.send()
@@ -292,7 +294,7 @@
 
 def dual_body(refineries, more, scalars, ins, outs, gathered, acc, product, *stream_acc):
     me, rows, src = scalars
-    swing, carry, streams, partial, previous, parts, annual, need, *arrived = ins
+    swing, carry, streams, previous, partial, parts, annual, need, *arrived = ins
     dual, annual_out = outs[0], outs[1]
     swing, carry = swing(), carry()
     size = swing.shape[1]
@@ -394,8 +396,7 @@
     annual_scratch = pltpu.VMEM((annuals, size, scenarios), F32)
     sends_shape = [pair] + [pair_q] * others + [tile]
     chunks = 4 if slots % 4 == 0 and columns % 4 == 0 else 1
-    parts_x = 4 if columns % 4 == 0 else 1
-    parts_y = 4 if rows % 4 == 0 else 1
+    parts_x, parts_y = 1, 1
 
     upper_rows = upper.reshape(columns, size)
     demand_rows = demand.reshape(rows, size)
@@ -418,15 +419,15 @@
         arrived = [exchanged(send, "refinery", d) for d, send in enumerate(sends, 1)]
         if iteration == 0:
             matrix_q, upper_full, partial_x = run(
-                functools.partial(dense_body, chunks),
+                functools.partial(dense_body, chunks, parts_x),
                 "dense",
                 [band_count, local_rows, local_cols],
                 [local_blocks, upper_rows, dual, primal, cost],
                 [matrix, state_x, state_x],
                 [pltpu.VMEM((rows * columns, size, size), F32)],
-                3 * rows * columns * unit,
+                16 * rows * columns * unit,
                 {0: (chunks, 0)},
-                {2: chunks},
+                {2: parts_x},
             )
         else:
             (partial_x,) = run(
@@ -436,16 +437,16 @@
                 [dual_q, matrix_q, primal, cost],
                 [state_x],
                 [],
-                2 * rows * columns * unit,
+                16 * rows * columns * unit,
                 {1: (parts_x, 1)},
                 {0: parts_x},
             )
-        image, streams, last, extrap, updated = run(
+        image, last, extrap, updated, streams, *send_streams = run(
             primal_body,
             "primal_step",
             [annual_ids, annual_cols],
             [annual_q, annual_blocks, own, carried_back, primal, upper_full, partial_x, *arrived],
-            [weekly, pair_q, tile, blocks_x, state_x],
+            [weekly, tile, blocks_x, state_x] + [pair_q] * refineries,
             [
                 pltpu.VMEM((columns, size, scenarios), F32),
                 pltpu.VMEM((weeks, size, scenarios), F32),
@@ -455,7 +456,7 @@
         )
         parts = lax.all_to_all(image, "period", 0, 0, tiled=True)
         previous = shifted(last, "period", 1)
-        others_streams = [exchanged(streams, "refinery", d) for d in range(1, refineries)]
+        others_streams = [exchanged(send, "refinery", d) for d, send in enumerate(send_streams, 1)]
         (partial_y,) = run(
             functools.partial(forward_body, parts_y),
             "forward",
@@ -463,7 +464,7 @@
             [extrap, matrix_q, dual, demand_rows],
             [state_y],
             [],
-            2 * rows * columns * unit,
+            16 * rows * columns * unit,
             {1: (parts_y, 0)},
             {0: parts_y},
         )
@@ -473,7 +474,7 @@
             "dual_step",
             [me, swing_rows, swing_src],
             [
-                swing_blocks, carry_blocks, streams, partial_y, previous, parts, annual, need,
+                swing_blocks, carry_blocks, streams, previous, partial_y, parts, annual, need,
                 *others_streams,
             ],
             [state_y, shape((size, scenarios), F32)] + sent,

time: 82 us -> 82.4 us (level)
  waiting for transfers between devices: 6.33 us -> 7.58 us
    ppermute x12, waiting for transfers between devices: 0.03 us -> 0.87 us  [exchanged(): return lax.ppermute(block, axis, [(i, i ^ d) for i in range(number)])]
  transfers between devices with their start and end apart: 20 -> 20, of which waited for: 2 -> 3; matrix products, arithmetic and copies ran while one was open for 0% -> 0% of each run, Pallas kernels for 19% -> 18%
where the time goes in v5:
time: 82.4 us; the launch traced here: 81.6 us
  starting transfers between devices  40.2 us (49%)
  Pallas kernels  32.3 us (39%)
  waiting for transfers between devices  7.58 us (9%)
  between operations  1.47 us (2%)
    pallas_call x9, Pallas kernels, run(): pl.pallas_call(kernel, name=name, in_specs=[SMEM] * ns + [HBM] * na, out_...  32.3 us
    ppermute x4, starting transfers between devices, shifted(): return lax.ppermute(block, axis, route)  13.1 us
    all_to_all x2, starting transfers between devices, body(): annual_q = lax.all_to_all(annual_send, 'period', 0, 0, tiled=True)  11.3 us
    all_to_all x2, starting transfers between devices, body(): parts = lax.all_to_all(image, 'period', 0, 0, tiled=True)  8.11 us
    ppermute x12, starting transfers between devices, exchanged(): return lax.ppermute(block, axis, [(i, i ^ d) for i in range(number)])  7.59 us
    ppermute x4, waiting for transfers between devices, shifted(): return lax.ppermute(block, axis, route)  6.71 us
  transfers between devices with their start and end apart: 20, of which 3 were waited for; matrix products, arithmetic and copies ran while one was open for 0% of the time, Pallas kernels for 18%

profile of v5, /device:TPU:0, one launch (start us, length us, event | category | flops | bytes accessed | tf_op | source)
XLA Modules:
  0.0 81.6 jit_solution(9345535267382806589)
XLA Ops:
  0.6 2.9 %first_duals.1 = (bf16[8,128,128]{2,1,0:T(8,128)(2,1)}, f32[2,128,128]{2,1,0:T(8,128)}, bf16[2,128,128]{2,1,0:T(8,128)(2,1)}, bf16[2,128,128]{2,1,0:T(8,128)(2,1...) custom-call(s32[1]{0:T(128)} %bitcast.refs_0_, s32[8]{0:T(128)} %refs_1_.11, s32[8]{0:T(128)} %refs_2_.9, ...), custom_call_target="tpu_custom_call" | custom-call | flops 37748736 | bytes 1507328 | tf_op jit(solution)/shard_map/first_duals/pallas_call | solution.py:106
  3.6 7.3 %all-to-all-start = ((bf16[8,128,128]{2,1,0:T(8,128)(2,1)}), bf16[8,128,128]{2,1,0:T(8,128)(2,1)}, u32[]{:S(2)}, u32[]{:S(2)}) async-start(bf16[8,128,128]{2,1,0:T(8,128)(2,1)} %get-tuple-element.39), calls=%async_computation | async-start | bytes 524288 | tf_op jit(solution)/shard_map/all_to_all | solution.py:417
  10.9 4.7 %collective-permute-start = (bf16[128,128]{1,0:T(8,128)(2,1)}, bf16[128,128]{1,0:T(8,128)(2,1)}, u32[]{:S(2)}, u32[]{:S(2)}) collective-permute-start(bf16[128,128]{1,0:T(8,128)(2,1)} %get-tuple-element.41), channel_id=1, source_target_pairs={{4,0},{8,4},{12,8},{16,12},{20,16},{24,20},{28,24},{0,28},{5,1},{9... | collective-permute-start | bytes 98312 | tf_op jit(solution)/shard_map/ppermute | solution.py:343
  15.6 1.5 %collective-permute-start.2 = (bf16[2,128,128]{2,1,0:T(8,128)(2,1)}, bf16[2,128,128]{2,1,0:T(8,128)(2,1)}, u32[]{:S(2)}, u32[]{:S(2)}) collective-permute-start(bf16[2,128,128]{2,1,0:T(8,128)(2,1)} %get-tuple-element.45), channel_id=1, source_target_pairs={{0,2},{1,3},{2,0},{3,1},{4,6},{5,7},{6,4},{7,5},{8,10},{9,11},{10,... | collective-permute-start | bytes 196616 | tf_op jit(solution)/shard_map/ppermute | solution.py:349
  17.1 0.4 collective-permute-start.3
  18.1 4.7 %dense.1 = (bf16[1024,1024]{1,0:T(8,128)(2,1)}, f32[1024,128]{1,0:T(8,128)}, f32[1024,128]{1,0:T(8,128)}) custom-call(s32[1]{0:T(128)S(6)} %copy.21.refs_0_, s32[96]{0:T(128)} %refs_1_.7, s32[96]{0:T(128)} %refs_2_.6, bf16[96,128,128]{2,1,0:T(8,128)(2,1)} %refs_3_.8, f32[8,128]{1,0:T(8,128)} %bitcast.6, f32[1024,128]{1,0:T(8,128)} %refs_2_.7, ...), custom_call_target="tpu_custom_call" | custom-call | flops 4294967296 | bytes 7868416 | tf_op jit(solution)/shard_map/dense/pallas_call | solution.py:106
  22.8 0.0 collective-permute-done.2.refs_10_
  22.8 0.0 collective-permute-done.3.refs_11_
  22.9 3.7 %primal_step.2 = (bf16[8,128,128]{2,1,0:T(8,128)(2,1)}, bf16[128,128]{1,0:T(8,128)(2,1)}, bf16[8,128,128]{2,1,0:T(8,128)(2,1)}, f32[1024,128]{1,0:T(8,128)}, bf1...) custom-call(s32[8]{0:T(128)} %refs_0_.4, ...), custom_call_target="tpu_custom_call" | custom-call | flops 67108864 | bytes 3801088 | tf_op jit(solution)/shard_map/primal_step/pallas_call | solution.py:106
  26.6 4.1 %all-to-all-start.1 = ((bf16[8,128,128]{2,1,0:T(8,128)(2,1)}), bf16[8,128,128]{2,1,0:T(8,128)(2,1)}, u32[]{:S(2)}, u32[]{:S(2)}) async-start(bf16[8,128,128]{2,1,0:T(8,128)(2,1)} %get-tuple-element.51), calls=%async_computation.1 | async-start | bytes 524288 | tf_op jit(solution)/shard_map/all_to_all | solution.py:457
  30.6 1.9 %collective-permute-start.4 = (bf16[128,128]{1,0:T(8,128)(2,1)}, bf16[128,128]{1,0:T(8,128)(2,1)}, u32[]{:S(2)}, u32[]{:S(2)}) collective-permute-start(bf16[128,128]{1,0:T(8,128)(2,1)} %get-tuple-element.48), channel_id=1, source_target_pairs={{28,0},{0,4},{4,8},{8,12},{12,16},{16,20},{20,24},{24,28},{29,1},{... | collective-permute-start | bytes 98312 | tf_op jit(solution)/shard_map/ppermute | solution.py:343
  32.5 0.0 collective-permute-start.5
  32.5 1.9 %collective-permute-start.6 = (bf16[2,128,128]{2,1,0:T(8,128)(2,1)}, bf16[2,128,128]{2,1,0:T(8,128)(2,1)}, u32[]{:S(2)}, u32[]{:S(2)}) collective-permute-start(bf16[2,128,128]{2,1,0:T(8,128)(2,1)} %get-tuple-element.53), channel_id=1, source_target_pairs={{0,2},{1,3},{2,0},{3,1},{4,6},{5,7},{6,4},{7,5},{8,10},{9,11},{10,... | collective-permute-start | bytes 196616 | tf_op jit(solution)/shard_map/ppermute | solution.py:349
  34.4 0.1 collective-permute-start.7
  34.5 3.4 %forward.2.refs_7_ = f32[1024,128]{1,0:T(8,128)} custom-call(bf16[8,128,128]{2,1,0:T(8,128)(2,1)} %get-tuple-element.49.refs_0_, bf16[1024,1024]{1,0:T(8,128)(2,1)} %get-tuple-element.50.refs_1_, f32[1024,128]{1,0:T(8,128)} %refs_2_.7, f32[8,128]{1,0:T(8,128)} %bitcast.7), custom_call_target="tpu_custom_call" | custom-call | flops 4294967296 | bytes 3411968 | tf_op jit(solution)/shard_map/forward/pallas_call | solution.py:106
  38.0 3.4 %collective-permute-done.4.refs_6_ = bf16[128,128]{1,0:T(8,128)(2,1)} collective-permute-done((bf16[128,128]{1,0:T(8,128)(2,1)}, bf16[128,128]{1,0:T(8,128)(2,1)}, u32[]{:S(2)}, u32[]{:S(2)}) %collective-permute-start.4) | collective-permute-done | bytes 32800 | tf_op jit(solution)/shard_map/ppermute | solution.py:343
  41.4 0.0 collective-permute-done.7.refs_13_
  41.4 3.8 %dual_step.2 = (f32[1024,128]{1,0:T(8,128)}, f32[128,128]{1,0:T(8,128)}, bf16[8,128,128]{2,1,0:T(8,128)(2,1)}, bf16[8,128,128]{2,1,0:T(8,128)(2,1)}, f32[2,128,1...) custom-call(s32[1]{0:T(128)} %bitcast.refs_0_, ...), custom_call_target="tpu_custom_call" | custom-call | flops 67108864 | bytes 2916864 | tf_op jit(solution)/shard_map/dual_step/pallas_call | solution.py:106
  45.2 4.1 %all-to-all-start.2 = ((bf16[8,128,128]{2,1,0:T(8,128)(2,1)}), bf16[8,128,128]{2,1,0:T(8,128)(2,1)}, u32[]{:S(2)}, u32[]{:S(2)}) async-start(bf16[8,128,128]{2,1,0:T(8,128)(2,1)} %get-tuple-element.55), calls=%async_computation.2 | async-start | bytes 524288 | tf_op jit(solution)/shard_map/all_to_all | solution.py:417
  49.3 4.6 %collective-permute-start.8 = (bf16[128,128]{1,0:T(8,128)(2,1)}, bf16[128,128]{1,0:T(8,128)(2,1)}, u32[]{:S(2)}, u32[]{:S(2)}) collective-permute-start(bf16[128,128]{1,0:T(8,128)(2,1)} %get-tuple-element.57), channel_id=1, source_target_pairs={{4,0},{8,4},{12,8},{16,12},{20,16},{24,20},{28,24},{0,28},{5,1},{9... | collective-permute-start | bytes 98312 | tf_op jit(solution)/shard_map/ppermute | solution.py:343
  53.9 1.5 %collective-permute-start.10 = (bf16[2,128,128]{2,1,0:T(8,128)(2,1)}, bf16[2,128,128]{2,1,0:T(8,128)(2,1)}, u32[]{:S(2)}, u32[]{:S(2)}) collective-permute-start(bf16[2,128,128]{2,1,0:T(8,128)(2,1)} %get-tuple-element.61), channel_id=1, source_target_pairs={{0,2},{1,3},{2,0},{3,1},{4,6},{5,7},{6,4},{7,5},{8,10},{9,11},{10,... | collective-permute-start | bytes 196616 | tf_op jit(solution)/shard_map/ppermute | solution.py:349
  55.4 0.4 collective-permute-start.11
  55.8 3.2 %adjoint.1.refs_8_ = f32[1024,128]{1,0:T(8,128)} custom-call(bf16[8,128,128]{2,1,0:T(8,128)(2,1)} %get-tuple-element.59.refs_0_, bf16[1024,1024]{1,0:T(8,128)(2,1)} %get-tuple-element.50.refs_1_, f32[1024,128]{1,0:T(8,128)} %get-tuple-element.58.refs_2_.refs_6_, f32[1024,128]{1,0:T(8,128)} %refs_3_.11), custom_call_target="tpu_custom_call" | custom-call | flops 4294967296 | bytes 3932160 | tf_op jit(solution)/shard_map/adjoint/pallas_call | solution.py:106
  59.0 0.8 %collective-permute-done.11.refs_11_ = bf16[2,128,128]{2,1,0:T(8,128)(2,1)} collective-permute-done((bf16[2,128,128]{2,1,0:T(8,128)(2,1)}, bf16[2,128,128]{2,1,0:T(8,128)(2,1)}, u32[]{:S(2)}, u32[]{:S(2)}) %collective-permute-start.11) | collective-permute-done | bytes 65568 | tf_op jit(solution)/shard_map/ppermute | solution.py:349
  59.8 3.6 %primal_step.3 = (bf16[8,128,128]{2,1,0:T(8,128)(2,1)}, bf16[128,128]{1,0:T(8,128)(2,1)}, bf16[8,128,128]{2,1,0:T(8,128)(2,1)}, f32[1024,128]{1,0:T(8,128)}, bf1...) custom-call(s32[8]{0:T(128)} %refs_0_.4, ...), custom_call_target="tpu_custom_call" | custom-call | flops 67108864 | bytes 3801088 | tf_op jit(solution)/shard_map/primal_step/pallas_call | solution.py:106
  63.4 4.1 %all-to-all-start.3 = ((bf16[8,128,128]{2,1,0:T(8,128)(2,1)}), bf16[8,128,128]{2,1,0:T(8,128)(2,1)}, u32[]{:S(2)}, u32[]{:S(2)}) async-start(bf16[8,128,128]{2,1,0:T(8,128)(2,1)} %get-tuple-element.68), calls=%async_computation.3 | async-start | bytes 524288 | tf_op jit(solution)/shard_map/all_to_all | solution.py:457
  67.5 1.9 %collective-permute-start.12 = (bf16[128,128]{1,0:T(8,128)(2,1)}, bf16[128,128]{1,0:T(8,128)(2,1)}, u32[]{:S(2)}, u32[]{:S(2)}) collective-permute-start(bf16[128,128]{1,0:T(8,128)(2,1)} %get-tuple-element.65), channel_id=1, source_target_pairs={{28,0},{0,4},{4,8},{8,12},{12,16},{16,20},{20,24},{24,28},{29,1},{... | collective-permute-start | bytes 98312 | tf_op jit(solution)/shard_map/ppermute | solution.py:343
  69.4 1.4 %collective-permute-start.14 = (bf16[2,128,128]{2,1,0:T(8,128)(2,1)}, bf16[2,128,128]{2,1,0:T(8,128)(2,1)}, u32[]{:S(2)}, u32[]{:S(2)}) collective-permute-start(bf16[2,128,128]{2,1,0:T(8,128)(2,1)} %get-tuple-element.71), channel_id=1, source_target_pairs={{0,2},{1,3},{2,0},{3,1},{4,6},{5,7},{6,4},{7,5},{8,10},{9,11},{10,... | collective-permute-start | bytes 196616 | tf_op jit(solution)/shard_map/ppermute | solution.py:349
  70.8 0.4 collective-permute-start.15
  71.2 3.5 %forward.3.refs_7_ = f32[1024,128]{1,0:T(8,128)} custom-call(bf16[8,128,128]{2,1,0:T(8,128)(2,1)} %get-tuple-element.66.refs_0_, bf16[1024,1024]{1,0:T(8,128)(2,1)} %get-tuple-element.50.refs_1_, f32[1024,128]{1,0:T(8,128)} %get-tuple-element.67.refs_2_, f32[8,128]{1,0:T(8,128)} %bitcast.8), custom_call_target="tpu_custom_call" | custom-call | flops 4294967296 | bytes 3411968 | tf_op jit(solution)/shard_map/forward/pallas_call | solution.py:106
  74.7 3.3 %collective-permute-done.12.refs_6_ = bf16[128,128]{1,0:T(8,128)(2,1)} collective-permute-done((bf16[128,128]{1,0:T(8,128)(2,1)}, bf16[128,128]{1,0:T(8,128)(2,1)}, u32[]{:S(2)}, u32[]{:S(2)}) %collective-permute-start.12) | collective-permute-done | bytes 32800 | tf_op jit(solution)/shard_map/ppermute | solution.py:343
  78.1 3.5 %dual_step.3 = (f32[1024,128]{1,0:T(8,128)}, f32[128,128]{1,0:T(8,128)}) custom-call(s32[1]{0:T(128)} %bitcast.refs_0_, s32[8]{0:T(128)} %refs_1_.11, s32[8]{0:T(128)} %refs_2_.9, bf16[8,128,128]{2,1,0:T(8,128)(2,1)} %refs_3_.13, bf16[1,128,128]{2,1,0:T(8,128)(2,1)} %refs_4_.5, bf16[2,128,128]{2,1,0:T(8,128)(2,1)} %get-tuple-element.64.refs_5_, ...), custom_call_target="tpu_custom_call" | custom-call | flops 67108864 | bytes 2032128 | tf_op jit(solution)/shard_map/dual_step/pallas_call | solution.py:106
  (17 shorter events, 0.0 us)
Async XLA Ops:
  3.6 19.3 %all-to-all-start = ((bf16[8,128,128]{2,1,0:T(8,128)(2,1)}), bf16[8,128,128]{2,1,0:T(8,128)(2,1)}, u32[]{:S(2)}, u32[]{:S(2)}) async-start(bf16[8,128,128]{2,1,0:T(8,128)(2,1)} %get-tuple-element.39), calls=%async_computation | async-start | bytes 524288 | tf_op jit(solution)/shard_map/all_to_all | solution.py:417
  10.9 12.0 %collective-permute-start = (bf16[128,128]{1,0:T(8,128)(2,1)}, bf16[128,128]{1,0:T(8,128)(2,1)}, u32[]{:S(2)}, u32[]{:S(2)}) collective-permute-start(bf16[128,128]{1,0:T(8,128)(2,1)} %get-tuple-element.41), channel_id=1, source_target_pairs={{4,0},{8,4},{12,8},{16,12},{20,16},{24,20},{28,24},{0,28},{5,1},{9... | collective-permute-start | bytes 98312 | tf_op jit(solution)/shard_map/ppermute | solution.py:343
  15.6 7.2 %collective-permute-start.1 = (bf16[2,128,128]{2,1,0:T(8,128)(2,1)}, bf16[2,128,128]{2,1,0:T(8,128)(2,1)}, u32[]{:S(2)}, u32[]{:S(2)}) collective-permute-start(bf16[2,128,128]{2,1,0:T(8,128)(2,1)} %get-tuple-element.44), channel_id=1, source_target_pairs={{0,1},{1,0},{2,3},{3,2},{4,5},{5,4},{6,7},{7,6},{8,9},{9,8},{10,11... | collective-permute-start | bytes 196616 | tf_op jit(solution)/shard_map/ppermute | solution.py:349
  15.6 7.2 %collective-permute-start.2 = (bf16[2,128,128]{2,1,0:T(8,128)(2,1)}, bf16[2,128,128]{2,1,0:T(8,128)(2,1)}, u32[]{:S(2)}, u32[]{:S(2)}) collective-permute-start(bf16[2,128,128]{2,1,0:T(8,128)(2,1)} %get-tuple-element.45), channel_id=1, source_target_pairs={{0,2},{1,3},{2,0},{3,1},{4,6},{5,7},{6,4},{7,5},{8,10},{9,11},{10,... | collective-permute-start | bytes 196616 | tf_op jit(solution)/shard_map/ppermute | solution.py:349
  17.1 5.8 %collective-permute-start.3 = (bf16[2,128,128]{2,1,0:T(8,128)(2,1)}, bf16[2,128,128]{2,1,0:T(8,128)(2,1)}, u32[]{:S(2)}, u32[]{:S(2)}) collective-permute-start(bf16[2,128,128]{2,1,0:T(8,128)(2,1)} %get-tuple-element.46), channel_id=1, source_target_pairs={{0,3},{1,2},{2,1},{3,0},{4,7},{5,6},{6,5},{7,4},{8,11},{9,10},{10,... | collective-permute-start | bytes 196616 | tf_op jit(solution)/shard_map/ppermute | solution.py:349
  26.6 14.8 %all-to-all-start.1 = ((bf16[8,128,128]{2,1,0:T(8,128)(2,1)}), bf16[8,128,128]{2,1,0:T(8,128)(2,1)}, u32[]{:S(2)}, u32[]{:S(2)}) async-start(bf16[8,128,128]{2,1,0:T(8,128)(2,1)} %get-tuple-element.51), calls=%async_computation.1 | async-start | bytes 524288 | tf_op jit(solution)/shard_map/all_to_all | solution.py:457
  30.6 10.7 %collective-permute-start.4 = (bf16[128,128]{1,0:T(8,128)(2,1)}, bf16[128,128]{1,0:T(8,128)(2,1)}, u32[]{:S(2)}, u32[]{:S(2)}) collective-permute-start(bf16[128,128]{1,0:T(8,128)(2,1)} %get-tuple-element.48), channel_id=1, source_target_pairs={{28,0},{0,4},{4,8},{8,12},{12,16},{16,20},{20,24},{24,28},{29,1},{... | collective-permute-start | bytes 98312 | tf_op jit(solution)/shard_map/ppermute | solution.py:343
  32.5 8.8 %collective-permute-start.5 = (bf16[2,128,128]{2,1,0:T(8,128)(2,1)}, bf16[2,128,128]{2,1,0:T(8,128)(2,1)}, u32[]{:S(2)}, u32[]{:S(2)}) collective-permute-start(bf16[2,128,128]{2,1,0:T(8,128)(2,1)} %get-tuple-element.52), channel_id=1, source_target_pairs={{0,1},{1,0},{2,3},{3,2},{4,5},{5,4},{6,7},{7,6},{8,9},{9,8},{10,11... | collective-permute-start | bytes 196616 | tf_op jit(solution)/shard_map/ppermute | solution.py:349
  32.5 8.8 %collective-permute-start.6 = (bf16[2,128,128]{2,1,0:T(8,128)(2,1)}, bf16[2,128,128]{2,1,0:T(8,128)(2,1)}, u32[]{:S(2)}, u32[]{:S(2)}) collective-permute-start(bf16[2,128,128]{2,1,0:T(8,128)(2,1)} %get-tuple-element.53), channel_id=1, source_target_pairs={{0,2},{1,3},{2,0},{3,1},{4,6},{5,7},{6,4},{7,5},{8,10},{9,11},{10,... | collective-permute-start | bytes 196616 | tf_op jit(solution)/shard_map/ppermute | solution.py:349
  34.4 7.0 %collective-permute-start.7 = (bf16[2,128,128]{2,1,0:T(8,128)(2,1)}, bf16[2,128,128]{2,1,0:T(8,128)(2,1)}, u32[]{:S(2)}, u32[]{:S(2)}) collective-permute-start(bf16[2,128,128]{2,1,0:T(8,128)(2,1)} %get-tuple-element.54), channel_id=1, source_target_pairs={{0,3},{1,2},{2,1},{3,0},{4,7},{5,6},{6,5},{7,4},{8,11},{9,10},{10,... | collective-permute-start | bytes 196616 | tf_op jit(solution)/shard_map/ppermute | solution.py:349
  45.2 14.6 %all-to-all-start.2 = ((bf16[8,128,128]{2,1,0:T(8,128)(2,1)}), bf16[8,128,128]{2,1,0:T(8,128)(2,1)}, u32[]{:S(2)}, u32[]{:S(2)}) async-start(bf16[8,128,128]{2,1,0:T(8,128)(2,1)} %get-tuple-element.55), calls=%async_computation.2 | async-start | bytes 524288 | tf_op jit(solution)/shard_map/all_to_all | solution.py:417
  49.3 9.7 %collective-permute-start.8 = (bf16[128,128]{1,0:T(8,128)(2,1)}, bf16[128,128]{1,0:T(8,128)(2,1)}, u32[]{:S(2)}, u32[]{:S(2)}) collective-permute-start(bf16[128,128]{1,0:T(8,128)(2,1)} %get-tuple-element.57), channel_id=1, source_target_pairs={{4,0},{8,4},{12,8},{16,12},{20,16},{24,20},{28,24},{0,28},{5,1},{9... | collective-permute-start | bytes 98312 | tf_op jit(solution)/shard_map/ppermute | solution.py:343
  53.9 5.1 %collective-permute-start.9 = (bf16[2,128,128]{2,1,0:T(8,128)(2,1)}, bf16[2,128,128]{2,1,0:T(8,128)(2,1)}, u32[]{:S(2)}, u32[]{:S(2)}) collective-permute-start(bf16[2,128,128]{2,1,0:T(8,128)(2,1)} %get-tuple-element.60), channel_id=1, source_target_pairs={{0,1},{1,0},{2,3},{3,2},{4,5},{5,4},{6,7},{7,6},{8,9},{9,8},{10,11... | collective-permute-start | bytes 196616 | tf_op jit(solution)/shard_map/ppermute | solution.py:349
  53.9 5.1 %collective-permute-start.10 = (bf16[2,128,128]{2,1,0:T(8,128)(2,1)}, bf16[2,128,128]{2,1,0:T(8,128)(2,1)}, u32[]{:S(2)}, u32[]{:S(2)}) collective-permute-start(bf16[2,128,128]{2,1,0:T(8,128)(2,1)} %get-tuple-element.61), channel_id=1, source_target_pairs={{0,2},{1,3},{2,0},{3,1},{4,6},{5,7},{6,4},{7,5},{8,10},{9,11},{10,... | collective-permute-start | bytes 196616 | tf_op jit(solution)/shard_map/ppermute | solution.py:349
  55.4 4.4 %collective-permute-start.11 = (bf16[2,128,128]{2,1,0:T(8,128)(2,1)}, bf16[2,128,128]{2,1,0:T(8,128)(2,1)}, u32[]{:S(2)}, u32[]{:S(2)}) collective-permute-start(bf16[2,128,128]{2,1,0:T(8,128)(2,1)} %get-tuple-element.62), channel_id=1, source_target_pairs={{0,3},{1,2},{2,1},{3,0},{4,7},{5,6},{6,5},{7,4},{8,11},{9,10},{10,... | collective-permute-start | bytes 196616 | tf_op jit(solution)/shard_map/ppermute | solution.py:349
  63.4 14.6 %all-to-all-start.3 = ((bf16[8,128,128]{2,1,0:T(8,128)(2,1)}), bf16[8,128,128]{2,1,0:T(8,128)(2,1)}, u32[]{:S(2)}, u32[]{:S(2)}) async-start(bf16[8,128,128]{2,1,0:T(8,128)(2,1)} %get-tuple-element.68), calls=%async_computation.3 | async-start | bytes 524288 | tf_op jit(solution)/shard_map/all_to_all | solution.py:457
  67.5 10.6 %collective-permute-start.12 = (bf16[128,128]{1,0:T(8,128)(2,1)}, bf16[128,128]{1,0:T(8,128)(2,1)}, u32[]{:S(2)}, u32[]{:S(2)}) collective-permute-start(bf16[128,128]{1,0:T(8,128)(2,1)} %get-tuple-element.65), channel_id=1, source_target_pairs={{28,0},{0,4},{4,8},{8,12},{12,16},{16,20},{20,24},{24,28},{29,1},{... | collective-permute-start | bytes 98312 | tf_op jit(solution)/shard_map/ppermute | solution.py:343
  69.4 8.7 %collective-permute-start.13 = (bf16[2,128,128]{2,1,0:T(8,128)(2,1)}, bf16[2,128,128]{2,1,0:T(8,128)(2,1)}, u32[]{:S(2)}, u32[]{:S(2)}) collective-permute-start(bf16[2,128,128]{2,1,0:T(8,128)(2,1)} %get-tuple-element.70), channel_id=1, source_target_pairs={{0,1},{1,0},{2,3},{3,2},{4,5},{5,4},{6,7},{7,6},{8,9},{9,8},{10,11... | collective-permute-start | bytes 196616 | tf_op jit(solution)/shard_map/ppermute | solution.py:349
  69.4 8.7 %collective-permute-start.14 = (bf16[2,128,128]{2,1,0:T(8,128)(2,1)}, bf16[2,128,128]{2,1,0:T(8,128)(2,1)}, u32[]{:S(2)}, u32[]{:S(2)}) collective-permute-start(bf16[2,128,128]{2,1,0:T(8,128)(2,1)} %get-tuple-element.71), channel_id=1, source_target_pairs={{0,2},{1,3},{2,0},{3,1},{4,6},{5,7},{6,4},{7,5},{8,10},{9,11},{10,... | collective-permute-start | bytes 196616 | tf_op jit(solution)/shard_map/ppermute | solution.py:349
  70.8 7.3 %collective-permute-start.15 = (bf16[2,128,128]{2,1,0:T(8,128)(2,1)}, bf16[2,128,128]{2,1,0:T(8,128)(2,1)}, u32[]{:S(2)}, u32[]{:S(2)}) collective-permute-start(bf16[2,128,128]{2,1,0:T(8,128)(2,1)} %get-tuple-element.72), channel_id=1, source_target_pairs={{0,3},{1,2},{2,1},{3,0},{4,7},{5,6},{6,5},{7,4},{8,11},{9,10},{10,... | collective-permute-start | bytes 196616 | tf_op jit(solution)/shard_map/ppermute | solution.py:349

commit v6 on v4

--- a/solution.py
+++ b/solution.py
@@ -109,7 +109,10 @@
         in_specs=[SMEM] * ns + [HBM] * na,
         out_specs=(HBM,) * no,
         out_shape=tuple(outs),
-        scratch_shapes=[pltpu.VMEM(a.shape, a.dtype) for a in (*arrays, *outs)]
+        scratch_shapes=[
+            (pltpu.SMEM if a.dtype == jnp.int32 else pltpu.VMEM)(a.shape, a.dtype)
+            for a in (*arrays, *outs)
+        ]
         + [
             pltpu.SemaphoreType.DMA((sum(count for count, _ in counts),)),
             pltpu.SemaphoreType.DMA((sum(out_counts),)),
@@ -172,29 +175,25 @@
     )
 
 
-def adjoint(matrix, turned, size, primal, prices, out, chunks):
-    step = out.ref.shape[0] // chunks
-    for j in range(chunks):
-        columns = slice(j * step, (j + 1) * step)
-        part = dot(turned, matrix()[:, columns])
-        if j == 0:
-            primal, prices = primal(), prices()
-        for h in range(step // size):
-            at = slice(j * step + h * size, j * step + (h + 1) * size)
-            out.ref[at] = primal[at] - PRIMAL_STEP * (
-                prices[at] - part[:, h * size : (h + 1) * size].T
-            )
-        out.send()
+def adjoint(matrix, turned, size, primal, prices, out):
+    part = dot(turned, matrix[...])
+    primal, prices = primal(), prices()
+    for j in range(part.shape[1] // size):
+        at = slice(j * size, (j + 1) * size)
+        out.ref[at] = primal[at] - PRIMAL_STEP * (prices[at] - part[:, at].T)
 
 
 def dense_body(chunks, scalars, ins, outs, acc):
-    count, rows, cols = scalars
-    blocks, upper, dual, primal, prices = ins
-    matrix, upper_full, out = outs
-    size = upper.target.shape[1]
-    width = upper_full.ref.shape[1]
+    rows, cols = scalars
+    count, dual, blocks, primal, prices = ins
+    matrix, out = outs
+    size = blocks.target.shape[1]
     tiles = matrix.ref.shape[1] // size
     acc[...] = jnp.zeros_like(acc)
+    count, dual = count(), dual()
+    turned = jnp.concatenate(
+        [dual[i * size : (i + 1) * size].astype(BF16).T for i in range(dual.shape[0] // size)], axis=1
+    )
     slots = blocks.target.shape[0] // chunks
     for c in range(chunks):
         here = blocks.piece()
@@ -208,33 +207,28 @@
         for j in range(tiles):
             at = (slice(i * size, (i + 1) * size), slice(j * size, (j + 1) * size))
             matrix.ref[at] = acc[i * tiles + j].astype(BF16)
-    matrix.send()
-    upper = upper()
-    for j in range(tiles):
-        upper_full.ref[j * size : (j + 1) * size] = column_of(upper[j : j + 1], width)
-    upper_full.send()
-    dual = dual()
-    turned = jnp.concatenate(
-        [dual[i * size : (i + 1) * size].astype(BF16).T for i in range(dual.shape[0] // size)], axis=1
-    )
-    adjoint(lambda: matrix.ref, turned, size, primal, prices, out, chunks)
-
-
-def adjoint_body(chunks, scalars, ins, outs):
+        matrix.send()
+    adjoint(matrix.ref, turned, size, primal, prices, out)
+
+
+def adjoint_body(scalars, ins, outs):
     dual_q, matrix, primal, prices = ins
     dual_q = dual_q()
     blocks, size, _ = dual_q.shape
     turned = jnp.concatenate([dual_q[i].T for i in range(blocks)], axis=1)
-    adjoint(matrix.piece, turned, size, primal, prices, outs[0], chunks)
-
-
-def primal_body(scalars, ins, outs, acc, image_acc, product):
+    adjoint(matrix(), turned, size, primal, prices, outs[0])
+
+
+def primal_body(scalars, ins, outs, acc, image_acc, product, bound):
     ids, cols = scalars
-    annual_q, annual, own, carried, primal, upper_full, partial, *arrived = ins
-    image, streams, last, extrap, updated = outs
+    upper, annual, annual_q, own, carried, *arrived, partial, primal = ins
+    image, last, extrap, updated, streams = outs
     blocks, size, _ = extrap.ref.shape
     acc[...] = jnp.zeros_like(acc)
     image_acc[...] = jnp.zeros_like(image_acc)
+    upper = upper()
+    for j in range(blocks):
+        bound[j] = column_of(upper[j : j + 1], bound.shape[2])
     annual, annual_q = annual(), annual_q()
     slots = annual.shape[0]
     for k in range(slots):
@@ -246,10 +240,10 @@
         total = total + piece()[...].astype(F32)
     acc[:SC] += total
     acc[blocks - 1] += carried()[...].astype(F32)
-    partial, primal, upper_full = partial(), primal(), upper_full()
+    partial, primal = partial(), primal()
     for j in range(blocks):
         at = slice(j * size, (j + 1) * size)
-        new = jnp.clip(partial[at] + PRIMAL_STEP * acc[j], 0.0, upper_full[at])
+        new = jnp.clip(partial[at] + PRIMAL_STEP * acc[j], 0.0, bound[j])
         updated.ref[at] = new
         ahead = (2.0 * new - primal[at]).astype(BF16)
         extrap.ref[j] = ahead
@@ -269,32 +263,23 @@
     image.ref[...] = image_acc[...].astype(BF16)
 
 
-def forward_body(chunks, scalars, ins, outs):
-    extrap, matrix, dual, demand = ins
+def forward_body(scalars, ins, outs):
+    extrap, demand, dual, matrix = ins
     out = outs[0]
-    extrap = extrap()
+    extrap, demand, dual = extrap(), demand(), dual()
     blocks, size, width = extrap.shape
     right = jnp.concatenate([extrap[j] for j in range(blocks)], axis=0)
-    step = out.ref.shape[0] // chunks
-    for i in range(chunks):
-        lines = slice(i * step, (i + 1) * step)
-        part = dot(matrix.piece()[lines], right)
-        if i == 0:
-            dual, demand = dual(), demand()
-        for h in range(step // size):
-            at = slice(i * step + h * size, i * step + (h + 1) * size)
-            row = i * (step // size) + h
-            out.ref[at] = dual[at] + DUAL_STEP * (
-                column_of(demand[row : row + 1], width) - part[h * size : (h + 1) * size]
-            )
-        out.send()
+    for i in range(demand.shape[0]):
+        at = slice(i * size, (i + 1) * size)
+        out.ref[at] = dual[at] + DUAL_STEP * column_of(demand[i : i + 1], width)
+    out.ref[...] -= DUAL_STEP * dot(matrix()[...], right)
 
 
 def dual_body(refineries, more, scalars, ins, outs, gathered, acc, product, *stream_acc):
     me, rows, src = scalars
-    swing, carry, streams, partial, previous, parts, annual, need, *arrived = ins
+    swing, streams, *arrived, carry, previous, parts, annual, need, partial = ins
     dual, annual_out = outs[0], outs[1]
-    swing, carry = swing(), carry()
+    swing = swing()
     size = swing.shape[1]
     mine = me[0]
     gathered[pl.ds(mine * SC, SC)] = streams()[...]
@@ -305,6 +290,7 @@
         product[m] = dot(swing[m], gathered[src[m]])
     for m in range(swing.shape[0]):
         acc[rows[m]] += product[m]
+    carry = carry()
     acc[0] += dot(carry[0], previous()[...])
     parts, annual = parts(), annual()
     total = parts[0].astype(F32)
@@ -393,9 +379,7 @@
     swing_scratch = pltpu.VMEM((swings, size, scenarios), F32)
     annual_scratch = pltpu.VMEM((annuals, size, scenarios), F32)
     sends_shape = [pair] + [pair_q] * others + [tile]
-    chunks = 4 if slots % 4 == 0 and columns % 4 == 0 else 1
-    parts_x = 4 if columns % 4 == 0 else 1
-    parts_y = 4 if rows % 4 == 0 else 1
+    chunks = 8 if slots % 8 == 0 else 1
 
     upper_rows = upper.reshape(columns, size)
     demand_rows = demand.reshape(rows, size)
@@ -417,39 +401,38 @@
         carried_back = shifted(carried, "period", -1)
         arrived = [exchanged(send, "refinery", d) for d, send in enumerate(sends, 1)]
         if iteration == 0:
-            matrix_q, upper_full, partial_x = run(
+            matrix_q, partial_x = run(
                 functools.partial(dense_body, chunks),
                 "dense",
-                [band_count, local_rows, local_cols],
-                [local_blocks, upper_rows, dual, primal, cost],
-                [matrix, state_x, state_x],
+                [local_rows, local_cols],
+                [band_count, dual, local_blocks, primal, cost],
+                [matrix, state_x],
                 [pltpu.VMEM((rows * columns, size, size), F32)],
-                3 * rows * columns * unit,
-                {0: (chunks, 0)},
-                {2: chunks},
+                16 * rows * columns * unit,
+                {2: (chunks, 0)},
+                {0: rows},
             )
         else:
             (partial_x,) = run(
-                functools.partial(adjoint_body, parts_x),
+                adjoint_body,
                 "adjoint",
                 [],
                 [dual_q, matrix_q, primal, cost],
                 [state_x],
                 [],
-                2 * rows * columns * unit,
-                {1: (parts_x, 1)},
-                {0: parts_x},
+                16 * rows * columns * unit,
             )
-        image, streams, last, extrap, updated = run(
+        image, last, extrap, updated, streams = run(
             primal_body,
             "primal_step",
             [annual_ids, annual_cols],
-            [annual_q, annual_blocks, own, carried_back, primal, upper_full, partial_x, *arrived],
-            [weekly, pair_q, tile, blocks_x, state_x],
+            [upper_rows, annual_blocks, annual_q, own, carried_back, *arrived, partial_x, primal],
+            [weekly, tile, blocks_x, state_x, pair_q],
             [
                 pltpu.VMEM((columns, size, scenarios), F32),
                 pltpu.VMEM((weeks, size, scenarios), F32),
                 annual_scratch,
+                pltpu.VMEM((columns, size, scenarios), F32),
             ],
             2 * annuals * unit,
         )
@@ -457,15 +440,13 @@
         previous = shifted(last, "period", 1)
         others_streams = [exchanged(streams, "refinery", d) for d in range(1, refineries)]
         (partial_y,) = run(
-            functools.partial(forward_body, parts_y),
+            forward_body,
             "forward",
             [],
-            [extrap, matrix_q, dual, demand_rows],
+            [extrap, demand_rows, dual, matrix_q],
             [state_y],
             [],
-            2 * rows * columns * unit,
-            {1: (parts_y, 0)},
-            {0: parts_y},
+            16 * rows * columns * unit,
         )
         sent = [weekly, blocks_y] + sends_shape if more else []
         dual, annual, *rest = run(
@@ -473,8 +454,8 @@
             "dual_step",
             [me, swing_rows, swing_src],
             [
-                swing_blocks, carry_blocks, streams, partial_y, previous, parts, annual, need,
-                *others_streams,
+                swing_blocks, streams, *others_streams, carry_blocks, previous, parts, annual,
+                need, partial_y,
             ],
             [state_y, shape((size, scenarios), F32)] + sent,
             [

time: 82 us -> 81.4 us (level)
  Pallas kernels: 32.9 us -> 31.1 us
  waiting for transfers between devices: 6.33 us -> 8 us
    pallas_call x9, Pallas kernels: 32.9 us -> 31.1 us  [run(): pl.pallas_call(kernel, name=name, in_specs=[SMEM] * ns + [HBM] * na, out_...]
    ppermute x12, waiting for transfers between devices: 0.03 us -> 1.06 us  [exchanged(): return lax.ppermute(block, axis, [(i, i ^ d) for i in range(number)])]
  transfers between devices with their start and end apart: 20 -> 20, of which waited for: 2 -> 3; matrix products, arithmetic and copies ran while one was open for 0% -> 0% of each run, Pallas kernels for 19% -> 18%
where the time goes in v6:
time: 81.4 us; the launch traced here: 80.7 us
  starting transfers between devices  40.1 us (49%)
  Pallas kernels  31.1 us (38%)
  waiting for transfers between devices  8 us (10%)
  between operations  1.47 us (2%)
    pallas_call x9, Pallas kernels, run(): pl.pallas_call(kernel, name=name, in_specs=[SMEM] * ns + [HBM] * na, out_...  31.1 us
    ppermute x4, starting transfers between devices, shifted(): return lax.ppermute(block, axis, route)  12.9 us
    all_to_all x2, starting transfers between devices, body(): annual_q = lax.all_to_all(annual_send, 'period', 0, 0, tiled=True)  11.4 us
    all_to_all x2, starting transfers between devices, body(): parts = lax.all_to_all(image, 'period', 0, 0, tiled=True)  8.12 us
    ppermute x12, starting transfers between devices, exchanged(): return lax.ppermute(block, axis, [(i, i ^ d) for i in range(number)])  7.71 us
    ppermute x4, waiting for transfers between devices, shifted(): return lax.ppermute(block, axis, route)  6.93 us
  transfers between devices with their start and end apart: 20, of which 3 were waited for; matrix products, arithmetic and copies ran while one was open for 0% of the time, Pallas kernels for 18%

profile of v6, /device:TPU:0, one launch (start us, length us, event | category | flops | bytes accessed | tf_op | source)
XLA Modules:
  0.0 80.7 jit_solution(17043711983553784874)
XLA Ops:
  0.6 2.9 %first_duals.1 = (bf16[8,128,128]{2,1,0:T(8,128)(2,1)}, f32[2,128,128]{2,1,0:T(8,128)}, bf16[2,128,128]{2,1,0:T(8,128)(2,1)}, bf16[2,128,128]{2,1,0:T(8,128)(2,1...) custom-call(s32[1]{0:T(128)} %bitcast.1.refs_0_, s32[8]{0:T(128)} %refs_1_.11, s32[8]{0:T(128)} %refs_2_.8, ...), custom_call_target="tpu_custom_call" | custom-call | flops 37748736 | bytes 1507328 | tf_op jit(solution)/shard_map/first_duals/pallas_call | solution.py:106
  3.6 7.3 %all-to-all-start = ((bf16[8,128,128]{2,1,0:T(8,128)(2,1)}), bf16[8,128,128]{2,1,0:T(8,128)(2,1)}, u32[]{:S(2)}, u32[]{:S(2)}) async-start(bf16[8,128,128]{2,1,0:T(8,128)(2,1)} %get-tuple-element.32), calls=%async_computation | async-start | bytes 524288 | tf_op jit(solution)/shard_map/all_to_all | solution.py:400
  10.9 4.7 %collective-permute-start = (bf16[128,128]{1,0:T(8,128)(2,1)}, bf16[128,128]{1,0:T(8,128)(2,1)}, u32[]{:S(2)}, u32[]{:S(2)}) collective-permute-start(bf16[128,128]{1,0:T(8,128)(2,1)} %get-tuple-element.34), channel_id=1, source_target_pairs={{4,0},{8,4},{12,8},{16,12},{20,16},{24,20},{28,24},{0,28},{5,1},{9... | collective-permute-start | bytes 98312 | tf_op jit(solution)/shard_map/ppermute | solution.py:327
  15.6 1.5 %collective-permute-start.2 = (bf16[2,128,128]{2,1,0:T(8,128)(2,1)}, bf16[2,128,128]{2,1,0:T(8,128)(2,1)}, u32[]{:S(2)}, u32[]{:S(2)}) collective-permute-start(bf16[2,128,128]{2,1,0:T(8,128)(2,1)} %get-tuple-element.36), channel_id=1, source_target_pairs={{0,2},{1,3},{2,0},{3,1},{4,6},{5,7},{6,4},{7,5},{8,10},{9,11},{10,... | collective-permute-start | bytes 196616 | tf_op jit(solution)/shard_map/ppermute | solution.py:333
  17.1 0.4 collective-permute-start.3
  18.1 4.6 %dense.1 = (bf16[1024,1024]{1,0:T(8,128)(2,1)}, f32[1024,128]{1,0:T(8,128)}) custom-call(s32[96]{0:T(128)} %refs_0_.3, s32[96]{0:T(128)} %refs_1_.7, s32[1]{0:T(128)S(6)} %copy.21.refs_2_, f32[1024,128]{1,0:T(8,128)} %refs_2_.6, bf16[96,128,128]{2,1,0:T(8,128)(2,1)} %refs_4_.3, f32[1024,128]{1,0:T(8,128)} %refs_11_.2, f32[1024,128]{1,0:T(8,128)} %refs_3_.11), custom_call_target="tpu_custom_call" | custom-call | flops 4294967296 | bytes 7340036 | tf_op jit(solution)/shard_map/dense/pallas_call | solution.py:106
  22.7 0.0 collective-permute-done.refs_6_
  22.7 0.0 collective-permute-done.1.refs_7_
  22.7 0.0 collective-permute-done.3.refs_9_
  22.7 3.4 %primal_step.2 = (bf16[8,128,128]{2,1,0:T(8,128)(2,1)}, bf16[128,128]{1,0:T(8,128)(2,1)}, bf16[8,128,128]{2,1,0:T(8,128)(2,1)}, f32[1024,128]{1,0:T(8,128)}, bf16[2,128,128]{2,1,0:T(8,128)(2,1)}) custom-call(s32[8]{0:T(128)} %refs_0_.5, s32[8]{0:T(128)} %refs_1_.10, f32[8,128]{1,0:T(8,128)} %bitcast.4, bf16[8,128,128]{2,1,0:T(8,128)(2,1)} %refs_3_.12, ...), custom_call_target="tpu_custom_call" | custom-call | flops 67108864 | bytes 3084288 | tf_op jit(solution)/shard_map/primal_step/pallas_call | solution.py:106
  26.2 4.1 %all-to-all-start.1 = ((bf16[8,128,128]{2,1,0:T(8,128)(2,1)}), bf16[8,128,128]{2,1,0:T(8,128)(2,1)}, u32[]{:S(2)}, u32[]{:S(2)}) async-start(bf16[8,128,128]{2,1,0:T(8,128)(2,1)} %get-tuple-element.41), calls=%async_computation.1 | async-start | bytes 524288 | tf_op jit(solution)/shard_map/all_to_all | solution.py:439
  30.2 1.7 %collective-permute-start.6 = (bf16[2,128,128]{2,1,0:T(8,128)(2,1)}, bf16[2,128,128]{2,1,0:T(8,128)(2,1)}, u32[]{:S(2)}, u32[]{:S(2)}) collective-permute-start(bf16[2,128,128]{2,1,0:T(8,128)(2,1)} %get-tuple-element.39.refs_4_), channel_id=1, source_target_pairs={{0,3},{1,2},{2,1},{3,0},{4,7},{5,6},{6,5},{7,4},{8,11},{9,10},{10,... | collective-permute-start | bytes 196616 | tf_op jit(solution)/shard_map/ppermute | solution.py:333
  32.0 0.2 collective-permute-start.5
  32.2 1.8 %collective-permute-start.7 = (bf16[128,128]{1,0:T(8,128)(2,1)}, bf16[128,128]{1,0:T(8,128)(2,1)}, u32[]{:S(2)}, u32[]{:S(2)}) collective-permute-start(bf16[128,128]{1,0:T(8,128)(2,1)} %get-tuple-element.40), channel_id=1, source_target_pairs={{28,0},{0,4},{4,8},{8,12},{12,16},{16,20},{20,24},{24,28},{29,1},{... | collective-permute-start | bytes 98312 | tf_op jit(solution)/shard_map/ppermute | solution.py:327
  34.0 3.4 %forward.2.refs_13_ = f32[1024,128]{1,0:T(8,128)} custom-call(bf16[8,128,128]{2,1,0:T(8,128)(2,1)} %get-tuple-element.42.refs_0_, f32[8,128]{1,0:T(8,128)} %bitcast.8, f32[1024,128]{1,0:T(8,128)} %refs_2_.6, bf16[1024,1024]{1,0:T(8,128)(2,1)} %get-tuple-element.43.refs_3_.refs_1_), custom_call_target="tpu_custom_call" | custom-call | flops 4294967296 | bytes 3411968 | tf_op jit(solution)/shard_map/forward/pallas_call | solution.py:106
  37.4 3.5 %collective-permute-done.7.refs_9_ = bf16[128,128]{1,0:T(8,128)(2,1)} collective-permute-done((bf16[128,128]{1,0:T(8,128)(2,1)}, bf16[128,128]{1,0:T(8,128)(2,1)}, u32[]{:S(2)}, u32[]{:S(2)}) %collective-permute-start.7) | collective-permute-done | bytes 32800 | tf_op jit(solution)/shard_map/ppermute | solution.py:327
  41.0 3.6 %dual_step.2 = (f32[1024,128]{1,0:T(8,128)}, f32[128,128]{1,0:T(8,128)}, bf16[8,128,128]{2,1,0:T(8,128)(2,1)}, bf16[8,128,128]{2,1,0:T(8,128)(2,1)}, f32[2,128,1...) custom-call(s32[1]{0:T(128)} %bitcast.1.refs_0_, ...), custom_call_target="tpu_custom_call" | custom-call | flops 67108864 | bytes 2916864 | tf_op jit(solution)/shard_map/dual_step/pallas_call | solution.py:106
  44.5 4.1 %all-to-all-start.2 = ((bf16[8,128,128]{2,1,0:T(8,128)(2,1)}), bf16[8,128,128]{2,1,0:T(8,128)(2,1)}, u32[]{:S(2)}, u32[]{:S(2)}) async-start(bf16[8,128,128]{2,1,0:T(8,128)(2,1)} %get-tuple-element.44), calls=%async_computation.2 | async-start | bytes 524288 | tf_op jit(solution)/shard_map/all_to_all | solution.py:400
  48.6 4.6 %collective-permute-start.8 = (bf16[128,128]{1,0:T(8,128)(2,1)}, bf16[128,128]{1,0:T(8,128)(2,1)}, u32[]{:S(2)}, u32[]{:S(2)}) collective-permute-start(bf16[128,128]{1,0:T(8,128)(2,1)} %get-tuple-element.46), channel_id=1, source_target_pairs={{4,0},{8,4},{12,8},{16,12},{20,16},{24,20},{28,24},{0,28},{5,1},{9... | collective-permute-start | bytes 98312 | tf_op jit(solution)/shard_map/ppermute | solution.py:327
  53.2 1.8 %collective-permute-start.10 = (bf16[2,128,128]{2,1,0:T(8,128)(2,1)}, bf16[2,128,128]{2,1,0:T(8,128)(2,1)}, u32[]{:S(2)}, u32[]{:S(2)}) collective-permute-start(bf16[2,128,128]{2,1,0:T(8,128)(2,1)} %get-tuple-element.48), channel_id=1, source_target_pairs={{0,2},{1,3},{2,0},{3,1},{4,6},{5,7},{6,4},{7,5},{8,10},{9,11},{10,... | collective-permute-start | bytes 196616 | tf_op jit(solution)/shard_map/ppermute | solution.py:333
  55.0 0.1 collective-permute-start.11
  55.2 3.2 %adjoint.1.refs_10_ = f32[1024,128]{1,0:T(8,128)} custom-call(bf16[8,128,128]{2,1,0:T(8,128)(2,1)} %get-tuple-element.50.refs_0_, bf16[1024,1024]{1,0:T(8,128)(2,1)} %get-tuple-element.43.refs_3_.refs_1_, f32[1024,128]{1,0:T(8,128)} %get-tuple-element.51.refs_2_.refs_11_, f32[1024,128]{1,0:T(8,128)} %refs_3_.11), custom_call_target="tpu_custom_call" | custom-call | flops 4294967296 | bytes 3932160 | tf_op jit(solution)/shard_map/adjoint/pallas_call | solution.py:106
  58.4 1.0 %collective-permute-done.11.refs_9_ = bf16[2,128,128]{2,1,0:T(8,128)(2,1)} collective-permute-done((bf16[2,128,128]{2,1,0:T(8,128)(2,1)}, bf16[2,128,128]{2,1,0:T(8,128)(2,1)}, u32[]{:S(2)}, u32[]{:S(2)}) %collective-permute-start.11) | collective-permute-done | bytes 65568 | tf_op jit(solution)/shard_map/ppermute | solution.py:333
  59.4 3.4 %primal_step.3 = (bf16[8,128,128]{2,1,0:T(8,128)(2,1)}, bf16[128,128]{1,0:T(8,128)(2,1)}, bf16[8,128,128]{2,1,0:T(8,128)(2,1)}, f32[1024,128]{1,0:T(8,128)}, bf16[2,128,128]{2,1,0:T(8,128)(2,1)}) custom-call(s32[8]{0:T(128)} %refs_0_.5, s32[8]{0:T(128)} %refs_1_.10, f32[8,128]{1,0:T(8,128)} %bitcast.5, bf16[8,128,128]{2,1,0:T(8,128)(2,1)} %refs_3_.12, ...), custom_call_target="tpu_custom_call" | custom-call | flops 67108864 | bytes 3084288 | tf_op jit(solution)/shard_map/primal_step/pallas_call | solution.py:106
  62.8 4.1 %all-to-all-start.3 = ((bf16[8,128,128]{2,1,0:T(8,128)(2,1)}), bf16[8,128,128]{2,1,0:T(8,128)(2,1)}, u32[]{:S(2)}, u32[]{:S(2)}) async-start(bf16[8,128,128]{2,1,0:T(8,128)(2,1)} %get-tuple-element.55), calls=%async_computation.3 | async-start | bytes 524288 | tf_op jit(solution)/shard_map/all_to_all | solution.py:439
  66.9 1.3 %collective-permute-start.14 = (bf16[2,128,128]{2,1,0:T(8,128)(2,1)}, bf16[2,128,128]{2,1,0:T(8,128)(2,1)}, u32[]{:S(2)}, u32[]{:S(2)}) collective-permute-start(bf16[2,128,128]{2,1,0:T(8,128)(2,1)} %get-tuple-element.53.refs_4_), channel_id=1, source_target_pairs={{0,3},{1,2},{2,1},{3,0},{4,7},{5,6},{6,5},{7,4},{8,11},{9,10},{10,... | collective-permute-start | bytes 196616 | tf_op jit(solution)/shard_map/ppermute | solution.py:333
  68.2 0.5 collective-permute-start.13
  68.8 0.1 collective-permute-start.12
  68.8 1.8 %collective-permute-start.15 = (bf16[128,128]{1,0:T(8,128)(2,1)}, bf16[128,128]{1,0:T(8,128)(2,1)}, u32[]{:S(2)}, u32[]{:S(2)}) collective-permute-start(bf16[128,128]{1,0:T(8,128)(2,1)} %get-tuple-element.54), channel_id=1, source_target_pairs={{28,0},{0,4},{4,8},{8,12},{12,16},{16,20},{20,24},{24,28},{29,1},{... | collective-permute-start | bytes 98312 | tf_op jit(solution)/shard_map/ppermute | solution.py:327
  70.7 3.4 %forward.3.refs_13_ = f32[1024,128]{1,0:T(8,128)} custom-call(bf16[8,128,128]{2,1,0:T(8,128)(2,1)} %get-tuple-element.57.refs_0_, f32[8,128]{1,0:T(8,128)} %bitcast.9, f32[1024,128]{1,0:T(8,128)} %get-tuple-element.58.refs_2_, bf16[1024,1024]{1,0:T(8,128)(2,1)} %get-tuple-element.43.refs_3_.refs_1_), custom_call_target="tpu_custom_call" | custom-call | flops 4294967296 | bytes 3411968 | tf_op jit(solution)/shard_map/forward/pallas_call | solution.py:106
  74.1 3.4 %collective-permute-done.15.refs_9_ = bf16[128,128]{1,0:T(8,128)(2,1)} collective-permute-done((bf16[128,128]{1,0:T(8,128)(2,1)}, bf16[128,128]{1,0:T(8,128)(2,1)}, u32[]{:S(2)}, u32[]{:S(2)}) %collective-permute-start.15) | collective-permute-done | bytes 32800 | tf_op jit(solution)/shard_map/ppermute | solution.py:327
  77.5 3.2 %dual_step.3 = (f32[1024,128]{1,0:T(8,128)}, f32[128,128]{1,0:T(8,128)}) custom-call(s32[1]{0:T(128)} %bitcast.1.refs_0_, s32[8]{0:T(128)} %refs_1_.11, s32[8]{0:T(128)} %refs_2_.8, bf16[8,128,128]{2,1,0:T(8,128)(2,1)} %refs_3_.13, bf16[2,128,128]{2,1,0:T(8,128)(2,1)} %get-tuple-element.53.refs_4_, bf16[2,128,128]{2,1,0:T(8,128)(2,1)} %collective-permute-done.12.refs_5_, ...), custom_call_target="tpu_custom_call" | custom-call | flops 67108864 | bytes 2032128 | tf_op jit(solution)/shard_map/dual_step/pallas_call | solution.py:106
  (17 shorter events, 0.0 us)
Async XLA Ops:
  3.6 19.1 %all-to-all-start = ((bf16[8,128,128]{2,1,0:T(8,128)(2,1)}), bf16[8,128,128]{2,1,0:T(8,128)(2,1)}, u32[]{:S(2)}, u32[]{:S(2)}) async-start(bf16[8,128,128]{2,1,0:T(8,128)(2,1)} %get-tuple-element.32), calls=%async_computation | async-start | bytes 524288 | tf_op jit(solution)/shard_map/all_to_all | solution.py:400
  10.9 11.8 %collective-permute-start = (bf16[128,128]{1,0:T(8,128)(2,1)}, bf16[128,128]{1,0:T(8,128)(2,1)}, u32[]{:S(2)}, u32[]{:S(2)}) collective-permute-start(bf16[128,128]{1,0:T(8,128)(2,1)} %get-tuple-element.34), channel_id=1, source_target_pairs={{4,0},{8,4},{12,8},{16,12},{20,16},{24,20},{28,24},{0,28},{5,1},{9... | collective-permute-start | bytes 98312 | tf_op jit(solution)/shard_map/ppermute | solution.py:327
  15.6 7.1 %collective-permute-start.1 = (bf16[2,128,128]{2,1,0:T(8,128)(2,1)}, bf16[2,128,128]{2,1,0:T(8,128)(2,1)}, u32[]{:S(2)}, u32[]{:S(2)}) collective-permute-start(bf16[2,128,128]{2,1,0:T(8,128)(2,1)} %get-tuple-element.35), channel_id=1, source_target_pairs={{0,1},{1,0},{2,3},{3,2},{4,5},{5,4},{6,7},{7,6},{8,9},{9,8},{10,11... | collective-permute-start | bytes 196616 | tf_op jit(solution)/shard_map/ppermute | solution.py:333
  15.6 7.1 %collective-permute-start.2 = (bf16[2,128,128]{2,1,0:T(8,128)(2,1)}, bf16[2,128,128]{2,1,0:T(8,128)(2,1)}, u32[]{:S(2)}, u32[]{:S(2)}) collective-permute-start(bf16[2,128,128]{2,1,0:T(8,128)(2,1)} %get-tuple-element.36), channel_id=1, source_target_pairs={{0,2},{1,3},{2,0},{3,1},{4,6},{5,7},{6,4},{7,5},{8,10},{9,11},{10,... | collective-permute-start | bytes 196616 | tf_op jit(solution)/shard_map/ppermute | solution.py:333
  17.1 5.6 %collective-permute-start.3 = (bf16[2,128,128]{2,1,0:T(8,128)(2,1)}, bf16[2,128,128]{2,1,0:T(8,128)(2,1)}, u32[]{:S(2)}, u32[]{:S(2)}) collective-permute-start(bf16[2,128,128]{2,1,0:T(8,128)(2,1)} %get-tuple-element.37), channel_id=1, source_target_pairs={{0,3},{1,2},{2,1},{3,0},{4,7},{5,6},{6,5},{7,4},{8,11},{9,10},{10,... | collective-permute-start | bytes 196616 | tf_op jit(solution)/shard_map/ppermute | solution.py:333
  26.2 14.8 %all-to-all-start.1 = ((bf16[8,128,128]{2,1,0:T(8,128)(2,1)}), bf16[8,128,128]{2,1,0:T(8,128)(2,1)}, u32[]{:S(2)}, u32[]{:S(2)}) async-start(bf16[8,128,128]{2,1,0:T(8,128)(2,1)} %get-tuple-element.41), calls=%async_computation.1 | async-start | bytes 524288 | tf_op jit(solution)/shard_map/all_to_all | solution.py:439
  30.2 10.7 %collective-permute-start.6 = (bf16[2,128,128]{2,1,0:T(8,128)(2,1)}, bf16[2,128,128]{2,1,0:T(8,128)(2,1)}, u32[]{:S(2)}, u32[]{:S(2)}) collective-permute-start(bf16[2,128,128]{2,1,0:T(8,128)(2,1)} %get-tuple-element.39.refs_4_), channel_id=1, source_target_pairs={{0,3},{1,2},{2,1},{3,0},{4,7},{5,6},{6,5},{7,4},{8,11},{9,10},{10,... | collective-permute-start | bytes 196616 | tf_op jit(solution)/shard_map/ppermute | solution.py:333
  32.0 9.0 %collective-permute-start.5 = (bf16[2,128,128]{2,1,0:T(8,128)(2,1)}, bf16[2,128,128]{2,1,0:T(8,128)(2,1)}, u32[]{:S(2)}, u32[]{:S(2)}) collective-permute-start(bf16[2,128,128]{2,1,0:T(8,128)(2,1)} %get-tuple-element.39.refs_4_), channel_id=1, source_target_pairs={{0,2},{1,3},{2,0},{3,1},{4,6},{5,7},{6,4},{7,5},{8,10},{9,11},{10,... | collective-permute-start | bytes 196616 | tf_op jit(solution)/shard_map/ppermute | solution.py:333
  32.2 8.7 %collective-permute-start.4 = (bf16[2,128,128]{2,1,0:T(8,128)(2,1)}, bf16[2,128,128]{2,1,0:T(8,128)(2,1)}, u32[]{:S(2)}, u32[]{:S(2)}) collective-permute-start(bf16[2,128,128]{2,1,0:T(8,128)(2,1)} %get-tuple-element.39.refs_4_), channel_id=1, source_target_pairs={{0,1},{1,0},{2,3},{3,2},{4,5},{5,4},{6,7},{7,6},{8,9},{9,8},{10,11... | collective-permute-start | bytes 196616 | tf_op jit(solution)/shard_map/ppermute | solution.py:333
  32.2 8.7 %collective-permute-start.7 = (bf16[128,128]{1,0:T(8,128)(2,1)}, bf16[128,128]{1,0:T(8,128)(2,1)}, u32[]{:S(2)}, u32[]{:S(2)}) collective-permute-start(bf16[128,128]{1,0:T(8,128)(2,1)} %get-tuple-element.40), channel_id=1, source_target_pairs={{28,0},{0,4},{4,8},{8,12},{12,16},{16,20},{20,24},{24,28},{29,1},{... | collective-permute-start | bytes 98312 | tf_op jit(solution)/shard_map/ppermute | solution.py:327
  44.5 14.9 %all-to-all-start.2 = ((bf16[8,128,128]{2,1,0:T(8,128)(2,1)}), bf16[8,128,128]{2,1,0:T(8,128)(2,1)}, u32[]{:S(2)}, u32[]{:S(2)}) async-start(bf16[8,128,128]{2,1,0:T(8,128)(2,1)} %get-tuple-element.44), calls=%async_computation.2 | async-start | bytes 524288 | tf_op jit(solution)/shard_map/all_to_all | solution.py:400
  48.6 9.8 %collective-permute-start.8 = (bf16[128,128]{1,0:T(8,128)(2,1)}, bf16[128,128]{1,0:T(8,128)(2,1)}, u32[]{:S(2)}, u32[]{:S(2)}) collective-permute-start(bf16[128,128]{1,0:T(8,128)(2,1)} %get-tuple-element.46), channel_id=1, source_target_pairs={{4,0},{8,4},{12,8},{16,12},{20,16},{24,20},{28,24},{0,28},{5,1},{9... | collective-permute-start | bytes 98312 | tf_op jit(solution)/shard_map/ppermute | solution.py:327
  53.2 5.1 %collective-permute-start.9 = (bf16[2,128,128]{2,1,0:T(8,128)(2,1)}, bf16[2,128,128]{2,1,0:T(8,128)(2,1)}, u32[]{:S(2)}, u32[]{:S(2)}) collective-permute-start(bf16[2,128,128]{2,1,0:T(8,128)(2,1)} %get-tuple-element.47), channel_id=1, source_target_pairs={{0,1},{1,0},{2,3},{3,2},{4,5},{5,4},{6,7},{7,6},{8,9},{9,8},{10,11... | collective-permute-start | bytes 196616 | tf_op jit(solution)/shard_map/ppermute | solution.py:333
  53.2 5.1 %collective-permute-start.10 = (bf16[2,128,128]{2,1,0:T(8,128)(2,1)}, bf16[2,128,128]{2,1,0:T(8,128)(2,1)}, u32[]{:S(2)}, u32[]{:S(2)}) collective-permute-start(bf16[2,128,128]{2,1,0:T(8,128)(2,1)} %get-tuple-element.48), channel_id=1, source_target_pairs={{0,2},{1,3},{2,0},{3,1},{4,6},{5,7},{6,4},{7,5},{8,10},{9,11},{10,... | collective-permute-start | bytes 196616 | tf_op jit(solution)/shard_map/ppermute | solution.py:333
  55.0 4.4 %collective-permute-start.11 = (bf16[2,128,128]{2,1,0:T(8,128)(2,1)}, bf16[2,128,128]{2,1,0:T(8,128)(2,1)}, u32[]{:S(2)}, u32[]{:S(2)}) collective-permute-start(bf16[2,128,128]{2,1,0:T(8,128)(2,1)} %get-tuple-element.49), channel_id=1, source_target_pairs={{0,3},{1,2},{2,1},{3,0},{4,7},{5,6},{6,5},{7,4},{8,11},{9,10},{10,... | collective-permute-start | bytes 196616 | tf_op jit(solution)/shard_map/ppermute | solution.py:333
  62.8 14.7 %all-to-all-start.3 = ((bf16[8,128,128]{2,1,0:T(8,128)(2,1)}), bf16[8,128,128]{2,1,0:T(8,128)(2,1)}, u32[]{:S(2)}, u32[]{:S(2)}) async-start(bf16[8,128,128]{2,1,0:T(8,128)(2,1)} %get-tuple-element.55), calls=%async_computation.3 | async-start | bytes 524288 | tf_op jit(solution)/shard_map/all_to_all | solution.py:439
  66.9 10.6 %collective-permute-start.14 = (bf16[2,128,128]{2,1,0:T(8,128)(2,1)}, bf16[2,128,128]{2,1,0:T(8,128)(2,1)}, u32[]{:S(2)}, u32[]{:S(2)}) collective-permute-start(bf16[2,128,128]{2,1,0:T(8,128)(2,1)} %get-tuple-element.53.refs_4_), channel_id=1, source_target_pairs={{0,3},{1,2},{2,1},{3,0},{4,7},{5,6},{6,5},{7,4},{8,11},{9,10},{10,... | collective-permute-start | bytes 196616 | tf_op jit(solution)/shard_map/ppermute | solution.py:333
  68.2 9.2 %collective-permute-start.13 = (bf16[2,128,128]{2,1,0:T(8,128)(2,1)}, bf16[2,128,128]{2,1,0:T(8,128)(2,1)}, u32[]{:S(2)}, u32[]{:S(2)}) collective-permute-start(bf16[2,128,128]{2,1,0:T(8,128)(2,1)} %get-tuple-element.53.refs_4_), channel_id=1, source_target_pairs={{0,2},{1,3},{2,0},{3,1},{4,6},{5,7},{6,4},{7,5},{8,10},{9,11},{10,... | collective-permute-start | bytes 196616 | tf_op jit(solution)/shard_map/ppermute | solution.py:333
  68.8 8.7 %collective-permute-start.12 = (bf16[2,128,128]{2,1,0:T(8,128)(2,1)}, bf16[2,128,128]{2,1,0:T(8,128)(2,1)}, u32[]{:S(2)}, u32[]{:S(2)}) collective-permute-start(bf16[2,128,128]{2,1,0:T(8,128)(2,1)} %get-tuple-element.53.refs_4_), channel_id=1, source_target_pairs={{0,1},{1,0},{2,3},{3,2},{4,5},{5,4},{6,7},{7,6},{8,9},{9,8},{10,11... | collective-permute-start | bytes 196616 | tf_op jit(solution)/shard_map/ppermute | solution.py:333
  68.8 8.6 %collective-permute-start.15 = (bf16[128,128]{1,0:T(8,128)(2,1)}, bf16[128,128]{1,0:T(8,128)(2,1)}, u32[]{:S(2)}, u32[]{:S(2)}) collective-permute-start(bf16[128,128]{1,0:T(8,128)(2,1)} %get-tuple-element.54), channel_id=1, source_target_pairs={{28,0},{0,4},{4,8},{8,12},{12,16},{16,20},{20,24},{24,28},{29,1},{... | collective-permute-start | bytes 98312 | tf_op jit(solution)/shard_map/ppermute | solution.py:327

commit v7 on v6

--- a/solution.py
+++ b/solution.py
@@ -275,7 +275,7 @@
     out.ref[...] -= DUAL_STEP * dot(matrix()[...], right)
 
 
-def dual_body(refineries, more, scalars, ins, outs, gathered, acc, product, *stream_acc):
+def dual_body(refineries, scalars, ins, outs, gathered, acc, product, stream_acc):
     me, rows, src = scalars
     swing, streams, *arrived, carry, previous, parts, annual, need, partial = ins
     dual, annual_out = outs[0], outs[1]
@@ -301,24 +301,100 @@
     )
     annual_out.ref[...] = new_annual
     annual_out.send()
-    if more:
-        rounded = new_annual.astype(BF16)
-        for w in range(parts.shape[0]):
-            outs[2].ref[w] = rounded
-        outs[2].send()
+    rounded = new_annual.astype(BF16)
+    for w in range(parts.shape[0]):
+        outs[2].ref[w] = rounded
+    outs[2].send()
     partial = partial()
     for i in range(acc.shape[0]):
         at = slice(i * size, (i + 1) * size)
         new = jnp.maximum(partial[at] - DUAL_STEP * acc[i], 0.0)
         dual.ref[at] = new
-        if more:
-            outs[3].ref[i] = new.astype(BF16)
+        outs[3].ref[i] = new.astype(BF16)
     dual.send()
-    if more:
-        outs[3].send()
-        send_duals(
-            refineries, outs[3].ref, mine, rows, src, swing, carry, outs[4:], *stream_acc, product
-        )
+    outs[3].send()
+    send_duals(
+        refineries, outs[3].ref, mine, rows, src, swing, carry, outs[4:], stream_acc, product
+    )
+
+
+def last_rows_body(refineries, scalars, ins, outs, gathered, acc, product):
+    me, rows, src = scalars
+    demand, dual, extrap, matrix, swing, streams, *arrived = ins
+    out = outs[0]
+    demand, dual, extrap = demand(), dual(), extrap()
+    blocks, size, width = extrap.shape
+    for i in range(demand.shape[0]):
+        at = slice(i * size, (i + 1) * size)
+        out.ref[at] = dual[at] + DUAL_STEP * column_of(demand[i : i + 1], width)
+    right = jnp.concatenate([extrap[j] for j in range(blocks)], axis=0)
+    out.ref[...] -= DUAL_STEP * dot(matrix()[...], right)
+    swing, mine = swing(), me[0]
+    gathered[pl.ds(mine * SC, SC)] = streams()[...]
+    for d, piece in enumerate(arrived, 1):
+        gathered[pl.ds(partner(mine, d, refineries, True) * SC, SC)] = piece()[...]
+    acc[...] = jnp.zeros_like(acc)
+    for m in range(swing.shape[0]):
+        product[m] = dot(swing[m], gathered[src[m]])
+    for m in range(swing.shape[0]):
+        acc[rows[m]] += product[m]
+    for i in range(acc.shape[0]):
+        at = slice(i * size, (i + 1) * size)
+        new = out.ref[at] - DUAL_STEP * acc[i]
+        out.ref[at] = jnp.maximum(new, 0.0) if i else new
+
+
+def finish_kernel(
+    row, annual, need, parts, carry, previous, dual_out, annual_out,
+    row_v, annual_v, need_v, parts_v, carry_v, previous_v, new_v, in_sems, out_sems,
+):
+    size = row_v.shape[0]
+    head = pl.ds(0, size)
+    sources = (row.at[head], carry, previous, annual, need, parts)
+    landing = (row_v, carry_v, previous_v, annual_v, need_v, parts_v)
+    copies = [
+        pltpu.make_async_copy(source, target, in_sems.at[i])
+        for i, (source, target) in enumerate(zip(sources, landing))
+    ]
+    for copy in copies:
+        copy.start()
+    for copy in copies[:3]:
+        copy.wait()
+    row_v[...] = jnp.maximum(row_v[...] - DUAL_STEP * dot(carry_v[0], previous_v[...]), 0.0)
+    first = pltpu.make_async_copy(row_v, dual_out.at[head], out_sems.at[0])
+    first.start()
+    for copy in copies[3:]:
+        copy.wait()
+    total = parts_v[0].astype(F32)
+    for w in range(1, parts_v.shape[0]):
+        total = total + parts_v[w].astype(F32)
+    new_v[...] = jnp.maximum(
+        annual_v[...] + DUAL_STEP * (column_of(need_v[...], annual_v.shape[1]) - total), 0.0
+    )
+    second = pltpu.make_async_copy(new_v, annual_out, out_sems.at[1])
+    second.start()
+    first.wait()
+    second.wait()
+
+
+def finish(dual, annual, need, parts, carry, previous):
+    size, width = annual.shape
+    arrays = (dual, annual, need, parts, carry, previous)
+    buffers = (annual, annual, need, parts, carry, previous, annual)
+    return pl.pallas_call(
+        finish_kernel,
+        name="finish",
+        in_specs=[HBM] * 6,
+        out_specs=(HBM, HBM),
+        out_shape=(shape(dual.shape, F32), shape(annual.shape, F32)),
+        scratch_shapes=[pltpu.VMEM(a.shape, a.dtype) for a in buffers]
+        + [pltpu.SemaphoreType.DMA((6,)), pltpu.SemaphoreType.DMA((2,))],
+        input_output_aliases={0: 0},
+        compiler_params=pltpu.CompilerParams(vmem_limit_bytes=64 << 20),
+        cost_estimate=pl.CostEstimate(
+            flops=2 * size * size * width, bytes_accessed=1_000_000, transcendentals=0
+        ),
+    )(*arrays)
 
 
 def shifted(block, axis, distance):
@@ -439,6 +515,22 @@
         parts = lax.all_to_all(image, "period", 0, 0, tiled=True)
         previous = shifted(last, "period", 1)
         others_streams = [exchanged(streams, "refinery", d) for d in range(1, refineries)]
+        if not more:
+            (dual,) = run(
+                functools.partial(last_rows_body, refineries),
+                "last_rows",
+                [me, swing_rows, swing_src],
+                [demand_rows, dual, extrap, matrix_q, swing_blocks, streams, *others_streams],
+                [state_y],
+                [
+                    pltpu.VMEM((refineries * SC, size, scenarios), BF16),
+                    pltpu.VMEM((rows, size, scenarios), F32),
+                    swing_scratch,
+                ],
+                unit,
+            )
+            dual, annual = finish(dual, annual, need, parts, carry_blocks, previous)
+            return updated, dual, annual
         (partial_y,) = run(
             forward_body,
             "forward",
@@ -448,9 +540,9 @@
             [],
             16 * rows * columns * unit,
         )
-        sent = [weekly, blocks_y] + sends_shape if more else []
+        sent = [weekly, blocks_y] + sends_shape
         dual, annual, *rest = run(
-            functools.partial(dual_body, refineries, more),
+            functools.partial(dual_body, refineries),
             "dual_step",
             [me, swing_rows, swing_src],
             [
@@ -463,13 +555,11 @@
                 pltpu.VMEM((rows, size, scenarios), F32),
                 swing_scratch,
             ]
-            + ([stream_scratch] if more else []),
+            + [stream_scratch],
             2 * swings * unit,
         )
-        if more:
-            annual_send, dual_q, own, *rest = rest
+        annual_send, dual_q, own, *rest = rest
         primal = updated
-    return primal, dual, annual
 
 
 def solution(mesh):

time: 81.4 us -> 80.1 us (0.984)
  waiting for transfers between devices: 8 us -> 6.86 us
    ppermute x4, waiting for transfers between devices: 6.93 us -> 3.55 us  [shifted(): return lax.ppermute(block, axis, route)]
    ppermute x12, waiting for transfers between devices: 1.06 us -> 3.3 us  [exchanged(): return lax.ppermute(block, axis, [(i, i ^ d) for i in range(number)])]
    pallas_call x9 -> x8, Pallas kernels: 31.1 us -> 29 us  [run(): pl.pallas_call(kernel, name=name, in_specs=[SMEM] * ns + [HBM] * na, out_...]
    pallas_call x0 -> x1, Pallas kernels: none -> 1.88 us  [finish(): pl.pallas_call(finish_kernel, name='finish', in_specs=[HBM] * 6, out_spec...]
  transfers between devices with their start and end apart: 20 -> 20, of which waited for: 3 -> 4; matrix products, arithmetic and copies ran while one was open for 0% -> 0% of each run, Pallas kernels for 18% -> 20%
where the time goes in v7:
time: 80.1 us; the launch traced here: 79.3 us
  starting transfers between devices  40.1 us (50%)
  Pallas kernels  30.9 us (39%)
  waiting for transfers between devices  6.86 us (9%)
  between operations  1.48 us (2%)
    pallas_call x8, Pallas kernels, run(): pl.pallas_call(kernel, name=name, in_specs=[SMEM] * ns + [HBM] * na, out_...  29 us
    ppermute x4, starting transfers between devices, shifted(): return lax.ppermute(block, axis, route)  12.9 us
    all_to_all x2, starting transfers between devices, body(): annual_q = lax.all_to_all(annual_send, 'period', 0, 0, tiled=True)  11.4 us
    all_to_all x2, starting transfers between devices, body(): parts = lax.all_to_all(image, 'period', 0, 0, tiled=True)  8.12 us
    ppermute x12, starting transfers between devices, exchanged(): return lax.ppermute(block, axis, [(i, i ^ d) for i in range(number)])  7.63 us
    ppermute x4, waiting for transfers between devices, shifted(): return lax.ppermute(block, axis, route)  3.55 us
    ppermute x12, waiting for transfers between devices, exchanged(): return lax.ppermute(block, axis, [(i, i ^ d) for i in range(number)])  3.3 us
    pallas_call x1, Pallas kernels, finish(): pl.pallas_call(finish_kernel, name='finish', in_specs=[HBM] * 6, out_spec...  1.88 us
  transfers between devices with their start and end apart: 20, of which 4 were waited for; matrix products, arithmetic and copies ran while one was open for 0% of the time, Pallas kernels for 20%

profile of v7, /device:TPU:0, one launch (start us, length us, event | category | flops | bytes accessed | tf_op | source)
XLA Modules:
  0.0 79.3 jit_solution(12099170505379417380)
XLA Ops:
  0.6 2.9 %first_duals.1 = (bf16[8,128,128]{2,1,0:T(8,128)(2,1)}, f32[2,128,128]{2,1,0:T(8,128)}, bf16[2,128,128]{2,1,0:T(8,128)(2,1)}, bf16[2,128,128]{2,1,0:T(8,128)(2,1...) custom-call(s32[1]{0:T(128)} %bitcast.1.refs_0_, s32[8]{0:T(128)} %refs_1_.11, s32[8]{0:T(128)} %refs_2_.8, ...), custom_call_target="tpu_custom_call" | custom-call | flops 37748736 | bytes 1507328 | tf_op jit(solution)/shard_map/first_duals/pallas_call | solution.py:106
  3.6 7.3 %all-to-all-start = ((bf16[8,128,128]{2,1,0:T(8,128)(2,1)}), bf16[8,128,128]{2,1,0:T(8,128)(2,1)}, u32[]{:S(2)}, u32[]{:S(2)}) async-start(bf16[8,128,128]{2,1,0:T(8,128)(2,1)} %get-tuple-element.32), calls=%async_computation | async-start | bytes 524288 | tf_op jit(solution)/shard_map/all_to_all | solution.py:476
  10.9 4.7 %collective-permute-start = (bf16[128,128]{1,0:T(8,128)(2,1)}, bf16[128,128]{1,0:T(8,128)(2,1)}, u32[]{:S(2)}, u32[]{:S(2)}) collective-permute-start(bf16[128,128]{1,0:T(8,128)(2,1)} %get-tuple-element.34), channel_id=1, source_target_pairs={{4,0},{8,4},{12,8},{16,12},{20,16},{24,20},{28,24},{0,28},{5,1},{9... | collective-permute-start | bytes 98312 | tf_op jit(solution)/shard_map/ppermute | solution.py:403
  15.6 0.0 collective-permute-start.1
  15.6 1.5 %collective-permute-start.2 = (bf16[2,128,128]{2,1,0:T(8,128)(2,1)}, bf16[2,128,128]{2,1,0:T(8,128)(2,1)}, u32[]{:S(2)}, u32[]{:S(2)}) collective-permute-start(bf16[2,128,128]{2,1,0:T(8,128)(2,1)} %get-tuple-element.36), channel_id=1, source_target_pairs={{0,2},{1,3},{2,0},{3,1},{4,6},{5,7},{6,4},{7,5},{8,10},{9,11},{10,... | collective-permute-start | bytes 196616 | tf_op jit(solution)/shard_map/ppermute | solution.py:409
  17.1 0.4 collective-permute-start.3
  18.1 4.6 %dense.1 = (bf16[1024,1024]{1,0:T(8,128)(2,1)}, f32[1024,128]{1,0:T(8,128)}) custom-call(s32[96]{0:T(128)} %refs_0_.3, s32[96]{0:T(128)} %refs_1_.7, s32[1]{0:T(128)S(6)} %copy.23.refs_2_, f32[1024,128]{1,0:T(8,128)} %refs_2_.6, bf16[96,128,128]{2,1,0:T(8,128)(2,1)} %refs_4_.3, f32[1024,128]{1,0:T(8,128)} %refs_11_.2, f32[1024,128]{1,0:T(8,128)} %refs_3_.10), custom_call_target="tpu_custom_call" | custom-call | flops 4294967296 | bytes 7340036 | tf_op jit(solution)/shard_map/dense/pallas_call | solution.py:106
  22.7 0.0 collective-permute-done.refs_6_
  22.7 3.4 %primal_step.2 = (bf16[8,128,128]{2,1,0:T(8,128)(2,1)}, bf16[128,128]{1,0:T(8,128)(2,1)}, bf16[8,128,128]{2,1,0:T(8,128)(2,1)}, f32[1024,128]{1,0:T(8,128)}, bf16[2,128,128]{2,1,0:T(8,128)(2,1)}) custom-call(s32[8]{0:T(128)} %refs_0_.5, s32[8]{0:T(128)} %refs_1_.10, f32[8,128]{1,0:T(8,128)} %bitcast.4, bf16[8,128,128]{2,1,0:T(8,128)(2,1)} %refs_3_.11, ...), custom_call_target="tpu_custom_call" | custom-call | flops 67108864 | bytes 3084288 | tf_op jit(solution)/shard_map/primal_step/pallas_call | solution.py:106
  26.2 4.1 %all-to-all-start.1 = ((bf16[8,128,128]{2,1,0:T(8,128)(2,1)}), bf16[8,128,128]{2,1,0:T(8,128)(2,1)}, u32[]{:S(2)}, u32[]{:S(2)}) async-start(bf16[8,128,128]{2,1,0:T(8,128)(2,1)} %get-tuple-element.41), calls=%async_computation.1 | async-start | bytes 524288 | tf_op jit(solution)/shard_map/all_to_all | solution.py:515
  30.2 1.4 %collective-permute-start.6 = (bf16[2,128,128]{2,1,0:T(8,128)(2,1)}, bf16[2,128,128]{2,1,0:T(8,128)(2,1)}, u32[]{:S(2)}, u32[]{:S(2)}) collective-permute-start(bf16[2,128,128]{2,1,0:T(8,128)(2,1)} %get-tuple-element.39.refs_4_), channel_id=1, source_target_pairs={{0,3},{1,2},{2,1},{3,0},{4,7},{5,6},{6,5},{7,4},{8,11},{9,10},{10,... | collective-permute-start | bytes 196616 | tf_op jit(solution)/shard_map/ppermute | solution.py:409
  31.7 0.5 collective-permute-start.5
  32.2 1.8 %collective-permute-start.7 = (bf16[128,128]{1,0:T(8,128)(2,1)}, bf16[128,128]{1,0:T(8,128)(2,1)}, u32[]{:S(2)}, u32[]{:S(2)}) collective-permute-start(bf16[128,128]{1,0:T(8,128)(2,1)} %get-tuple-element.40), channel_id=1, source_target_pairs={{28,0},{0,4},{4,8},{8,12},{12,16},{16,20},{20,24},{24,28},{29,1},{... | collective-permute-start | bytes 98312 | tf_op jit(solution)/shard_map/ppermute | solution.py:403
  34.0 3.4 %forward.1.refs_13_ = f32[1024,128]{1,0:T(8,128)} custom-call(bf16[8,128,128]{2,1,0:T(8,128)(2,1)} %get-tuple-element.42.refs_0_, f32[8,128]{1,0:T(8,128)} %bitcast.6, f32[1024,128]{1,0:T(8,128)} %refs_2_.6, bf16[1024,1024]{1,0:T(8,128)(2,1)} %get-tuple-element.43.refs_3_.refs_1_.refs_6_), custom_call_target="tpu_custom_call" | custom-call | flops 4294967296 | bytes 3411968 | tf_op jit(solution)/shard_map/forward/pallas_call | solution.py:106
  37.4 3.5 %collective-permute-done.7.refs_9_ = bf16[128,128]{1,0:T(8,128)(2,1)} collective-permute-done((bf16[128,128]{1,0:T(8,128)(2,1)}, bf16[128,128]{1,0:T(8,128)(2,1)}, u32[]{:S(2)}, u32[]{:S(2)}) %collective-permute-start.7) | collective-permute-done | bytes 32800 | tf_op jit(solution)/shard_map/ppermute | solution.py:403
  41.0 3.6 %dual_step.1 = (f32[1024,128]{1,0:T(8,128)}, f32[128,128]{1,0:T(8,128)}, bf16[8,128,128]{2,1,0:T(8,128)(2,1)}, bf16[8,128,128]{2,1,0:T(8,128)(2,1)}, f32[2,128,1...) custom-call(s32[1]{0:T(128)} %bitcast.1.refs_0_, ...), custom_call_target="tpu_custom_call" | custom-call | flops 67108864 | bytes 2916864 | tf_op jit(solution)/shard_map/dual_step/pallas_call | solution.py:106
  44.5 4.1 %all-to-all-start.2 = ((bf16[8,128,128]{2,1,0:T(8,128)(2,1)}), bf16[8,128,128]{2,1,0:T(8,128)(2,1)}, u32[]{:S(2)}, u32[]{:S(2)}) async-start(bf16[8,128,128]{2,1,0:T(8,128)(2,1)} %get-tuple-element.44), calls=%async_computation.2 | async-start | bytes 524288 | tf_op jit(solution)/shard_map/all_to_all | solution.py:476
  48.6 4.6 %collective-permute-start.8 = (bf16[128,128]{1,0:T(8,128)(2,1)}, bf16[128,128]{1,0:T(8,128)(2,1)}, u32[]{:S(2)}, u32[]{:S(2)}) collective-permute-start(bf16[128,128]{1,0:T(8,128)(2,1)} %get-tuple-element.46), channel_id=1, source_target_pairs={{4,0},{8,4},{12,8},{16,12},{20,16},{24,20},{28,24},{0,28},{5,1},{9... | collective-permute-start | bytes 98312 | tf_op jit(solution)/shard_map/ppermute | solution.py:403
  53.2 1.5 %collective-permute-start.10 = (bf16[2,128,128]{2,1,0:T(8,128)(2,1)}, bf16[2,128,128]{2,1,0:T(8,128)(2,1)}, u32[]{:S(2)}, u32[]{:S(2)}) collective-permute-start(bf16[2,128,128]{2,1,0:T(8,128)(2,1)} %get-tuple-element.48), channel_id=1, source_target_pairs={{0,2},{1,3},{2,0},{3,1},{4,6},{5,7},{6,4},{7,5},{8,10},{9,11},{10,... | collective-permute-start | bytes 196616 | tf_op jit(solution)/shard_map/ppermute | solution.py:409
  54.7 0.4 collective-permute-start.11
  55.1 3.2 %adjoint.1.refs_10_ = f32[1024,128]{1,0:T(8,128)} custom-call(bf16[8,128,128]{2,1,0:T(8,128)(2,1)} %get-tuple-element.50.refs_0_, bf16[1024,1024]{1,0:T(8,128)(2,1)} %get-tuple-element.43.refs_3_.refs_1_.refs_6_, f32[1024,128]{1,0:T(8,128)} %get-tuple-element.51.refs_2_.refs_11_, f32[1024,128]{1,0:T(8,128)} %refs_3_.10), custom_call_target="tpu_custom_call" | custom-call | flops 4294967296 | bytes 3932160 | tf_op jit(solution)/shard_map/adjoint/pallas_call | solution.py:106
  58.3 0.9 %collective-permute-done.11.refs_9_ = bf16[2,128,128]{2,1,0:T(8,128)(2,1)} collective-permute-done((bf16[2,128,128]{2,1,0:T(8,128)(2,1)}, bf16[2,128,128]{2,1,0:T(8,128)(2,1)}, u32[]{:S(2)}, u32[]{:S(2)}) %collective-permute-start.11) | collective-permute-done | bytes 65568 | tf_op jit(solution)/shard_map/ppermute | solution.py:409
  59.2 3.4 %primal_step.3 = (bf16[8,128,128]{2,1,0:T(8,128)(2,1)}, bf16[128,128]{1,0:T(8,128)(2,1)}, bf16[8,128,128]{2,1,0:T(8,128)(2,1)}, f32[1024,128]{1,0:T(8,128)}, bf16[2,128,128]{2,1,0:T(8,128)(2,1)}) custom-call(s32[8]{0:T(128)} %refs_0_.5, s32[8]{0:T(128)} %refs_1_.10, f32[8,128]{1,0:T(8,128)} %bitcast.5, bf16[8,128,128]{2,1,0:T(8,128)(2,1)} %refs_3_.11, ...), custom_call_target="tpu_custom_call" | custom-call | flops 67108864 | bytes 3084288 | tf_op jit(solution)/shard_map/primal_step/pallas_call | solution.py:106
  62.6 4.1 %all-to-all-start.3 = ((bf16[8,128,128]{2,1,0:T(8,128)(2,1)}), bf16[8,128,128]{2,1,0:T(8,128)(2,1)}, u32[]{:S(2)}, u32[]{:S(2)}) async-start(bf16[8,128,128]{2,1,0:T(8,128)(2,1)} %get-tuple-element.57), calls=%async_computation.3 | async-start | bytes 524288 | tf_op jit(solution)/shard_map/all_to_all | solution.py:515
  66.6 1.3 %collective-permute-start.14 = (bf16[2,128,128]{2,1,0:T(8,128)(2,1)}, bf16[2,128,128]{2,1,0:T(8,128)(2,1)}, u32[]{:S(2)}, u32[]{:S(2)}) collective-permute-start(bf16[2,128,128]{2,1,0:T(8,128)(2,1)} %get-tuple-element.55.refs_8_), channel_id=1, source_target_pairs={{0,3},{1,2},{2,1},{3,0},{4,7},{5,6},{6,5},{7,4},{8,11},{9,10},{10,... | collective-permute-start | bytes 196616 | tf_op jit(solution)/shard_map/ppermute | solution.py:409
  67.9 0.6 collective-permute-start.13
  68.5 0.1 collective-permute-start.12
  68.6 1.8 %collective-permute-start.15 = (bf16[128,128]{1,0:T(8,128)(2,1)}, bf16[128,128]{1,0:T(8,128)(2,1)}, u32[]{:S(2)}, u32[]{:S(2)}) collective-permute-start(bf16[128,128]{1,0:T(8,128)(2,1)} %get-tuple-element.58), channel_id=1, source_target_pairs={{28,0},{0,4},{4,8},{8,12},{12,16},{16,20},{20,24},{24,28},{29,1},{... | collective-permute-start | bytes 98312 | tf_op jit(solution)/shard_map/ppermute | solution.py:403
  70.4 0.7 collective-permute-done.14.refs_11_
  71.1 1.7 %collective-permute-done.13.refs_10_ = bf16[2,128,128]{2,1,0:T(8,128)(2,1)} collective-permute-done((bf16[2,128,128]{2,1,0:T(8,128)(2,1)}, bf16[2,128,128]{2,1,0:T(8,128)(2,1)}, u32[]{:S(2)}, u32[]{:S(2)}) %collective-permute-start.13) | collective-permute-done | bytes 65568 | tf_op jit(solution)/shard_map/ppermute | solution.py:409
  72.8 4.5 %last_rows.1.row = f32[1024,128]{1,0:T(8,128)} custom-call(s32[1]{0:T(128)} %bitcast.1.refs_0_, s32[8]{0:T(128)} %refs_1_.11, s32[8]{0:T(128)} %refs_2_.8, f32[8,128]{1,0:T(8,128)} %bitcast.7, f32[1024,128]{1,0:T(8,128)} %get-tuple-element.53.refs_4_, bf16[8,128,128]{2,1,0:T(8,128)(2,1)} %get-tuple-element.54.refs_5_, ...), custom_call_target="tpu_custom_call" | custom-call | flops 4194304 | bytes 3936256 | tf_op jit(solution)/shard_map/last_rows/pallas_call | solution.py:106
  77.4 1.9 %finish.1 = (f32[1024,128]{1,0:T(8,128)}, f32[128,128]{1,0:T(8,128)}) custom-call(f32[1024,128]{1,0:T(8,128)} %last_rows.1.row, f32[128,128]{1,0:T(8,128)} %get-tuple-element.56.annual, f32[1,128]{1,0:T(1,128)} %bitcast.9, bf16[8,128,128]{2,1,0:T(8,128)(2,1)} %all-to-all-done.3.parts, bf16[1,128,128]{2,1,0:T(8,128)(2,1)} %carry.1, ...), custom_call_target="tpu_custom_call", output_to_operand_aliasing={{0}: (0, {})} | custom-call | flops 4194304 | bytes 1000000 | tf_op jit(solution)/shard_map/finish/pallas_call | solution.py:384
  (17 shorter events, 0.0 us)
Async XLA Ops:
  3.6 19.1 %all-to-all-start = ((bf16[8,128,128]{2,1,0:T(8,128)(2,1)}), bf16[8,128,128]{2,1,0:T(8,128)(2,1)}, u32[]{:S(2)}, u32[]{:S(2)}) async-start(bf16[8,128,128]{2,1,0:T(8,128)(2,1)} %get-tuple-element.32), calls=%async_computation | async-start | bytes 524288 | tf_op jit(solution)/shard_map/all_to_all | solution.py:476
  10.9 11.8 %collective-permute-start = (bf16[128,128]{1,0:T(8,128)(2,1)}, bf16[128,128]{1,0:T(8,128)(2,1)}, u32[]{:S(2)}, u32[]{:S(2)}) collective-permute-start(bf16[128,128]{1,0:T(8,128)(2,1)} %get-tuple-element.34), channel_id=1, source_target_pairs={{4,0},{8,4},{12,8},{16,12},{20,16},{24,20},{28,24},{0,28},{5,1},{9... | collective-permute-start | bytes 98312 | tf_op jit(solution)/shard_map/ppermute | solution.py:403
  15.6 7.1 %collective-permute-start.1 = (bf16[2,128,128]{2,1,0:T(8,128)(2,1)}, bf16[2,128,128]{2,1,0:T(8,128)(2,1)}, u32[]{:S(2)}, u32[]{:S(2)}) collective-permute-start(bf16[2,128,128]{2,1,0:T(8,128)(2,1)} %get-tuple-element.35), channel_id=1, source_target_pairs={{0,1},{1,0},{2,3},{3,2},{4,5},{5,4},{6,7},{7,6},{8,9},{9,8},{10,11... | collective-permute-start | bytes 196616 | tf_op jit(solution)/shard_map/ppermute | solution.py:409
  15.6 7.1 %collective-permute-start.2 = (bf16[2,128,128]{2,1,0:T(8,128)(2,1)}, bf16[2,128,128]{2,1,0:T(8,128)(2,1)}, u32[]{:S(2)}, u32[]{:S(2)}) collective-permute-start(bf16[2,128,128]{2,1,0:T(8,128)(2,1)} %get-tuple-element.36), channel_id=1, source_target_pairs={{0,2},{1,3},{2,0},{3,1},{4,6},{5,7},{6,4},{7,5},{8,10},{9,11},{10,... | collective-permute-start | bytes 196616 | tf_op jit(solution)/shard_map/ppermute | solution.py:409
  17.1 5.6 %collective-permute-start.3 = (bf16[2,128,128]{2,1,0:T(8,128)(2,1)}, bf16[2,128,128]{2,1,0:T(8,128)(2,1)}, u32[]{:S(2)}, u32[]{:S(2)}) collective-permute-start(bf16[2,128,128]{2,1,0:T(8,128)(2,1)} %get-tuple-element.37), channel_id=1, source_target_pairs={{0,3},{1,2},{2,1},{3,0},{4,7},{5,6},{6,5},{7,4},{8,11},{9,10},{10,... | collective-permute-start | bytes 196616 | tf_op jit(solution)/shard_map/ppermute | solution.py:409
  26.2 14.8 %all-to-all-start.1 = ((bf16[8,128,128]{2,1,0:T(8,128)(2,1)}), bf16[8,128,128]{2,1,0:T(8,128)(2,1)}, u32[]{:S(2)}, u32[]{:S(2)}) async-start(bf16[8,128,128]{2,1,0:T(8,128)(2,1)} %get-tuple-element.41), calls=%async_computation.1 | async-start | bytes 524288 | tf_op jit(solution)/shard_map/all_to_all | solution.py:515
  30.2 10.7 %collective-permute-start.6 = (bf16[2,128,128]{2,1,0:T(8,128)(2,1)}, bf16[2,128,128]{2,1,0:T(8,128)(2,1)}, u32[]{:S(2)}, u32[]{:S(2)}) collective-permute-start(bf16[2,128,128]{2,1,0:T(8,128)(2,1)} %get-tuple-element.39.refs_4_), channel_id=1, source_target_pairs={{0,3},{1,2},{2,1},{3,0},{4,7},{5,6},{6,5},{7,4},{8,11},{9,10},{10,... | collective-permute-start | bytes 196616 | tf_op jit(solution)/shard_map/ppermute | solution.py:409
  31.7 9.3 %collective-permute-start.5 = (bf16[2,128,128]{2,1,0:T(8,128)(2,1)}, bf16[2,128,128]{2,1,0:T(8,128)(2,1)}, u32[]{:S(2)}, u32[]{:S(2)}) collective-permute-start(bf16[2,128,128]{2,1,0:T(8,128)(2,1)} %get-tuple-element.39.refs_4_), channel_id=1, source_target_pairs={{0,2},{1,3},{2,0},{3,1},{4,6},{5,7},{6,4},{7,5},{8,10},{9,11},{10,... | collective-permute-start | bytes 196616 | tf_op jit(solution)/shard_map/ppermute | solution.py:409
  32.2 8.7 %collective-permute-start.4 = (bf16[2,128,128]{2,1,0:T(8,128)(2,1)}, bf16[2,128,128]{2,1,0:T(8,128)(2,1)}, u32[]{:S(2)}, u32[]{:S(2)}) collective-permute-start(bf16[2,128,128]{2,1,0:T(8,128)(2,1)} %get-tuple-element.39.refs_4_), channel_id=1, source_target_pairs={{0,1},{1,0},{2,3},{3,2},{4,5},{5,4},{6,7},{7,6},{8,9},{9,8},{10,11... | collective-permute-start | bytes 196616 | tf_op jit(solution)/shard_map/ppermute | solution.py:409
  32.2 8.7 %collective-permute-start.7 = (bf16[128,128]{1,0:T(8,128)(2,1)}, bf16[128,128]{1,0:T(8,128)(2,1)}, u32[]{:S(2)}, u32[]{:S(2)}) collective-permute-start(bf16[128,128]{1,0:T(8,128)(2,1)} %get-tuple-element.40), channel_id=1, source_target_pairs={{28,0},{0,4},{4,8},{8,12},{12,16},{16,20},{20,24},{24,28},{29,1},{... | collective-permute-start | bytes 98312 | tf_op jit(solution)/shard_map/ppermute | solution.py:403
  44.5 14.6 %all-to-all-start.2 = ((bf16[8,128,128]{2,1,0:T(8,128)(2,1)}), bf16[8,128,128]{2,1,0:T(8,128)(2,1)}, u32[]{:S(2)}, u32[]{:S(2)}) async-start(bf16[8,128,128]{2,1,0:T(8,128)(2,1)} %get-tuple-element.44), calls=%async_computation.2 | async-start | bytes 524288 | tf_op jit(solution)/shard_map/all_to_all | solution.py:476
  48.6 9.7 %collective-permute-start.8 = (bf16[128,128]{1,0:T(8,128)(2,1)}, bf16[128,128]{1,0:T(8,128)(2,1)}, u32[]{:S(2)}, u32[]{:S(2)}) collective-permute-start(bf16[128,128]{1,0:T(8,128)(2,1)} %get-tuple-element.46), channel_id=1, source_target_pairs={{4,0},{8,4},{12,8},{16,12},{20,16},{24,20},{28,24},{0,28},{5,1},{9... | collective-permute-start | bytes 98312 | tf_op jit(solution)/shard_map/ppermute | solution.py:403
  53.2 5.1 %collective-permute-start.9 = (bf16[2,128,128]{2,1,0:T(8,128)(2,1)}, bf16[2,128,128]{2,1,0:T(8,128)(2,1)}, u32[]{:S(2)}, u32[]{:S(2)}) collective-permute-start(bf16[2,128,128]{2,1,0:T(8,128)(2,1)} %get-tuple-element.47), channel_id=1, source_target_pairs={{0,1},{1,0},{2,3},{3,2},{4,5},{5,4},{6,7},{7,6},{8,9},{9,8},{10,11... | collective-permute-start | bytes 196616 | tf_op jit(solution)/shard_map/ppermute | solution.py:409
  53.2 5.1 %collective-permute-start.10 = (bf16[2,128,128]{2,1,0:T(8,128)(2,1)}, bf16[2,128,128]{2,1,0:T(8,128)(2,1)}, u32[]{:S(2)}, u32[]{:S(2)}) collective-permute-start(bf16[2,128,128]{2,1,0:T(8,128)(2,1)} %get-tuple-element.48), channel_id=1, source_target_pairs={{0,2},{1,3},{2,0},{3,1},{4,6},{5,7},{6,4},{7,5},{8,10},{9,11},{10,... | collective-permute-start | bytes 196616 | tf_op jit(solution)/shard_map/ppermute | solution.py:409
  54.7 4.4 %collective-permute-start.11 = (bf16[2,128,128]{2,1,0:T(8,128)(2,1)}, bf16[2,128,128]{2,1,0:T(8,128)(2,1)}, u32[]{:S(2)}, u32[]{:S(2)}) collective-permute-start(bf16[2,128,128]{2,1,0:T(8,128)(2,1)} %get-tuple-element.49), channel_id=1, source_target_pairs={{0,3},{1,2},{2,1},{3,0},{4,7},{5,6},{6,5},{7,4},{8,11},{9,10},{10,... | collective-permute-start | bytes 196616 | tf_op jit(solution)/shard_map/ppermute | solution.py:409
  62.6 14.8 %all-to-all-start.3 = ((bf16[8,128,128]{2,1,0:T(8,128)(2,1)}), bf16[8,128,128]{2,1,0:T(8,128)(2,1)}, u32[]{:S(2)}, u32[]{:S(2)}) async-start(bf16[8,128,128]{2,1,0:T(8,128)(2,1)} %get-tuple-element.57), calls=%async_computation.3 | async-start | bytes 524288 | tf_op jit(solution)/shard_map/all_to_all | solution.py:515
  66.6 4.5 %collective-permute-start.14 = (bf16[2,128,128]{2,1,0:T(8,128)(2,1)}, bf16[2,128,128]{2,1,0:T(8,128)(2,1)}, u32[]{:S(2)}, u32[]{:S(2)}) collective-permute-start(bf16[2,128,128]{2,1,0:T(8,128)(2,1)} %get-tuple-element.55.refs_8_), channel_id=1, source_target_pairs={{0,3},{1,2},{2,1},{3,0},{4,7},{5,6},{6,5},{7,4},{8,11},{9,10},{10,... | collective-permute-start | bytes 196616 | tf_op jit(solution)/shard_map/ppermute | solution.py:409
  67.9 4.9 %collective-permute-start.13 = (bf16[2,128,128]{2,1,0:T(8,128)(2,1)}, bf16[2,128,128]{2,1,0:T(8,128)(2,1)}, u32[]{:S(2)}, u32[]{:S(2)}) collective-permute-start(bf16[2,128,128]{2,1,0:T(8,128)(2,1)} %get-tuple-element.55.refs_8_), channel_id=1, source_target_pairs={{0,2},{1,3},{2,0},{3,1},{4,6},{5,7},{6,4},{7,5},{8,10},{9,11},{10,... | collective-permute-start | bytes 196616 | tf_op jit(solution)/shard_map/ppermute | solution.py:409
  68.5 4.3 %collective-permute-start.12 = (bf16[2,128,128]{2,1,0:T(8,128)(2,1)}, bf16[2,128,128]{2,1,0:T(8,128)(2,1)}, u32[]{:S(2)}, u32[]{:S(2)}) collective-permute-start(bf16[2,128,128]{2,1,0:T(8,128)(2,1)} %get-tuple-element.55.refs_8_), channel_id=1, source_target_pairs={{0,1},{1,0},{2,3},{3,2},{4,5},{5,4},{6,7},{7,6},{8,9},{9,8},{10,11... | collective-permute-start | bytes 196616 | tf_op jit(solution)/shard_map/ppermute | solution.py:409
  68.6 8.8 %collective-permute-start.15 = (bf16[128,128]{1,0:T(8,128)(2,1)}, bf16[128,128]{1,0:T(8,128)(2,1)}, u32[]{:S(2)}, u32[]{:S(2)}) collective-permute-start(bf16[128,128]{1,0:T(8,128)(2,1)} %get-tuple-element.58), channel_id=1, source_target_pairs={{28,0},{0,4},{4,8},{8,12},{12,16},{16,20},{20,24},{24,28},{29,1},{... | collective-permute-start | bytes 98312 | tf_op jit(solution)/shard_map/ppermute | solution.py:403

commit v8 on v7

--- a/solution.py
+++ b/solution.py
@@ -159,8 +159,8 @@
 
 
 def first_duals_body(refineries, scalars, ins, outs, acc, product, dual_q):
-    me, rows, src = scalars
-    annual, dual, carry, swing = ins
+    (me,) = scalars
+    rows, src, annual, dual, carry, swing = ins
     weekly = outs[0]
     rounded = annual()[...].astype(BF16)
     for w in range(weekly.ref.shape[0]):
@@ -171,7 +171,7 @@
     for i in range(dual_q.shape[0]):
         dual_q[i] = dual[i * size : (i + 1) * size].astype(BF16)
     send_duals(
-        refineries, dual_q, me[0], rows, src, swing(), carry(), outs[1:], acc, product
+        refineries, dual_q, me[0], rows(), src(), swing(), carry(), outs[1:], acc, product
     )
 
 
@@ -184,8 +184,8 @@
 
 
 def dense_body(chunks, scalars, ins, outs, acc):
-    rows, cols = scalars
-    count, dual, blocks, primal, prices = ins
+    rows, cols, count, dual, blocks, primal, prices = ins
+    rows, cols = rows(), cols()
     matrix, out = outs
     size = blocks.target.shape[1]
     tiles = matrix.ref.shape[1] // size
@@ -220,13 +220,12 @@
 
 
 def primal_body(scalars, ins, outs, acc, image_acc, product, bound):
-    ids, cols = scalars
-    upper, annual, annual_q, own, carried, *arrived, partial, primal = ins
+    ids, cols, upper, annual, annual_q, own, carried, *arrived, partial, primal = ins
     image, last, extrap, updated, streams = outs
     blocks, size, _ = extrap.ref.shape
     acc[...] = jnp.zeros_like(acc)
     image_acc[...] = jnp.zeros_like(image_acc)
-    upper = upper()
+    ids, cols, upper = ids(), cols(), upper()
     for j in range(blocks):
         bound[j] = column_of(upper[j : j + 1], bound.shape[2])
     annual, annual_q = annual(), annual_q()
@@ -276,10 +275,10 @@
 
 
 def dual_body(refineries, scalars, ins, outs, gathered, acc, product, stream_acc):
-    me, rows, src = scalars
-    swing, streams, *arrived, carry, previous, parts, annual, need, partial = ins
+    (me,) = scalars
+    rows, src, swing, streams, *arrived, carry, previous, parts, annual, need, partial = ins
     dual, annual_out = outs[0], outs[1]
-    swing = swing()
+    rows, src, swing = rows(), src(), swing()
     size = swing.shape[1]
     mine = me[0]
     gathered[pl.ds(mine * SC, SC)] = streams()[...]
@@ -319,8 +318,9 @@
 
 
 def last_rows_body(refineries, scalars, ins, outs, gathered, acc, product):
-    me, rows, src = scalars
-    demand, dual, extrap, matrix, swing, streams, *arrived = ins
+    (me,) = scalars
+    rows, src, demand, dual, extrap, matrix, swing, streams, *arrived = ins
+    rows, src = rows(), src()
     out = outs[0]
     demand, dual, extrap = demand(), dual(), extrap()
     blocks, size, width = extrap.shape
@@ -464,8 +464,8 @@
     annual_send, own, *rest = run(
         functools.partial(first_duals_body, refineries),
         "first_duals",
-        [me, swing_rows, swing_src],
-        [annual, dual, carry_blocks, swing_blocks],
+        [me],
+        [swing_rows, swing_src, annual, dual, carry_blocks, swing_blocks],
         [weekly] + sends_shape,
         [stream_scratch, swing_scratch, pltpu.VMEM(blocks_y.shape, BF16)],
         (swings + 1) * unit,
@@ -480,12 +480,12 @@
             matrix_q, partial_x = run(
                 functools.partial(dense_body, chunks),
                 "dense",
-                [local_rows, local_cols],
-                [band_count, dual, local_blocks, primal, cost],
+                [],
+                [local_rows, local_cols, band_count, dual, local_blocks, primal, cost],
                 [matrix, state_x],
                 [pltpu.VMEM((rows * columns, size, size), F32)],
                 16 * rows * columns * unit,
-                {2: (chunks, 0)},
+                {4: (chunks, 0)},
                 {0: rows},
             )
         else:
@@ -501,8 +501,8 @@
         image, last, extrap, updated, streams = run(
             primal_body,
             "primal_step",
-            [annual_ids, annual_cols],
-            [upper_rows, annual_blocks, annual_q, own, carried_back, *arrived, partial_x, primal],
+            [],
+            [annual_ids, annual_cols, upper_rows, annual_blocks, annual_q, own, carried_back, *arrived, partial_x, primal],
             [weekly, tile, blocks_x, state_x, pair_q],
             [
                 pltpu.VMEM((columns, size, scenarios), F32),
@@ -519,8 +519,8 @@
             (dual,) = run(
                 functools.partial(last_rows_body, refineries),
                 "last_rows",
-                [me, swing_rows, swing_src],
-                [demand_rows, dual, extrap, matrix_q, swing_blocks, streams, *others_streams],
+                [me],
+                [swing_rows, swing_src, demand_rows, dual, extrap, matrix_q, swing_blocks, streams, *others_streams],
                 [state_y],
                 [
                     pltpu.VMEM((refineries * SC, size, scenarios), BF16),
@@ -544,9 +544,9 @@
         dual, annual, *rest = run(
             functools.partial(dual_body, refineries),
             "dual_step",
-            [me, swing_rows, swing_src],
+            [me],
             [
-                swing_blocks, streams, *others_streams, carry_blocks, previous, parts, annual,
+                swing_rows, swing_src, swing_blocks, streams, *others_streams, carry_blocks, previous, parts, annual,
                 need, partial_y,
             ],
             [state_y, shape((size, scenarios), F32)] + sent,

time: 80.1 us -> 76.5 us (0.955)
  Pallas kernels: 30.9 us -> 27 us
    pallas_call x8, Pallas kernels: 29 us -> 25.1 us  [run(): pl.pallas_call(kernel, name=name, in_specs=[SMEM] * ns + [HBM] * na, out_...]
  transfers between devices with their start and end apart: 20 -> 20, of which waited for: 4 -> 5; matrix products, arithmetic and copies ran while one was open for 0% -> 0% of each run, Pallas kernels for 20% -> 19%
where the time goes in v8:
time: 76.5 us; the launch traced here: 75.8 us
  starting transfers between devices  40.1 us (52%)
  Pallas kernels  27 us (35%)
  waiting for transfers between devices  7.33 us (10%)
  between operations  1.46 us (2%)
    pallas_call x8, Pallas kernels, run(): pl.pallas_call(kernel, name=name, in_specs=[SMEM] * ns + [HBM] * na, out_...  25.1 us
    ppermute x4, starting transfers between devices, shifted(): return lax.ppermute(block, axis, route)  12.9 us
    all_to_all x2, starting transfers between devices, body(): annual_q = lax.all_to_all(annual_send, 'period', 0, 0, tiled=True)  11.4 us
    all_to_all x2, starting transfers between devices, body(): parts = lax.all_to_all(image, 'period', 0, 0, tiled=True)  8.12 us
    ppermute x12, starting transfers between devices, exchanged(): return lax.ppermute(block, axis, [(i, i ^ d) for i in range(number)])  7.66 us
    ppermute x4, waiting for transfers between devices, shifted(): return lax.ppermute(block, axis, route)  4 us
    ppermute x12, waiting for transfers between devices, exchanged(): return lax.ppermute(block, axis, [(i, i ^ d) for i in range(number)])  3.31 us
    pallas_call x1, Pallas kernels, finish(): pl.pallas_call(finish_kernel, name='finish', in_specs=[HBM] * 6, out_spec...  1.88 us
  transfers between devices with their start and end apart: 20, of which 5 were waited for; matrix products, arithmetic and copies ran while one was open for 0% of the time, Pallas kernels for 19%

profile of v8, /device:TPU:0, one launch (start us, length us, event | category | flops | bytes accessed | tf_op | source)
XLA Modules:
  0.0 75.8 jit_solution(16018919210180610109)
XLA Ops:
  0.6 2.3 %first_duals.1 = (bf16[8,128,128]{2,1,0:T(8,128)(2,1)}, f32[2,128,128]{2,1,0:T(8,128)}, bf16[2,128,128]{2,1,0:T(8,128)(2,1)}, bf16[2,128,128]{2,1,0:T(8,128)(2,1...) custom-call(s32[1]{0:T(128)} %bitcast.1.refs_0_, s32[8]{0:T(128)} %refs_1_.11, s32[8]{0:T(128)} %refs_2_.8, ...), custom_call_target="tpu_custom_call" | custom-call | flops 37748736 | bytes 1507392 | tf_op jit(solution)/shard_map/first_duals/pallas_call | solution.py:106
  2.9 7.3 %all-to-all-start = ((bf16[8,128,128]{2,1,0:T(8,128)(2,1)}), bf16[8,128,128]{2,1,0:T(8,128)(2,1)}, u32[]{:S(2)}, u32[]{:S(2)}) async-start(bf16[8,128,128]{2,1,0:T(8,128)(2,1)} %get-tuple-element.32), calls=%async_computation | async-start | bytes 524288 | tf_op jit(solution)/shard_map/all_to_all | solution.py:476
  10.2 4.7 %collective-permute-start = (bf16[128,128]{1,0:T(8,128)(2,1)}, bf16[128,128]{1,0:T(8,128)(2,1)}, u32[]{:S(2)}, u32[]{:S(2)}) collective-permute-start(bf16[128,128]{1,0:T(8,128)(2,1)} %get-tuple-element.34), channel_id=1, source_target_pairs={{4,0},{8,4},{12,8},{16,12},{20,16},{24,20},{28,24},{0,28},{5,1},{9... | collective-permute-start | bytes 98312 | tf_op jit(solution)/shard_map/ppermute | solution.py:403
  14.9 0.0 collective-permute-start.1
  15.0 1.5 %collective-permute-start.2 = (bf16[2,128,128]{2,1,0:T(8,128)(2,1)}, bf16[2,128,128]{2,1,0:T(8,128)(2,1)}, u32[]{:S(2)}, u32[]{:S(2)}) collective-permute-start(bf16[2,128,128]{2,1,0:T(8,128)(2,1)} %get-tuple-element.36), channel_id=1, source_target_pairs={{0,2},{1,3},{2,0},{3,1},{4,6},{5,7},{6,4},{7,5},{8,10},{9,11},{10,... | collective-permute-start | bytes 196616 | tf_op jit(solution)/shard_map/ppermute | solution.py:409
  16.4 0.4 collective-permute-start.3
  17.5 3.9 %dense.1 = (bf16[1024,1024]{1,0:T(8,128)(2,1)}, f32[1024,128]{1,0:T(8,128)}) custom-call(s32[96]{0:T(128)} %refs_0_.3, s32[96]{0:T(128)} %refs_1_.7, s32[1]{0:T(128)S(6)} %copy.23.refs_2_, f32[1024,128]{1,0:T(8,128)} %refs_2_.6, bf16[96,128,128]{2,1,0:T(8,128)(2,1)} %refs_4_.3, f32[1024,128]{1,0:T(8,128)} %refs_11_.2, f32[1024,128]{1,0:T(8,128)} %refs_3_.10), custom_call_target="tpu_custom_call" | custom-call | flops 4294967296 | bytes 7340804 | tf_op jit(solution)/shard_map/dense/pallas_call | solution.py:106
  21.4 2.7 %primal_step.2 = (bf16[8,128,128]{2,1,0:T(8,128)(2,1)}, bf16[128,128]{1,0:T(8,128)(2,1)}, bf16[8,128,128]{2,1,0:T(8,128)(2,1)}, f32[1024,128]{1,0:T(8,128)}, bf16[2,128,128]{2,1,0:T(8,128)(2,1)}) custom-call(s32[8]{0:T(128)} %refs_0_.5, s32[8]{0:T(128)} %refs_1_.10, f32[8,128]{1,0:T(8,128)} %bitcast.4, bf16[8,128,128]{2,1,0:T(8,128)(2,1)} %refs_3_.11, ...), custom_call_target="tpu_custom_call" | custom-call | flops 67108864 | bytes 3084352 | tf_op jit(solution)/shard_map/primal_step/pallas_call | solution.py:106
  24.2 4.1 %all-to-all-start.1 = ((bf16[8,128,128]{2,1,0:T(8,128)(2,1)}), bf16[8,128,128]{2,1,0:T(8,128)(2,1)}, u32[]{:S(2)}, u32[]{:S(2)}) async-start(bf16[8,128,128]{2,1,0:T(8,128)(2,1)} %get-tuple-element.41), calls=%async_computation.1 | async-start | bytes 524288 | tf_op jit(solution)/shard_map/all_to_all | solution.py:515
  28.3 1.4 %collective-permute-start.6 = (bf16[2,128,128]{2,1,0:T(8,128)(2,1)}, bf16[2,128,128]{2,1,0:T(8,128)(2,1)}, u32[]{:S(2)}, u32[]{:S(2)}) collective-permute-start(bf16[2,128,128]{2,1,0:T(8,128)(2,1)} %get-tuple-element.39.refs_4_), channel_id=1, source_target_pairs={{0,3},{1,2},{2,1},{3,0},{4,7},{5,6},{6,5},{7,4},{8,11},{9,10},{10,... | collective-permute-start | bytes 196616 | tf_op jit(solution)/shard_map/ppermute | solution.py:409
  29.7 0.5 collective-permute-start.5
  30.3 1.8 %collective-permute-start.7 = (bf16[128,128]{1,0:T(8,128)(2,1)}, bf16[128,128]{1,0:T(8,128)(2,1)}, u32[]{:S(2)}, u32[]{:S(2)}) collective-permute-start(bf16[128,128]{1,0:T(8,128)(2,1)} %get-tuple-element.40), channel_id=1, source_target_pairs={{28,0},{0,4},{4,8},{8,12},{12,16},{16,20},{20,24},{24,28},{29,1},{... | collective-permute-start | bytes 98312 | tf_op jit(solution)/shard_map/ppermute | solution.py:403
  32.0 3.4 %forward.1.refs_13_ = f32[1024,128]{1,0:T(8,128)} custom-call(bf16[8,128,128]{2,1,0:T(8,128)(2,1)} %get-tuple-element.42.refs_0_, f32[8,128]{1,0:T(8,128)} %bitcast.6, f32[1024,128]{1,0:T(8,128)} %refs_2_.6, bf16[1024,1024]{1,0:T(8,128)(2,1)} %get-tuple-element.43.refs_3_.refs_1_.refs_6_), custom_call_target="tpu_custom_call" | custom-call | flops 4294967296 | bytes 3411968 | tf_op jit(solution)/shard_map/forward/pallas_call | solution.py:106
  35.4 3.5 %collective-permute-done.7.refs_9_ = bf16[128,128]{1,0:T(8,128)(2,1)} collective-permute-done((bf16[128,128]{1,0:T(8,128)(2,1)}, bf16[128,128]{1,0:T(8,128)(2,1)}, u32[]{:S(2)}, u32[]{:S(2)}) %collective-permute-start.7) | collective-permute-done | bytes 32800 | tf_op jit(solution)/shard_map/ppermute | solution.py:403
  39.0 2.9 %dual_step.1 = (f32[1024,128]{1,0:T(8,128)}, f32[128,128]{1,0:T(8,128)}, bf16[8,128,128]{2,1,0:T(8,128)(2,1)}, bf16[8,128,128]{2,1,0:T(8,128)(2,1)}, f32[2,128,1...) custom-call(s32[1]{0:T(128)} %bitcast.1.refs_0_, ...), custom_call_target="tpu_custom_call" | custom-call | flops 67108864 | bytes 2916928 | tf_op jit(solution)/shard_map/dual_step/pallas_call | solution.py:106
  41.9 4.1 %all-to-all-start.2 = ((bf16[8,128,128]{2,1,0:T(8,128)(2,1)}), bf16[8,128,128]{2,1,0:T(8,128)(2,1)}, u32[]{:S(2)}, u32[]{:S(2)}) async-start(bf16[8,128,128]{2,1,0:T(8,128)(2,1)} %get-tuple-element.44), calls=%async_computation.2 | async-start | bytes 524288 | tf_op jit(solution)/shard_map/all_to_all | solution.py:476
  46.0 4.6 %collective-permute-start.8 = (bf16[128,128]{1,0:T(8,128)(2,1)}, bf16[128,128]{1,0:T(8,128)(2,1)}, u32[]{:S(2)}, u32[]{:S(2)}) collective-permute-start(bf16[128,128]{1,0:T(8,128)(2,1)} %get-tuple-element.46), channel_id=1, source_target_pairs={{4,0},{8,4},{12,8},{16,12},{20,16},{24,20},{28,24},{0,28},{5,1},{9... | collective-permute-start | bytes 98312 | tf_op jit(solution)/shard_map/ppermute | solution.py:403
  50.6 1.5 %collective-permute-start.10 = (bf16[2,128,128]{2,1,0:T(8,128)(2,1)}, bf16[2,128,128]{2,1,0:T(8,128)(2,1)}, u32[]{:S(2)}, u32[]{:S(2)}) collective-permute-start(bf16[2,128,128]{2,1,0:T(8,128)(2,1)} %get-tuple-element.48), channel_id=1, source_target_pairs={{0,2},{1,3},{2,0},{3,1},{4,6},{5,7},{6,4},{7,5},{8,10},{9,11},{10,... | collective-permute-start | bytes 196616 | tf_op jit(solution)/shard_map/ppermute | solution.py:409
  52.1 0.4 collective-permute-start.11
  52.5 3.2 %adjoint.1.refs_10_ = f32[1024,128]{1,0:T(8,128)} custom-call(bf16[8,128,128]{2,1,0:T(8,128)(2,1)} %get-tuple-element.50.refs_0_, bf16[1024,1024]{1,0:T(8,128)(2,1)} %get-tuple-element.43.refs_3_.refs_1_.refs_6_, f32[1024,128]{1,0:T(8,128)} %get-tuple-element.51.refs_2_.refs_11_, f32[1024,128]{1,0:T(8,128)} %refs_3_.10), custom_call_target="tpu_custom_call" | custom-call | flops 4294967296 | bytes 3932160 | tf_op jit(solution)/shard_map/adjoint/pallas_call | solution.py:106
  55.7 0.9 %collective-permute-done.11.refs_9_ = bf16[2,128,128]{2,1,0:T(8,128)(2,1)} collective-permute-done((bf16[2,128,128]{2,1,0:T(8,128)(2,1)}, bf16[2,128,128]{2,1,0:T(8,128)(2,1)}, u32[]{:S(2)}, u32[]{:S(2)}) %collective-permute-start.11) | collective-permute-done | bytes 65568 | tf_op jit(solution)/shard_map/ppermute | solution.py:409
  56.6 2.7 %primal_step.3 = (bf16[8,128,128]{2,1,0:T(8,128)(2,1)}, bf16[128,128]{1,0:T(8,128)(2,1)}, bf16[8,128,128]{2,1,0:T(8,128)(2,1)}, f32[1024,128]{1,0:T(8,128)}, bf16[2,128,128]{2,1,0:T(8,128)(2,1)}) custom-call(s32[8]{0:T(128)} %refs_0_.5, s32[8]{0:T(128)} %refs_1_.10, f32[8,128]{1,0:T(8,128)} %bitcast.5, bf16[8,128,128]{2,1,0:T(8,128)(2,1)} %refs_3_.11, ...), custom_call_target="tpu_custom_call" | custom-call | flops 67108864 | bytes 3084352 | tf_op jit(solution)/shard_map/primal_step/pallas_call | solution.py:106
  59.3 4.1 %all-to-all-start.3 = ((bf16[8,128,128]{2,1,0:T(8,128)(2,1)}), bf16[8,128,128]{2,1,0:T(8,128)(2,1)}, u32[]{:S(2)}, u32[]{:S(2)}) async-start(bf16[8,128,128]{2,1,0:T(8,128)(2,1)} %get-tuple-element.57), calls=%async_computation.3 | async-start | bytes 524288 | tf_op jit(solution)/shard_map/all_to_all | solution.py:515
  63.4 1.3 %collective-permute-start.14 = (bf16[2,128,128]{2,1,0:T(8,128)(2,1)}, bf16[2,128,128]{2,1,0:T(8,128)(2,1)}, u32[]{:S(2)}, u32[]{:S(2)}) collective-permute-start(bf16[2,128,128]{2,1,0:T(8,128)(2,1)} %get-tuple-element.55.refs_8_), channel_id=1, source_target_pairs={{0,3},{1,2},{2,1},{3,0},{4,7},{5,6},{6,5},{7,4},{8,11},{9,10},{10,... | collective-permute-start | bytes 196616 | tf_op jit(solution)/shard_map/ppermute | solution.py:409
  64.6 0.5 collective-permute-start.13
  65.2 0.1 collective-permute-start.12
  65.3 1.8 %collective-permute-start.15 = (bf16[128,128]{1,0:T(8,128)(2,1)}, bf16[128,128]{1,0:T(8,128)(2,1)}, u32[]{:S(2)}, u32[]{:S(2)}) collective-permute-start(bf16[128,128]{1,0:T(8,128)(2,1)} %get-tuple-element.58), channel_id=1, source_target_pairs={{28,0},{0,4},{4,8},{8,12},{12,16},{16,20},{20,24},{24,28},{29,1},{... | collective-permute-start | bytes 98312 | tf_op jit(solution)/shard_map/ppermute | solution.py:403
  67.1 0.7 collective-permute-done.14.refs_11_
  67.9 1.7 %collective-permute-done.13.refs_10_ = bf16[2,128,128]{2,1,0:T(8,128)(2,1)} collective-permute-done((bf16[2,128,128]{2,1,0:T(8,128)(2,1)}, bf16[2,128,128]{2,1,0:T(8,128)(2,1)}, u32[]{:S(2)}, u32[]{:S(2)}) %collective-permute-start.13) | collective-permute-done | bytes 65568 | tf_op jit(solution)/shard_map/ppermute | solution.py:409
  69.6 3.9 %last_rows.1.row = f32[1024,128]{1,0:T(8,128)} custom-call(s32[1]{0:T(128)} %bitcast.1.refs_0_, s32[8]{0:T(128)} %refs_1_.11, s32[8]{0:T(128)} %refs_2_.8, f32[8,128]{1,0:T(8,128)} %bitcast.7, f32[1024,128]{1,0:T(8,128)} %get-tuple-element.53.refs_4_, bf16[8,128,128]{2,1,0:T(8,128)(2,1)} %get-tuple-element.54.refs_5_, ...), custom_call_target="tpu_custom_call" | custom-call | flops 4194304 | bytes 3936320 | tf_op jit(solution)/shard_map/last_rows/pallas_call | solution.py:106
  73.5 0.5 collective-permute-done.15.previous
  73.9 1.9 %finish.1 = (f32[1024,128]{1,0:T(8,128)}, f32[128,128]{1,0:T(8,128)}) custom-call(f32[1024,128]{1,0:T(8,128)} %last_rows.1.row, f32[128,128]{1,0:T(8,128)} %get-tuple-element.56.annual, f32[1,128]{1,0:T(1,128)} %bitcast.9, bf16[8,128,128]{2,1,0:T(8,128)(2,1)} %all-to-all-done.3.parts, bf16[1,128,128]{2,1,0:T(8,128)(2,1)} %carry.1, ...), custom_call_target="tpu_custom_call", output_to_operand_aliasing={{0}: (0, {})} | custom-call | flops 4194304 | bytes 1000000 | tf_op jit(solution)/shard_map/finish/pallas_call | solution.py:384
  (17 shorter events, 0.0 us)
Async XLA Ops:
  2.9 18.5 %all-to-all-start = ((bf16[8,128,128]{2,1,0:T(8,128)(2,1)}), bf16[8,128,128]{2,1,0:T(8,128)(2,1)}, u32[]{:S(2)}, u32[]{:S(2)}) async-start(bf16[8,128,128]{2,1,0:T(8,128)(2,1)} %get-tuple-element.32), calls=%async_computation | async-start | bytes 524288 | tf_op jit(solution)/shard_map/all_to_all | solution.py:476
  10.2 11.2 %collective-permute-start = (bf16[128,128]{1,0:T(8,128)(2,1)}, bf16[128,128]{1,0:T(8,128)(2,1)}, u32[]{:S(2)}, u32[]{:S(2)}) collective-permute-start(bf16[128,128]{1,0:T(8,128)(2,1)} %get-tuple-element.34), channel_id=1, source_target_pairs={{4,0},{8,4},{12,8},{16,12},{20,16},{24,20},{28,24},{0,28},{5,1},{9... | collective-permute-start | bytes 98312 | tf_op jit(solution)/shard_map/ppermute | solution.py:403
  14.9 6.5 %collective-permute-start.1 = (bf16[2,128,128]{2,1,0:T(8,128)(2,1)}, bf16[2,128,128]{2,1,0:T(8,128)(2,1)}, u32[]{:S(2)}, u32[]{:S(2)}) collective-permute-start(bf16[2,128,128]{2,1,0:T(8,128)(2,1)} %get-tuple-element.35), channel_id=1, source_target_pairs={{0,1},{1,0},{2,3},{3,2},{4,5},{5,4},{6,7},{7,6},{8,9},{9,8},{10,11... | collective-permute-start | bytes 196616 | tf_op jit(solution)/shard_map/ppermute | solution.py:409
  15.0 6.5 %collective-permute-start.2 = (bf16[2,128,128]{2,1,0:T(8,128)(2,1)}, bf16[2,128,128]{2,1,0:T(8,128)(2,1)}, u32[]{:S(2)}, u32[]{:S(2)}) collective-permute-start(bf16[2,128,128]{2,1,0:T(8,128)(2,1)} %get-tuple-element.36), channel_id=1, source_target_pairs={{0,2},{1,3},{2,0},{3,1},{4,6},{5,7},{6,4},{7,5},{8,10},{9,11},{10,... | collective-permute-start | bytes 196616 | tf_op jit(solution)/shard_map/ppermute | solution.py:409
  16.4 5.0 %collective-permute-start.3 = (bf16[2,128,128]{2,1,0:T(8,128)(2,1)}, bf16[2,128,128]{2,1,0:T(8,128)(2,1)}, u32[]{:S(2)}, u32[]{:S(2)}) collective-permute-start(bf16[2,128,128]{2,1,0:T(8,128)(2,1)} %get-tuple-element.37), channel_id=1, source_target_pairs={{0,3},{1,2},{2,1},{3,0},{4,7},{5,6},{6,5},{7,4},{8,11},{9,10},{10,... | collective-permute-start | bytes 196616 | tf_op jit(solution)/shard_map/ppermute | solution.py:409
  24.2 14.8 %all-to-all-start.1 = ((bf16[8,128,128]{2,1,0:T(8,128)(2,1)}), bf16[8,128,128]{2,1,0:T(8,128)(2,1)}, u32[]{:S(2)}, u32[]{:S(2)}) async-start(bf16[8,128,128]{2,1,0:T(8,128)(2,1)} %get-tuple-element.41), calls=%async_computation.1 | async-start | bytes 524288 | tf_op jit(solution)/shard_map/all_to_all | solution.py:515
  28.3 10.7 %collective-permute-start.6 = (bf16[2,128,128]{2,1,0:T(8,128)(2,1)}, bf16[2,128,128]{2,1,0:T(8,128)(2,1)}, u32[]{:S(2)}, u32[]{:S(2)}) collective-permute-start(bf16[2,128,128]{2,1,0:T(8,128)(2,1)} %get-tuple-element.39.refs_4_), channel_id=1, source_target_pairs={{0,3},{1,2},{2,1},{3,0},{4,7},{5,6},{6,5},{7,4},{8,11},{9,10},{10,... | collective-permute-start | bytes 196616 | tf_op jit(solution)/shard_map/ppermute | solution.py:409
  29.7 9.3 %collective-permute-start.5 = (bf16[2,128,128]{2,1,0:T(8,128)(2,1)}, bf16[2,128,128]{2,1,0:T(8,128)(2,1)}, u32[]{:S(2)}, u32[]{:S(2)}) collective-permute-start(bf16[2,128,128]{2,1,0:T(8,128)(2,1)} %get-tuple-element.39.refs_4_), channel_id=1, source_target_pairs={{0,2},{1,3},{2,0},{3,1},{4,6},{5,7},{6,4},{7,5},{8,10},{9,11},{10,... | collective-permute-start | bytes 196616 | tf_op jit(solution)/shard_map/ppermute | solution.py:409
  30.2 8.7 %collective-permute-start.4 = (bf16[2,128,128]{2,1,0:T(8,128)(2,1)}, bf16[2,128,128]{2,1,0:T(8,128)(2,1)}, u32[]{:S(2)}, u32[]{:S(2)}) collective-permute-start(bf16[2,128,128]{2,1,0:T(8,128)(2,1)} %get-tuple-element.39.refs_4_), channel_id=1, source_target_pairs={{0,1},{1,0},{2,3},{3,2},{4,5},{5,4},{6,7},{7,6},{8,9},{9,8},{10,11... | collective-permute-start | bytes 196616 | tf_op jit(solution)/shard_map/ppermute | solution.py:409
  30.3 8.7 %collective-permute-start.7 = (bf16[128,128]{1,0:T(8,128)(2,1)}, bf16[128,128]{1,0:T(8,128)(2,1)}, u32[]{:S(2)}, u32[]{:S(2)}) collective-permute-start(bf16[128,128]{1,0:T(8,128)(2,1)} %get-tuple-element.40), channel_id=1, source_target_pairs={{28,0},{0,4},{4,8},{8,12},{12,16},{16,20},{20,24},{24,28},{29,1},{... | collective-permute-start | bytes 98312 | tf_op jit(solution)/shard_map/ppermute | solution.py:403
  41.9 14.6 %all-to-all-start.2 = ((bf16[8,128,128]{2,1,0:T(8,128)(2,1)}), bf16[8,128,128]{2,1,0:T(8,128)(2,1)}, u32[]{:S(2)}, u32[]{:S(2)}) async-start(bf16[8,128,128]{2,1,0:T(8,128)(2,1)} %get-tuple-element.44), calls=%async_computation.2 | async-start | bytes 524288 | tf_op jit(solution)/shard_map/all_to_all | solution.py:476
  46.0 9.7 %collective-permute-start.8 = (bf16[128,128]{1,0:T(8,128)(2,1)}, bf16[128,128]{1,0:T(8,128)(2,1)}, u32[]{:S(2)}, u32[]{:S(2)}) collective-permute-start(bf16[128,128]{1,0:T(8,128)(2,1)} %get-tuple-element.46), channel_id=1, source_target_pairs={{4,0},{8,4},{12,8},{16,12},{20,16},{24,20},{28,24},{0,28},{5,1},{9... | collective-permute-start | bytes 98312 | tf_op jit(solution)/shard_map/ppermute | solution.py:403
  50.6 5.1 %collective-permute-start.9 = (bf16[2,128,128]{2,1,0:T(8,128)(2,1)}, bf16[2,128,128]{2,1,0:T(8,128)(2,1)}, u32[]{:S(2)}, u32[]{:S(2)}) collective-permute-start(bf16[2,128,128]{2,1,0:T(8,128)(2,1)} %get-tuple-element.47), channel_id=1, source_target_pairs={{0,1},{1,0},{2,3},{3,2},{4,5},{5,4},{6,7},{7,6},{8,9},{9,8},{10,11... | collective-permute-start | bytes 196616 | tf_op jit(solution)/shard_map/ppermute | solution.py:409
  50.6 5.1 %collective-permute-start.10 = (bf16[2,128,128]{2,1,0:T(8,128)(2,1)}, bf16[2,128,128]{2,1,0:T(8,128)(2,1)}, u32[]{:S(2)}, u32[]{:S(2)}) collective-permute-start(bf16[2,128,128]{2,1,0:T(8,128)(2,1)} %get-tuple-element.48), channel_id=1, source_target_pairs={{0,2},{1,3},{2,0},{3,1},{4,6},{5,7},{6,4},{7,5},{8,10},{9,11},{10,... | collective-permute-start | bytes 196616 | tf_op jit(solution)/shard_map/ppermute | solution.py:409
  52.1 4.4 %collective-permute-start.11 = (bf16[2,128,128]{2,1,0:T(8,128)(2,1)}, bf16[2,128,128]{2,1,0:T(8,128)(2,1)}, u32[]{:S(2)}, u32[]{:S(2)}) collective-permute-start(bf16[2,128,128]{2,1,0:T(8,128)(2,1)} %get-tuple-element.49), channel_id=1, source_target_pairs={{0,3},{1,2},{2,1},{3,0},{4,7},{5,6},{6,5},{7,4},{8,11},{9,10},{10,... | collective-permute-start | bytes 196616 | tf_op jit(solution)/shard_map/ppermute | solution.py:409
  59.3 14.6 %all-to-all-start.3 = ((bf16[8,128,128]{2,1,0:T(8,128)(2,1)}), bf16[8,128,128]{2,1,0:T(8,128)(2,1)}, u32[]{:S(2)}, u32[]{:S(2)}) async-start(bf16[8,128,128]{2,1,0:T(8,128)(2,1)} %get-tuple-element.57), calls=%async_computation.3 | async-start | bytes 524288 | tf_op jit(solution)/shard_map/all_to_all | solution.py:515
  63.4 4.5 %collective-permute-start.14 = (bf16[2,128,128]{2,1,0:T(8,128)(2,1)}, bf16[2,128,128]{2,1,0:T(8,128)(2,1)}, u32[]{:S(2)}, u32[]{:S(2)}) collective-permute-start(bf16[2,128,128]{2,1,0:T(8,128)(2,1)} %get-tuple-element.55.refs_8_), channel_id=1, source_target_pairs={{0,3},{1,2},{2,1},{3,0},{4,7},{5,6},{6,5},{7,4},{8,11},{9,10},{10,... | collective-permute-start | bytes 196616 | tf_op jit(solution)/shard_map/ppermute | solution.py:409
  64.6 4.9 %collective-permute-start.13 = (bf16[2,128,128]{2,1,0:T(8,128)(2,1)}, bf16[2,128,128]{2,1,0:T(8,128)(2,1)}, u32[]{:S(2)}, u32[]{:S(2)}) collective-permute-start(bf16[2,128,128]{2,1,0:T(8,128)(2,1)} %get-tuple-element.55.refs_8_), channel_id=1, source_target_pairs={{0,2},{1,3},{2,0},{3,1},{4,6},{5,7},{6,4},{7,5},{8,10},{9,11},{10,... | collective-permute-start | bytes 196616 | tf_op jit(solution)/shard_map/ppermute | solution.py:409
  65.2 4.4 %collective-permute-start.12 = (bf16[2,128,128]{2,1,0:T(8,128)(2,1)}, bf16[2,128,128]{2,1,0:T(8,128)(2,1)}, u32[]{:S(2)}, u32[]{:S(2)}) collective-permute-start(bf16[2,128,128]{2,1,0:T(8,128)(2,1)} %get-tuple-element.55.refs_8_), channel_id=1, source_target_pairs={{0,1},{1,0},{2,3},{3,2},{4,5},{5,4},{6,7},{7,6},{8,9},{9,8},{10,11... | collective-permute-start | bytes 196616 | tf_op jit(solution)/shard_map/ppermute | solution.py:409
  65.3 8.6 %collective-permute-start.15 = (bf16[128,128]{1,0:T(8,128)(2,1)}, bf16[128,128]{1,0:T(8,128)(2,1)}, u32[]{:S(2)}, u32[]{:S(2)}) collective-permute-start(bf16[128,128]{1,0:T(8,128)(2,1)} %get-tuple-element.58), channel_id=1, source_target_pairs={{28,0},{0,4},{4,8},{8,12},{12,16},{16,20},{20,24},{24,28},{29,1},{... | collective-permute-start | bytes 98312 | tf_op jit(solution)/shard_map/ppermute | solution.py:403

commit v9 on v8

--- a/solution.py
+++ b/solution.py
@@ -484,7 +484,7 @@
                 [local_rows, local_cols, band_count, dual, local_blocks, primal, cost],
                 [matrix, state_x],
                 [pltpu.VMEM((rows * columns, size, size), F32)],
-                16 * rows * columns * unit,
+                2 * rows * columns * unit,
                 {4: (chunks, 0)},
                 {0: rows},
             )
@@ -496,7 +496,7 @@
                 [dual_q, matrix_q, primal, cost],
                 [state_x],
                 [],
-                16 * rows * columns * unit,
+                2 * rows * columns * unit,
             )
         image, last, extrap, updated, streams = run(
             primal_body,

time: 76.5 us -> 75.8 us (level)
  waiting for transfers between devices: 7.33 us -> 5.33 us
  starting transfers between devices: 40.1 us -> 41.1 us
    ppermute x12, waiting for transfers between devices: 3.31 us -> 1.75 us  [exchanged(): return lax.ppermute(block, axis, [(i, i ^ d) for i in range(number)])]
    all_to_all x2, starting transfers between devices: 8.12 us -> 9.07 us  [body(): parts = lax.all_to_all(image, 'period', 0, 0, tiled=True)]
  transfers between devices with their start and end apart: 20 -> 20, of which waited for: 5 -> 3; matrix products, arithmetic and copies ran while one was open for 0% -> 0% of each run, Pallas kernels for 19% -> 19%
where the time goes in v9:
time: 75.8 us; the launch traced here: 74.9 us
  starting transfers between devices  41.1 us (54%)
  Pallas kernels  27 us (36%)
  waiting for transfers between devices  5.33 us (7%)
  between operations  1.5 us (2%)
    pallas_call x8, Pallas kernels, run(): pl.pallas_call(kernel, name=name, in_specs=[SMEM] * ns + [HBM] * na, out_...  25.1 us
    ppermute x4, starting transfers between devices, shifted(): return lax.ppermute(block, axis, route)  13 us
    all_to_all x2, starting transfers between devices, body(): annual_q = lax.all_to_all(annual_send, 'period', 0, 0, tiled=True)  11.4 us
    all_to_all x2, starting transfers between devices, body(): parts = lax.all_to_all(image, 'period', 0, 0, tiled=True)  9.07 us
    ppermute x12, starting transfers between devices, exchanged(): return lax.ppermute(block, axis, [(i, i ^ d) for i in range(number)])  7.64 us
    ppermute x4, waiting for transfers between devices, shifted(): return lax.ppermute(block, axis, route)  3.57 us
    pallas_call x1, Pallas kernels, finish(): pl.pallas_call(finish_kernel, name='finish', in_specs=[HBM] * 6, out_spec...  1.88 us
    ppermute x12, waiting for transfers between devices, exchanged(): return lax.ppermute(block, axis, [(i, i ^ d) for i in range(number)])  1.75 us
  transfers between devices with their start and end apart: 20, of which 3 were waited for; matrix products, arithmetic and copies ran while one was open for 0% of the time, Pallas kernels for 19%

profile of v9, /device:TPU:0, one launch (start us, length us, event | category | flops | bytes accessed | tf_op | source)
XLA Modules:
  0.0 74.9 jit_solution(11004911088876577619)
XLA Ops:
  0.6 2.3 %first_duals.1 = (bf16[8,128,128]{2,1,0:T(8,128)(2,1)}, f32[2,128,128]{2,1,0:T(8,128)}, bf16[2,128,128]{2,1,0:T(8,128)(2,1)}, bf16[2,128,128]{2,1,0:T(8,128)(2,1...) custom-call(s32[1]{0:T(128)} %bitcast.1.refs_0_, s32[8]{0:T(128)} %refs_1_.11, s32[8]{0:T(128)} %refs_2_.8, ...), custom_call_target="tpu_custom_call" | custom-call | flops 37748736 | bytes 1507392 | tf_op jit(solution)/shard_map/first_duals/pallas_call | solution.py:106
  2.9 7.3 %all-to-all-start = ((bf16[8,128,128]{2,1,0:T(8,128)(2,1)}), bf16[8,128,128]{2,1,0:T(8,128)(2,1)}, u32[]{:S(2)}, u32[]{:S(2)}) async-start(bf16[8,128,128]{2,1,0:T(8,128)(2,1)} %get-tuple-element.32), calls=%async_computation | async-start | bytes 524288 | tf_op jit(solution)/shard_map/all_to_all | solution.py:476
  10.2 0.0 collective-permute-start.1
  10.2 1.6 %collective-permute-start.2 = (bf16[2,128,128]{2,1,0:T(8,128)(2,1)}, bf16[2,128,128]{2,1,0:T(8,128)(2,1)}, u32[]{:S(2)}, u32[]{:S(2)}) collective-permute-start(bf16[2,128,128]{2,1,0:T(8,128)(2,1)} %get-tuple-element.36), channel_id=1, source_target_pairs={{0,2},{1,3},{2,0},{3,1},{4,6},{5,7},{6,4},{7,5},{8,10},{9,11},{10,... | collective-permute-start | bytes 196616 | tf_op jit(solution)/shard_map/ppermute | solution.py:409
  11.8 0.3 collective-permute-start.3
  12.1 4.7 %collective-permute-start = (bf16[128,128]{1,0:T(8,128)(2,1)}, bf16[128,128]{1,0:T(8,128)(2,1)}, u32[]{:S(2)}, u32[]{:S(2)}) collective-permute-start(bf16[128,128]{1,0:T(8,128)(2,1)} %get-tuple-element.34), channel_id=1, source_target_pairs={{4,0},{8,4},{12,8},{16,12},{20,16},{24,20},{28,24},{0,28},{5,1},{9... | collective-permute-start | bytes 98312 | tf_op jit(solution)/shard_map/ppermute | solution.py:403
  17.5 3.9 %dense.1 = (bf16[1024,1024]{1,0:T(8,128)(2,1)}, f32[1024,128]{1,0:T(8,128)}) custom-call(s32[96]{0:T(128)} %refs_0_.3, s32[96]{0:T(128)} %refs_1_.7, s32[1]{0:T(128)S(6)} %copy.23.refs_2_, f32[1024,128]{1,0:T(8,128)} %refs_2_.6, bf16[96,128,128]{2,1,0:T(8,128)(2,1)} %refs_4_.3, f32[1024,128]{1,0:T(8,128)} %refs_11_.2, f32[1024,128]{1,0:T(8,128)} %refs_3_.10), custom_call_target="tpu_custom_call" | custom-call | flops 536870912 | bytes 7340804 | tf_op jit(solution)/shard_map/dense/pallas_call | solution.py:106
  21.4 0.0 collective-permute-done.refs_6_
  21.4 0.0 collective-permute-done.1.refs_7_
  21.4 2.7 %primal_step.2 = (bf16[8,128,128]{2,1,0:T(8,128)(2,1)}, bf16[128,128]{1,0:T(8,128)(2,1)}, bf16[8,128,128]{2,1,0:T(8,128)(2,1)}, f32[1024,128]{1,0:T(8,128)}, bf16[2,128,128]{2,1,0:T(8,128)(2,1)}) custom-call(s32[8]{0:T(128)} %refs_0_.5, s32[8]{0:T(128)} %refs_1_.10, f32[8,128]{1,0:T(8,128)} %bitcast.4, bf16[8,128,128]{2,1,0:T(8,128)(2,1)} %refs_3_.11, ...), custom_call_target="tpu_custom_call" | custom-call | flops 67108864 | bytes 3084352 | tf_op jit(solution)/shard_map/primal_step/pallas_call | solution.py:106
  24.2 4.1 %all-to-all-start.1 = ((bf16[8,128,128]{2,1,0:T(8,128)(2,1)}), bf16[8,128,128]{2,1,0:T(8,128)(2,1)}, u32[]{:S(2)}, u32[]{:S(2)}) async-start(bf16[8,128,128]{2,1,0:T(8,128)(2,1)} %get-tuple-element.41), calls=%async_computation.1 | async-start | bytes 524288 | tf_op jit(solution)/shard_map/all_to_all | solution.py:515
  28.3 1.2 %collective-permute-start.6 = (bf16[2,128,128]{2,1,0:T(8,128)(2,1)}, bf16[2,128,128]{2,1,0:T(8,128)(2,1)}, u32[]{:S(2)}, u32[]{:S(2)}) collective-permute-start(bf16[2,128,128]{2,1,0:T(8,128)(2,1)} %get-tuple-element.39.refs_4_), channel_id=1, source_target_pairs={{0,3},{1,2},{2,1},{3,0},{4,7},{5,6},{6,5},{7,4},{8,11},{9,10},{10,... | collective-permute-start | bytes 196616 | tf_op jit(solution)/shard_map/ppermute | solution.py:409
  29.4 0.8 %collective-permute-start.5 = (bf16[2,128,128]{2,1,0:T(8,128)(2,1)}, bf16[2,128,128]{2,1,0:T(8,128)(2,1)}, u32[]{:S(2)}, u32[]{:S(2)}) collective-permute-start(bf16[2,128,128]{2,1,0:T(8,128)(2,1)} %get-tuple-element.39.refs_4_), channel_id=1, source_target_pairs={{0,2},{1,3},{2,0},{3,1},{4,6},{5,7},{6,4},{7,5},{8,10},{9,11},{10,... | collective-permute-start | bytes 196616 | tf_op jit(solution)/shard_map/ppermute | solution.py:409
  30.3 1.8 %collective-permute-start.7 = (bf16[128,128]{1,0:T(8,128)(2,1)}, bf16[128,128]{1,0:T(8,128)(2,1)}, u32[]{:S(2)}, u32[]{:S(2)}) collective-permute-start(bf16[128,128]{1,0:T(8,128)(2,1)} %get-tuple-element.40), channel_id=1, source_target_pairs={{28,0},{0,4},{4,8},{8,12},{12,16},{16,20},{20,24},{24,28},{29,1},{... | collective-permute-start | bytes 98312 | tf_op jit(solution)/shard_map/ppermute | solution.py:403
  32.0 3.4 %forward.1.refs_13_ = f32[1024,128]{1,0:T(8,128)} custom-call(bf16[8,128,128]{2,1,0:T(8,128)(2,1)} %get-tuple-element.42.refs_0_, f32[8,128]{1,0:T(8,128)} %bitcast.6, f32[1024,128]{1,0:T(8,128)} %refs_2_.6, bf16[1024,1024]{1,0:T(8,128)(2,1)} %get-tuple-element.43.refs_3_.refs_1_.refs_6_), custom_call_target="tpu_custom_call" | custom-call | flops 4294967296 | bytes 3411968 | tf_op jit(solution)/shard_map/forward/pallas_call | solution.py:106
  35.4 3.6 %collective-permute-done.7.refs_9_ = bf16[128,128]{1,0:T(8,128)(2,1)} collective-permute-done((bf16[128,128]{1,0:T(8,128)(2,1)}, bf16[128,128]{1,0:T(8,128)(2,1)}, u32[]{:S(2)}, u32[]{:S(2)}) %collective-permute-start.7) | collective-permute-done | bytes 32800 | tf_op jit(solution)/shard_map/ppermute | solution.py:403
  39.0 2.9 %dual_step.1 = (f32[1024,128]{1,0:T(8,128)}, f32[128,128]{1,0:T(8,128)}, bf16[8,128,128]{2,1,0:T(8,128)(2,1)}, bf16[8,128,128]{2,1,0:T(8,128)(2,1)}, f32[2,128,1...) custom-call(s32[1]{0:T(128)} %bitcast.1.refs_0_, ...), custom_call_target="tpu_custom_call" | custom-call | flops 67108864 | bytes 2916928 | tf_op jit(solution)/shard_map/dual_step/pallas_call | solution.py:106
  41.9 4.1 %all-to-all-start.2 = ((bf16[8,128,128]{2,1,0:T(8,128)(2,1)}), bf16[8,128,128]{2,1,0:T(8,128)(2,1)}, u32[]{:S(2)}, u32[]{:S(2)}) async-start(bf16[8,128,128]{2,1,0:T(8,128)(2,1)} %get-tuple-element.44), calls=%async_computation.2 | async-start | bytes 524288 | tf_op jit(solution)/shard_map/all_to_all | solution.py:476
  46.0 0.1 collective-permute-start.9
  46.1 1.3 %collective-permute-start.10 = (bf16[2,128,128]{2,1,0:T(8,128)(2,1)}, bf16[2,128,128]{2,1,0:T(8,128)(2,1)}, u32[]{:S(2)}, u32[]{:S(2)}) collective-permute-start(bf16[2,128,128]{2,1,0:T(8,128)(2,1)} %get-tuple-element.48), channel_id=1, source_target_pairs={{0,2},{1,3},{2,0},{3,1},{4,6},{5,7},{6,4},{7,5},{8,10},{9,11},{10,... | collective-permute-start | bytes 196616 | tf_op jit(solution)/shard_map/ppermute | solution.py:409
  47.3 0.6 collective-permute-start.11
  47.9 4.6 %collective-permute-start.8 = (bf16[128,128]{1,0:T(8,128)(2,1)}, bf16[128,128]{1,0:T(8,128)(2,1)}, u32[]{:S(2)}, u32[]{:S(2)}) collective-permute-start(bf16[128,128]{1,0:T(8,128)(2,1)} %get-tuple-element.46), channel_id=1, source_target_pairs={{4,0},{8,4},{12,8},{16,12},{20,16},{24,20},{28,24},{0,28},{5,1},{9... | collective-permute-start | bytes 98312 | tf_op jit(solution)/shard_map/ppermute | solution.py:403
  52.5 3.2 %adjoint.1.refs_10_ = f32[1024,128]{1,0:T(8,128)} custom-call(bf16[8,128,128]{2,1,0:T(8,128)(2,1)} %get-tuple-element.50.refs_0_, bf16[1024,1024]{1,0:T(8,128)(2,1)} %get-tuple-element.43.refs_3_.refs_1_.refs_6_, f32[1024,128]{1,0:T(8,128)} %get-tuple-element.51.refs_2_.refs_11_, f32[1024,128]{1,0:T(8,128)} %refs_3_.10), custom_call_target="tpu_custom_call" | custom-call | flops 536870912 | bytes 3932160 | tf_op jit(solution)/shard_map/adjoint/pallas_call | solution.py:106
  55.7 2.8 %primal_step.3 = (bf16[8,128,128]{2,1,0:T(8,128)(2,1)}, bf16[128,128]{1,0:T(8,128)(2,1)}, bf16[8,128,128]{2,1,0:T(8,128)(2,1)}, f32[1024,128]{1,0:T(8,128)}, bf16[2,128,128]{2,1,0:T(8,128)(2,1)}) custom-call(s32[8]{0:T(128)} %refs_0_.5, s32[8]{0:T(128)} %refs_1_.10, f32[8,128]{1,0:T(8,128)} %bitcast.5, bf16[8,128,128]{2,1,0:T(8,128)(2,1)} %refs_3_.11, ...), custom_call_target="tpu_custom_call" | custom-call | flops 67108864 | bytes 3084352 | tf_op jit(solution)/shard_map/primal_step/pallas_call | solution.py:106
  58.5 5.0 %all-to-all-start.3 = ((bf16[8,128,128]{2,1,0:T(8,128)(2,1)}), bf16[8,128,128]{2,1,0:T(8,128)(2,1)}, u32[]{:S(2)}, u32[]{:S(2)}) async-start(bf16[8,128,128]{2,1,0:T(8,128)(2,1)} %get-tuple-element.57), calls=%async_computation.3 | async-start | bytes 524288 | tf_op jit(solution)/shard_map/all_to_all | solution.py:515
  63.5 1.3 %collective-permute-start.13 = (bf16[2,128,128]{2,1,0:T(8,128)(2,1)}, bf16[2,128,128]{2,1,0:T(8,128)(2,1)}, u32[]{:S(2)}, u32[]{:S(2)}) collective-permute-start(bf16[2,128,128]{2,1,0:T(8,128)(2,1)} %get-tuple-element.55.refs_8_), channel_id=1, source_target_pairs={{0,2},{1,3},{2,0},{3,1},{4,6},{5,7},{6,4},{7,5},{8,10},{9,11},{10,... | collective-permute-start | bytes 196616 | tf_op jit(solution)/shard_map/ppermute | solution.py:409
  64.8 0.6 collective-permute-start.12
  65.4 2.0 %collective-permute-start.15 = (bf16[128,128]{1,0:T(8,128)(2,1)}, bf16[128,128]{1,0:T(8,128)(2,1)}, u32[]{:S(2)}, u32[]{:S(2)}) collective-permute-start(bf16[128,128]{1,0:T(8,128)(2,1)} %get-tuple-element.58), channel_id=1, source_target_pairs={{28,0},{0,4},{4,8},{8,12},{12,16},{16,20},{20,24},{24,28},{29,1},{... | collective-permute-start | bytes 98312 | tf_op jit(solution)/shard_map/ppermute | solution.py:403
  67.4 0.8 %collective-permute-done.14.refs_11_ = bf16[2,128,128]{2,1,0:T(8,128)(2,1)} collective-permute-done((bf16[2,128,128]{2,1,0:T(8,128)(2,1)}, bf16[2,128,128]{2,1,0:T(8,128)(2,1)}, u32[]{:S(2)}, u32[]{:S(2)}) %collective-permute-start.14) | collective-permute-done | bytes 65568 | tf_op jit(solution)/shard_map/ppermute | solution.py:409
  68.2 0.9 %collective-permute-done.13.refs_10_ = bf16[2,128,128]{2,1,0:T(8,128)(2,1)} collective-permute-done((bf16[2,128,128]{2,1,0:T(8,128)(2,1)}, bf16[2,128,128]{2,1,0:T(8,128)(2,1)}, u32[]{:S(2)}, u32[]{:S(2)}) %collective-permute-start.13) | collective-permute-done | bytes 65568 | tf_op jit(solution)/shard_map/ppermute | solution.py:409
  69.1 3.9 %last_rows.1.row = f32[1024,128]{1,0:T(8,128)} custom-call(s32[1]{0:T(128)} %bitcast.1.refs_0_, s32[8]{0:T(128)} %refs_1_.11, s32[8]{0:T(128)} %refs_2_.8, f32[8,128]{1,0:T(8,128)} %bitcast.7, f32[1024,128]{1,0:T(8,128)} %get-tuple-element.53.refs_4_, bf16[8,128,128]{2,1,0:T(8,128)(2,1)} %get-tuple-element.54.refs_5_, ...), custom_call_target="tpu_custom_call" | custom-call | flops 4194304 | bytes 3936320 | tf_op jit(solution)/shard_map/last_rows/pallas_call | solution.py:106
  73.0 1.9 %finish.1 = (f32[1024,128]{1,0:T(8,128)}, f32[128,128]{1,0:T(8,128)}) custom-call(f32[1024,128]{1,0:T(8,128)} %last_rows.1.row, f32[128,128]{1,0:T(8,128)} %get-tuple-element.56.annual, f32[1,128]{1,0:T(1,128)} %bitcast.9, bf16[8,128,128]{2,1,0:T(8,128)(2,1)} %all-to-all-done.3.parts, bf16[1,128,128]{2,1,0:T(8,128)(2,1)} %carry.1, ...), custom_call_target="tpu_custom_call", output_to_operand_aliasing={{0}: (0, {})} | custom-call | flops 4194304 | bytes 1000000 | tf_op jit(solution)/shard_map/finish/pallas_call | solution.py:384
  (17 shorter events, 0.0 us)
Async XLA Ops:
  2.9 18.5 %all-to-all-start = ((bf16[8,128,128]{2,1,0:T(8,128)(2,1)}), bf16[8,128,128]{2,1,0:T(8,128)(2,1)}, u32[]{:S(2)}, u32[]{:S(2)}) async-start(bf16[8,128,128]{2,1,0:T(8,128)(2,1)} %get-tuple-element.32), calls=%async_computation | async-start | bytes 524288 | tf_op jit(solution)/shard_map/all_to_all | solution.py:476
  10.2 11.2 %collective-permute-start.1 = (bf16[2,128,128]{2,1,0:T(8,128)(2,1)}, bf16[2,128,128]{2,1,0:T(8,128)(2,1)}, u32[]{:S(2)}, u32[]{:S(2)}) collective-permute-start(bf16[2,128,128]{2,1,0:T(8,128)(2,1)} %get-tuple-element.35), channel_id=1, source_target_pairs={{0,1},{1,0},{2,3},{3,2},{4,5},{5,4},{6,7},{7,6},{8,9},{9,8},{10,11... | collective-permute-start | bytes 196616 | tf_op jit(solution)/shard_map/ppermute | solution.py:409
  10.2 11.2 %collective-permute-start.2 = (bf16[2,128,128]{2,1,0:T(8,128)(2,1)}, bf16[2,128,128]{2,1,0:T(8,128)(2,1)}, u32[]{:S(2)}, u32[]{:S(2)}) collective-permute-start(bf16[2,128,128]{2,1,0:T(8,128)(2,1)} %get-tuple-element.36), channel_id=1, source_target_pairs={{0,2},{1,3},{2,0},{3,1},{4,6},{5,7},{6,4},{7,5},{8,10},{9,11},{10,... | collective-permute-start | bytes 196616 | tf_op jit(solution)/shard_map/ppermute | solution.py:409
  11.8 9.6 %collective-permute-start.3 = (bf16[2,128,128]{2,1,0:T(8,128)(2,1)}, bf16[2,128,128]{2,1,0:T(8,128)(2,1)}, u32[]{:S(2)}, u32[]{:S(2)}) collective-permute-start(bf16[2,128,128]{2,1,0:T(8,128)(2,1)} %get-tuple-element.37), channel_id=1, source_target_pairs={{0,3},{1,2},{2,1},{3,0},{4,7},{5,6},{6,5},{7,4},{8,11},{9,10},{10,... | collective-permute-start | bytes 196616 | tf_op jit(solution)/shard_map/ppermute | solution.py:409
  12.1 9.3 %collective-permute-start = (bf16[128,128]{1,0:T(8,128)(2,1)}, bf16[128,128]{1,0:T(8,128)(2,1)}, u32[]{:S(2)}, u32[]{:S(2)}) collective-permute-start(bf16[128,128]{1,0:T(8,128)(2,1)} %get-tuple-element.34), channel_id=1, source_target_pairs={{4,0},{8,4},{12,8},{16,12},{20,16},{24,20},{28,24},{0,28},{5,1},{9... | collective-permute-start | bytes 98312 | tf_op jit(solution)/shard_map/ppermute | solution.py:403
  24.2 14.8 %all-to-all-start.1 = ((bf16[8,128,128]{2,1,0:T(8,128)(2,1)}), bf16[8,128,128]{2,1,0:T(8,128)(2,1)}, u32[]{:S(2)}, u32[]{:S(2)}) async-start(bf16[8,128,128]{2,1,0:T(8,128)(2,1)} %get-tuple-element.41), calls=%async_computation.1 | async-start | bytes 524288 | tf_op jit(solution)/shard_map/all_to_all | solution.py:515
  28.3 10.7 %collective-permute-start.6 = (bf16[2,128,128]{2,1,0:T(8,128)(2,1)}, bf16[2,128,128]{2,1,0:T(8,128)(2,1)}, u32[]{:S(2)}, u32[]{:S(2)}) collective-permute-start(bf16[2,128,128]{2,1,0:T(8,128)(2,1)} %get-tuple-element.39.refs_4_), channel_id=1, source_target_pairs={{0,3},{1,2},{2,1},{3,0},{4,7},{5,6},{6,5},{7,4},{8,11},{9,10},{10,... | collective-permute-start | bytes 196616 | tf_op jit(solution)/shard_map/ppermute | solution.py:409
  29.4 9.6 %collective-permute-start.5 = (bf16[2,128,128]{2,1,0:T(8,128)(2,1)}, bf16[2,128,128]{2,1,0:T(8,128)(2,1)}, u32[]{:S(2)}, u32[]{:S(2)}) collective-permute-start(bf16[2,128,128]{2,1,0:T(8,128)(2,1)} %get-tuple-element.39.refs_4_), channel_id=1, source_target_pairs={{0,2},{1,3},{2,0},{3,1},{4,6},{5,7},{6,4},{7,5},{8,10},{9,11},{10,... | collective-permute-start | bytes 196616 | tf_op jit(solution)/shard_map/ppermute | solution.py:409
  30.3 8.7 %collective-permute-start.4 = (bf16[2,128,128]{2,1,0:T(8,128)(2,1)}, bf16[2,128,128]{2,1,0:T(8,128)(2,1)}, u32[]{:S(2)}, u32[]{:S(2)}) collective-permute-start(bf16[2,128,128]{2,1,0:T(8,128)(2,1)} %get-tuple-element.39.refs_4_), channel_id=1, source_target_pairs={{0,1},{1,0},{2,3},{3,2},{4,5},{5,4},{6,7},{7,6},{8,9},{9,8},{10,11... | collective-permute-start | bytes 196616 | tf_op jit(solution)/shard_map/ppermute | solution.py:409
  30.3 8.7 %collective-permute-start.7 = (bf16[128,128]{1,0:T(8,128)(2,1)}, bf16[128,128]{1,0:T(8,128)(2,1)}, u32[]{:S(2)}, u32[]{:S(2)}) collective-permute-start(bf16[128,128]{1,0:T(8,128)(2,1)} %get-tuple-element.40), channel_id=1, source_target_pairs={{28,0},{0,4},{4,8},{8,12},{12,16},{16,20},{20,24},{24,28},{29,1},{... | collective-permute-start | bytes 98312 | tf_op jit(solution)/shard_map/ppermute | solution.py:403
  41.9 13.8 %all-to-all-start.2 = ((bf16[8,128,128]{2,1,0:T(8,128)(2,1)}), bf16[8,128,128]{2,1,0:T(8,128)(2,1)}, u32[]{:S(2)}, u32[]{:S(2)}) async-start(bf16[8,128,128]{2,1,0:T(8,128)(2,1)} %get-tuple-element.44), calls=%async_computation.2 | async-start | bytes 524288 | tf_op jit(solution)/shard_map/all_to_all | solution.py:476
  46.0 9.7 %collective-permute-start.9 = (bf16[2,128,128]{2,1,0:T(8,128)(2,1)}, bf16[2,128,128]{2,1,0:T(8,128)(2,1)}, u32[]{:S(2)}, u32[]{:S(2)}) collective-permute-start(bf16[2,128,128]{2,1,0:T(8,128)(2,1)} %get-tuple-element.47), channel_id=1, source_target_pairs={{0,1},{1,0},{2,3},{3,2},{4,5},{5,4},{6,7},{7,6},{8,9},{9,8},{10,11... | collective-permute-start | bytes 196616 | tf_op jit(solution)/shard_map/ppermute | solution.py:409
  46.1 9.6 %collective-permute-start.10 = (bf16[2,128,128]{2,1,0:T(8,128)(2,1)}, bf16[2,128,128]{2,1,0:T(8,128)(2,1)}, u32[]{:S(2)}, u32[]{:S(2)}) collective-permute-start(bf16[2,128,128]{2,1,0:T(8,128)(2,1)} %get-tuple-element.48), channel_id=1, source_target_pairs={{0,2},{1,3},{2,0},{3,1},{4,6},{5,7},{6,4},{7,5},{8,10},{9,11},{10,... | collective-permute-start | bytes 196616 | tf_op jit(solution)/shard_map/ppermute | solution.py:409
  47.3 8.4 %collective-permute-start.11 = (bf16[2,128,128]{2,1,0:T(8,128)(2,1)}, bf16[2,128,128]{2,1,0:T(8,128)(2,1)}, u32[]{:S(2)}, u32[]{:S(2)}) collective-permute-start(bf16[2,128,128]{2,1,0:T(8,128)(2,1)} %get-tuple-element.49), channel_id=1, source_target_pairs={{0,3},{1,2},{2,1},{3,0},{4,7},{5,6},{6,5},{7,4},{8,11},{9,10},{10,... | collective-permute-start | bytes 196616 | tf_op jit(solution)/shard_map/ppermute | solution.py:409
  47.9 7.7 %collective-permute-start.8 = (bf16[128,128]{1,0:T(8,128)(2,1)}, bf16[128,128]{1,0:T(8,128)(2,1)}, u32[]{:S(2)}, u32[]{:S(2)}) collective-permute-start(bf16[128,128]{1,0:T(8,128)(2,1)} %get-tuple-element.46), channel_id=1, source_target_pairs={{4,0},{8,4},{12,8},{16,12},{20,16},{24,20},{28,24},{0,28},{5,1},{9... | collective-permute-start | bytes 98312 | tf_op jit(solution)/shard_map/ppermute | solution.py:403
  58.5 14.5 %all-to-all-start.3 = ((bf16[8,128,128]{2,1,0:T(8,128)(2,1)}), bf16[8,128,128]{2,1,0:T(8,128)(2,1)}, u32[]{:S(2)}, u32[]{:S(2)}) async-start(bf16[8,128,128]{2,1,0:T(8,128)(2,1)} %get-tuple-element.57), calls=%async_computation.3 | async-start | bytes 524288 | tf_op jit(solution)/shard_map/all_to_all | solution.py:515
  63.5 4.7 %collective-permute-start.14 = (bf16[2,128,128]{2,1,0:T(8,128)(2,1)}, bf16[2,128,128]{2,1,0:T(8,128)(2,1)}, u32[]{:S(2)}, u32[]{:S(2)}) collective-permute-start(bf16[2,128,128]{2,1,0:T(8,128)(2,1)} %get-tuple-element.55.refs_8_), channel_id=1, source_target_pairs={{0,3},{1,2},{2,1},{3,0},{4,7},{5,6},{6,5},{7,4},{8,11},{9,10},{10,... | collective-permute-start | bytes 196616 | tf_op jit(solution)/shard_map/ppermute | solution.py:409
  63.5 5.6 %collective-permute-start.13 = (bf16[2,128,128]{2,1,0:T(8,128)(2,1)}, bf16[2,128,128]{2,1,0:T(8,128)(2,1)}, u32[]{:S(2)}, u32[]{:S(2)}) collective-permute-start(bf16[2,128,128]{2,1,0:T(8,128)(2,1)} %get-tuple-element.55.refs_8_), channel_id=1, source_target_pairs={{0,2},{1,3},{2,0},{3,1},{4,6},{5,7},{6,4},{7,5},{8,10},{9,11},{10,... | collective-permute-start | bytes 196616 | tf_op jit(solution)/shard_map/ppermute | solution.py:409
  64.8 4.3 %collective-permute-start.12 = (bf16[2,128,128]{2,1,0:T(8,128)(2,1)}, bf16[2,128,128]{2,1,0:T(8,128)(2,1)}, u32[]{:S(2)}, u32[]{:S(2)}) collective-permute-start(bf16[2,128,128]{2,1,0:T(8,128)(2,1)} %get-tuple-element.55.refs_8_), channel_id=1, source_target_pairs={{0,1},{1,0},{2,3},{3,2},{4,5},{5,4},{6,7},{7,6},{8,9},{9,8},{10,11... | collective-permute-start | bytes 196616 | tf_op jit(solution)/shard_map/ppermute | solution.py:409
  65.4 7.7 %collective-permute-start.15 = (bf16[128,128]{1,0:T(8,128)(2,1)}, bf16[128,128]{1,0:T(8,128)(2,1)}, u32[]{:S(2)}, u32[]{:S(2)}) collective-permute-start(bf16[128,128]{1,0:T(8,128)(2,1)} %get-tuple-element.58), channel_id=1, source_target_pairs={{28,0},{0,4},{4,8},{8,12},{12,16},{16,20},{20,24},{24,28},{29,1},{... | collective-permute-start | bytes 98312 | tf_op jit(solution)/shard_map/ppermute | solution.py:403

commit v10 on v9

--- a/solution.py
+++ b/solution.py
@@ -175,6 +175,12 @@
     )
 
 
+def turned_blocks(dual, size):
+    return jnp.concatenate(
+        [dual[i * size : (i + 1) * size].astype(BF16).T for i in range(dual.shape[0] // size)], axis=1
+    )
+
+
 def adjoint(matrix, turned, size, primal, prices, out):
     part = dot(turned, matrix[...])
     primal, prices = primal(), prices()
@@ -191,9 +197,7 @@
     tiles = matrix.ref.shape[1] // size
     acc[...] = jnp.zeros_like(acc)
     count, dual = count(), dual()
-    turned = jnp.concatenate(
-        [dual[i * size : (i + 1) * size].astype(BF16).T for i in range(dual.shape[0] // size)], axis=1
-    )
+    turned = turned_blocks(dual, size)
     slots = blocks.target.shape[0] // chunks
     for c in range(chunks):
         here = blocks.piece()
@@ -211,12 +215,9 @@
     adjoint(matrix.ref, turned, size, primal, prices, out)
 
 
-def adjoint_body(scalars, ins, outs):
-    dual_q, matrix, primal, prices = ins
-    dual_q = dual_q()
-    blocks, size, _ = dual_q.shape
-    turned = jnp.concatenate([dual_q[i].T for i in range(blocks)], axis=1)
-    adjoint(matrix(), turned, size, primal, prices, outs[0])
+def adjoint_body(size, scalars, ins, outs):
+    dual, matrix, primal, prices = ins
+    adjoint(matrix(), turned_blocks(dual(), size), size, primal, prices, outs[0])
 
 
 def primal_body(scalars, ins, outs, acc, image_acc, product, bound):
@@ -274,7 +275,7 @@
     out.ref[...] -= DUAL_STEP * dot(matrix()[...], right)
 
 
-def dual_body(refineries, scalars, ins, outs, gathered, acc, product, stream_acc):
+def dual_body(refineries, scalars, ins, outs, gathered, acc, product, stream_acc, dual_q):
     (me,) = scalars
     rows, src, swing, streams, *arrived, carry, previous, parts, annual, need, partial = ins
     dual, annual_out = outs[0], outs[1]
@@ -309,39 +310,42 @@
         at = slice(i * size, (i + 1) * size)
         new = jnp.maximum(partial[at] - DUAL_STEP * acc[i], 0.0)
         dual.ref[at] = new
-        outs[3].ref[i] = new.astype(BF16)
+        dual_q[i] = new.astype(BF16)
     dual.send()
-    outs[3].send()
     send_duals(
-        refineries, outs[3].ref, mine, rows, src, swing, carry, outs[4:], stream_acc, product
-    )
-
-
-def last_rows_body(refineries, scalars, ins, outs, gathered, acc, product):
+        refineries, dual_q, mine, rows, src, swing, carry, outs[3:], stream_acc, product
+    )
+
+
+def last_rows_body(refineries, chunks, scalars, ins, outs, gathered, acc, product):
     (me,) = scalars
-    rows, src, demand, dual, extrap, matrix, swing, streams, *arrived = ins
-    rows, src = rows(), src()
+    rows, src, demand, swing, streams, *arrived, dual, extrap, matrix = ins
     out = outs[0]
-    demand, dual, extrap = demand(), dual(), extrap()
-    blocks, size, width = extrap.shape
-    for i in range(demand.shape[0]):
-        at = slice(i * size, (i + 1) * size)
-        out.ref[at] = dual[at] + DUAL_STEP * column_of(demand[i : i + 1], width)
-    right = jnp.concatenate([extrap[j] for j in range(blocks)], axis=0)
-    out.ref[...] -= DUAL_STEP * dot(matrix()[...], right)
-    swing, mine = swing(), me[0]
+    rows, src, demand, swing, mine = rows(), src(), demand(), swing(), me[0]
+    size, width = swing.shape[1], gathered.shape[2]
+    acc[...] = jnp.zeros_like(acc)
     gathered[pl.ds(mine * SC, SC)] = streams()[...]
     for d, piece in enumerate(arrived, 1):
         gathered[pl.ds(partner(mine, d, refineries, True) * SC, SC)] = piece()[...]
-    acc[...] = jnp.zeros_like(acc)
     for m in range(swing.shape[0]):
         product[m] = dot(swing[m], gathered[src[m]])
     for m in range(swing.shape[0]):
         acc[rows[m]] += product[m]
-    for i in range(acc.shape[0]):
+    dual, extrap = dual(), extrap()
+    for i in range(demand.shape[0]):
         at = slice(i * size, (i + 1) * size)
-        new = out.ref[at] - DUAL_STEP * acc[i]
-        out.ref[at] = jnp.maximum(new, 0.0) if i else new
+        out.ref[at] = dual[at] + DUAL_STEP * (column_of(demand[i : i + 1], width) - acc[i])
+    right = jnp.concatenate([extrap[j] for j in range(extrap.shape[0])], axis=0)
+    step = out.ref.shape[0] // chunks
+    for c in range(chunks):
+        lines = slice(c * step, (c + 1) * step)
+        new = out.ref[lines] - DUAL_STEP * dot(matrix.piece()[lines], right)
+        if c:
+            out.ref[lines] = jnp.maximum(new, 0.0)
+        else:
+            out.ref[:size] = new[:size]
+            out.ref[size:step] = jnp.maximum(new[size:], 0.0)
+        out.send()
 
 
 def finish_kernel(
@@ -455,6 +459,7 @@
     swing_scratch = pltpu.VMEM((swings, size, scenarios), F32)
     annual_scratch = pltpu.VMEM((annuals, size, scenarios), F32)
     sends_shape = [pair] + [pair_q] * others + [tile]
+    pieces_y = 4 if rows % 8 == 0 else 1
     chunks = 8 if slots % 8 == 0 else 1
 
     upper_rows = upper.reshape(columns, size)
@@ -490,10 +495,10 @@
             )
         else:
             (partial_x,) = run(
-                adjoint_body,
+                functools.partial(adjoint_body, size),
                 "adjoint",
                 [],
-                [dual_q, matrix_q, primal, cost],
+                [dual, matrix_q, primal, cost],
                 [state_x],
                 [],
                 2 * rows * columns * unit,
@@ -517,10 +522,13 @@
         others_streams = [exchanged(streams, "refinery", d) for d in range(1, refineries)]
         if not more:
             (dual,) = run(
-                functools.partial(last_rows_body, refineries),
+                functools.partial(last_rows_body, refineries, pieces_y),
                 "last_rows",
                 [me],
-                [swing_rows, swing_src, demand_rows, dual, extrap, matrix_q, swing_blocks, streams, *others_streams],
+                [
+                    swing_rows, swing_src, demand_rows, swing_blocks, streams, *others_streams,
+                    dual, extrap, matrix_q,
+                ],
                 [state_y],
                 [
                     pltpu.VMEM((refineries * SC, size, scenarios), BF16),
@@ -528,6 +536,8 @@
                     swing_scratch,
                 ],
                 unit,
+                {7 + others: (pieces_y, 0)},
+                {0: pieces_y},
             )
             dual, annual = finish(dual, annual, need, parts, carry_blocks, previous)
             return updated, dual, annual
@@ -540,7 +550,7 @@
             [],
             16 * rows * columns * unit,
         )
-        sent = [weekly, blocks_y] + sends_shape
+        sent = [weekly] + sends_shape
         dual, annual, *rest = run(
             functools.partial(dual_body, refineries),
             "dual_step",
@@ -555,10 +565,10 @@
                 pltpu.VMEM((rows, size, scenarios), F32),
                 swing_scratch,
             ]
-            + [stream_scratch],
+            + [stream_scratch, pltpu.VMEM(blocks_y.shape, BF16)],
             2 * swings * unit,
         )
-        annual_send, dual_q, own, *rest = rest
+        annual_send, own, *rest = rest
         primal = updated
 
 

time: 75.8 us -> 75.3 us (level)
  no operation moved by 1% of the time
where the time goes in v10:
time: 75.3 us; the launch traced here: 74.6 us
  starting transfers between devices  41 us (54%)
  Pallas kernels  26.6 us (35%)
  waiting for transfers between devices  5.53 us (7%)
  between operations  1.5 us (2%)
    pallas_call x8, Pallas kernels, run(): pl.pallas_call(kernel, name=name, in_specs=[SMEM] * ns + [HBM] * na, out_...  24.7 us
    ppermute x4, starting transfers between devices, shifted(): return lax.ppermute(block, axis, route)  13.1 us
    all_to_all x2, starting transfers between devices, body(): annual_q = lax.all_to_all(annual_send, 'period', 0, 0, tiled=True)  11.3 us
    all_to_all x2, starting transfers between devices, body(): parts = lax.all_to_all(image, 'period', 0, 0, tiled=True)  8.95 us
    ppermute x12, starting transfers between devices, exchanged(): return lax.ppermute(block, axis, [(i, i ^ d) for i in range(number)])  7.57 us
    ppermute x4, waiting for transfers between devices, shifted(): return lax.ppermute(block, axis, route)  3.27 us
    ppermute x12, waiting for transfers between devices, exchanged(): return lax.ppermute(block, axis, [(i, i ^ d) for i in range(number)])  2.25 us
    pallas_call x1, Pallas kernels, finish(): pl.pallas_call(finish_kernel, name='finish', in_specs=[HBM] * 6, out_spec...  1.88 us
  transfers between devices with their start and end apart: 20, of which 3 were waited for; matrix products, arithmetic and copies ran while one was open for 0% of the time, Pallas kernels for 19%

profile of v10, /device:TPU:0, one launch (start us, length us, event | category | flops | bytes accessed | tf_op | source)
XLA Modules:
  0.0 74.6 jit_solution(8960171001101603041)
XLA Ops:
  0.6 2.3 %first_duals.1 = (bf16[8,128,128]{2,1,0:T(8,128)(2,1)}, f32[2,128,128]{2,1,0:T(8,128)}, bf16[2,128,128]{2,1,0:T(8,128)(2,1)}, bf16[2,128,128]{2,1,0:T(8,128)(2,1...) custom-call(s32[1]{0:T(128)} %bitcast.1.refs_0_, s32[8]{0:T(128)} %refs_1_.11, s32[8]{0:T(128)} %refs_2_.8, ...), custom_call_target="tpu_custom_call" | custom-call | flops 37748736 | bytes 1507392 | tf_op jit(solution)/shard_map/first_duals/pallas_call | solution.py:106
  2.9 7.3 %all-to-all-start = ((bf16[8,128,128]{2,1,0:T(8,128)(2,1)}), bf16[8,128,128]{2,1,0:T(8,128)(2,1)}, u32[]{:S(2)}, u32[]{:S(2)}) async-start(bf16[8,128,128]{2,1,0:T(8,128)(2,1)} %get-tuple-element.31), calls=%async_computation | async-start | bytes 524288 | tf_op jit(solution)/shard_map/all_to_all | solution.py:481
  10.2 0.0 collective-permute-start.1
  10.2 1.6 %collective-permute-start.2 = (bf16[2,128,128]{2,1,0:T(8,128)(2,1)}, bf16[2,128,128]{2,1,0:T(8,128)(2,1)}, u32[]{:S(2)}, u32[]{:S(2)}) collective-permute-start(bf16[2,128,128]{2,1,0:T(8,128)(2,1)} %get-tuple-element.35), channel_id=1, source_target_pairs={{0,2},{1,3},{2,0},{3,1},{4,6},{5,7},{6,4},{7,5},{8,10},{9,11},{10,... | collective-permute-start | bytes 196616 | tf_op jit(solution)/shard_map/ppermute | solution.py:413
  11.8 0.3 collective-permute-start.3
  12.1 4.7 %collective-permute-start = (bf16[128,128]{1,0:T(8,128)(2,1)}, bf16[128,128]{1,0:T(8,128)(2,1)}, u32[]{:S(2)}, u32[]{:S(2)}) collective-permute-start(bf16[128,128]{1,0:T(8,128)(2,1)} %get-tuple-element.33), channel_id=1, source_target_pairs={{4,0},{8,4},{12,8},{16,12},{20,16},{24,20},{28,24},{0,28},{5,1},{9... | collective-permute-start | bytes 98312 | tf_op jit(solution)/shard_map/ppermute | solution.py:407
  17.4 3.9 %dense.1 = (bf16[1024,1024]{1,0:T(8,128)(2,1)}, f32[1024,128]{1,0:T(8,128)}) custom-call(s32[96]{0:T(128)} %refs_0_.3, s32[96]{0:T(128)} %refs_1_.7, s32[1]{0:T(128)S(6)} %copy.23.refs_2_, f32[1024,128]{1,0:T(8,128)} %refs_2_.6, bf16[96,128,128]{2,1,0:T(8,128)(2,1)} %refs_4_.4, f32[1024,128]{1,0:T(8,128)} %refs_11_.2, f32[1024,128]{1,0:T(8,128)} %refs_3_.10), custom_call_target="tpu_custom_call" | custom-call | flops 536870912 | bytes 7340804 | tf_op jit(solution)/shard_map/dense/pallas_call | solution.py:106
  21.4 2.7 %primal_step.2 = (bf16[8,128,128]{2,1,0:T(8,128)(2,1)}, bf16[128,128]{1,0:T(8,128)(2,1)}, bf16[8,128,128]{2,1,0:T(8,128)(2,1)}, f32[1024,128]{1,0:T(8,128)}, bf16[2,128,128]{2,1,0:T(8,128)(2,1)}) custom-call(s32[8]{0:T(128)} %refs_0_.5, s32[8]{0:T(128)} %refs_1_.10, f32[8,128]{1,0:T(8,128)} %bitcast.4, bf16[8,128,128]{2,1,0:T(8,128)(2,1)} %refs_3_.11, ...), custom_call_target="tpu_custom_call" | custom-call | flops 67108864 | bytes 3084352 | tf_op jit(solution)/shard_map/primal_step/pallas_call | solution.py:106
  24.2 4.1 %all-to-all-start.1 = ((bf16[8,128,128]{2,1,0:T(8,128)(2,1)}), bf16[8,128,128]{2,1,0:T(8,128)(2,1)}, u32[]{:S(2)}, u32[]{:S(2)}) async-start(bf16[8,128,128]{2,1,0:T(8,128)(2,1)} %get-tuple-element.40), calls=%async_computation.1 | async-start | bytes 524288 | tf_op jit(solution)/shard_map/all_to_all | solution.py:520
  28.2 1.2 %collective-permute-start.6 = (bf16[2,128,128]{2,1,0:T(8,128)(2,1)}, bf16[2,128,128]{2,1,0:T(8,128)(2,1)}, u32[]{:S(2)}, u32[]{:S(2)}) collective-permute-start(bf16[2,128,128]{2,1,0:T(8,128)(2,1)} %get-tuple-element.38.refs_4_), channel_id=1, source_target_pairs={{0,3},{1,2},{2,1},{3,0},{4,7},{5,6},{6,5},{7,4},{8,11},{9,10},{10,... | collective-permute-start | bytes 196616 | tf_op jit(solution)/shard_map/ppermute | solution.py:413
  29.4 0.5 collective-permute-start.5
  29.9 0.2 collective-permute-start.4
  30.2 1.8 %collective-permute-start.7 = (bf16[128,128]{1,0:T(8,128)(2,1)}, bf16[128,128]{1,0:T(8,128)(2,1)}, u32[]{:S(2)}, u32[]{:S(2)}) collective-permute-start(bf16[128,128]{1,0:T(8,128)(2,1)} %get-tuple-element.39), channel_id=1, source_target_pairs={{28,0},{0,4},{4,8},{8,12},{12,16},{16,20},{20,24},{24,28},{29,1},{... | collective-permute-start | bytes 98312 | tf_op jit(solution)/shard_map/ppermute | solution.py:407
  32.0 3.4 %forward.1.refs_13_ = f32[1024,128]{1,0:T(8,128)} custom-call(bf16[8,128,128]{2,1,0:T(8,128)(2,1)} %get-tuple-element.41.refs_0_, f32[8,128]{1,0:T(8,128)} %bitcast.6, f32[1024,128]{1,0:T(8,128)} %refs_2_.6, bf16[1024,1024]{1,0:T(8,128)(2,1)} %get-tuple-element.42.refs_3_.refs_1_.refs_11_), custom_call_target="tpu_custom_call" | custom-call | flops 4294967296 | bytes 3411968 | tf_op jit(solution)/shard_map/forward/pallas_call | solution.py:106
  35.4 3.3 %collective-permute-done.7.refs_9_ = bf16[128,128]{1,0:T(8,128)(2,1)} collective-permute-done((bf16[128,128]{1,0:T(8,128)(2,1)}, bf16[128,128]{1,0:T(8,128)(2,1)}, u32[]{:S(2)}, u32[]{:S(2)}) %collective-permute-start.7) | collective-permute-done | bytes 32800 | tf_op jit(solution)/shard_map/ppermute | solution.py:407
  38.7 2.8 %dual_step.1 = (f32[1024,128]{1,0:T(8,128)}, f32[128,128]{1,0:T(8,128)}, bf16[8,128,128]{2,1,0:T(8,128)(2,1)}, f32[2,128,128]{2,1,0:T(8,128)}, bf16[2,128,128]{2...) custom-call(s32[1]{0:T(128)} %bitcast.1.refs_0_, ...), custom_call_target="tpu_custom_call" | custom-call | flops 67108864 | bytes 2654784 | tf_op jit(solution)/shard_map/dual_step/pallas_call | solution.py:106
  41.5 4.1 %all-to-all-start.2 = ((bf16[8,128,128]{2,1,0:T(8,128)(2,1)}), bf16[8,128,128]{2,1,0:T(8,128)(2,1)}, u32[]{:S(2)}, u32[]{:S(2)}) async-start(bf16[8,128,128]{2,1,0:T(8,128)(2,1)} %get-tuple-element.43), calls=%async_computation.2 | async-start | bytes 524288 | tf_op jit(solution)/shard_map/all_to_all | solution.py:481
  45.6 0.1 collective-permute-start.9
  45.7 1.6 %collective-permute-start.10 = (bf16[2,128,128]{2,1,0:T(8,128)(2,1)}, bf16[2,128,128]{2,1,0:T(8,128)(2,1)}, u32[]{:S(2)}, u32[]{:S(2)}) collective-permute-start(bf16[2,128,128]{2,1,0:T(8,128)(2,1)} %get-tuple-element.47), channel_id=1, source_target_pairs={{0,2},{1,3},{2,0},{3,1},{4,6},{5,7},{6,4},{7,5},{8,10},{9,11},{10,... | collective-permute-start | bytes 196616 | tf_op jit(solution)/shard_map/ppermute | solution.py:413
  47.2 0.3 collective-permute-start.11
  47.5 4.6 %collective-permute-start.8 = (bf16[128,128]{1,0:T(8,128)(2,1)}, bf16[128,128]{1,0:T(8,128)(2,1)}, u32[]{:S(2)}, u32[]{:S(2)}) collective-permute-start(bf16[128,128]{1,0:T(8,128)(2,1)} %get-tuple-element.45), channel_id=1, source_target_pairs={{4,0},{8,4},{12,8},{16,12},{20,16},{24,20},{28,24},{0,28},{5,1},{9... | collective-permute-start | bytes 98312 | tf_op jit(solution)/shard_map/ppermute | solution.py:407
  52.1 3.3 %adjoint.1.refs_10_ = f32[1024,128]{1,0:T(8,128)} custom-call(f32[1024,128]{1,0:T(8,128)} %get-tuple-element.49.refs_0_.refs_9_, bf16[1024,1024]{1,0:T(8,128)(2,1)} %get-tuple-element.42.refs_3_.refs_1_.refs_11_, f32[1024,128]{1,0:T(8,128)} %get-tuple-element.50.refs_2_.refs_11_, f32[1024,128]{1,0:T(8,128)} %refs_3_.10), custom_call_target="tpu_custom_call" | custom-call | flops 536870912 | bytes 4194304 | tf_op jit(solution)/shard_map/adjoint/pallas_call | solution.py:106
  55.4 2.7 %primal_step.3 = (bf16[8,128,128]{2,1,0:T(8,128)(2,1)}, bf16[128,128]{1,0:T(8,128)(2,1)}, bf16[8,128,128]{2,1,0:T(8,128)(2,1)}, f32[1024,128]{1,0:T(8,128)}, bf16[2,128,128]{2,1,0:T(8,128)(2,1)}) custom-call(s32[8]{0:T(128)} %refs_0_.5, s32[8]{0:T(128)} %refs_1_.10, f32[8,128]{1,0:T(8,128)} %bitcast.5, bf16[8,128,128]{2,1,0:T(8,128)(2,1)} %refs_3_.11, ...), custom_call_target="tpu_custom_call" | custom-call | flops 67108864 | bytes 3084352 | tf_op jit(solution)/shard_map/primal_step/pallas_call | solution.py:106
  58.2 4.9 %all-to-all-start.3 = ((bf16[8,128,128]{2,1,0:T(8,128)(2,1)}), bf16[8,128,128]{2,1,0:T(8,128)(2,1)}, u32[]{:S(2)}, u32[]{:S(2)}) async-start(bf16[8,128,128]{2,1,0:T(8,128)(2,1)} %get-tuple-element.55), calls=%async_computation.3 | async-start | bytes 524288 | tf_op jit(solution)/shard_map/all_to_all | solution.py:520
  63.1 0.3 collective-permute-start.14
  63.4 1.2 %collective-permute-start.13 = (bf16[2,128,128]{2,1,0:T(8,128)(2,1)}, bf16[2,128,128]{2,1,0:T(8,128)(2,1)}, u32[]{:S(2)}, u32[]{:S(2)}) collective-permute-start(bf16[2,128,128]{2,1,0:T(8,128)(2,1)} %get-tuple-element.52.refs_5_), channel_id=1, source_target_pairs={{0,2},{1,3},{2,0},{3,1},{4,6},{5,7},{6,4},{7,5},{8,10},{9,11},{10,... | collective-permute-start | bytes 196616 | tf_op jit(solution)/shard_map/ppermute | solution.py:413
  64.6 0.3 collective-permute-start.12
  64.9 2.0 %collective-permute-start.15 = (bf16[128,128]{1,0:T(8,128)(2,1)}, bf16[128,128]{1,0:T(8,128)(2,1)}, u32[]{:S(2)}, u32[]{:S(2)}) collective-permute-start(bf16[128,128]{1,0:T(8,128)(2,1)} %get-tuple-element.56), channel_id=1, source_target_pairs={{28,0},{0,4},{4,8},{8,12},{12,16},{16,20},{20,24},{24,28},{29,1},{... | collective-permute-start | bytes 98312 | tf_op jit(solution)/shard_map/ppermute | solution.py:407
  67.0 0.8 %collective-permute-done.14.refs_8_ = bf16[2,128,128]{2,1,0:T(8,128)(2,1)} collective-permute-done((bf16[2,128,128]{2,1,0:T(8,128)(2,1)}, bf16[2,128,128]{2,1,0:T(8,128)(2,1)}, u32[]{:S(2)}, u32[]{:S(2)}) %collective-permute-start.14) | collective-permute-done | bytes 65568 | tf_op jit(solution)/shard_map/ppermute | solution.py:413
  67.8 1.4 %collective-permute-done.13.refs_7_ = bf16[2,128,128]{2,1,0:T(8,128)(2,1)} collective-permute-done((bf16[2,128,128]{2,1,0:T(8,128)(2,1)}, bf16[2,128,128]{2,1,0:T(8,128)(2,1)}, u32[]{:S(2)}, u32[]{:S(2)}) %collective-permute-start.13) | collective-permute-done | bytes 65568 | tf_op jit(solution)/shard_map/ppermute | solution.py:413
  69.2 3.5 %last_rows.1.row = f32[1024,128]{1,0:T(8,128)} custom-call(s32[1]{0:T(128)} %bitcast.1.refs_0_, s32[8]{0:T(128)} %refs_1_.11, s32[8]{0:T(128)} %refs_2_.8, f32[8,128]{1,0:T(8,128)} %bitcast.7, bf16[8,128,128]{2,1,0:T(8,128)(2,1)} %refs_4_.5, bf16[2,128,128]{2,1,0:T(8,128)(2,1)} %get-tuple-element.52.refs_5_, ...), custom_call_target="tpu_custom_call" | custom-call | flops 4194304 | bytes 3936320 | tf_op jit(solution)/shard_map/last_rows/pallas_call | solution.py:106
  72.7 1.9 %finish.1 = (f32[1024,128]{1,0:T(8,128)}, f32[128,128]{1,0:T(8,128)}) custom-call(f32[1024,128]{1,0:T(8,128)} %last_rows.1.row, f32[128,128]{1,0:T(8,128)} %get-tuple-element.54.annual, f32[1,128]{1,0:T(1,128)} %bitcast.9, bf16[8,128,128]{2,1,0:T(8,128)(2,1)} %all-to-all-done.3.parts, bf16[1,128,128]{2,1,0:T(8,128)(2,1)} %carry.1, ...), custom_call_target="tpu_custom_call", output_to_operand_aliasing={{0}: (0, {})} | custom-call | flops 4194304 | bytes 1000000 | tf_op jit(solution)/shard_map/finish/pallas_call | solution.py:388
  (17 shorter events, 0.0 us)
Async XLA Ops:
  2.9 18.5 %all-to-all-start = ((bf16[8,128,128]{2,1,0:T(8,128)(2,1)}), bf16[8,128,128]{2,1,0:T(8,128)(2,1)}, u32[]{:S(2)}, u32[]{:S(2)}) async-start(bf16[8,128,128]{2,1,0:T(8,128)(2,1)} %get-tuple-element.31), calls=%async_computation | async-start | bytes 524288 | tf_op jit(solution)/shard_map/all_to_all | solution.py:481
  10.2 11.2 %collective-permute-start.1 = (bf16[2,128,128]{2,1,0:T(8,128)(2,1)}, bf16[2,128,128]{2,1,0:T(8,128)(2,1)}, u32[]{:S(2)}, u32[]{:S(2)}) collective-permute-start(bf16[2,128,128]{2,1,0:T(8,128)(2,1)} %get-tuple-element.34), channel_id=1, source_target_pairs={{0,1},{1,0},{2,3},{3,2},{4,5},{5,4},{6,7},{7,6},{8,9},{9,8},{10,11... | collective-permute-start | bytes 196616 | tf_op jit(solution)/shard_map/ppermute | solution.py:413
  10.2 11.2 %collective-permute-start.2 = (bf16[2,128,128]{2,1,0:T(8,128)(2,1)}, bf16[2,128,128]{2,1,0:T(8,128)(2,1)}, u32[]{:S(2)}, u32[]{:S(2)}) collective-permute-start(bf16[2,128,128]{2,1,0:T(8,128)(2,1)} %get-tuple-element.35), channel_id=1, source_target_pairs={{0,2},{1,3},{2,0},{3,1},{4,6},{5,7},{6,4},{7,5},{8,10},{9,11},{10,... | collective-permute-start | bytes 196616 | tf_op jit(solution)/shard_map/ppermute | solution.py:413
  11.8 9.6 %collective-permute-start.3 = (bf16[2,128,128]{2,1,0:T(8,128)(2,1)}, bf16[2,128,128]{2,1,0:T(8,128)(2,1)}, u32[]{:S(2)}, u32[]{:S(2)}) collective-permute-start(bf16[2,128,128]{2,1,0:T(8,128)(2,1)} %get-tuple-element.36), channel_id=1, source_target_pairs={{0,3},{1,2},{2,1},{3,0},{4,7},{5,6},{6,5},{7,4},{8,11},{9,10},{10,... | collective-permute-start | bytes 196616 | tf_op jit(solution)/shard_map/ppermute | solution.py:413
  12.1 9.3 %collective-permute-start = (bf16[128,128]{1,0:T(8,128)(2,1)}, bf16[128,128]{1,0:T(8,128)(2,1)}, u32[]{:S(2)}, u32[]{:S(2)}) collective-permute-start(bf16[128,128]{1,0:T(8,128)(2,1)} %get-tuple-element.33), channel_id=1, source_target_pairs={{4,0},{8,4},{12,8},{16,12},{20,16},{24,20},{28,24},{0,28},{5,1},{9... | collective-permute-start | bytes 98312 | tf_op jit(solution)/shard_map/ppermute | solution.py:407
  24.2 14.5 %all-to-all-start.1 = ((bf16[8,128,128]{2,1,0:T(8,128)(2,1)}), bf16[8,128,128]{2,1,0:T(8,128)(2,1)}, u32[]{:S(2)}, u32[]{:S(2)}) async-start(bf16[8,128,128]{2,1,0:T(8,128)(2,1)} %get-tuple-element.40), calls=%async_computation.1 | async-start | bytes 524288 | tf_op jit(solution)/shard_map/all_to_all | solution.py:520
  28.2 10.4 %collective-permute-start.6 = (bf16[2,128,128]{2,1,0:T(8,128)(2,1)}, bf16[2,128,128]{2,1,0:T(8,128)(2,1)}, u32[]{:S(2)}, u32[]{:S(2)}) collective-permute-start(bf16[2,128,128]{2,1,0:T(8,128)(2,1)} %get-tuple-element.38.refs_4_), channel_id=1, source_target_pairs={{0,3},{1,2},{2,1},{3,0},{4,7},{5,6},{6,5},{7,4},{8,11},{9,10},{10,... | collective-permute-start | bytes 196616 | tf_op jit(solution)/shard_map/ppermute | solution.py:413
  29.4 9.3 %collective-permute-start.5 = (bf16[2,128,128]{2,1,0:T(8,128)(2,1)}, bf16[2,128,128]{2,1,0:T(8,128)(2,1)}, u32[]{:S(2)}, u32[]{:S(2)}) collective-permute-start(bf16[2,128,128]{2,1,0:T(8,128)(2,1)} %get-tuple-element.38.refs_4_), channel_id=1, source_target_pairs={{0,2},{1,3},{2,0},{3,1},{4,6},{5,7},{6,4},{7,5},{8,10},{9,11},{10,... | collective-permute-start | bytes 196616 | tf_op jit(solution)/shard_map/ppermute | solution.py:413
  29.9 8.7 %collective-permute-start.4 = (bf16[2,128,128]{2,1,0:T(8,128)(2,1)}, bf16[2,128,128]{2,1,0:T(8,128)(2,1)}, u32[]{:S(2)}, u32[]{:S(2)}) collective-permute-start(bf16[2,128,128]{2,1,0:T(8,128)(2,1)} %get-tuple-element.38.refs_4_), channel_id=1, source_target_pairs={{0,1},{1,0},{2,3},{3,2},{4,5},{5,4},{6,7},{7,6},{8,9},{9,8},{10,11... | collective-permute-start | bytes 196616 | tf_op jit(solution)/shard_map/ppermute | solution.py:413
  30.2 8.5 %collective-permute-start.7 = (bf16[128,128]{1,0:T(8,128)(2,1)}, bf16[128,128]{1,0:T(8,128)(2,1)}, u32[]{:S(2)}, u32[]{:S(2)}) collective-permute-start(bf16[128,128]{1,0:T(8,128)(2,1)} %get-tuple-element.39), channel_id=1, source_target_pairs={{28,0},{0,4},{4,8},{8,12},{12,16},{16,20},{20,24},{24,28},{29,1},{... | collective-permute-start | bytes 98312 | tf_op jit(solution)/shard_map/ppermute | solution.py:407
  41.5 13.9 %all-to-all-start.2 = ((bf16[8,128,128]{2,1,0:T(8,128)(2,1)}), bf16[8,128,128]{2,1,0:T(8,128)(2,1)}, u32[]{:S(2)}, u32[]{:S(2)}) async-start(bf16[8,128,128]{2,1,0:T(8,128)(2,1)} %get-tuple-element.43), calls=%async_computation.2 | async-start | bytes 524288 | tf_op jit(solution)/shard_map/all_to_all | solution.py:481
  45.6 9.8 %collective-permute-start.9 = (bf16[2,128,128]{2,1,0:T(8,128)(2,1)}, bf16[2,128,128]{2,1,0:T(8,128)(2,1)}, u32[]{:S(2)}, u32[]{:S(2)}) collective-permute-start(bf16[2,128,128]{2,1,0:T(8,128)(2,1)} %get-tuple-element.46), channel_id=1, source_target_pairs={{0,1},{1,0},{2,3},{3,2},{4,5},{5,4},{6,7},{7,6},{8,9},{9,8},{10,11... | collective-permute-start | bytes 196616 | tf_op jit(solution)/shard_map/ppermute | solution.py:413
  45.7 9.7 %collective-permute-start.10 = (bf16[2,128,128]{2,1,0:T(8,128)(2,1)}, bf16[2,128,128]{2,1,0:T(8,128)(2,1)}, u32[]{:S(2)}, u32[]{:S(2)}) collective-permute-start(bf16[2,128,128]{2,1,0:T(8,128)(2,1)} %get-tuple-element.47), channel_id=1, source_target_pairs={{0,2},{1,3},{2,0},{3,1},{4,6},{5,7},{6,4},{7,5},{8,10},{9,11},{10,... | collective-permute-start | bytes 196616 | tf_op jit(solution)/shard_map/ppermute | solution.py:413
  47.2 8.2 %collective-permute-start.11 = (bf16[2,128,128]{2,1,0:T(8,128)(2,1)}, bf16[2,128,128]{2,1,0:T(8,128)(2,1)}, u32[]{:S(2)}, u32[]{:S(2)}) collective-permute-start(bf16[2,128,128]{2,1,0:T(8,128)(2,1)} %get-tuple-element.48), channel_id=1, source_target_pairs={{0,3},{1,2},{2,1},{3,0},{4,7},{5,6},{6,5},{7,4},{8,11},{9,10},{10,... | collective-permute-start | bytes 196616 | tf_op jit(solution)/shard_map/ppermute | solution.py:413
  47.5 7.8 %collective-permute-start.8 = (bf16[128,128]{1,0:T(8,128)(2,1)}, bf16[128,128]{1,0:T(8,128)(2,1)}, u32[]{:S(2)}, u32[]{:S(2)}) collective-permute-start(bf16[128,128]{1,0:T(8,128)(2,1)} %get-tuple-element.45), channel_id=1, source_target_pairs={{4,0},{8,4},{12,8},{16,12},{20,16},{24,20},{28,24},{0,28},{5,1},{9... | collective-permute-start | bytes 98312 | tf_op jit(solution)/shard_map/ppermute | solution.py:407
  58.2 14.5 %all-to-all-start.3 = ((bf16[8,128,128]{2,1,0:T(8,128)(2,1)}), bf16[8,128,128]{2,1,0:T(8,128)(2,1)}, u32[]{:S(2)}, u32[]{:S(2)}) async-start(bf16[8,128,128]{2,1,0:T(8,128)(2,1)} %get-tuple-element.55), calls=%async_computation.3 | async-start | bytes 524288 | tf_op jit(solution)/shard_map/all_to_all | solution.py:520
  63.1 4.7 %collective-permute-start.14 = (bf16[2,128,128]{2,1,0:T(8,128)(2,1)}, bf16[2,128,128]{2,1,0:T(8,128)(2,1)}, u32[]{:S(2)}, u32[]{:S(2)}) collective-permute-start(bf16[2,128,128]{2,1,0:T(8,128)(2,1)} %get-tuple-element.52.refs_5_), channel_id=1, source_target_pairs={{0,3},{1,2},{2,1},{3,0},{4,7},{5,6},{6,5},{7,4},{8,11},{9,10},{10,... | collective-permute-start | bytes 196616 | tf_op jit(solution)/shard_map/ppermute | solution.py:413
  63.4 5.8 %collective-permute-start.13 = (bf16[2,128,128]{2,1,0:T(8,128)(2,1)}, bf16[2,128,128]{2,1,0:T(8,128)(2,1)}, u32[]{:S(2)}, u32[]{:S(2)}) collective-permute-start(bf16[2,128,128]{2,1,0:T(8,128)(2,1)} %get-tuple-element.52.refs_5_), channel_id=1, source_target_pairs={{0,2},{1,3},{2,0},{3,1},{4,6},{5,7},{6,4},{7,5},{8,10},{9,11},{10,... | collective-permute-start | bytes 196616 | tf_op jit(solution)/shard_map/ppermute | solution.py:413
  64.6 4.6 %collective-permute-start.12 = (bf16[2,128,128]{2,1,0:T(8,128)(2,1)}, bf16[2,128,128]{2,1,0:T(8,128)(2,1)}, u32[]{:S(2)}, u32[]{:S(2)}) collective-permute-start(bf16[2,128,128]{2,1,0:T(8,128)(2,1)} %get-tuple-element.52.refs_5_), channel_id=1, source_target_pairs={{0,1},{1,0},{2,3},{3,2},{4,5},{5,4},{6,7},{7,6},{8,9},{9,8},{10,11... | collective-permute-start | bytes 196616 | tf_op jit(solution)/shard_map/ppermute | solution.py:413
  64.9 7.8 %collective-permute-start.15 = (bf16[128,128]{1,0:T(8,128)(2,1)}, bf16[128,128]{1,0:T(8,128)(2,1)}, u32[]{:S(2)}, u32[]{:S(2)}) collective-permute-start(bf16[128,128]{1,0:T(8,128)(2,1)} %get-tuple-element.56), channel_id=1, source_target_pairs={{28,0},{0,4},{4,8},{8,12},{12,16},{16,20},{20,24},{24,28},{29,1},{... | collective-permute-start | bytes 98312 | tf_op jit(solution)/shard_map/ppermute | solution.py:407

commit v11 on v10

--- a/solution.py
+++ b/solution.py
@@ -216,12 +216,13 @@
 
 
 def adjoint_body(size, scalars, ins, outs):
-    dual, matrix, primal, prices = ins
+    dual, matrix, primal, prices, carried = ins
     adjoint(matrix(), turned_blocks(dual(), size), size, primal, prices, outs[0])
-
-
-def primal_body(scalars, ins, outs, acc, image_acc, product, bound):
-    ids, cols, upper, annual, annual_q, own, carried, *arrived, partial, primal = ins
+    outs[0].ref[-size:] += PRIMAL_STEP * carried()[...].astype(F32)
+
+
+def primal_body(with_carry, scalars, ins, outs, acc, image_acc, product, bound):
+    ids, cols, upper, annual, annual_q, own, *arrived, partial, primal = ins
     image, last, extrap, updated, streams = outs
     blocks, size, _ = extrap.ref.shape
     acc[...] = jnp.zeros_like(acc)
@@ -235,11 +236,12 @@
         product[k] = dot_transposed(annual[k], annual_q[ids[k]])
     for k in range(slots):
         acc[cols[k]] += product[k]
+    if with_carry:
+        acc[blocks - 1] += arrived.pop(0)()[...].astype(F32)
     total = own()[...]
     for piece in arrived:
         total = total + piece()[...].astype(F32)
     acc[:SC] += total
-    acc[blocks - 1] += carried()[...].astype(F32)
     partial, primal = partial(), primal()
     for j in range(blocks):
         at = slice(j * size, (j + 1) * size)
@@ -480,7 +482,8 @@
         sends, carried = rest[:others], rest[others]
         annual_q = lax.all_to_all(annual_send, "period", 0, 0, tiled=True)
         carried_back = shifted(carried, "period", -1)
-        arrived = [exchanged(send, "refinery", d) for d, send in enumerate(sends, 1)]
+        carries = [carried_back] if iteration == 0 else []
+        arrived = carries + [exchanged(send, "refinery", d) for d, send in enumerate(sends, 1)]
         if iteration == 0:
             matrix_q, partial_x = run(
                 functools.partial(dense_body, chunks),
@@ -498,16 +501,16 @@
                 functools.partial(adjoint_body, size),
                 "adjoint",
                 [],
-                [dual, matrix_q, primal, cost],
+                [dual, matrix_q, primal, cost, carried_back],
                 [state_x],
                 [],
-                2 * rows * columns * unit,
+                90 * rows * columns * unit,
             )
         image, last, extrap, updated, streams = run(
-            primal_body,
+            functools.partial(primal_body, iteration == 0),
             "primal_step",
             [],
-            [annual_ids, annual_cols, upper_rows, annual_blocks, annual_q, own, carried_back, *arrived, partial_x, primal],
+            [annual_ids, annual_cols, upper_rows, annual_blocks, annual_q, own, *arrived, partial_x, primal],
             [weekly, tile, blocks_x, state_x, pair_q],
             [
                 pltpu.VMEM((columns, size, scenarios), F32),

time: 75.3 us -> 74.9 us (level)
  starting transfers between devices: 41 us -> 37 us
  waiting for transfers between devices: 5.53 us -> 9.2 us
    ppermute x4, starting transfers between devices: 13.1 us -> 9.87 us  [shifted(): return lax.ppermute(block, axis, route)]
    all_to_all x2, waiting for transfers between devices: 0.01 us -> 2.68 us  [body(): annual_q = lax.all_to_all(annual_send, 'period', 0, 0, tiled=True)]
    ppermute x12, waiting for transfers between devices: 2.25 us -> 3.17 us  [exchanged(): return lax.ppermute(block, axis, [(i, i ^ d) for i in range(number)])]
    all_to_all x2, starting transfers between devices: 8.95 us -> 8.11 us  [body(): parts = lax.all_to_all(image, 'period', 0, 0, tiled=True)]
  transfers between devices with their start and end apart: 20 -> 20, of which waited for: 3 -> 6; matrix products, arithmetic and copies ran while one was open for 0% -> 0% of each run, Pallas kernels for 19% -> 19%
where the time goes in v11:
time: 74.9 us; the launch traced here: 74.2 us
  starting transfers between devices  37 us (49%)
  Pallas kernels  26.6 us (36%)
  waiting for transfers between devices  9.2 us (12%)
  between operations  1.47 us (2%)
    pallas_call x8, Pallas kernels, run(): pl.pallas_call(kernel, name=name, in_specs=[SMEM] * ns + [HBM] * na, out_...  24.7 us
    all_to_all x2, starting transfers between devices, body(): annual_q = lax.all_to_all(annual_send, 'period', 0, 0, tiled=True)  11.3 us
    ppermute x4, starting transfers between devices, shifted(): return lax.ppermute(block, axis, route)  9.87 us
    all_to_all x2, starting transfers between devices, body(): parts = lax.all_to_all(image, 'period', 0, 0, tiled=True)  8.11 us
    ppermute x12, starting transfers between devices, exchanged(): return lax.ppermute(block, axis, [(i, i ^ d) for i in range(number)])  7.64 us
    ppermute x4, waiting for transfers between devices, shifted(): return lax.ppermute(block, axis, route)  3.34 us
    ppermute x12, waiting for transfers between devices, exchanged(): return lax.ppermute(block, axis, [(i, i ^ d) for i in range(number)])  3.17 us
    all_to_all x2, waiting for transfers between devices, body(): annual_q = lax.all_to_all(annual_send, 'period', 0, 0, tiled=True)  2.68 us
  transfers between devices with their start and end apart: 20, of which 6 were waited for; matrix products, arithmetic and copies ran while one was open for 0% of the time, Pallas kernels for 19%

profile of v11, /device:TPU:0, one launch (start us, length us, event | category | flops | bytes accessed | tf_op | source)
XLA Modules:
  0.0 74.2 jit_solution(13338045567230632207)
XLA Ops:
  0.6 2.3 %first_duals.1 = (bf16[8,128,128]{2,1,0:T(8,128)(2,1)}, f32[2,128,128]{2,1,0:T(8,128)}, bf16[2,128,128]{2,1,0:T(8,128)(2,1)}, bf16[2,128,128]{2,1,0:T(8,128)(2,1...) custom-call(s32[1]{0:T(128)} %bitcast.1.refs_0_, s32[8]{0:T(128)} %refs_1_.11, s32[8]{0:T(128)} %refs_2_.8, ...), custom_call_target="tpu_custom_call" | custom-call | flops 37748736 | bytes 1507392 | tf_op jit(solution)/shard_map/first_duals/pallas_call | solution.py:106
  2.9 7.3 %all-to-all-start = ((bf16[8,128,128]{2,1,0:T(8,128)(2,1)}), bf16[8,128,128]{2,1,0:T(8,128)(2,1)}, u32[]{:S(2)}, u32[]{:S(2)}) async-start(bf16[8,128,128]{2,1,0:T(8,128)(2,1)} %get-tuple-element.31), calls=%async_computation | async-start | bytes 524288 | tf_op jit(solution)/shard_map/all_to_all | solution.py:483
  10.2 1.6 %collective-permute-start.2 = (bf16[2,128,128]{2,1,0:T(8,128)(2,1)}, bf16[2,128,128]{2,1,0:T(8,128)(2,1)}, u32[]{:S(2)}, u32[]{:S(2)}) collective-permute-start(bf16[2,128,128]{2,1,0:T(8,128)(2,1)} %get-tuple-element.35), channel_id=1, source_target_pairs={{0,2},{1,3},{2,0},{3,1},{4,6},{5,7},{6,4},{7,5},{8,10},{9,11},{10,... | collective-permute-start | bytes 196616 | tf_op jit(solution)/shard_map/ppermute | solution.py:415
  11.8 0.3 collective-permute-start.3
  12.1 4.7 %collective-permute-start = (bf16[128,128]{1,0:T(8,128)(2,1)}, bf16[128,128]{1,0:T(8,128)(2,1)}, u32[]{:S(2)}, u32[]{:S(2)}) collective-permute-start(bf16[128,128]{1,0:T(8,128)(2,1)} %get-tuple-element.33), channel_id=1, source_target_pairs={{4,0},{8,4},{12,8},{16,12},{20,16},{24,20},{28,24},{0,28},{5,1},{9... | collective-permute-start | bytes 98312 | tf_op jit(solution)/shard_map/ppermute | solution.py:409
  17.4 3.9 %dense.1 = (bf16[1024,1024]{1,0:T(8,128)(2,1)}, f32[1024,128]{1,0:T(8,128)}) custom-call(s32[96]{0:T(128)} %refs_0_.3, s32[96]{0:T(128)} %refs_1_.7, s32[1]{0:T(128)S(6)} %copy.23.refs_2_, f32[1024,128]{1,0:T(8,128)} %refs_2_.6, bf16[96,128,128]{2,1,0:T(8,128)(2,1)} %refs_4_.4, f32[1024,128]{1,0:T(8,128)} %refs_11_.2, f32[1024,128]{1,0:T(8,128)} %refs_3_.10), custom_call_target="tpu_custom_call" | custom-call | flops 536870912 | bytes 7340804 | tf_op jit(solution)/shard_map/dense/pallas_call | solution.py:106
  21.4 2.7 %primal_step.2 = (bf16[8,128,128]{2,1,0:T(8,128)(2,1)}, bf16[128,128]{1,0:T(8,128)(2,1)}, bf16[8,128,128]{2,1,0:T(8,128)(2,1)}, f32[1024,128]{1,0:T(8,128)}, bf16[2,128,128]{2,1,0:T(8,128)(2,1)}) custom-call(s32[8]{0:T(128)} %refs_0_.5, s32[8]{0:T(128)} %refs_1_.10, f32[8,128]{1,0:T(8,128)} %bitcast.4, bf16[8,128,128]{2,1,0:T(8,128)(2,1)} %refs_3_.11, ...), custom_call_target="tpu_custom_call" | custom-call | flops 67108864 | bytes 3084352 | tf_op jit(solution)/shard_map/primal_step/pallas_call | solution.py:106
  24.2 4.1 %all-to-all-start.1 = ((bf16[8,128,128]{2,1,0:T(8,128)(2,1)}), bf16[8,128,128]{2,1,0:T(8,128)(2,1)}, u32[]{:S(2)}, u32[]{:S(2)}) async-start(bf16[8,128,128]{2,1,0:T(8,128)(2,1)} %get-tuple-element.40), calls=%async_computation.1 | async-start | bytes 524288 | tf_op jit(solution)/shard_map/all_to_all | solution.py:523
  28.2 1.2 %collective-permute-start.6 = (bf16[2,128,128]{2,1,0:T(8,128)(2,1)}, bf16[2,128,128]{2,1,0:T(8,128)(2,1)}, u32[]{:S(2)}, u32[]{:S(2)}) collective-permute-start(bf16[2,128,128]{2,1,0:T(8,128)(2,1)} %get-tuple-element.38.refs_4_), channel_id=1, source_target_pairs={{0,3},{1,2},{2,1},{3,0},{4,7},{5,6},{6,5},{7,4},{8,11},{9,10},{10,... | collective-permute-start | bytes 196616 | tf_op jit(solution)/shard_map/ppermute | solution.py:415
  29.4 0.5 collective-permute-start.5
  29.9 0.2 collective-permute-start.4
  30.2 1.8 %collective-permute-start.7 = (bf16[128,128]{1,0:T(8,128)(2,1)}, bf16[128,128]{1,0:T(8,128)(2,1)}, u32[]{:S(2)}, u32[]{:S(2)}) collective-permute-start(bf16[128,128]{1,0:T(8,128)(2,1)} %get-tuple-element.39), channel_id=1, source_target_pairs={{28,0},{0,4},{4,8},{8,12},{12,16},{16,20},{20,24},{24,28},{29,1},{... | collective-permute-start | bytes 98312 | tf_op jit(solution)/shard_map/ppermute | solution.py:409
  32.0 3.4 %forward.1.refs_13_ = f32[1024,128]{1,0:T(8,128)} custom-call(bf16[8,128,128]{2,1,0:T(8,128)(2,1)} %get-tuple-element.41.refs_0_, f32[8,128]{1,0:T(8,128)} %bitcast.6, f32[1024,128]{1,0:T(8,128)} %refs_2_.6, bf16[1024,1024]{1,0:T(8,128)(2,1)} %get-tuple-element.42.refs_3_.refs_1_.refs_11_), custom_call_target="tpu_custom_call" | custom-call | flops 4294967296 | bytes 3411968 | tf_op jit(solution)/shard_map/forward/pallas_call | solution.py:106
  35.4 3.3 %collective-permute-done.7.refs_9_ = bf16[128,128]{1,0:T(8,128)(2,1)} collective-permute-done((bf16[128,128]{1,0:T(8,128)(2,1)}, bf16[128,128]{1,0:T(8,128)(2,1)}, u32[]{:S(2)}, u32[]{:S(2)}) %collective-permute-start.7) | collective-permute-done | bytes 32800 | tf_op jit(solution)/shard_map/ppermute | solution.py:409
  38.7 2.8 %dual_step.1 = (f32[1024,128]{1,0:T(8,128)}, f32[128,128]{1,0:T(8,128)}, bf16[8,128,128]{2,1,0:T(8,128)(2,1)}, f32[2,128,128]{2,1,0:T(8,128)}, bf16[2,128,128]{2...) custom-call(s32[1]{0:T(128)} %bitcast.1.refs_0_, ...), custom_call_target="tpu_custom_call" | custom-call | flops 67108864 | bytes 2654784 | tf_op jit(solution)/shard_map/dual_step/pallas_call | solution.py:106
  41.5 1.5 %collective-permute-start.11 = (bf16[128,128]{1,0:T(8,128)(2,1)}, bf16[128,128]{1,0:T(8,128)(2,1)}, u32[]{:S(2)}, u32[]{:S(2)}) collective-permute-start(bf16[128,128]{1,0:T(8,128)(2,1)} %get-tuple-element.50), channel_id=1, source_target_pairs={{4,0},{8,4},{12,8},{16,12},{20,16},{24,20},{28,24},{0,28},{5,1},{9... | collective-permute-start | bytes 98312 | tf_op jit(solution)/shard_map/ppermute | solution.py:409
  43.0 4.0 %all-to-all-start.2 = ((bf16[8,128,128]{2,1,0:T(8,128)(2,1)}), bf16[8,128,128]{2,1,0:T(8,128)(2,1)}, u32[]{:S(2)}, u32[]{:S(2)}) async-start(bf16[8,128,128]{2,1,0:T(8,128)(2,1)} %get-tuple-element.43), calls=%async_computation.2 | async-start | bytes 524288 | tf_op jit(solution)/shard_map/all_to_all | solution.py:483
  47.2 1.6 %collective-permute-start.9 = (bf16[2,128,128]{2,1,0:T(8,128)(2,1)}, bf16[2,128,128]{2,1,0:T(8,128)(2,1)}, u32[]{:S(2)}, u32[]{:S(2)}) collective-permute-start(bf16[2,128,128]{2,1,0:T(8,128)(2,1)} %get-tuple-element.46), channel_id=1, source_target_pairs={{0,2},{1,3},{2,0},{3,1},{4,6},{5,7},{6,4},{7,5},{8,10},{9,11},{10,... | collective-permute-start | bytes 196616 | tf_op jit(solution)/shard_map/ppermute | solution.py:415
  48.7 0.3 collective-permute-start.10
  49.0 3.3 %adjoint.1.refs_9_ = f32[1024,128]{1,0:T(8,128)} custom-call(f32[1024,128]{1,0:T(8,128)} %get-tuple-element.48.refs_0_.refs_9_, bf16[1024,1024]{1,0:T(8,128)(2,1)} %get-tuple-element.42.refs_3_.refs_1_.refs_11_, f32[1024,128]{1,0:T(8,128)} %get-tuple-element.49.refs_2_.refs_10_, f32[1024,128]{1,0:T(8,128)} %refs_3_.10, ...), custom_call_target="tpu_custom_call" | custom-call | flops 24159191040 | bytes 4227072 | tf_op jit(solution)/shard_map/adjoint/pallas_call | solution.py:106
  52.4 0.7 collective-permute-done.10.refs_8_
  53.1 2.7 %all-to-all-done.2.refs_4_ = bf16[8,128,128]{2,1,0:T(8,128)(2,1)} async-done(((bf16[8,128,128]{2,1,0:T(8,128)(2,1)}), bf16[8,128,128]{2,1,0:T(8,128)(2,1)}, u32[]{:S(2)}, u32[]{:S(2)}) %all-to-all-start.2) | async-done | bytes 262176 | tf_op jit(solution)/shard_map/all_to_all | solution.py:483
  55.8 2.7 %primal_step.3 = (bf16[8,128,128]{2,1,0:T(8,128)(2,1)}, bf16[128,128]{1,0:T(8,128)(2,1)}, bf16[8,128,128]{2,1,0:T(8,128)(2,1)}, f32[1024,128]{1,0:T(8,128)}, bf16[2,128,128]{2,1,0:T(8,128)(2,1)}) custom-call(s32[8]{0:T(128)} %refs_0_.5, s32[8]{0:T(128)} %refs_1_.10, f32[8,128]{1,0:T(8,128)} %bitcast.5, bf16[8,128,128]{2,1,0:T(8,128)(2,1)} %refs_3_.11, ...), custom_call_target="tpu_custom_call" | custom-call | flops 67108864 | bytes 3051584 | tf_op jit(solution)/shard_map/primal_step/pallas_call | solution.py:106
  58.5 4.1 %all-to-all-start.3 = ((bf16[8,128,128]{2,1,0:T(8,128)(2,1)}), bf16[8,128,128]{2,1,0:T(8,128)(2,1)}, u32[]{:S(2)}, u32[]{:S(2)}) async-start(bf16[8,128,128]{2,1,0:T(8,128)(2,1)} %get-tuple-element.55), calls=%async_computation.3 | async-start | bytes 524288 | tf_op jit(solution)/shard_map/all_to_all | solution.py:523
  62.5 0.3 collective-permute-start.14
  62.9 1.3 %collective-permute-start.13 = (bf16[2,128,128]{2,1,0:T(8,128)(2,1)}, bf16[2,128,128]{2,1,0:T(8,128)(2,1)}, u32[]{:S(2)}, u32[]{:S(2)}) collective-permute-start(bf16[2,128,128]{2,1,0:T(8,128)(2,1)} %get-tuple-element.52.refs_5_), channel_id=1, source_target_pairs={{0,2},{1,3},{2,0},{3,1},{4,6},{5,7},{6,4},{7,5},{8,10},{9,11},{10,... | collective-permute-start | bytes 196616 | tf_op jit(solution)/shard_map/ppermute | solution.py:415
  64.2 0.3 collective-permute-start.12
  64.5 1.8 %collective-permute-start.15 = (bf16[128,128]{1,0:T(8,128)(2,1)}, bf16[128,128]{1,0:T(8,128)(2,1)}, u32[]{:S(2)}, u32[]{:S(2)}) collective-permute-start(bf16[128,128]{1,0:T(8,128)(2,1)} %get-tuple-element.56), channel_id=1, source_target_pairs={{28,0},{0,4},{4,8},{8,12},{12,16},{16,20},{20,24},{24,28},{29,1},{... | collective-permute-start | bytes 98312 | tf_op jit(solution)/shard_map/ppermute | solution.py:409
  66.3 1.0 %collective-permute-done.14.refs_8_ = bf16[2,128,128]{2,1,0:T(8,128)(2,1)} collective-permute-done((bf16[2,128,128]{2,1,0:T(8,128)(2,1)}, bf16[2,128,128]{2,1,0:T(8,128)(2,1)}, u32[]{:S(2)}, u32[]{:S(2)}) %collective-permute-start.14) | collective-permute-done | bytes 65568 | tf_op jit(solution)/shard_map/ppermute | solution.py:415
  67.3 1.5 %collective-permute-done.13.refs_7_ = bf16[2,128,128]{2,1,0:T(8,128)(2,1)} collective-permute-done((bf16[2,128,128]{2,1,0:T(8,128)(2,1)}, bf16[2,128,128]{2,1,0:T(8,128)(2,1)}, u32[]{:S(2)}, u32[]{:S(2)}) %collective-permute-start.13) | collective-permute-done | bytes 65568 | tf_op jit(solution)/shard_map/ppermute | solution.py:415
  68.7 3.5 %last_rows.1.row = f32[1024,128]{1,0:T(8,128)} custom-call(s32[1]{0:T(128)} %bitcast.1.refs_0_, s32[8]{0:T(128)} %refs_1_.11, s32[8]{0:T(128)} %refs_2_.8, f32[8,128]{1,0:T(8,128)} %bitcast.7, bf16[8,128,128]{2,1,0:T(8,128)(2,1)} %refs_4_.5, bf16[2,128,128]{2,1,0:T(8,128)(2,1)} %get-tuple-element.52.refs_5_, ...), custom_call_target="tpu_custom_call" | custom-call | flops 4194304 | bytes 3936320 | tf_op jit(solution)/shard_map/last_rows/pallas_call | solution.py:106
  72.3 1.9 %finish.1 = (f32[1024,128]{1,0:T(8,128)}, f32[128,128]{1,0:T(8,128)}) custom-call(f32[1024,128]{1,0:T(8,128)} %last_rows.1.row, f32[128,128]{1,0:T(8,128)} %get-tuple-element.54.annual, f32[1,128]{1,0:T(1,128)} %bitcast.9, bf16[8,128,128]{2,1,0:T(8,128)(2,1)} %all-to-all-done.3.parts, bf16[1,128,128]{2,1,0:T(8,128)(2,1)} %carry.1, ...), custom_call_target="tpu_custom_call", output_to_operand_aliasing={{0}: (0, {})} | custom-call | flops 4194304 | bytes 1000000 | tf_op jit(solution)/shard_map/finish/pallas_call | solution.py:390
  (17 shorter events, 0.2 us)
Async XLA Ops:
  2.9 18.5 %all-to-all-start = ((bf16[8,128,128]{2,1,0:T(8,128)(2,1)}), bf16[8,128,128]{2,1,0:T(8,128)(2,1)}, u32[]{:S(2)}, u32[]{:S(2)}) async-start(bf16[8,128,128]{2,1,0:T(8,128)(2,1)} %get-tuple-element.31), calls=%async_computation | async-start | bytes 524288 | tf_op jit(solution)/shard_map/all_to_all | solution.py:483
  10.2 11.2 %collective-permute-start.1 = (bf16[2,128,128]{2,1,0:T(8,128)(2,1)}, bf16[2,128,128]{2,1,0:T(8,128)(2,1)}, u32[]{:S(2)}, u32[]{:S(2)}) collective-permute-start(bf16[2,128,128]{2,1,0:T(8,128)(2,1)} %get-tuple-element.34), channel_id=1, source_target_pairs={{0,1},{1,0},{2,3},{3,2},{4,5},{5,4},{6,7},{7,6},{8,9},{9,8},{10,11... | collective-permute-start | bytes 196616 | tf_op jit(solution)/shard_map/ppermute | solution.py:415
  10.2 11.2 %collective-permute-start.2 = (bf16[2,128,128]{2,1,0:T(8,128)(2,1)}, bf16[2,128,128]{2,1,0:T(8,128)(2,1)}, u32[]{:S(2)}, u32[]{:S(2)}) collective-permute-start(bf16[2,128,128]{2,1,0:T(8,128)(2,1)} %get-tuple-element.35), channel_id=1, source_target_pairs={{0,2},{1,3},{2,0},{3,1},{4,6},{5,7},{6,4},{7,5},{8,10},{9,11},{10,... | collective-permute-start | bytes 196616 | tf_op jit(solution)/shard_map/ppermute | solution.py:415
  11.8 9.6 %collective-permute-start.3 = (bf16[2,128,128]{2,1,0:T(8,128)(2,1)}, bf16[2,128,128]{2,1,0:T(8,128)(2,1)}, u32[]{:S(2)}, u32[]{:S(2)}) collective-permute-start(bf16[2,128,128]{2,1,0:T(8,128)(2,1)} %get-tuple-element.36), channel_id=1, source_target_pairs={{0,3},{1,2},{2,1},{3,0},{4,7},{5,6},{6,5},{7,4},{8,11},{9,10},{10,... | collective-permute-start | bytes 196616 | tf_op jit(solution)/shard_map/ppermute | solution.py:415
  12.1 9.3 %collective-permute-start = (bf16[128,128]{1,0:T(8,128)(2,1)}, bf16[128,128]{1,0:T(8,128)(2,1)}, u32[]{:S(2)}, u32[]{:S(2)}) collective-permute-start(bf16[128,128]{1,0:T(8,128)(2,1)} %get-tuple-element.33), channel_id=1, source_target_pairs={{4,0},{8,4},{12,8},{16,12},{20,16},{24,20},{28,24},{0,28},{5,1},{9... | collective-permute-start | bytes 98312 | tf_op jit(solution)/shard_map/ppermute | solution.py:409
  24.2 14.5 %all-to-all-start.1 = ((bf16[8,128,128]{2,1,0:T(8,128)(2,1)}), bf16[8,128,128]{2,1,0:T(8,128)(2,1)}, u32[]{:S(2)}, u32[]{:S(2)}) async-start(bf16[8,128,128]{2,1,0:T(8,128)(2,1)} %get-tuple-element.40), calls=%async_computation.1 | async-start | bytes 524288 | tf_op jit(solution)/shard_map/all_to_all | solution.py:523
  28.2 10.4 %collective-permute-start.6 = (bf16[2,128,128]{2,1,0:T(8,128)(2,1)}, bf16[2,128,128]{2,1,0:T(8,128)(2,1)}, u32[]{:S(2)}, u32[]{:S(2)}) collective-permute-start(bf16[2,128,128]{2,1,0:T(8,128)(2,1)} %get-tuple-element.38.refs_4_), channel_id=1, source_target_pairs={{0,3},{1,2},{2,1},{3,0},{4,7},{5,6},{6,5},{7,4},{8,11},{9,10},{10,... | collective-permute-start | bytes 196616 | tf_op jit(solution)/shard_map/ppermute | solution.py:415
  29.4 9.3 %collective-permute-start.5 = (bf16[2,128,128]{2,1,0:T(8,128)(2,1)}, bf16[2,128,128]{2,1,0:T(8,128)(2,1)}, u32[]{:S(2)}, u32[]{:S(2)}) collective-permute-start(bf16[2,128,128]{2,1,0:T(8,128)(2,1)} %get-tuple-element.38.refs_4_), channel_id=1, source_target_pairs={{0,2},{1,3},{2,0},{3,1},{4,6},{5,7},{6,4},{7,5},{8,10},{9,11},{10,... | collective-permute-start | bytes 196616 | tf_op jit(solution)/shard_map/ppermute | solution.py:415
  29.9 8.7 %collective-permute-start.4 = (bf16[2,128,128]{2,1,0:T(8,128)(2,1)}, bf16[2,128,128]{2,1,0:T(8,128)(2,1)}, u32[]{:S(2)}, u32[]{:S(2)}) collective-permute-start(bf16[2,128,128]{2,1,0:T(8,128)(2,1)} %get-tuple-element.38.refs_4_), channel_id=1, source_target_pairs={{0,1},{1,0},{2,3},{3,2},{4,5},{5,4},{6,7},{7,6},{8,9},{9,8},{10,11... | collective-permute-start | bytes 196616 | tf_op jit(solution)/shard_map/ppermute | solution.py:415
  30.2 8.5 %collective-permute-start.7 = (bf16[128,128]{1,0:T(8,128)(2,1)}, bf16[128,128]{1,0:T(8,128)(2,1)}, u32[]{:S(2)}, u32[]{:S(2)}) collective-permute-start(bf16[128,128]{1,0:T(8,128)(2,1)} %get-tuple-element.39), channel_id=1, source_target_pairs={{28,0},{0,4},{4,8},{8,12},{12,16},{16,20},{20,24},{24,28},{29,1},{... | collective-permute-start | bytes 98312 | tf_op jit(solution)/shard_map/ppermute | solution.py:409
  41.5 7.5 %collective-permute-start.11 = (bf16[128,128]{1,0:T(8,128)(2,1)}, bf16[128,128]{1,0:T(8,128)(2,1)}, u32[]{:S(2)}, u32[]{:S(2)}) collective-permute-start(bf16[128,128]{1,0:T(8,128)(2,1)} %get-tuple-element.50), channel_id=1, source_target_pairs={{4,0},{8,4},{12,8},{16,12},{20,16},{24,20},{28,24},{0,28},{5,1},{9... | collective-permute-start | bytes 98312 | tf_op jit(solution)/shard_map/ppermute | solution.py:409
  43.0 12.7 %all-to-all-start.2 = ((bf16[8,128,128]{2,1,0:T(8,128)(2,1)}), bf16[8,128,128]{2,1,0:T(8,128)(2,1)}, u32[]{:S(2)}, u32[]{:S(2)}) async-start(bf16[8,128,128]{2,1,0:T(8,128)(2,1)} %get-tuple-element.43), calls=%async_computation.2 | async-start | bytes 524288 | tf_op jit(solution)/shard_map/all_to_all | solution.py:483
  47.1 5.3 %collective-permute-start.8 = (bf16[2,128,128]{2,1,0:T(8,128)(2,1)}, bf16[2,128,128]{2,1,0:T(8,128)(2,1)}, u32[]{:S(2)}, u32[]{:S(2)}) collective-permute-start(bf16[2,128,128]{2,1,0:T(8,128)(2,1)} %get-tuple-element.45), channel_id=1, source_target_pairs={{0,1},{1,0},{2,3},{3,2},{4,5},{5,4},{6,7},{7,6},{8,9},{9,8},{10,11... | collective-permute-start | bytes 196616 | tf_op jit(solution)/shard_map/ppermute | solution.py:415
  47.2 5.2 %collective-permute-start.9 = (bf16[2,128,128]{2,1,0:T(8,128)(2,1)}, bf16[2,128,128]{2,1,0:T(8,128)(2,1)}, u32[]{:S(2)}, u32[]{:S(2)}) collective-permute-start(bf16[2,128,128]{2,1,0:T(8,128)(2,1)} %get-tuple-element.46), channel_id=1, source_target_pairs={{0,2},{1,3},{2,0},{3,1},{4,6},{5,7},{6,4},{7,5},{8,10},{9,11},{10,... | collective-permute-start | bytes 196616 | tf_op jit(solution)/shard_map/ppermute | solution.py:415
  48.7 4.4 %collective-permute-start.10 = (bf16[2,128,128]{2,1,0:T(8,128)(2,1)}, bf16[2,128,128]{2,1,0:T(8,128)(2,1)}, u32[]{:S(2)}, u32[]{:S(2)}) collective-permute-start(bf16[2,128,128]{2,1,0:T(8,128)(2,1)} %get-tuple-element.47), channel_id=1, source_target_pairs={{0,3},{1,2},{2,1},{3,0},{4,7},{5,6},{6,5},{7,4},{8,11},{9,10},{10,... | collective-permute-start | bytes 196616 | tf_op jit(solution)/shard_map/ppermute | solution.py:415
  58.5 13.8 %all-to-all-start.3 = ((bf16[8,128,128]{2,1,0:T(8,128)(2,1)}), bf16[8,128,128]{2,1,0:T(8,128)(2,1)}, u32[]{:S(2)}, u32[]{:S(2)}) async-start(bf16[8,128,128]{2,1,0:T(8,128)(2,1)} %get-tuple-element.55), calls=%async_computation.3 | async-start | bytes 524288 | tf_op jit(solution)/shard_map/all_to_all | solution.py:523
  62.5 4.7 %collective-permute-start.14 = (bf16[2,128,128]{2,1,0:T(8,128)(2,1)}, bf16[2,128,128]{2,1,0:T(8,128)(2,1)}, u32[]{:S(2)}, u32[]{:S(2)}) collective-permute-start(bf16[2,128,128]{2,1,0:T(8,128)(2,1)} %get-tuple-element.52.refs_5_), channel_id=1, source_target_pairs={{0,3},{1,2},{2,1},{3,0},{4,7},{5,6},{6,5},{7,4},{8,11},{9,10},{10,... | collective-permute-start | bytes 196616 | tf_op jit(solution)/shard_map/ppermute | solution.py:415
  62.9 5.8 %collective-permute-start.13 = (bf16[2,128,128]{2,1,0:T(8,128)(2,1)}, bf16[2,128,128]{2,1,0:T(8,128)(2,1)}, u32[]{:S(2)}, u32[]{:S(2)}) collective-permute-start(bf16[2,128,128]{2,1,0:T(8,128)(2,1)} %get-tuple-element.52.refs_5_), channel_id=1, source_target_pairs={{0,2},{1,3},{2,0},{3,1},{4,6},{5,7},{6,4},{7,5},{8,10},{9,11},{10,... | collective-permute-start | bytes 196616 | tf_op jit(solution)/shard_map/ppermute | solution.py:415
  64.2 4.5 %collective-permute-start.12 = (bf16[2,128,128]{2,1,0:T(8,128)(2,1)}, bf16[2,128,128]{2,1,0:T(8,128)(2,1)}, u32[]{:S(2)}, u32[]{:S(2)}) collective-permute-start(bf16[2,128,128]{2,1,0:T(8,128)(2,1)} %get-tuple-element.52.refs_5_), channel_id=1, source_target_pairs={{0,1},{1,0},{2,3},{3,2},{4,5},{5,4},{6,7},{7,6},{8,9},{9,8},{10,11... | collective-permute-start | bytes 196616 | tf_op jit(solution)/shard_map/ppermute | solution.py:415
  64.5 7.8 %collective-permute-start.15 = (bf16[128,128]{1,0:T(8,128)(2,1)}, bf16[128,128]{1,0:T(8,128)(2,1)}, u32[]{:S(2)}, u32[]{:S(2)}) collective-permute-start(bf16[128,128]{1,0:T(8,128)(2,1)} %get-tuple-element.56), channel_id=1, source_target_pairs={{28,0},{0,4},{4,8},{8,12},{12,16},{16,20},{20,24},{24,28},{29,1},{... | collective-permute-start | bytes 98312 | tf_op jit(solution)/shard_map/ppermute | solution.py:409
